TPU v7x, 256 devices: a whole 4x4x8 slice. The times are simulated.
256 devices in a mesh: row: 16 (over y, z_hi), col: 16 (over x, z_lo, core).
Axes of the slice: x: 4, y: 4, z: 8 (z_hi: 4, z_lo: 2; z = z_hi * 2 + z_lo), core: 2. Of those that a mesh axis runs over, the one named last changes fastest.
Arguments:
- feat_one: bfloat16 [32768, 128], P(('row', 'col')), may hold values from -16 to 16
- feat_two: bfloat16 [32768, 128], P(('col', 'row')), may hold values from -16 to 16
- value_one: bfloat16 [32768, 128], P(('row', 'col')), may hold values from -6 to 6
- value_two: bfloat16 [32768, 128], P(('col', 'row')), may hold values from -6 to 6
Outputs:
- matched_one: float32 [32768, 128], P(('row', 'col'))
- flow_one: float32 [2, 32768], P(None, ('row', 'col'))
- matched_two: float32 [32768, 128], P(('col', 'row'))
- flow_two: float32 [2, 32768], P(None, ('col', 'row'))
All inputs are finite; a program needn't handle non-finite values.
Results may differ from a plain program's by a relative error of at most 0.0011.
Values may be sent and summed in bfloat16 or wider, within the bound.
No kernel may reach another device: no remote copies, remote signals or barrier semaphores. Data moves between devices by JAX's collectives and lax.ppermute only.
A program may use at most 128 MiB of HBM per device.

v0:
```python
import math

import jax
import jax.numpy as jnp
from jax import lax
from jax.sharding import PartitionSpec as P

GRID_W = 256


def merged(value, axis, join):
    pieces = jax.tree.map(lambda part: lax.all_gather(part, axis), value)
    head = jax.tree.map(lambda part: part[0], pieces)
    tail = jax.tree.map(lambda part: part[1:], pieces)
    total, _ = lax.scan(lambda total, section: (join(total, section), None), head, tail)
    return total


def token_coords(start, count, total):
    index = start + lax.iota(jnp.int32, count)
    across = (index % GRID_W).astype(jnp.float32) / GRID_W
    down = (index // GRID_W).astype(jnp.float32) / (total // GRID_W)
    return (across, down)


def flash_merge(first, second):
    peak_a, total_a, acc_a, across_a, down_a = first
    peak_b, total_b, acc_b, across_b, down_b = second
    peak = jnp.maximum(peak_a, peak_b)
    factor_a = jnp.exp(peak_a - peak)
    factor_b = jnp.exp(peak_b - peak)
    return (
        peak,
        total_a * factor_a + total_b * factor_b,
        acc_a * factor_a[:, None] + acc_b * factor_b[:, None],
        across_a * factor_a + across_b * factor_b,
        down_a * factor_a + down_b * factor_b,
    )


def finish(total, acc, across, down, own_across, own_down):
    matched = acc / total[:, None]
    flow = jnp.stack([across / total - own_across, down / total - own_down])
    return (matched, flow)


def own_rows(stats, start, shard):
    return tuple((lax.dynamic_slice_in_dim(piece, start, shard, 0) for piece in stats))


def body(feat_one, feat_two, value_one, value_two):
    shard = feat_one.shape[0]
    width = feat_one.shape[1]
    rows_count = lax.axis_size("row")
    cols_count = lax.axis_size("col")
    total = shard * rows_count * cols_count
    block = min(512, shard * min(rows_count, cols_count))
    src_feat, src_value = (
        lax.all_gather(feat_one, "col", axis=0, tiled=True),
        lax.all_gather(value_one, "col", axis=0, tiled=True),
    )
    tgt_feat, tgt_value = (
        lax.all_gather(feat_two, "row", axis=0, tiled=True),
        lax.all_gather(value_two, "row", axis=0, tiled=True),
    )
    n_src = src_feat.shape[0]
    n_tgt = tgt_feat.shape[0]
    row_index = lax.axis_index("row")
    col_index = lax.axis_index("col")
    src_start = row_index * n_src
    tgt_start = col_index * n_tgt
    tgt_across, tgt_down = token_coords(tgt_start, n_tgt, total)
    tgt_blocks = n_tgt // block
    across_blocks = tgt_across.reshape(tgt_blocks, block)
    down_blocks = tgt_down.reshape(tgt_blocks, block)
    value_blocks = tgt_value.reshape(tgt_blocks, block, width)
    scale = 1.0 / math.sqrt(width)

    def sweep(carry, block_index):
        start = block_index * block
        rows_feat = lax.dynamic_slice_in_dim(src_feat, start, block, 0)
        rows_value = lax.dynamic_slice_in_dim(src_value, start, block, 0)
        rows_across, rows_down = token_coords(src_start + start, block, total)
        scores = (
            lax.dot_general(
                rows_feat, tgt_feat, (((1,), (1,)), ((), ())), preferred_element_type=jnp.float32
            )
            * scale
        )
        tiled = scores.reshape(block, tgt_blocks, block)
        row_peak = jnp.max(tiled, axis=2)
        row_weight = jnp.exp(tiled - row_peak[:, :, None]).astype(jnp.bfloat16)
        weight_f = row_weight.astype(jnp.float32)
        part_total = jnp.sum(weight_f, axis=2)
        part_across = jnp.sum(weight_f * across_blocks[None], axis=2)
        part_down = jnp.sum(weight_f * down_blocks[None], axis=2)
        part_acc = jnp.einsum(
            "rkt,ktc->rkc", row_weight, value_blocks, preferred_element_type=jnp.float32
        )
        row_top = jnp.max(row_peak, axis=1)
        factor = jnp.exp(row_peak - row_top[:, None])
        row_out = (
            row_top,
            jnp.sum(factor * part_total, axis=1),
            jnp.sum(factor[:, :, None] * part_acc, axis=1),
            jnp.sum(factor * part_across, axis=1),
            jnp.sum(factor * part_down, axis=1),
        )
        col_peak = jnp.max(scores, axis=0)
        col_weight = jnp.exp(scores - col_peak[None]).astype(jnp.bfloat16)
        cweight_f = col_weight.astype(jnp.float32)
        col_acc = lax.dot_general(
            col_weight, rows_value, (((0,), (0,)), ((), ())), preferred_element_type=jnp.float32
        )
        col_part = (
            col_peak,
            jnp.sum(cweight_f, axis=0),
            col_acc,
            jnp.sum(cweight_f * rows_across[:, None], axis=0),
            jnp.sum(cweight_f * rows_down[:, None], axis=0),
        )
        return (flash_merge(carry, col_part), row_out)

    init = (
        jnp.full((n_tgt,), -jnp.inf, jnp.float32),
        jnp.zeros((n_tgt,), jnp.float32),
        jnp.zeros((n_tgt, width), jnp.float32),
        jnp.zeros((n_tgt,), jnp.float32),
        jnp.zeros((n_tgt,), jnp.float32),
    )
    col_stats, row_out = lax.scan(sweep, init, jnp.arange(n_src // block, dtype=jnp.int32))
    row_stats = (
        row_out[0].reshape(n_src),
        row_out[1].reshape(n_src),
        row_out[2].reshape(n_src, width),
        row_out[3].reshape(n_src),
        row_out[4].reshape(n_src),
    )
    one_across, one_down = token_coords(src_start + col_index * shard, shard, total)
    two_across, two_down = token_coords(tgt_start + row_index * shard, shard, total)
    row_whole = merged(row_stats, "col", flash_merge)
    col_whole = merged(col_stats, "row", flash_merge)
    row_mine = own_rows(row_whole, col_index * shard, shard)
    col_mine = own_rows(col_whole, row_index * shard, shard)
    row_total, row_acc, row_across, row_down = (row_mine[1], row_mine[2], row_mine[3], row_mine[4])
    col_total, col_acc, col_across, col_down = (col_mine[1], col_mine[2], col_mine[3], col_mine[4])
    matched_one, flow_one = finish(row_total, row_acc, row_across, row_down, one_across, one_down)
    matched_two, flow_two = finish(col_total, col_acc, col_across, col_down, two_across, two_down)
    return (matched_one, flow_one, matched_two, flow_two)


def solution(mesh):
    return jax.shard_map(
        body,
        mesh=mesh,
        in_specs=(
            P(("row", "col"), None),
            P(("col", "row"), None),
            P(("row", "col"), None),
            P(("col", "row"), None),
        ),
        out_specs=(
            P(("row", "col"), None),
            P(None, ("row", "col")),
            P(("col", "row"), None),
            P(None, ("col", "row")),
        ),
        check_vma=False,
    )
```

profile of v0, /device:TPU:1, one launch (start us, length us, event | category | flops | bytes accessed | tf_op | source)
XLA Modules:
  0.0 647.2 jit_solution(12044280065613223616)
XLA Ops:
  7.3 25.1 %all_gather.57 = bf16[2048,128]{1,0:T(8,128)(2,1)} all-gather(bf16[128,128]{1,0:T(8,128)(2,1)} %param.10), channel_id=1, replica_groups=mesh['row'=16,'col'=16] {'col'}, dimensions={0}, use_global_device_ids=true | all-gather | bytes 557056 | tf_op jit(solution)/shard_map/all_gather | solution.py:59
  32.4 44.2 %all_gather.58 = bf16[2048,128]{1,0:T(8,128)(2,1)} all-gather(bf16[128,128]{1,0:T(8,128)(2,1)} %param.11), channel_id=1, replica_groups=mesh['row'=16,'col'=16] {'row'}, dimensions={0}, use_global_device_ids=true | all-gather | bytes 557056 | tf_op jit(solution)/shard_map/all_gather | solution.py:63
  76.6 28.0 %all_gather.59 = bf16[2048,128]{1,0:T(8,128)(2,1)} all-gather(bf16[128,128]{1,0:T(8,128)(2,1)} %param.12), channel_id=1, replica_groups=mesh['row'=16,'col'=16] {'col'}, dimensions={0}, use_global_device_ids=true | all-gather | bytes 557056 | tf_op jit(solution)/shard_map/all_gather | solution.py:60
  104.6 36.9 %all_gather.60 = bf16[2048,128]{1,0:T(8,128)(2,1)} all-gather(bf16[128,128]{1,0:T(8,128)(2,1)} %param.13), channel_id=1, replica_groups=mesh['row'=16,'col'=16] {'row'}, dimensions={0}, use_global_device_ids=true | all-gather | bytes 557056 | tf_op jit(solution)/shard_map/all_gather | solution.py:64
  141.5 126.1 %while.71 = (s32[]{:T(128)}, f32[2048]{0:T(1024)S(1)}, f32[2048]{0:T(1024)S(1)}, f32[2048,128]{1,0:T(8,128)S(1)}, f32[2048]{0:T(1024)S(1)}, /*index=5*/f32[2048]...) while((s32[]{:T(128)}, f32[2048]{0:T(1024)S(1)}, ...), condition=%wide.region_14.15_spmd.clone.clone.clone, body=%wide.region_0.14_spmd.clone.clone.clone.sunk | while | flops 827875328 | bytes 38144836 | solution.py:131
  142.7 3.8 fusion.81
  146.5 6.0 reshape.130
  152.5 2.8 reduce_max.52
  155.4 7.1 %fusion.87 = (f32[512,4]{1,0:T(8,128)S(1)}, f32[512,4]{1,0:T(8,128)S(1)}, f32[512,4]{1,0:T(8,128)S(1)}, bf16[512,4,512]{2,1,0:T(4,128)(2,1)S(1)}) fusion(f32[4,512]{1,0:T(4,128)S(1)} %mul.484, f32[4,512]{1,0:T(4,128)S(1)} %mul.485, f32[512,4,512]{2,1,0:T(4,128)} %reshape.130, f32[512,4]{1,0:T(8,128)S(1)} %reduce_max.52), kind=kLoop, calls=%fused_computation.33.clone.1 | loop fusion | flops 8382464 | bytes 6340608 | tf_op jit(solution)/shard_map/while/body/eval_jaxpr/reduce_sum | solution.py:96
  167.3 3.1 fusion.82
  170.5 2.5 fusion.85
  174.2 3.8 fusion.81
  178.0 6.0 reshape.130
  184.0 2.8 reduce_max.52
  186.9 7.1 %fusion.87 = (f32[512,4]{1,0:T(8,128)S(1)}, f32[512,4]{1,0:T(8,128)S(1)}, f32[512,4]{1,0:T(8,128)S(1)}, bf16[512,4,512]{2,1,0:T(4,128)(2,1)S(1)}) fusion(f32[4,512]{1,0:T(4,128)S(1)} %mul.484, f32[4,512]{1,0:T(4,128)S(1)} %mul.485, f32[512,4,512]{2,1,0:T(4,128)} %reshape.130, f32[512,4]{1,0:T(8,128)S(1)} %reduce_max.52), kind=kLoop, calls=%fused_computation.33.clone.1 | loop fusion | flops 8382464 | bytes 6340608 | tf_op jit(solution)/shard_map/while/body/eval_jaxpr/reduce_sum | solution.py:96
  198.8 3.1 fusion.82
  202.0 2.5 fusion.85
  205.8 3.8 fusion.81
  209.5 6.0 reshape.130
  215.6 2.8 reduce_max.52
  218.5 7.1 %fusion.87 = (f32[512,4]{1,0:T(8,128)S(1)}, f32[512,4]{1,0:T(8,128)S(1)}, f32[512,4]{1,0:T(8,128)S(1)}, bf16[512,4,512]{2,1,0:T(4,128)(2,1)S(1)}) fusion(f32[4,512]{1,0:T(4,128)S(1)} %mul.484, f32[4,512]{1,0:T(4,128)S(1)} %mul.485, f32[512,4,512]{2,1,0:T(4,128)} %reshape.130, f32[512,4]{1,0:T(8,128)S(1)} %reduce_max.52), kind=kLoop, calls=%fused_computation.33.clone.1 | loop fusion | flops 8382464 | bytes 6340608 | tf_op jit(solution)/shard_map/while/body/eval_jaxpr/reduce_sum | solution.py:96
  230.3 3.1 fusion.82
  233.5 2.5 fusion.85
  237.3 3.8 fusion.81
  241.0 6.0 reshape.130
  247.1 2.8 reduce_max.52
  250.0 7.1 %fusion.87 = (f32[512,4]{1,0:T(8,128)S(1)}, f32[512,4]{1,0:T(8,128)S(1)}, f32[512,4]{1,0:T(8,128)S(1)}, bf16[512,4,512]{2,1,0:T(4,128)(2,1)S(1)}) fusion(f32[4,512]{1,0:T(4,128)S(1)} %mul.484, f32[4,512]{1,0:T(4,128)S(1)} %mul.485, f32[512,4,512]{2,1,0:T(4,128)} %reshape.130, f32[512,4]{1,0:T(8,128)S(1)} %reduce_max.52), kind=kLoop, calls=%fused_computation.33.clone.1 | loop fusion | flops 8382464 | bytes 6340608 | tf_op jit(solution)/shard_map/while/body/eval_jaxpr/reduce_sum | solution.py:96
  261.8 3.1 fusion.82
  265.0 2.5 fusion.85
  269.4 37.0 %all-gather = f32[32768]{0:T(1024)S(1)} all-gather(f32[2048]{0:T(1024)S(1)} %get-tuple-element.378), channel_id=2, replica_groups=mesh['row'=16,'col'=16] {'row'}, dimensions={0}, use_global_device_ids=true | all-gather | bytes 139264 | tf_op jit(solution)/shard_map/all_gather | solution.py:12
  306.4 36.2 %all-gather.1 = f32[32768]{0:T(1024)S(1)} all-gather(f32[2048]{0:T(1024)S(1)} %get-tuple-element.379), channel_id=3, replica_groups=mesh['row'=16,'col'=16] {'row'}, dimensions={0}, use_global_device_ids=true | all-gather | bytes 139264 | tf_op jit(solution)/shard_map/all_gather | solution.py:12
  342.6 41.4 %all-gather.3 = f32[32768]{0:T(1024)S(1)} all-gather(f32[2048]{0:T(1024)S(1)} %get-tuple-element.381), channel_id=5, replica_groups=mesh['row'=16,'col'=16] {'row'}, dimensions={0}, use_global_device_ids=true | all-gather | bytes 139264 | tf_op jit(solution)/shard_map/all_gather | solution.py:12
  384.1 39.5 %all-gather.4 = f32[32768]{0:T(1024)S(1)} all-gather(f32[2048]{0:T(1024)S(1)} %get-tuple-element.382), channel_id=6, replica_groups=mesh['row'=16,'col'=16] {'row'}, dimensions={0}, use_global_device_ids=true | all-gather | bytes 139264 | tf_op jit(solution)/shard_map/all_gather | solution.py:12
  423.6 65.8 %all-gather.5 = f32[16,1,2048]{2,1,0:T(1,128)S(1)} all-gather(f32[1,1,2048]{2,1,0:T(1,128)S(1)} %reshape.102), channel_id=1, replica_groups=mesh['row'=16,'col'=16] {'col'}, dimensions={0}, use_global_device_ids=true | all-gather | bytes 139264 | tf_op jit(solution)/shard_map/all_gather | solution.py:12
  489.4 20.1 %all-gather.6 = f32[16,1,2048]{2,1,0:T(1,128)S(1)} all-gather(f32[1,1,2048]{2,1,0:T(1,128)S(1)} %reshape.104), channel_id=1, replica_groups=mesh['row'=16,'col'=16] {'col'}, dimensions={0}, use_global_device_ids=true | all-gather | bytes 139264 | tf_op jit(solution)/shard_map/all_gather | solution.py:12
  509.6 17.7 %all-gather.7 = f32[16,1,2048]{2,1,0:T(1,128)S(1)} all-gather(f32[1,1,2048]{2,1,0:T(1,128)S(1)} %reshape.106), channel_id=1, replica_groups=mesh['row'=16,'col'=16] {'col'}, dimensions={0}, use_global_device_ids=true | all-gather | bytes 139264 | tf_op jit(solution)/shard_map/all_gather | solution.py:12
  527.3 19.2 %all-gather.8 = f32[16,1,2048]{2,1,0:T(1,128)S(1)} all-gather(f32[1,1,2048]{2,1,0:T(1,128)S(1)} %reshape.108), channel_id=1, replica_groups=mesh['row'=16,'col'=16] {'col'}, dimensions={0}, use_global_device_ids=true | all-gather | bytes 139264 | tf_op jit(solution)/shard_map/all_gather | solution.py:12
  546.9 11.2 %slice.115 = f32[30720,128]{1,0:T(8,128)} slice(f32[32768,128]{1,0:T(8,128)} %all-gather.14.cloned.1.call-done), slice={[2048:32768], [0:128]} | slice | bytes 31457280 | tf_op jit(solution)/shard_map/slice | solution.py:14
  558.1 33.2 %while.70 = (s32[]{:T(128)}, f32[2048]{0:T(1024)S(1)}, f32[2048]{0:T(1024)S(1)}, f32[2048,128]{1,0:T(8,128)S(1)}, f32[2048]{0:T(1024)S(1)}, /*index=5*/f32[2048]...) while((s32[]{:T(128)}, f32[2048]{0:T(1024)S(1)}, ...), condition=%wide.region_18.19_spmd, body=%wide.region_17.18_spmd.sunk | while | flops 811010 | bytes 3358849 | solution.py:15
  558.2 2.1 fusion.74
  560.5 2.2 fusion.74
  567.2 2.1 fusion.74
  571.6 2.2 fusion.74
  576.1 2.1 fusion.74
  582.7 2.1 fusion.74
  589.3 2.1 fusion.74
  591.4 12.4 %slice.105 = f32[15,2048,128]{2,1,0:T(8,128)} slice(f32[16,2048,128]{2,1,0:T(8,128)} %all-gather.12.cloned.1.call-done), slice={[1:16], [0:2048], [0:128]} | slice | bytes 31457280 | tf_op jit(solution)/shard_map/slice | solution.py:14
  605.2 33.0 %while.69 = (s32[]{:T(128)}, f32[2048]{0:T(1024)S(1)}, f32[2048]{0:T(1024)S(1)}, f32[2048,128]{1,0:T(8,128)S(1)}, f32[2048]{0:T(1024)S(1)}, /*index=5*/f32[2048]...) while((s32[]{:T(128)}, f32[2048]{0:T(1024)S(1)}, ...), condition=%wide.region_16.17_spmd, body=%wide.region_15.16_spmd.sunk | while | flops 811010 | bytes 3358849 | solution.py:15
  (272 shorter events, 77.5 us)
Async XLA Ops:
  7.2 539.7 %all-gather.14.cloned.1.call-start = ((), (), s32[]{:S(2)}) async-start(), calls=%async_computation.1 | async-start | bytes 17825792 | tf_op jit(solution)/shard_map/all_gather | solution.py:12
  267.6 1.0 copy-start
  268.6 322.8 %all-gather.12.cloned.1.call-start = ((), (), s32[]{:S(2)}) async-start(), calls=%async_computation | async-start | bytes 17825792 | tf_op jit(solution)/shard_map/all_gather | solution.py:12
  489.4 68.7 %copy-start.1 = (f32[16,1,2048]{2,1,0:T(1,128)}, f32[16,1,2048]{2,1,0:T(1,128)S(1)}, u32[]{:S(2)}) copy-start(f32[16,1,2048]{2,1,0:T(1,128)S(1)} %all-gather.5) | copy-start | bytes 393220
  509.5 48.6 %copy-start.2 = (f32[16,1,2048]{2,1,0:T(1,128)}, f32[16,1,2048]{2,1,0:T(1,128)S(1)}, u32[]{:S(2)}) copy-start(f32[16,1,2048]{2,1,0:T(1,128)S(1)} %all-gather.6) | copy-start | bytes 393220
  527.3 30.8 %copy-start.3 = (f32[16,1,2048]{2,1,0:T(1,128)}, f32[16,1,2048]{2,1,0:T(1,128)S(1)}, u32[]{:S(2)}) copy-start(f32[16,1,2048]{2,1,0:T(1,128)S(1)} %all-gather.7) | copy-start | bytes 393220
  546.6 11.6 %copy-start.4 = (f32[16,1,2048]{2,1,0:T(1,128)}, f32[16,1,2048]{2,1,0:T(1,128)S(1)}, u32[]{:S(2)}) copy-start(f32[16,1,2048]{2,1,0:T(1,128)S(1)} %all-gather.8) | copy-start | bytes 393220
  546.9 11.2 %slice-start = ((f32[32768,128]{1,0:T(8,128)}), f32[2048,128]{1,0:T(8,128)S(1)}, s32[]{:S(2)}) async-start(f32[32768,128]{1,0:T(8,128)} %all-gather.14.cloned.1.call-done), calls=%async_computation.2 | async-start | bytes 2097152 | tf_op jit(solution)/shard_map/slice | solution.py:13
  591.4 13.8 %slice-start.1 = ((f32[16,1,2048]{2,1,0:T(1,128)}), f32[1,1,2048]{2,1,0:T(1,128)S(1)}, s32[]{:S(2)}) async-start(f32[16,1,2048]{2,1,0:T(1,128)} %copy-done.1), calls=%async_computation.3 | async-start | bytes 16384 | tf_op jit(solution)/shard_map/slice | solution.py:13
  591.4 13.8 %slice-start.2 = ((f32[16,1,2048]{2,1,0:T(1,128)}), f32[1,1,2048]{2,1,0:T(1,128)S(1)}, s32[]{:S(2)}) async-start(f32[16,1,2048]{2,1,0:T(1,128)} %copy-done.2), calls=%async_computation.4 | async-start | bytes 16384 | tf_op jit(solution)/shard_map/slice | solution.py:13
  591.4 13.8 %slice-start.3 = ((f32[16,1,2048]{2,1,0:T(1,128)}), f32[1,1,2048]{2,1,0:T(1,128)S(1)}, s32[]{:S(2)}) async-start(f32[16,1,2048]{2,1,0:T(1,128)} %copy-done.3), calls=%async_computation.5 | async-start | bytes 16384 | tf_op jit(solution)/shard_map/slice | solution.py:13
  591.4 13.8 %slice-start.4 = ((f32[16,1,2048]{2,1,0:T(1,128)}), f32[1,1,2048]{2,1,0:T(1,128)S(1)}, s32[]{:S(2)}) async-start(f32[16,1,2048]{2,1,0:T(1,128)} %copy-done.4), calls=%async_computation.6 | async-start | bytes 16384 | tf_op jit(solution)/shard_map/slice | solution.py:13
Sparse Core Ops, SparseCore 0:
  268.7 212.5 all-gather.13
  483.1 96.1 all-gather.11
where the time goes:
time: 650 us; the launch traced here: 647 us
  blocking collectives  411 us (63%)
  other arithmetic  122 us (19%)
  local copies, waits for them, and re-layouts  62 us (10%)
  matrix products  32.4 us (5%)
  between operations  14.4 us (2%)
    all_gather x8, blocking collectives, merged(): pieces = jax.tree.map(lambda part: lax.all_gather(part, axis), value)  277 us
    add x30, other arithmetic, flash_merge(): acc_a * factor_a[:, None] + acc_b * factor_b[:, None]  62.8 us
    all_gather x1, blocking collectives, body(): lax.all_gather(feat_two, 'row', axis=0, tiled=True)  44.2 us
    all_gather x1, blocking collectives, body(): lax.all_gather(value_two, 'row', axis=0, tiled=True)  36.9 us
    reduce_sum x4, other arithmetic, sweep(): part_down = jnp.sum(weight_f * down_blocks[None], axis=2)  28.4 us
    all_gather x1, blocking collectives, body(): lax.all_gather(value_one, 'col', axis=0, tiled=True)  28 us
    all_gather x1, blocking collectives, body(): lax.all_gather(feat_one, 'col', axis=0, tiled=True)  25.1 us
    reshape x4, local copies, waits for them, and re-layouts, sweep(): tiled = scores.reshape(block, tgt_blocks, block)  24.1 us
  transfers between devices with their start and end apart: 2, of which 0 were waited for; matrix products, arithmetic and copies ran while one was open for 7% of the time, Pallas kernels for 0%

commit v1 on v0

v1 whole, which is shorter than its diff:
```python
import math

import jax
import jax.numpy as jnp
from jax import lax
from jax.experimental import pallas as pl
from jax.experimental.pallas import tpu as pltpu
from jax.sharding import PartitionSpec as P

GRID_W = 256
SUB = 4
SHARD = 128
WIDTH = 128
BLOCK = SUB * SHARD
ROWS = WIDTH + 8
AUG = WIDTH + 16
TOTAL_ROW, ACROSS_ROW, DOWN_ROW, PEAK_ROW = 0, 1, 2, 3
VMEM = pl.BlockSpec(memory_space=pltpu.VMEM)


def slow_shift(axis, value, step):
    pairs = [(i, ((i // SUB + step) % SUB) * SUB + i % SUB) for i in range(SUB * SUB)]
    return lax.ppermute(value, axis, pairs)


def fast_shift(axis, value, step):
    pairs = [(i, (i // SUB) * SUB + (i % SUB + step) % SUB) for i in range(SUB * SUB)]
    return lax.ppermute(value, axis, pairs)


def fast_swap(axis, value, step):
    return lax.ppermute(value, axis, [(i, i ^ step) for i in range(SUB * SUB)])


def pack_kernel(feat_one, value_one, feat_two, value_two, out_one, out_two):
    for feat, value, out in ((feat_one, value_one, out_one), (feat_two, value_two, out_two)):
        out[:, :WIDTH] = feat[...]
        out[:, WIDTH:] = value[...].astype(jnp.float32).T.astype(jnp.bfloat16)


def piece_coords(start, total):
    across = (start % GRID_W).astype(jnp.float32) / GRID_W
    down = (start // GRID_W).astype(jnp.float32) / (total // GRID_W)
    return across, down


def score_kernel(total, scale, *refs):
    ins, outs, (feats, values, acc) = refs[:8], refs[8:16], refs[16:]
    row, col = lax.axis_index("row"), lax.axis_index("col")
    sub = lax.broadcasted_iota(jnp.int32, (AUG - WIDTH, SHARD), 0)
    lane = lax.broadcasted_iota(jnp.int32, (AUG - WIDTH, SHARD), 1).astype(jnp.float32) / GRID_W
    for side in range(2):
        group, member = (row, col) if side == 0 else (col, row)
        for block in range(SUB):
            source = ins[side * SUB + block]
            slow = (member // SUB + block) % SUB
            for piece in range(SUB):
                fast = member % SUB
                fast = fast ^ piece if side == 0 else (fast + piece) % SUB
                start = ((group * SUB + slow) * SUB + fast) * SHARD
                across, down = piece_coords(start, total)
                extra = jnp.where(sub == DOWN_ROW, down, 0.0)
                extra = jnp.where(sub == ACROSS_ROW, across + lane, extra)
                extra = jnp.where(sub == TOTAL_ROW, 1.0, extra)
                span = slice(piece * SHARD, (piece + 1) * SHARD)
                feats[side * SUB + block, span, :] = source[piece, :, :WIDTH]
                values[side * SUB + block, :WIDTH, span] = source[piece, :, WIDTH:]
                values[side * SUB + block, WIDTH:, span] = extra.astype(jnp.bfloat16)

    def step(index, _):
        other = (1 - index // SUB) * SUB
        query = feats[index]
        peaks, parts = [], []
        for block in range(SUB):
            score = lax.dot_general(
                feats[other + block], query, (((1,), (1,)), ((), ())),
                preferred_element_type=jnp.float32,
            ) * scale
            peak = jnp.max(score, axis=0, keepdims=True)
            weight = jnp.exp2(score - peak).astype(jnp.bfloat16)
            parts.append(
                jnp.dot(values[other + block], weight, preferred_element_type=jnp.float32)[:ROWS]
            )
            peaks.append(peak)
        store_merged(acc.at[index], peaks, parts)
        return 0

    lax.fori_loop(0, 2 * SUB, step, 0)
    for index in range(2 * SUB):
        outs[index][...] = acc[index]


def merge(peaks, parts):
    top = peaks[0]
    for peak in peaks[1:]:
        top = jnp.maximum(top, peak)
    whole = None
    for peak, part in zip(peaks, parts):
        term = part * jnp.exp2(peak - top)
        whole = term if whole is None else whole + term
    return top, whole


def store_merged(out, peaks, parts):
    top, whole = merge(peaks, parts)
    sub = lax.broadcasted_iota(jnp.int32, (ROWS - WIDTH, top.shape[1]), 0)
    out[:WIDTH, :] = whole[:WIDTH]
    out[WIDTH:, :] = jnp.where(sub == PEAK_ROW, top, whole[WIDTH:])


def peak_of(part):
    return part[WIDTH + PEAK_ROW : WIDTH + PEAK_ROW + 1, :]


def merge_kernel(*refs):
    ins, outs = refs[: 2 * SUB], refs[2 * SUB :]
    for side in range(2):
        for piece in range(SUB):
            span = slice(piece * SHARD, (piece + 1) * SHARD)
            parts = [ref[:, span] for ref in ins[side * SUB : (side + 1) * SUB]]
            store_merged(outs[side * SUB + piece], [peak_of(part) for part in parts], parts)


def finish_kernel(total, *refs):
    ins, outs = refs[: 2 * SUB], refs[2 * SUB :]
    row, col = lax.axis_index("row"), lax.axis_index("col")
    lane = lax.broadcasted_iota(jnp.int32, (1, SHARD), 1).astype(jnp.float32) / GRID_W
    for side in range(2):
        group, member = (row, col) if side == 0 else (col, row)
        own_across, own_down = piece_coords((group * SUB * SUB + member) * SHARD, total)
        parts = [ref[...] for ref in ins[side * SUB : (side + 1) * SUB]]
        _, whole = merge([peak_of(part) for part in parts], parts)
        inverse = 1.0 / whole[WIDTH + TOTAL_ROW : WIDTH + TOTAL_ROW + 1, :]
        matched, flow = outs[2 * side], outs[2 * side + 1]
        matched[...] = (whole[:WIDTH] * inverse).T
        across = whole[WIDTH + ACROSS_ROW : WIDTH + ACROSS_ROW + 1, :] * inverse
        down = whole[WIDTH + DOWN_ROW : WIDTH + DOWN_ROW + 1, :] * inverse
        flow[0:1, :] = across - (own_across + lane)
        flow[1:2, :] = down - own_down


def call(kernel, shapes, args, scratch=(), cost=None):
    return pl.pallas_call(
        kernel,
        out_shape=shapes,
        in_specs=[VMEM] * len(args),
        out_specs=[VMEM] * len(shapes),
        scratch_shapes=list(scratch),
        compiler_params=pltpu.CompilerParams(vmem_limit_bytes=48 << 20),
        cost_estimate=cost,
    )(*args)


def body(feat_one, feat_two, value_one, value_two):
    total = feat_one.shape[0] * lax.axis_size("row") * lax.axis_size("col")
    scale = math.log2(math.e) / math.sqrt(WIDTH)
    packed = jax.ShapeDtypeStruct((SHARD, 2 * WIDTH), jnp.bfloat16)
    own_one, own_two = call(
        pack_kernel, [packed] * 2, (feat_one, value_one, feat_two, value_two)
    )
    one = [own_one] + [fast_swap("col", own_one, step) for step in range(1, SUB)]
    two = [own_two] + [fast_shift("row", own_two, -step) for step in range(1, SUB)]
    one, two = jnp.stack(one), jnp.stack(two)
    ones = [one] + [slow_shift("col", one, -step) for step in range(1, SUB)]
    twos = [two] + [slow_shift("row", two, -step) for step in range(1, SUB)]

    def score(*refs):
        score_kernel(total, scale, *refs)

    def finish(*refs):
        finish_kernel(total, *refs)

    wide = jax.ShapeDtypeStruct((ROWS, BLOCK), jnp.float32)
    narrow = jax.ShapeDtypeStruct((ROWS, SHARD), jnp.float32)
    parts = call(
        score,
        [wide] * (2 * SUB),
        (*ones, *twos),
        scratch=[
            pltpu.VMEM((2 * SUB, BLOCK, WIDTH), jnp.bfloat16),
            pltpu.VMEM((2 * SUB, AUG, BLOCK), jnp.bfloat16),
            pltpu.VMEM((2 * SUB, ROWS, BLOCK), jnp.float32),
        ],
    )
    rows, cols = parts[:SUB], parts[SUB:]
    rows = [rows[0]] + [slow_shift("col", rows[step], step) for step in range(1, SUB)]
    cols = [cols[0]] + [slow_shift("row", cols[step], step) for step in range(1, SUB)]
    parts = call(merge_kernel, [narrow] * (2 * SUB), (*rows, *cols))
    rows, cols = parts[:SUB], parts[SUB:]
    rows = [rows[0]] + [fast_swap("col", rows[step], step) for step in range(1, SUB)]
    cols = [cols[0]] + [fast_shift("row", cols[step], step) for step in range(1, SUB)]
    matched = jax.ShapeDtypeStruct((SHARD, WIDTH), jnp.float32)
    flow = jax.ShapeDtypeStruct((2, SHARD), jnp.float32)
    return tuple(call(finish, [matched, flow] * 2, (*rows, *cols)))


def solution(mesh):
    return jax.shard_map(
        body,
        mesh=mesh,
        in_specs=(
            P(("row", "col"), None),
            P(("col", "row"), None),
            P(("row", "col"), None),
            P(("col", "row"), None),
        ),
        out_specs=(
            P(("row", "col"), None),
            P(None, ("row", "col")),
            P(("col", "row"), None),
            P(None, ("col", "row")),
        ),
        check_vma=False,
    )
```

time: 650 us -> 98.2 us (0.15)
  blocking collectives: 411 us -> 0 us
  other arithmetic: 122 us -> 0.07 us
  local copies, waits for them, and re-layouts: 62 us -> 3.02 us
  starting transfers between devices: 0.08 us -> 43.8 us
  matrix products: 32.4 us -> 0 us
  waiting for transfers between devices: 0.75 us -> 31.2 us
  Pallas kernels: 0 us -> 18.5 us
  between operations: 14.4 us -> 0.69 us
    all_gather x12 -> x0, blocking collectives: 411 us -> none  [the longest x8 277 us: merged(): pieces = jax.tree.map(lambda part: lax.all_gather(part, axis), value)]
    add x98 -> x0, other arithmetic: 63.6 us -> none  [the longest x30 62.8 us: flash_merge(): acc_a * factor_a[:, None] + acc_b * factor_b[:, None]]
    reduce_sum x12 -> x0, other arithmetic: 44.9 us -> none  [the longest x4 28.4 us: sweep(): part_down = jnp.sum(weight_f * down_blocks[None], axis=2)]
    ppermute x0 -> x24, starting transfers between devices: none -> 43.8 us  [the longest x12 18.8 us: slow_shift(): return lax.ppermute(value, axis, pairs)]
    dot_general x12 -> x0, matrix products: 32.4 us -> none  [the longest x4 15.1 us: sweep(): lax.dot_general(rows_feat, tgt_feat, (((1,), (1,)), ((), ())), preferred_...]
    ppermute x0 -> x24, waiting for transfers between devices: none -> 31.2 us  [the longest x12 20 us: slow_shift(): return lax.ppermute(value, axis, pairs)]
    reshape x4 -> x0, local copies, waits for them, and re-layouts: 24.1 us -> none  [sweep(): tiled = scores.reshape(block, tgt_blocks, block)]
    slice x28 -> x0, local copies, waits for them, and re-layouts: 23.7 us -> none  [the longest x14 23.7 us: merged(): tail = jax.tree.map(lambda part: part[1:], pieces)]
  transfers between devices with their start and end apart: 2 -> 24, of which waited for: 0 -> 12; matrix products, arithmetic and copies ran while one was open for 7% -> 0% of each run, Pallas kernels for 0% -> 0%
where the time goes in v1:
time: 98.2 us; the launch traced here: 97.3 us
  starting transfers between devices  43.8 us (45%)
  waiting for transfers between devices  31.2 us (32%)
  Pallas kernels  18.5 us (19%)
  local copies, waits for them, and re-layouts  3.02 us (3%)
    ppermute x12, waiting for transfers between devices, slow_shift(): return lax.ppermute(value, axis, pairs)  20 us
    ppermute x12, starting transfers between devices, slow_shift(): return lax.ppermute(value, axis, pairs)  18.8 us
    pallas_call x4, Pallas kernels, call(): pl.pallas_call(kernel, out_shape=shapes, in_specs=[VMEM] * len(args), out...  18.5 us
    ppermute x6, starting transfers between devices, fast_shift(): return lax.ppermute(value, axis, pairs)  18.2 us
    ppermute x6, waiting for transfers between devices, fast_shift(): return lax.ppermute(value, axis, pairs)  11.2 us
    ppermute x6, starting transfers between devices, fast_swap(): return lax.ppermute(value, axis, [(i, i ^ step) for i in range(SUB * SUB)])  6.79 us
    unnamed x8, local copies, waits for them, and re-layouts  3.02 us
  transfers between devices with their start and end apart: 24, of which 12 were waited for; matrix products, arithmetic and copies ran while one was open for 0% of the time, Pallas kernels for 0%

profile of v1, /device:TPU:1, one launch (start us, length us, event | category | flops | bytes accessed | tf_op | source)
XLA Modules:
  0.0 97.3 jit_solution(1046226652958004528)
XLA Ops:
  0.6 0.7 copy-done
  1.4 0.8 copy-done.1
  2.2 0.8 copy-done.2
  2.9 0.8 copy-done.3
  3.7 0.1 shard_map.75
  3.8 3.9 %collective-permute-start.8 = (bf16[128,256]{1,0:T(8,128)(2,1)S(1)}, bf16[128,256]{1,0:T(8,128)(2,1)S(1)}, u32[]{:S(2)}, u32[]{:S(2)}) collective-permute-start(bf16[128,256]{1,0:T(8,128)(2,1)S(1)} %get-tuple-element.23), channel_id=1, source_target_pairs={{0,16},{16,32},{32,48},{48,0},{64,80},{80,96},{96,112},{112,64},{1... | collective-permute-start | bytes 196616 | tf_op jit(solution)/shard_map/ppermute | solution.py:28
  7.7 5.1 %collective-permute-start.7 = (bf16[128,256]{1,0:T(8,128)(2,1)S(1)}, bf16[128,256]{1,0:T(8,128)(2,1)S(1)}, u32[]{:S(2)}, u32[]{:S(2)}) collective-permute-start(bf16[128,256]{1,0:T(8,128)(2,1)S(1)} %get-tuple-element.23), channel_id=1, source_target_pairs={{0,32},{16,48},{32,0},{48,16},{64,96},{80,112},{96,64},{112,80},{1... | collective-permute-start | bytes 196616 | tf_op jit(solution)/shard_map/ppermute | solution.py:28
  12.8 2.4 %collective-permute-start.6 = (bf16[128,256]{1,0:T(8,128)(2,1)S(1)}, bf16[128,256]{1,0:T(8,128)(2,1)S(1)}, u32[]{:S(2)}, u32[]{:S(2)}) collective-permute-start(bf16[128,256]{1,0:T(8,128)(2,1)S(1)} %get-tuple-element.23), channel_id=1, source_target_pairs={{0,48},{16,0},{32,16},{48,32},{64,112},{80,64},{96,80},{112,96},{1... | collective-permute-start | bytes 196616 | tf_op jit(solution)/shard_map/ppermute | solution.py:28
  15.2 0.0 collective-permute-done.8
  15.2 0.4 collective-permute-done.7
  15.5 4.9 %collective-permute-done.6 = bf16[128,256]{1,0:T(8,128)(2,1)S(1)} collective-permute-done((bf16[128,256]{1,0:T(8,128)(2,1)S(1)}, bf16[128,256]{1,0:T(8,128)(2,1)S(1)}, u32[]{:S(2)}, u32[]{:S(2)}) %collective-permute-start.6) | collective-permute-done | bytes 65568 | tf_op jit(solution)/shard_map/ppermute | solution.py:28
  20.5 1.4 %collective-permute-start.11 = (bf16[4,128,256]{2,1,0:T(8,128)(2,1)S(1)}, bf16[4,128,256]{2,1,0:T(8,128)(2,1)S(1)}, u32[]{:S(2)}, u32[]{:S(2)}) collective-permute-start(bf16[4,128,256]{2,1,0:T(8,128)(2,1)S(1)} %pad_maximum_fusion.1.refs_4_), channel_id=1, source_target_pairs={{0,64},{16,80},{32,96},{48,112},{64,128},{80,144},{96,160},{112,17... | collective-permute-start | bytes 786440 | tf_op jit(solution)/shard_map/ppermute | solution.py:23
  21.9 0.2 collective-permute-start.2
  22.1 1.9 %collective-permute-start.1 = (bf16[128,256]{1,0:T(8,128)(2,1)S(1)}, bf16[128,256]{1,0:T(8,128)(2,1)S(1)}, u32[]{:S(2)}, u32[]{:S(2)}) collective-permute-start(bf16[128,256]{1,0:T(8,128)(2,1)S(1)} %get-tuple-element.22), channel_id=1, source_target_pairs={{0,2},{1,3},{2,0},{3,1},{4,6},{5,7},{6,4},{7,5},{8,10},{9,11},{10,... | collective-permute-start | bytes 196616 | tf_op jit(solution)/shard_map/ppermute | solution.py:32
  24.0 2.6 %collective-permute-start.10 = (bf16[4,128,256]{2,1,0:T(8,128)(2,1)S(1)}, bf16[4,128,256]{2,1,0:T(8,128)(2,1)S(1)}, u32[]{:S(2)}, u32[]{:S(2)}) collective-permute-start(bf16[4,128,256]{2,1,0:T(8,128)(2,1)S(1)} %pad_maximum_fusion.1.refs_4_), channel_id=1, source_target_pairs={{0,128},{16,144},{32,160},{48,176},{64,192},{80,208},{96,224},{112... | collective-permute-start | bytes 786440 | tf_op jit(solution)/shard_map/ppermute | solution.py:23
  26.6 1.5 %collective-permute-start.9 = (bf16[4,128,256]{2,1,0:T(8,128)(2,1)S(1)}, bf16[4,128,256]{2,1,0:T(8,128)(2,1)S(1)}, u32[]{:S(2)}, u32[]{:S(2)}) collective-permute-start(bf16[4,128,256]{2,1,0:T(8,128)(2,1)S(1)} %pad_maximum_fusion.1.refs_4_), channel_id=1, source_target_pairs={{0,192},{16,208},{32,224},{48,240},{64,0},{80,16},{96,32},{112,48}... | collective-permute-start | bytes 786440 | tf_op jit(solution)/shard_map/ppermute | solution.py:23
  28.1 1.3 %collective-permute-start.5 = (bf16[4,128,256]{2,1,0:T(8,128)(2,1)S(1)}, bf16[4,128,256]{2,1,0:T(8,128)(2,1)S(1)}, u32[]{:S(2)}, u32[]{:S(2)}) collective-permute-start(bf16[4,128,256]{2,1,0:T(8,128)(2,1)S(1)} %pad_maximum_fusion.refs_0_), channel_id=1, source_target_pairs={{0,4},{1,5},{2,6},{3,7},{4,8},{5,9},{6,10},{7,11},{8,12},{9,13},{1... | collective-permute-start | bytes 786440 | tf_op jit(solution)/shard_map/ppermute | solution.py:23
  29.4 2.5 %collective-permute-start.4 = (bf16[4,128,256]{2,1,0:T(8,128)(2,1)S(1)}, bf16[4,128,256]{2,1,0:T(8,128)(2,1)S(1)}, u32[]{:S(2)}, u32[]{:S(2)}) collective-permute-start(bf16[4,128,256]{2,1,0:T(8,128)(2,1)S(1)} %pad_maximum_fusion.refs_0_), channel_id=1, source_target_pairs={{0,8},{1,9},{2,10},{3,11},{4,12},{5,13},{6,14},{7,15},{8,0},{9,1},... | collective-permute-start | bytes 786440 | tf_op jit(solution)/shard_map/ppermute | solution.py:23
  31.9 1.2 %collective-permute-start.3 = (bf16[4,128,256]{2,1,0:T(8,128)(2,1)S(1)}, bf16[4,128,256]{2,1,0:T(8,128)(2,1)S(1)}, u32[]{:S(2)}, u32[]{:S(2)}) collective-permute-start(bf16[4,128,256]{2,1,0:T(8,128)(2,1)S(1)} %pad_maximum_fusion.refs_0_), channel_id=1, source_target_pairs={{0,12},{1,13},{2,14},{3,15},{4,0},{5,1},{6,2},{7,3},{8,4},{9,5},{1... | collective-permute-start | bytes 786440 | tf_op jit(solution)/shard_map/ppermute | solution.py:23
  33.0 3.0 %collective-permute-done.10.refs_6_ = bf16[4,128,256]{2,1,0:T(8,128)(2,1)S(1)} collective-permute-done((bf16[4,128,256]{2,1,0:T(8,128)(2,1)S(1)}, bf16[4,128,256]{2,1,0:T(8,128)(2,1)S(1)}, u32[]{:S(2)}, u32[]{:S(2)}) %collective-permute-start.10) | collective-permute-done | bytes 262176 | tf_op jit(solution)/shard_map/ppermute | solution.py:23
  36.0 1.9 %collective-permute-done.9.refs_5_ = bf16[4,128,256]{2,1,0:T(8,128)(2,1)S(1)} collective-permute-done((bf16[4,128,256]{2,1,0:T(8,128)(2,1)S(1)}, bf16[4,128,256]{2,1,0:T(8,128)(2,1)S(1)}, u32[]{:S(2)}, u32[]{:S(2)}) %collective-permute-start.9) | collective-permute-done | bytes 262176 | tf_op jit(solution)/shard_map/ppermute | solution.py:23
  37.8 0.0 collective-permute-done.5.refs_3_
  37.8 5.3 %collective-permute-done.4.refs_2_ = bf16[4,128,256]{2,1,0:T(8,128)(2,1)S(1)} collective-permute-done((bf16[4,128,256]{2,1,0:T(8,128)(2,1)S(1)}, bf16[4,128,256]{2,1,0:T(8,128)(2,1)S(1)}, u32[]{:S(2)}, u32[]{:S(2)}) %collective-permute-start.4) | collective-permute-done | bytes 262176 | tf_op jit(solution)/shard_map/ppermute | solution.py:23
  43.2 17.4 %shard_map.76 = (f32[136,512]{1,0:T(8,128)S(1)}, f32[136,512]{1,0:T(8,128)S(1)}, f32[136,512]{1,0:T(8,128)S(1)}, f32[136,512]{1,0:T(8,128)S(1)}, f32[136,512]{1,...) custom-call(bf16[4,128,256]{2,1,0:T(8,128)(2,1)S(1)} %pad_maximum_fusion.refs_0_, ...), custom_call_target="tpu_custom_call" | custom-call | tf_op jit(solution)/shard_map/pallas_call | solution.py:143
  60.6 1.5 %collective-permute-start.12 = (f32[136,512]{1,0:T(8,128)S(1)}, f32[136,512]{1,0:T(8,128)S(1)}, u32[]{:S(2)}, u32[]{:S(2)}) collective-permute-start(f32[136,512]{1,0:T(8,128)S(1)} %get-tuple-element.25), channel_id=1, source_target_pairs={{0,4},{1,5},{2,6},{3,7},{4,8},{5,9},{6,10},{7,11},{8,12},{9,13},{1... | collective-permute-start | bytes 835592 | tf_op jit(solution)/shard_map/ppermute | solution.py:23
  62.0 2.8 %collective-permute-start.13 = (f32[136,512]{1,0:T(8,128)S(1)}, f32[136,512]{1,0:T(8,128)S(1)}, u32[]{:S(2)}, u32[]{:S(2)}) collective-permute-start(f32[136,512]{1,0:T(8,128)S(1)} %get-tuple-element.26), channel_id=1, source_target_pairs={{0,8},{1,9},{2,10},{3,11},{4,12},{5,13},{6,14},{7,15},{8,0},{9,1},... | collective-permute-start | bytes 835592 | tf_op jit(solution)/shard_map/ppermute | solution.py:23
  64.9 0.0 collective-permute-start.14
  64.9 1.6 %collective-permute-start.15 = (f32[136,512]{1,0:T(8,128)S(1)}, f32[136,512]{1,0:T(8,128)S(1)}, u32[]{:S(2)}, u32[]{:S(2)}) collective-permute-start(f32[136,512]{1,0:T(8,128)S(1)} %get-tuple-element.29), channel_id=1, source_target_pairs={{0,64},{16,80},{32,96},{48,112},{64,128},{80,144},{96,160},{112,17... | collective-permute-start | bytes 835592 | tf_op jit(solution)/shard_map/ppermute | solution.py:23
  66.4 1.3 %collective-permute-start.16 = (f32[136,512]{1,0:T(8,128)S(1)}, f32[136,512]{1,0:T(8,128)S(1)}, u32[]{:S(2)}, u32[]{:S(2)}) collective-permute-start(f32[136,512]{1,0:T(8,128)S(1)} %get-tuple-element.30), channel_id=1, source_target_pairs={{0,128},{16,144},{32,160},{48,176},{64,192},{80,208},{96,224},{112... | collective-permute-start | bytes 835592 | tf_op jit(solution)/shard_map/ppermute | solution.py:23
  67.8 1.4 %collective-permute-done.12.refs_1_ = f32[136,512]{1,0:T(8,128)S(1)} collective-permute-done((f32[136,512]{1,0:T(8,128)S(1)}, f32[136,512]{1,0:T(8,128)S(1)}, u32[]{:S(2)}, u32[]{:S(2)}) %collective-permute-start.12) | collective-permute-done | bytes 278560 | tf_op jit(solution)/shard_map/ppermute | solution.py:23
  69.2 1.3 %collective-permute-start.17 = (f32[136,512]{1,0:T(8,128)S(1)}, f32[136,512]{1,0:T(8,128)S(1)}, u32[]{:S(2)}, u32[]{:S(2)}) collective-permute-start(f32[136,512]{1,0:T(8,128)S(1)} %get-tuple-element.31), channel_id=1, source_target_pairs={{0,192},{16,208},{32,224},{48,240},{64,0},{80,16},{96,32},{112,48}... | collective-permute-start | bytes 835592 | tf_op jit(solution)/shard_map/ppermute | solution.py:23
  70.5 6.6 %collective-permute-done.13.refs_2_ = f32[136,512]{1,0:T(8,128)S(1)} collective-permute-done((f32[136,512]{1,0:T(8,128)S(1)}, f32[136,512]{1,0:T(8,128)S(1)}, u32[]{:S(2)}, u32[]{:S(2)}) %collective-permute-start.13) | collective-permute-done | bytes 278560 | tf_op jit(solution)/shard_map/ppermute | solution.py:23
  77.1 1.1 %collective-permute-done.16.refs_6_ = f32[136,512]{1,0:T(8,128)S(1)} collective-permute-done((f32[136,512]{1,0:T(8,128)S(1)}, f32[136,512]{1,0:T(8,128)S(1)}, u32[]{:S(2)}, u32[]{:S(2)}) %collective-permute-start.16) | collective-permute-done | bytes 278560 | tf_op jit(solution)/shard_map/ppermute | solution.py:23
  78.2 0.7 collective-permute-done.17.refs_7_
  78.9 0.2 shard_map.77
  79.1 2.9 %collective-permute-start.18 = (f32[136,128]{1,0:T(8,128)S(1)}, f32[136,128]{1,0:T(8,128)S(1)}, u32[]{:S(2)}, u32[]{:S(2)}) collective-permute-start(f32[136,128]{1,0:T(8,128)S(1)} %get-tuple-element.33), channel_id=1, source_target_pairs={{0,1},{1,0},{2,3},{3,2},{4,5},{5,4},{6,7},{7,6},{8,9},{9,8},{10,11... | collective-permute-start | bytes 208904 | tf_op jit(solution)/shard_map/ppermute | solution.py:32
  82.0 0.1 collective-permute-start.19
  82.1 1.7 %collective-permute-start.20 = (f32[136,128]{1,0:T(8,128)S(1)}, f32[136,128]{1,0:T(8,128)S(1)}, u32[]{:S(2)}, u32[]{:S(2)}) collective-permute-start(f32[136,128]{1,0:T(8,128)S(1)} %get-tuple-element.35), channel_id=1, source_target_pairs={{0,3},{1,2},{2,1},{3,0},{4,7},{5,6},{6,5},{7,4},{8,11},{9,10},{10,... | collective-permute-start | bytes 208904 | tf_op jit(solution)/shard_map/ppermute | solution.py:32
  83.8 1.3 %collective-permute-start.21 = (f32[136,128]{1,0:T(8,128)S(1)}, f32[136,128]{1,0:T(8,128)S(1)}, u32[]{:S(2)}, u32[]{:S(2)}) collective-permute-start(f32[136,128]{1,0:T(8,128)S(1)} %get-tuple-element.37), channel_id=1, source_target_pairs={{0,16},{16,32},{32,48},{48,0},{64,80},{80,96},{96,112},{112,64},{1... | collective-permute-start | bytes 208904 | tf_op jit(solution)/shard_map/ppermute | solution.py:28
  85.1 3.9 %collective-permute-start.22 = (f32[136,128]{1,0:T(8,128)S(1)}, f32[136,128]{1,0:T(8,128)S(1)}, u32[]{:S(2)}, u32[]{:S(2)}) collective-permute-start(f32[136,128]{1,0:T(8,128)S(1)} %get-tuple-element.38), channel_id=1, source_target_pairs={{0,32},{16,48},{32,0},{48,16},{64,96},{80,112},{96,64},{112,80},{1... | collective-permute-start | bytes 208904 | tf_op jit(solution)/shard_map/ppermute | solution.py:28
  88.9 0.0 collective-permute-done.18.refs_1_
  88.9 1.6 %collective-permute-start.23 = (f32[136,128]{1,0:T(8,128)S(1)}, f32[136,128]{1,0:T(8,128)S(1)}, u32[]{:S(2)}, u32[]{:S(2)}) collective-permute-start(f32[136,128]{1,0:T(8,128)S(1)} %get-tuple-element.39), channel_id=1, source_target_pairs={{0,48},{16,0},{32,16},{48,32},{64,112},{80,64},{96,80},{112,96},{1... | collective-permute-start | bytes 208904 | tf_op jit(solution)/shard_map/ppermute | solution.py:28
  90.5 0.0 collective-permute-done.19.refs_2_
  90.6 0.0 collective-permute-done.20.refs_3_
  90.6 1.7 %collective-permute-done.21.refs_5_ = f32[136,128]{1,0:T(8,128)S(1)} collective-permute-done((f32[136,128]{1,0:T(8,128)S(1)}, f32[136,128]{1,0:T(8,128)S(1)}, u32[]{:S(2)}, u32[]{:S(2)}) %collective-permute-start.21) | collective-permute-done | bytes 69664 | tf_op jit(solution)/shard_map/ppermute | solution.py:28
  92.2 1.9 %collective-permute-done.22.refs_6_ = f32[136,128]{1,0:T(8,128)S(1)} collective-permute-done((f32[136,128]{1,0:T(8,128)S(1)}, f32[136,128]{1,0:T(8,128)S(1)}, u32[]{:S(2)}, u32[]{:S(2)}) %collective-permute-start.22) | collective-permute-done | bytes 69664 | tf_op jit(solution)/shard_map/ppermute | solution.py:28
  94.1 2.3 %collective-permute-done.23.refs_7_ = f32[136,128]{1,0:T(8,128)S(1)} collective-permute-done((f32[136,128]{1,0:T(8,128)S(1)}, f32[136,128]{1,0:T(8,128)S(1)}, u32[]{:S(2)}, u32[]{:S(2)}) %collective-permute-start.23) | collective-permute-done | bytes 69664 | tf_op jit(solution)/shard_map/ppermute | solution.py:28
  96.5 0.8 shard_map.78
  (14 shorter events, 0.1 us)
Async XLA Ops:
  0.6 0.8 copy-start
  1.4 0.8 copy-start.1
  2.1 0.8 copy-start.2
  2.9 0.8 copy-start.3
  3.8 11.4 %collective-permute-start.8 = (bf16[128,256]{1,0:T(8,128)(2,1)S(1)}, bf16[128,256]{1,0:T(8,128)(2,1)S(1)}, u32[]{:S(2)}, u32[]{:S(2)}) collective-permute-start(bf16[128,256]{1,0:T(8,128)(2,1)S(1)} %get-tuple-element.23), channel_id=1, source_target_pairs={{0,16},{16,32},{32,48},{48,0},{64,80},{80,96},{96,112},{112,64},{1... | collective-permute-start | bytes 196616 | tf_op jit(solution)/shard_map/ppermute | solution.py:28
  7.7 7.9 %collective-permute-start.7 = (bf16[128,256]{1,0:T(8,128)(2,1)S(1)}, bf16[128,256]{1,0:T(8,128)(2,1)S(1)}, u32[]{:S(2)}, u32[]{:S(2)}) collective-permute-start(bf16[128,256]{1,0:T(8,128)(2,1)S(1)} %get-tuple-element.23), channel_id=1, source_target_pairs={{0,32},{16,48},{32,0},{48,16},{64,96},{80,112},{96,64},{112,80},{1... | collective-permute-start | bytes 196616 | tf_op jit(solution)/shard_map/ppermute | solution.py:28
  12.8 7.7 %collective-permute-start.6 = (bf16[128,256]{1,0:T(8,128)(2,1)S(1)}, bf16[128,256]{1,0:T(8,128)(2,1)S(1)}, u32[]{:S(2)}, u32[]{:S(2)}) collective-permute-start(bf16[128,256]{1,0:T(8,128)(2,1)S(1)} %get-tuple-element.23), channel_id=1, source_target_pairs={{0,48},{16,0},{32,16},{48,32},{64,112},{80,64},{96,80},{112,96},{1... | collective-permute-start | bytes 196616 | tf_op jit(solution)/shard_map/ppermute | solution.py:28
  20.5 11.4 %collective-permute-start.11 = (bf16[4,128,256]{2,1,0:T(8,128)(2,1)S(1)}, bf16[4,128,256]{2,1,0:T(8,128)(2,1)S(1)}, u32[]{:S(2)}, u32[]{:S(2)}) collective-permute-start(bf16[4,128,256]{2,1,0:T(8,128)(2,1)S(1)} %pad_maximum_fusion.1.refs_4_), channel_id=1, source_target_pairs={{0,64},{16,80},{32,96},{48,112},{64,128},{80,144},{96,160},{112,17... | collective-permute-start | bytes 786440 | tf_op jit(solution)/shard_map/ppermute | solution.py:23
  21.9 4.8 %collective-permute-start.2 = (bf16[128,256]{1,0:T(8,128)(2,1)S(1)}, bf16[128,256]{1,0:T(8,128)(2,1)S(1)}, u32[]{:S(2)}, u32[]{:S(2)}) collective-permute-start(bf16[128,256]{1,0:T(8,128)(2,1)S(1)} %get-tuple-element.22), channel_id=1, source_target_pairs={{0,3},{1,2},{2,1},{3,0},{4,7},{5,6},{6,5},{7,4},{8,11},{9,10},{10,... | collective-permute-start | bytes 196616 | tf_op jit(solution)/shard_map/ppermute | solution.py:32
  22.1 6.0 %collective-permute-start.1 = (bf16[128,256]{1,0:T(8,128)(2,1)S(1)}, bf16[128,256]{1,0:T(8,128)(2,1)S(1)}, u32[]{:S(2)}, u32[]{:S(2)}) collective-permute-start(bf16[128,256]{1,0:T(8,128)(2,1)S(1)} %get-tuple-element.22), channel_id=1, source_target_pairs={{0,2},{1,3},{2,0},{3,1},{4,6},{5,7},{6,4},{7,5},{8,10},{9,11},{10,... | collective-permute-start | bytes 196616 | tf_op jit(solution)/shard_map/ppermute | solution.py:32
  24.0 4.1 %collective-permute-start = (bf16[128,256]{1,0:T(8,128)(2,1)S(1)}, bf16[128,256]{1,0:T(8,128)(2,1)S(1)}, u32[]{:S(2)}, u32[]{:S(2)}) collective-permute-start(bf16[128,256]{1,0:T(8,128)(2,1)S(1)} %get-tuple-element.22), channel_id=1, source_target_pairs={{0,1},{1,0},{2,3},{3,2},{4,5},{5,4},{6,7},{7,6},{8,9},{9,8},{10,11... | collective-permute-start | bytes 196616 | tf_op jit(solution)/shard_map/ppermute | solution.py:32
  24.0 12.0 %collective-permute-start.10 = (bf16[4,128,256]{2,1,0:T(8,128)(2,1)S(1)}, bf16[4,128,256]{2,1,0:T(8,128)(2,1)S(1)}, u32[]{:S(2)}, u32[]{:S(2)}) collective-permute-start(bf16[4,128,256]{2,1,0:T(8,128)(2,1)S(1)} %pad_maximum_fusion.1.refs_4_), channel_id=1, source_target_pairs={{0,128},{16,144},{32,160},{48,176},{64,192},{80,208},{96,224},{112... | collective-permute-start | bytes 786440 | tf_op jit(solution)/shard_map/ppermute | solution.py:23
  26.6 11.2 %collective-permute-start.9 = (bf16[4,128,256]{2,1,0:T(8,128)(2,1)S(1)}, bf16[4,128,256]{2,1,0:T(8,128)(2,1)S(1)}, u32[]{:S(2)}, u32[]{:S(2)}) collective-permute-start(bf16[4,128,256]{2,1,0:T(8,128)(2,1)S(1)} %pad_maximum_fusion.1.refs_4_), channel_id=1, source_target_pairs={{0,192},{16,208},{32,224},{48,240},{64,0},{80,16},{96,32},{112,48}... | collective-permute-start | bytes 786440 | tf_op jit(solution)/shard_map/ppermute | solution.py:23
  28.1 9.7 %collective-permute-start.5 = (bf16[4,128,256]{2,1,0:T(8,128)(2,1)S(1)}, bf16[4,128,256]{2,1,0:T(8,128)(2,1)S(1)}, u32[]{:S(2)}, u32[]{:S(2)}) collective-permute-start(bf16[4,128,256]{2,1,0:T(8,128)(2,1)S(1)} %pad_maximum_fusion.refs_0_), channel_id=1, source_target_pairs={{0,4},{1,5},{2,6},{3,7},{4,8},{5,9},{6,10},{7,11},{8,12},{9,13},{1... | collective-permute-start | bytes 786440 | tf_op jit(solution)/shard_map/ppermute | solution.py:23
  29.4 13.8 %collective-permute-start.4 = (bf16[4,128,256]{2,1,0:T(8,128)(2,1)S(1)}, bf16[4,128,256]{2,1,0:T(8,128)(2,1)S(1)}, u32[]{:S(2)}, u32[]{:S(2)}) collective-permute-start(bf16[4,128,256]{2,1,0:T(8,128)(2,1)S(1)} %pad_maximum_fusion.refs_0_), channel_id=1, source_target_pairs={{0,8},{1,9},{2,10},{3,11},{4,12},{5,13},{6,14},{7,15},{8,0},{9,1},... | collective-permute-start | bytes 786440 | tf_op jit(solution)/shard_map/ppermute | solution.py:23
  31.9 11.3 %collective-permute-start.3 = (bf16[4,128,256]{2,1,0:T(8,128)(2,1)S(1)}, bf16[4,128,256]{2,1,0:T(8,128)(2,1)S(1)}, u32[]{:S(2)}, u32[]{:S(2)}) collective-permute-start(bf16[4,128,256]{2,1,0:T(8,128)(2,1)S(1)} %pad_maximum_fusion.refs_0_), channel_id=1, source_target_pairs={{0,12},{1,13},{2,14},{3,15},{4,0},{5,1},{6,2},{7,3},{8,4},{9,5},{1... | collective-permute-start | bytes 786440 | tf_op jit(solution)/shard_map/ppermute | solution.py:23
  60.6 8.6 %collective-permute-start.12 = (f32[136,512]{1,0:T(8,128)S(1)}, f32[136,512]{1,0:T(8,128)S(1)}, u32[]{:S(2)}, u32[]{:S(2)}) collective-permute-start(f32[136,512]{1,0:T(8,128)S(1)} %get-tuple-element.25), channel_id=1, source_target_pairs={{0,4},{1,5},{2,6},{3,7},{4,8},{5,9},{6,10},{7,11},{8,12},{9,13},{1... | collective-permute-start | bytes 835592 | tf_op jit(solution)/shard_map/ppermute | solution.py:23
  62.0 15.1 %collective-permute-start.13 = (f32[136,512]{1,0:T(8,128)S(1)}, f32[136,512]{1,0:T(8,128)S(1)}, u32[]{:S(2)}, u32[]{:S(2)}) collective-permute-start(f32[136,512]{1,0:T(8,128)S(1)} %get-tuple-element.26), channel_id=1, source_target_pairs={{0,8},{1,9},{2,10},{3,11},{4,12},{5,13},{6,14},{7,15},{8,0},{9,1},... | collective-permute-start | bytes 835592 | tf_op jit(solution)/shard_map/ppermute | solution.py:23
  64.9 12.2 %collective-permute-start.14 = (f32[136,512]{1,0:T(8,128)S(1)}, f32[136,512]{1,0:T(8,128)S(1)}, u32[]{:S(2)}, u32[]{:S(2)}) collective-permute-start(f32[136,512]{1,0:T(8,128)S(1)} %get-tuple-element.27), channel_id=1, source_target_pairs={{0,12},{1,13},{2,14},{3,15},{4,0},{5,1},{6,2},{7,3},{8,4},{9,5},{1... | collective-permute-start | bytes 835592 | tf_op jit(solution)/shard_map/ppermute | solution.py:23
  64.9 12.2 %collective-permute-start.15 = (f32[136,512]{1,0:T(8,128)S(1)}, f32[136,512]{1,0:T(8,128)S(1)}, u32[]{:S(2)}, u32[]{:S(2)}) collective-permute-start(f32[136,512]{1,0:T(8,128)S(1)} %get-tuple-element.29), channel_id=1, source_target_pairs={{0,64},{16,80},{32,96},{48,112},{64,128},{80,144},{96,160},{112,17... | collective-permute-start | bytes 835592 | tf_op jit(solution)/shard_map/ppermute | solution.py:23
  66.4 11.8 %collective-permute-start.16 = (f32[136,512]{1,0:T(8,128)S(1)}, f32[136,512]{1,0:T(8,128)S(1)}, u32[]{:S(2)}, u32[]{:S(2)}) collective-permute-start(f32[136,512]{1,0:T(8,128)S(1)} %get-tuple-element.30), channel_id=1, source_target_pairs={{0,128},{16,144},{32,160},{48,176},{64,192},{80,208},{96,224},{112... | collective-permute-start | bytes 835592 | tf_op jit(solution)/shard_map/ppermute | solution.py:23
  69.2 9.7 %collective-permute-start.17 = (f32[136,512]{1,0:T(8,128)S(1)}, f32[136,512]{1,0:T(8,128)S(1)}, u32[]{:S(2)}, u32[]{:S(2)}) collective-permute-start(f32[136,512]{1,0:T(8,128)S(1)} %get-tuple-element.31), channel_id=1, source_target_pairs={{0,192},{16,208},{32,224},{48,240},{64,0},{80,16},{96,32},{112,48}... | collective-permute-start | bytes 835592 | tf_op jit(solution)/shard_map/ppermute | solution.py:23
  79.1 9.8 %collective-permute-start.18 = (f32[136,128]{1,0:T(8,128)S(1)}, f32[136,128]{1,0:T(8,128)S(1)}, u32[]{:S(2)}, u32[]{:S(2)}) collective-permute-start(f32[136,128]{1,0:T(8,128)S(1)} %get-tuple-element.33), channel_id=1, source_target_pairs={{0,1},{1,0},{2,3},{3,2},{4,5},{5,4},{6,7},{7,6},{8,9},{9,8},{10,11... | collective-permute-start | bytes 208904 | tf_op jit(solution)/shard_map/ppermute | solution.py:32
  82.0 8.5 %collective-permute-start.19 = (f32[136,128]{1,0:T(8,128)S(1)}, f32[136,128]{1,0:T(8,128)S(1)}, u32[]{:S(2)}, u32[]{:S(2)}) collective-permute-start(f32[136,128]{1,0:T(8,128)S(1)} %get-tuple-element.34), channel_id=1, source_target_pairs={{0,2},{1,3},{2,0},{3,1},{4,6},{5,7},{6,4},{7,5},{8,10},{9,11},{10,... | collective-permute-start | bytes 208904 | tf_op jit(solution)/shard_map/ppermute | solution.py:32
  82.1 8.4 %collective-permute-start.20 = (f32[136,128]{1,0:T(8,128)S(1)}, f32[136,128]{1,0:T(8,128)S(1)}, u32[]{:S(2)}, u32[]{:S(2)}) collective-permute-start(f32[136,128]{1,0:T(8,128)S(1)} %get-tuple-element.35), channel_id=1, source_target_pairs={{0,3},{1,2},{2,1},{3,0},{4,7},{5,6},{6,5},{7,4},{8,11},{9,10},{10,... | collective-permute-start | bytes 208904 | tf_op jit(solution)/shard_map/ppermute | solution.py:32
  83.8 8.5 %collective-permute-start.21 = (f32[136,128]{1,0:T(8,128)S(1)}, f32[136,128]{1,0:T(8,128)S(1)}, u32[]{:S(2)}, u32[]{:S(2)}) collective-permute-start(f32[136,128]{1,0:T(8,128)S(1)} %get-tuple-element.37), channel_id=1, source_target_pairs={{0,16},{16,32},{32,48},{48,0},{64,80},{80,96},{96,112},{112,64},{1... | collective-permute-start | bytes 208904 | tf_op jit(solution)/shard_map/ppermute | solution.py:28
  85.1 9.1 %collective-permute-start.22 = (f32[136,128]{1,0:T(8,128)S(1)}, f32[136,128]{1,0:T(8,128)S(1)}, u32[]{:S(2)}, u32[]{:S(2)}) collective-permute-start(f32[136,128]{1,0:T(8,128)S(1)} %get-tuple-element.38), channel_id=1, source_target_pairs={{0,32},{16,48},{32,0},{48,16},{64,96},{80,112},{96,64},{112,80},{1... | collective-permute-start | bytes 208904 | tf_op jit(solution)/shard_map/ppermute | solution.py:28
  88.9 7.5 %collective-permute-start.23 = (f32[136,128]{1,0:T(8,128)S(1)}, f32[136,128]{1,0:T(8,128)S(1)}, u32[]{:S(2)}, u32[]{:S(2)}) collective-permute-start(f32[136,128]{1,0:T(8,128)S(1)} %get-tuple-element.39), channel_id=1, source_target_pairs={{0,48},{16,0},{32,16},{48,32},{64,112},{80,64},{96,80},{112,96},{1... | collective-permute-start | bytes 208904 | tf_op jit(solution)/shard_map/ppermute | solution.py:28

commit v2 on v1

v2 whole, which is shorter than its diff:
```python
import functools
import math

import jax
import jax.numpy as jnp
from jax import lax
from jax.experimental import pallas as pl
from jax.experimental.pallas import tpu as pltpu
from jax.sharding import PartitionSpec as P

GRID_W = 256
SUB = 4
SHARD = 128
WIDTH = 128
BLOCK = SUB * SHARD
ROWS = WIDTH + 8
AUG = 16
TOTAL_ROW, ACROSS_ROW, DOWN_ROW, PEAK_ROW = 0, 1, 2, 3
VMEM = pl.BlockSpec(memory_space=pltpu.VMEM)
HBM = pl.BlockSpec(memory_space=pltpu.HBM)


def slow_shift(axis, value, step):
    pairs = [(i, ((i // SUB + step) % SUB) * SUB + i % SUB) for i in range(SUB * SUB)]
    return lax.ppermute(value, axis, pairs)


def fast_shift(axis, value, step):
    pairs = [(i, (i // SUB) * SUB + (i % SUB + step) % SUB) for i in range(SUB * SUB)]
    return lax.ppermute(value, axis, pairs)


def fast_swap(axis, value, step):
    return lax.ppermute(value, axis, [(i, i ^ step) for i in range(SUB * SUB)])


def pack_kernel(feat_one, value_one, feat_two, value_two, out_one, out_two, held, sems):
    copies = [
        pltpu.make_async_copy(feat_one, out_one.at[:, :WIDTH], sems.at[0]),
        pltpu.make_async_copy(feat_two, out_two.at[:, :WIDTH], sems.at[1]),
        pltpu.make_async_copy(value_one, held.at[0], sems.at[2]),
        pltpu.make_async_copy(value_two, held.at[1], sems.at[3]),
    ]
    for copy in copies:
        copy.start()
    for side, out in ((0, out_one), (1, out_two)):
        copies[2 + side].wait()
        out[:, WIDTH:] = held[side].astype(jnp.float32).T.astype(jnp.bfloat16)
    copies[0].wait()
    copies[1].wait()


def piece_coords(start, total):
    across = (start % GRID_W).astype(jnp.float32) / GRID_W
    down = (start // GRID_W).astype(jnp.float32) / (total // GRID_W)
    return across, down


def coord_rows(start, total):
    across, down = piece_coords(start, total)
    sub = lax.broadcasted_iota(jnp.int32, (AUG, SHARD), 0)
    lane = lax.broadcasted_iota(jnp.int32, (AUG, SHARD), 1).astype(jnp.float32) / GRID_W
    rows = jnp.where(sub == DOWN_ROW, down, 0.0)
    rows = jnp.where(sub == ACROSS_ROW, across + lane, rows)
    rows = jnp.where(sub == TOTAL_ROW, 1.0, rows)
    return rows.astype(jnp.bfloat16)


def block_of(pieces, starts, total):
    keys = jnp.concatenate([piece[:, :WIDTH] for piece in pieces], axis=0)
    values = jnp.concatenate([piece[:, WIDTH:] for piece in pieces], axis=1)
    extra = jnp.concatenate([coord_rows(start, total) for start in starts], axis=1)
    return keys, jnp.concatenate([values, extra], axis=0)


def start_one(slow, fast_high, fast_low):
    row, col = lax.axis_index("row"), lax.axis_index("col")
    x = (col // SUB + slow) % SUB
    fast = (col % SUB) ^ (2 * fast_high + fast_low)
    return ((row * SUB + x) * SUB + fast) * SHARD


def start_two(slow, fast):
    row, col = lax.axis_index("row"), lax.axis_index("col")
    y = (row // SUB + slow) % SUB
    z = (row % SUB + fast) % SUB
    return ((col * SUB + y) * SUB + z) * SHARD


def merge(peaks, parts):
    top = peaks[0]
    for peak in peaks[1:]:
        top = jnp.maximum(top, peak)
    whole = None
    for peak, part in zip(peaks, parts):
        term = part * jnp.exp2(peak - top)
        whole = term if whole is None else whole + term
    return top, whole


def with_peak(top, whole):
    sub = lax.broadcasted_iota(jnp.int32, (ROWS - WIDTH, top.shape[1]), 0)
    return jnp.concatenate(
        [whole[:WIDTH], jnp.where(sub == PEAK_ROW, top, whole[WIDTH:])], axis=0
    )


def peak_of(part):
    return part[WIDTH + PEAK_ROW : WIDTH + PEAK_ROW + 1, :]


def merged(parts):
    return with_peak(*merge([peak_of(part) for part in parts], parts))


def attend(scale, query, blocks):
    peaks, parts = [], []
    for keys, values in blocks:
        score = lax.dot_general(
            keys, query, (((1,), (1,)), ((), ())), preferred_element_type=jnp.float32
        ) * scale
        peak = jnp.max(score, axis=0, keepdims=True)
        weight = jnp.exp2(score - peak).astype(jnp.bfloat16)
        parts.append(jnp.dot(values, weight, preferred_element_type=jnp.float32)[:ROWS])
        peaks.append(peak)
    return with_peak(*merge(peaks, parts))


def one_block(ones, slow, total):
    pieces = [ones[low * 2 + high][slow] for low in range(2) for high in range(2)]
    starts = [start_one(slow, high, low) for low in range(2) for high in range(2)]
    return block_of(pieces, starts, total)


def two_block(two, slow, total):
    return block_of(
        [two[piece] for piece in range(SUB)],
        [start_two(slow, piece) for piece in range(SUB)],
        total,
    )


def col_kernel(total, scale, *refs):
    ones, two, out = refs[:SUB], refs[SUB], refs[SUB + 1]
    query = jnp.concatenate([two[piece, :, :WIDTH] for piece in range(SUB)], axis=0)
    out[...] = attend(scale, query, [one_block(ones, slow, total) for slow in range(SUB)])


def row_kernel(total, scale, first, *refs):
    ones, twos, (keep, send) = refs[:SUB], refs[SUB : 2 * SUB], refs[2 * SUB :]

    def step(slow, _):
        query = jnp.concatenate([ref[first + slow, :, :WIDTH] for ref in ones], axis=0)
        blocks = [two_block(two, block, total) for block, two in enumerate(twos)]
        whole = attend(scale, query, blocks)
        keep[slow] = whole[:, : BLOCK // 2]
        send[slow] = whole[:, BLOCK // 2 :]
        return 0

    lax.fori_loop(0, keep.shape[0], step, 0)


def halve_kernel(mine, theirs, mine_b, theirs_b, keep, send):
    half = SUB // 2
    for slow in range(half):
        for first, one, two in ((0, mine, theirs), (half, mine_b, theirs_b)):
            whole = merged([one[slow], two[slow]])
            keep[first + slow] = whole[:, :SHARD]
            send[first + slow] = whole[:, SHARD:]


def pair_kernel(mine, theirs, *outs):
    for slow in range(SUB):
        outs[slow][...] = merged([mine[slow], theirs[slow]])


def block_kernel(*refs):
    ins, outs = refs[:SUB], refs[SUB:]
    for piece in range(SUB):
        span = slice(piece * SHARD, (piece + 1) * SHARD)
        outs[piece][...] = merged([ref[:, span] for ref in ins])


def finish_kernel(total, own_start, *refs):
    ins, (matched, flow) = refs[:SUB], refs[SUB:]
    own_across, own_down = piece_coords(own_start(), total)
    lane = lax.broadcasted_iota(jnp.int32, (1, SHARD), 1).astype(jnp.float32) / GRID_W
    parts = [ref[...] for ref in ins]
    _, whole = merge([peak_of(part) for part in parts], parts)
    inverse = 1.0 / whole[WIDTH + TOTAL_ROW : WIDTH + TOTAL_ROW + 1, :]
    matched[...] = (whole[:WIDTH] * inverse).T
    across = whole[WIDTH + ACROSS_ROW : WIDTH + ACROSS_ROW + 1, :] * inverse
    down = whole[WIDTH + DOWN_ROW : WIDTH + DOWN_ROW + 1, :] * inverse
    flow[0:1, :] = across - (own_across + lane)
    flow[1:2, :] = down - own_down


def call(kernel, shapes, args, scratch=(), work=0, specs=None, vmem=48 << 20):
    moved = sum(math.prod(a.shape) * a.dtype.itemsize for a in (*args, *shapes))
    return pl.pallas_call(
        kernel,
        out_shape=shapes,
        in_specs=specs or [VMEM] * len(args),
        out_specs=[VMEM] * len(shapes),
        scratch_shapes=list(scratch),
        compiler_params=pltpu.CompilerParams(vmem_limit_bytes=vmem),
        cost_estimate=pl.CostEstimate(
            flops=4 * WIDTH * work, bytes_accessed=moved, transcendentals=work
        ),
    )(*args)


def together(values):
    return lax.optimization_barrier(values)


def f32(*shape):
    return jax.ShapeDtypeStruct(shape, jnp.float32)


def body(feat_one, feat_two, value_one, value_two):
    total = feat_one.shape[0] * lax.axis_size("row") * lax.axis_size("col")
    scale = math.log2(math.e) / math.sqrt(WIDTH)
    packed = jax.ShapeDtypeStruct((SHARD, 2 * WIDTH), jnp.bfloat16)
    own_one, own_two = call(
        pack_kernel,
        [packed] * 2,
        (feat_one, value_one, feat_two, value_two),
        scratch=[
            pltpu.VMEM((2, SHARD, WIDTH), jnp.bfloat16),
            pltpu.SemaphoreType.DMA((4,)),
        ],
        specs=[HBM] * 4,
        vmem=62 << 20,
    )

    two = [own_two] + [fast_shift("row", own_two, -step) for step in range(1, SUB)]
    one = [own_one, fast_swap("col", own_one, 2)]
    one, two = together((jnp.stack(one), jnp.stack(two)))
    one = [one] + [slow_shift("col", one, -step) for step in range(1, SUB)]
    near, far = slow_shift("row", two, -1), slow_shift("row", two, 1)
    one, near, far = together((jnp.stack(one, axis=1), near, far))
    twos = [two, near, slow_shift("row", two, -2), far]
    other = fast_swap("col", one, 1)
    ones = [one[0], one[1], other[0], other[1]]

    def col_scores(*refs):
        col_kernel(total, scale, *refs)

    def row_scores_of(first):
        return functools.partial(row_kernel, total, scale, first)

    def finish_one(*refs):
        finish_kernel(total, lambda: start_one(0, 0, 0), *refs)

    def finish_two(*refs):
        finish_kernel(total, lambda: start_two(0, 0), *refs)

    work = BLOCK * BLOCK * SUB
    cols = [None] * SUB
    for step in (0, 1, 3, 2):
        if step == 2:
            twos[2], _ = together((twos[2], cols[0]))
        (cols[step],) = call(col_scores, [f32(ROWS, BLOCK)], (*ones, twos[step]), work=work)
    ones, _ = together((ones, cols))
    cols = [cols[0]] + [slow_shift("row", cols[step], step) for step in range(1, SUB)]
    half = SUB // 2
    shapes = [f32(half, ROWS, BLOCK // 2)] * 2
    keep, send = call(row_scores_of(0), shapes, (*ones, *twos), work=half * work)
    theirs = fast_swap("col", send, 1)
    ones, cols, keep = together((ones, cols, keep))
    keep_b, send_b = call(row_scores_of(half), shapes, (*ones, *twos), work=half * work)
    theirs_b = fast_swap("col", send_b, 1)
    cols = call(block_kernel, [f32(ROWS, SHARD)] * SUB, cols)
    cols = [cols[0]] + [fast_shift("row", cols[step], step) for step in range(1, SUB)]
    keep, send = call(
        halve_kernel, [f32(SUB, ROWS, SHARD)] * 2, (keep, theirs, keep_b, theirs_b)
    )
    theirs = fast_swap("col", send, 2)
    rows = call(pair_kernel, [f32(ROWS, SHARD)] * SUB, (keep, theirs))
    rows = [rows[0]] + [slow_shift("col", rows[step], step) for step in range(1, SUB)]
    outs = [f32(SHARD, WIDTH), f32(2, SHARD)]
    matched_two, flow_two = call(finish_two, outs, cols)
    matched_one, flow_one = call(finish_one, outs, rows)
    return matched_one, flow_one, matched_two, flow_two


def solution(mesh):
    return jax.shard_map(
        body,
        mesh=mesh,
        in_specs=(
            P(("row", "col"), None),
            P(("col", "row"), None),
            P(("row", "col"), None),
            P(("col", "row"), None),
        ),
        out_specs=(
            P(("row", "col"), None),
            P(None, ("row", "col")),
            P(("col", "row"), None),
            P(None, ("col", "row")),
        ),
        check_vma=False,
    )
```

time: 98.2 us -> 91.5 us (0.932)
  waiting for transfers between devices: 31.2 us -> 22.2 us
  local copies, waits for them, and re-layouts: 3.02 us -> 0.07 us
  starting transfers between devices: 43.8 us -> 45.7 us
  Pallas kernels: 18.5 us -> 20.3 us
    ppermute x6, waiting for transfers between devices: 11.2 us -> 5.48 us  [fast_shift(): return lax.ppermute(value, axis, pairs)]
    ppermute x12, waiting for transfers between devices: 20 us -> 15.5 us  [slow_shift(): return lax.ppermute(value, axis, pairs)]
    unnamed x8 -> x2, local copies, waits for them, and re-layouts: 3.02 us -> 0.01 us
    ppermute x6 -> x5, starting transfers between devices: 6.79 us -> 9.52 us  [fast_swap(): return lax.ppermute(value, axis, [(i, i ^ step) for i in range(SUB * SUB)])]
    ppermute x6, starting transfers between devices: 18.2 us -> 15.8 us  [fast_shift(): return lax.ppermute(value, axis, pairs)]
    pallas_call x4 -> x12, Pallas kernels: 18.5 us -> 20.3 us  [call(): pl.pallas_call(kernel, out_shape=shapes, in_specs=specs or [VMEM] * len(a...]
    ppermute x12, starting transfers between devices: 18.8 us -> 20.4 us  [slow_shift(): return lax.ppermute(value, axis, pairs)]
    ppermute x6 -> x5, waiting for transfers between devices: 0.02 us -> 1.19 us  [fast_swap(): return lax.ppermute(value, axis, [(i, i ^ step) for i in range(SUB * SUB)])]
  transfers between devices with their start and end apart: 24 -> 23, of which waited for: 12 -> 8; matrix products, arithmetic and copies ran while one was open for 0% -> 1% of each run, Pallas kernels for 0% -> 15%
where the time goes in v2:
time: 91.5 us; the launch traced here: 90.1 us
  starting transfers between devices  45.7 us (50%)
  waiting for transfers between devices  22.2 us (24%)
  Pallas kernels  20.3 us (22%)
  other arithmetic  0.99 us (1%)
    ppermute x12, starting transfers between devices, slow_shift(): return lax.ppermute(value, axis, pairs)  20.4 us
    pallas_call x12, Pallas kernels, call(): pl.pallas_call(kernel, out_shape=shapes, in_specs=specs or [VMEM] * len(a...  20.3 us
    ppermute x6, starting transfers between devices, fast_shift(): return lax.ppermute(value, axis, pairs)  15.8 us
    ppermute x12, waiting for transfers between devices, slow_shift(): return lax.ppermute(value, axis, pairs)  15.5 us
    ppermute x5, starting transfers between devices, fast_swap(): return lax.ppermute(value, axis, [(i, i ^ step) for i in range(SUB * SUB)])  9.52 us
    ppermute x6, waiting for transfers between devices, fast_shift(): return lax.ppermute(value, axis, pairs)  5.48 us
  transfers between devices with their start and end apart: 23, of which 8 were waited for; matrix products, arithmetic and copies ran while one was open for 1% of the time, Pallas kernels for 15%

profile of v2, /device:TPU:1, one launch (start us, length us, event | category | flops | bytes accessed | tf_op | source)
XLA Modules:
  0.0 90.1 jit_solution(5045983870232254158)
XLA Ops:
  0.6 1.7 %shard_map.75 = (bf16[128,256]{1,0:T(8,128)(2,1)}, bf16[128,256]{1,0:T(8,128)(2,1)}) custom-call(bf16[128,128]{1,0:T(8,128)(2,1)} %feat_one.1, bf16[128,128]{1,0:T(8,128)(2,1)} %value_one.1, bf16[128,128]{1,0:T(8,128)(2,1)} %feat_two.1, bf16[128,128]{1,0:T(8,128)(2,1)} %value_two.1), custom_call_target="tpu_custom_call" | custom-call | bytes 262144 | tf_op jit(solution)/shard_map/pallas_call | solution.py:200
  2.3 2.6 %collective-permute-start = (bf16[128,256]{1,0:T(8,128)(2,1)}, bf16[128,256]{1,0:T(8,128)(2,1)S(1)}, u32[]{:S(2)}, u32[]{:S(2)}) collective-permute-start(bf16[128,256]{1,0:T(8,128)(2,1)} %get-tuple-element.43), channel_id=1, source_target_pairs={{0,2},{1,3},{2,0},{3,1},{4,6},{5,7},{6,4},{7,5},{8,10},{9,11},{10,... | collective-permute-start | bytes 196616 | tf_op jit(solution)/shard_map/ppermute | solution.py:34
  4.9 5.1 %collective-permute-start.1 = (bf16[128,256]{1,0:T(8,128)(2,1)}, bf16[128,256]{1,0:T(8,128)(2,1)S(1)}, u32[]{:S(2)}, u32[]{:S(2)}) collective-permute-start(bf16[128,256]{1,0:T(8,128)(2,1)} %get-tuple-element.44), channel_id=1, source_target_pairs={{0,48},{16,0},{32,16},{48,32},{64,112},{80,64},{96,80},{112,96},{1... | collective-permute-start | bytes 196616 | tf_op jit(solution)/shard_map/ppermute | solution.py:30
  10.0 1.2 %collective-permute-start.2 = (bf16[128,256]{1,0:T(8,128)(2,1)}, bf16[128,256]{1,0:T(8,128)(2,1)S(1)}, u32[]{:S(2)}, u32[]{:S(2)}) collective-permute-start(bf16[128,256]{1,0:T(8,128)(2,1)} %get-tuple-element.44), channel_id=1, source_target_pairs={{0,32},{16,48},{32,0},{48,16},{64,96},{80,112},{96,64},{112,80},{1... | collective-permute-start | bytes 196616 | tf_op jit(solution)/shard_map/ppermute | solution.py:30
  11.2 2.1 %collective-permute-start.3 = (bf16[128,256]{1,0:T(8,128)(2,1)}, bf16[128,256]{1,0:T(8,128)(2,1)S(1)}, u32[]{:S(2)}, u32[]{:S(2)}) collective-permute-start(bf16[128,256]{1,0:T(8,128)(2,1)} %get-tuple-element.44), channel_id=1, source_target_pairs={{0,16},{16,32},{32,48},{48,0},{64,80},{80,96},{96,112},{112,64},{1... | collective-permute-start | bytes 196616 | tf_op jit(solution)/shard_map/ppermute | solution.py:30
  13.3 0.0 collective-permute-done
  13.3 0.9 pad_maximum_fusion.2
  14.1 0.0 collective-permute-done.1
  14.2 3.3 %collective-permute-done.2 = bf16[128,256]{1,0:T(8,128)(2,1)S(1)} collective-permute-done((bf16[128,256]{1,0:T(8,128)(2,1)}, bf16[128,256]{1,0:T(8,128)(2,1)S(1)}, u32[]{:S(2)}, u32[]{:S(2)}) %collective-permute-start.2) | collective-permute-done | bytes 65568 | tf_op jit(solution)/shard_map/ppermute | solution.py:30
  17.5 0.4 collective-permute-done.3
  18.0 2.8 %collective-permute-start.7 = (bf16[4,128,256]{2,1,0:T(8,128)(2,1)S(1)}, bf16[4,128,256]{2,1,0:T(8,128)(2,1)S(1)}, u32[]{:S(2)}, u32[]{:S(2)}) collective-permute-start(bf16[4,128,256]{2,1,0:T(8,128)(2,1)S(1)} %pad_maximum_fusion.1.refs_4_), channel_id=1, source_target_pairs={{0,192},{16,208},{32,224},{48,240},{64,0},{80,16},{96,32},{112,48}... | collective-permute-start | bytes 786440 | tf_op jit(solution)/shard_map/ppermute | solution.py:25
  20.8 0.0 collective-permute-start.8
  20.8 2.7 %collective-permute-start.5 = (bf16[2,128,256]{2,1,0:T(8,128)(2,1)S(1)}, bf16[2,128,256]{2,1,0:T(8,128)(2,1)S(1)}, u32[]{:S(2)}, u32[]{:S(2)}) collective-permute-start(bf16[2,128,256]{2,1,0:T(8,128)(2,1)S(1)} %pad_maximum_fusion.2), channel_id=1, source_target_pairs={{0,8},{1,9},{2,10},{3,11},{4,12},{5,13},{6,14},{7,15},{8,0},{9,1},... | collective-permute-start | bytes 393224 | tf_op jit(solution)/shard_map/ppermute | solution.py:25
  23.5 0.3 collective-permute-start.6
  23.8 2.4 %collective-permute-start.4 = (bf16[2,128,256]{2,1,0:T(8,128)(2,1)S(1)}, bf16[2,128,256]{2,1,0:T(8,128)(2,1)S(1)}, u32[]{:S(2)}, u32[]{:S(2)}) collective-permute-start(bf16[2,128,256]{2,1,0:T(8,128)(2,1)S(1)} %pad_maximum_fusion.2), channel_id=1, source_target_pairs={{0,12},{1,13},{2,14},{3,15},{4,0},{5,1},{6,2},{7,3},{8,4},{9,5},{1... | collective-permute-start | bytes 393224 | tf_op jit(solution)/shard_map/ppermute | solution.py:25
  26.2 0.0 collective-permute-done.5
  26.2 4.0 %collective-permute-done.6 = bf16[2,128,256]{2,1,0:T(8,128)(2,1)S(1)} collective-permute-done((bf16[2,128,256]{2,1,0:T(8,128)(2,1)S(1)}, bf16[2,128,256]{2,1,0:T(8,128)(2,1)S(1)}, u32[]{:S(2)}, u32[]{:S(2)}) %collective-permute-start.6) | collective-permute-done | bytes 131104 | tf_op jit(solution)/shard_map/ppermute | solution.py:25
  30.3 0.1 pad_maximum_fusion
  30.3 0.0 collective-permute-done.8.refs_4_.refs_7_
  30.3 2.7 %collective-permute-start.9 = (bf16[2,4,128,256]{3,2,1,0:T(8,128)(2,1)S(1)}, bf16[2,4,128,256]{3,2,1,0:T(8,128)(2,1)S(1)}, u32[]{:S(2)}, u32[]{:S(2)}) collective-permute-start(bf16[2,4,128,256]{3,2,1,0:T(8,128)(2,1)S(1)} %pad_maximum_fusion), channel_id=1, source_target_pairs={{0,1},{1,0},{2,3},{3,2},{4,5},{5,4},{6,7},{7,6},{8,9},{9,8},{10,11... | collective-permute-start | bytes 1572872 | tf_op jit(solution)/shard_map/ppermute | solution.py:34
  33.0 1.9 %collective-permute-start.10 = (bf16[4,128,256]{2,1,0:T(8,128)(2,1)S(1)}, bf16[4,128,256]{2,1,0:T(8,128)(2,1)S(1)}, u32[]{:S(2)}, u32[]{:S(2)}) collective-permute-start(bf16[4,128,256]{2,1,0:T(8,128)(2,1)S(1)} %pad_maximum_fusion.1.refs_4_), channel_id=1, source_target_pairs={{0,128},{16,144},{32,160},{48,176},{64,192},{80,208},{96,224},{112... | collective-permute-start | bytes 786440 | tf_op jit(solution)/shard_map/ppermute | solution.py:25
  35.0 2.1 %shard_map.76.refs_0_ = f32[136,512]{1,0:T(8,128)S(1)} custom-call(bf16[4,128,256]{2,1,0:T(8,128)(2,1)S(1)} %get-tuple-element.58.refs_0_, bf16[4,128,256]{2,1,0:T(8,128)(2,1)S(1)} %get-tuple-element.59.refs_1_, bf16[4,128,256]{2,1,0:T(8,128)(2,1)S(1)} %get-tuple-element.60.refs_2_, bf16[4,128,256]{2,1,0:T(8,128)(2,1)S(1)} %get-tuple-element.61.refs_3_, ...), custom_call_target="tpu_custom_call" | custom-call | flops 536870912 | bytes 1589248 | tf_op jit(solution)/shard_map/pallas_call | solution.py:200
  37.1 2.1 %shard_map.79 = f32[136,512]{1,0:T(8,128)S(1)} custom-call(bf16[4,128,256]{2,1,0:T(8,128)(2,1)S(1)} %get-tuple-element.58.refs_0_, bf16[4,128,256]{2,1,0:T(8,128)(2,1)S(1)} %get-tuple-element.59.refs_1_, bf16[4,128,256]{2,1,0:T(8,128)(2,1)S(1)} %get-tuple-element.60.refs_2_, bf16[4,128,256]{2,1,0:T(8,128)(2,1)S(1)} %get-tuple-element.61.refs_3_, ...), custom_call_target="tpu_custom_call" | custom-call | flops 536870912 | bytes 1589248 | tf_op jit(solution)/shard_map/pallas_call | solution.py:200
  39.2 2.9 %collective-permute-done.10.refs_4_.refs_6_ = bf16[4,128,256]{2,1,0:T(8,128)(2,1)S(1)} collective-permute-done((bf16[4,128,256]{2,1,0:T(8,128)(2,1)S(1)}, bf16[4,128,256]{2,1,0:T(8,128)(2,1)S(1)}, u32[]{:S(2)}, u32[]{:S(2)}) %collective-permute-start.10) | collective-permute-done | bytes 262176 | tf_op jit(solution)/shard_map/ppermute | solution.py:25
  42.1 2.1 %shard_map.78 = f32[136,512]{1,0:T(8,128)S(1)} custom-call(bf16[4,128,256]{2,1,0:T(8,128)(2,1)S(1)} %get-tuple-element.58.refs_0_, bf16[4,128,256]{2,1,0:T(8,128)(2,1)S(1)} %get-tuple-element.59.refs_1_, bf16[4,128,256]{2,1,0:T(8,128)(2,1)S(1)} %get-tuple-element.60.refs_2_, bf16[4,128,256]{2,1,0:T(8,128)(2,1)S(1)} %get-tuple-element.61.refs_3_, ...), custom_call_target="tpu_custom_call" | custom-call | flops 536870912 | bytes 1589248 | tf_op jit(solution)/shard_map/pallas_call | solution.py:200
  44.2 2.1 %shard_map.77 = f32[136,512]{1,0:T(8,128)S(1)} custom-call(bf16[4,128,256]{2,1,0:T(8,128)(2,1)S(1)} %get-tuple-element.58.refs_0_, bf16[4,128,256]{2,1,0:T(8,128)(2,1)S(1)} %get-tuple-element.59.refs_1_, bf16[4,128,256]{2,1,0:T(8,128)(2,1)S(1)} %get-tuple-element.60.refs_2_, bf16[4,128,256]{2,1,0:T(8,128)(2,1)S(1)} %get-tuple-element.61.refs_3_, ...), custom_call_target="tpu_custom_call" | custom-call | flops 536870912 | bytes 1589248 | tf_op jit(solution)/shard_map/pallas_call | solution.py:200
  46.3 3.0 %collective-permute-start.13 = (f32[136,512]{1,0:T(8,128)S(1)}, f32[136,512]{1,0:T(8,128)S(1)}, u32[]{:S(2)}, u32[]{:S(2)}) collective-permute-start(f32[136,512]{1,0:T(8,128)S(1)} %shard_map.79), channel_id=1, source_target_pairs={{0,192},{16,208},{32,224},{48,240},{64,0},{80,16},{96,32},{112,48}... | collective-permute-start | bytes 835592 | tf_op jit(solution)/shard_map/ppermute | solution.py:25
  49.4 0.7 collective-permute-start.11
  50.1 4.2 %shard_map.80 = (f32[2,136,256]{2,1,0:T(8,128)S(1)}, f32[2,136,256]{2,1,0:T(8,128)S(1)}) custom-call(bf16[4,128,256]{2,1,0:T(8,128)(2,1)S(1)} %get-tuple-element.58.refs_0_, bf16[4,128,256]{2,1,0:T(8,128)(2,1)S(1)} %get-tuple-element.59.refs_1_, bf16[4,128,256]{2,1,0:T(8,128)(2,1)S(1)} %get-tuple-element.60.refs_2_, ...), custom_call_target="tpu_custom_call" | custom-call | flops 1073741824 | bytes 2654208 | tf_op jit(solution)/shard_map/pallas_call | solution.py:200
  54.3 2.0 %collective-permute-start.14 = (f32[2,136,256]{2,1,0:T(8,128)S(1)}, f32[2,136,256]{2,1,0:T(8,128)S(1)}, u32[]{:S(2)}, u32[]{:S(2)}) collective-permute-start(f32[2,136,256]{2,1,0:T(8,128)S(1)} %get-tuple-element.57), channel_id=1, source_target_pairs={{0,1},{1,0},{2,3},{3,2},{4,5},{5,4},{6,7},{7,6},{8,9},{9,8},{10,11... | collective-permute-start | bytes 835592 | tf_op jit(solution)/shard_map/ppermute | solution.py:34
  56.2 0.0 collective-permute-done.13.refs_3_
  56.2 1.5 %collective-permute-done.12.refs_2_ = f32[136,512]{1,0:T(8,128)S(1)} collective-permute-done((f32[136,512]{1,0:T(8,128)S(1)}, f32[136,512]{1,0:T(8,128)S(1)}, u32[]{:S(2)}, u32[]{:S(2)}) %collective-permute-start.12) | collective-permute-done | bytes 278560 | tf_op jit(solution)/shard_map/ppermute | solution.py:25
  57.7 7.0 %collective-permute-done.11.refs_1_ = f32[136,512]{1,0:T(8,128)S(1)} collective-permute-done((f32[136,512]{1,0:T(8,128)S(1)}, f32[136,512]{1,0:T(8,128)S(1)}, u32[]{:S(2)}, u32[]{:S(2)}) %collective-permute-start.11) | collective-permute-done | bytes 278560 | tf_op jit(solution)/shard_map/ppermute | solution.py:25
  64.8 4.2 %shard_map.81 = (f32[2,136,256]{2,1,0:T(8,128)S(1)}, f32[2,136,256]{2,1,0:T(8,128)S(1)}) custom-call(bf16[4,128,256]{2,1,0:T(8,128)(2,1)S(1)} %get-tuple-element.58.refs_0_, bf16[4,128,256]{2,1,0:T(8,128)(2,1)S(1)} %get-tuple-element.59.refs_1_, bf16[4,128,256]{2,1,0:T(8,128)(2,1)S(1)} %get-tuple-element.60.refs_2_, ...), custom_call_target="tpu_custom_call" | custom-call | flops 1073741824 | bytes 2654208 | tf_op jit(solution)/shard_map/pallas_call | solution.py:200
  69.0 0.9 %collective-permute-start.15 = (f32[2,136,256]{2,1,0:T(8,128)S(1)}, f32[2,136,256]{2,1,0:T(8,128)S(1)}, u32[]{:S(2)}, u32[]{:S(2)}) collective-permute-start(f32[2,136,256]{2,1,0:T(8,128)S(1)} %get-tuple-element.63), channel_id=1, source_target_pairs={{0,1},{1,0},{2,3},{3,2},{4,5},{5,4},{6,7},{7,6},{8,9},{9,8},{10,11... | collective-permute-start | bytes 835592 | tf_op jit(solution)/shard_map/ppermute | solution.py:34
  69.9 1.2 %collective-permute-done.15.theirs_b = f32[2,136,256]{2,1,0:T(8,128)S(1)} collective-permute-done((f32[2,136,256]{2,1,0:T(8,128)S(1)}, f32[2,136,256]{2,1,0:T(8,128)S(1)}, u32[]{:S(2)}, u32[]{:S(2)}) %collective-permute-start.15) | collective-permute-done | bytes 278560 | tf_op jit(solution)/shard_map/ppermute | solution.py:34
  71.1 0.1 shard_map.82
  71.2 1.4 %collective-permute-start.16 = (f32[4,136,128]{2,1,0:T(8,128)S(1)}, f32[4,136,128]{2,1,0:T(8,128)S(1)}, u32[]{:S(2)}, u32[]{:S(2)}) collective-permute-start(f32[4,136,128]{2,1,0:T(8,128)S(1)} %get-tuple-element.65), channel_id=1, source_target_pairs={{0,2},{1,3},{2,0},{3,1},{4,6},{5,7},{6,4},{7,5},{8,10},{9,11},{10,... | collective-permute-start | bytes 835592 | tf_op jit(solution)/shard_map/ppermute | solution.py:34
  72.6 0.1 shard_map.85
  72.7 0.3 collective-permute-start.20
  73.1 4.0 %collective-permute-start.21 = (f32[136,128]{1,0:T(8,128)S(1)}, f32[136,128]{1,0:T(8,128)S(1)}, u32[]{:S(2)}, u32[]{:S(2)}) collective-permute-start(f32[136,128]{1,0:T(8,128)S(1)} %get-tuple-element.78), channel_id=1, source_target_pairs={{0,32},{16,48},{32,0},{48,16},{64,96},{80,112},{96,64},{112,80},{1... | collective-permute-start | bytes 208904 | tf_op jit(solution)/shard_map/ppermute | solution.py:30
  77.0 3.2 %collective-permute-start.22 = (f32[136,128]{1,0:T(8,128)S(1)}, f32[136,128]{1,0:T(8,128)S(1)}, u32[]{:S(2)}, u32[]{:S(2)}) collective-permute-start(f32[136,128]{1,0:T(8,128)S(1)} %get-tuple-element.79), channel_id=1, source_target_pairs={{0,48},{16,0},{32,16},{48,32},{64,112},{80,64},{96,80},{112,96},{1... | collective-permute-start | bytes 208904 | tf_op jit(solution)/shard_map/ppermute | solution.py:30
  80.3 0.1 collective-permute-start.17
  80.4 4.1 %collective-permute-start.18 = (f32[136,128]{1,0:T(8,128)S(1)}, f32[136,128]{1,0:T(8,128)S(1)}, u32[]{:S(2)}, u32[]{:S(2)}) collective-permute-start(f32[136,128]{1,0:T(8,128)S(1)} %get-tuple-element.68), channel_id=1, source_target_pairs={{0,8},{1,9},{2,10},{3,11},{4,12},{5,13},{6,14},{7,15},{8,0},{9,1},... | collective-permute-start | bytes 208904 | tf_op jit(solution)/shard_map/ppermute | solution.py:25
  84.5 2.3 %collective-permute-start.19 = (f32[136,128]{1,0:T(8,128)S(1)}, f32[136,128]{1,0:T(8,128)S(1)}, u32[]{:S(2)}, u32[]{:S(2)}) collective-permute-start(f32[136,128]{1,0:T(8,128)S(1)} %get-tuple-element.69), channel_id=1, source_target_pairs={{0,12},{1,13},{2,14},{3,15},{4,0},{5,1},{6,2},{7,3},{8,4},{9,5},{1... | collective-permute-start | bytes 208904 | tf_op jit(solution)/shard_map/ppermute | solution.py:25
  86.8 1.7 %collective-permute-done.21.refs_2_ = f32[136,128]{1,0:T(8,128)S(1)} collective-permute-done((f32[136,128]{1,0:T(8,128)S(1)}, f32[136,128]{1,0:T(8,128)S(1)}, u32[]{:S(2)}, u32[]{:S(2)}) %collective-permute-start.21) | collective-permute-done | bytes 69664 | tf_op jit(solution)/shard_map/ppermute | solution.py:30
  88.5 0.8 shard_map.86
  89.3 0.8 shard_map.84
  (17 shorter events, 0.2 us)
Async XLA Ops:
  2.3 10.9 %collective-permute-start = (bf16[128,256]{1,0:T(8,128)(2,1)}, bf16[128,256]{1,0:T(8,128)(2,1)S(1)}, u32[]{:S(2)}, u32[]{:S(2)}) collective-permute-start(bf16[128,256]{1,0:T(8,128)(2,1)} %get-tuple-element.43), channel_id=1, source_target_pairs={{0,2},{1,3},{2,0},{3,1},{4,6},{5,7},{6,4},{7,5},{8,10},{9,11},{10,... | collective-permute-start | bytes 196616 | tf_op jit(solution)/shard_map/ppermute | solution.py:34
  4.9 9.3 %collective-permute-start.1 = (bf16[128,256]{1,0:T(8,128)(2,1)}, bf16[128,256]{1,0:T(8,128)(2,1)S(1)}, u32[]{:S(2)}, u32[]{:S(2)}) collective-permute-start(bf16[128,256]{1,0:T(8,128)(2,1)} %get-tuple-element.44), channel_id=1, source_target_pairs={{0,48},{16,0},{32,16},{48,32},{64,112},{80,64},{96,80},{112,96},{1... | collective-permute-start | bytes 196616 | tf_op jit(solution)/shard_map/ppermute | solution.py:30
  10.0 7.5 %collective-permute-start.2 = (bf16[128,256]{1,0:T(8,128)(2,1)}, bf16[128,256]{1,0:T(8,128)(2,1)S(1)}, u32[]{:S(2)}, u32[]{:S(2)}) collective-permute-start(bf16[128,256]{1,0:T(8,128)(2,1)} %get-tuple-element.44), channel_id=1, source_target_pairs={{0,32},{16,48},{32,0},{48,16},{64,96},{80,112},{96,64},{112,80},{1... | collective-permute-start | bytes 196616 | tf_op jit(solution)/shard_map/ppermute | solution.py:30
  11.2 6.8 %collective-permute-start.3 = (bf16[128,256]{1,0:T(8,128)(2,1)}, bf16[128,256]{1,0:T(8,128)(2,1)S(1)}, u32[]{:S(2)}, u32[]{:S(2)}) collective-permute-start(bf16[128,256]{1,0:T(8,128)(2,1)} %get-tuple-element.44), channel_id=1, source_target_pairs={{0,16},{16,32},{32,48},{48,0},{64,80},{80,96},{96,112},{112,64},{1... | collective-permute-start | bytes 196616 | tf_op jit(solution)/shard_map/ppermute | solution.py:30
  13.3 4.7 %copy-start = (bf16[128,256]{1,0:T(8,128)(2,1)S(1)}, bf16[128,256]{1,0:T(8,128)(2,1)}, u32[]{:S(2)}) copy-start(bf16[128,256]{1,0:T(8,128)(2,1)} %get-tuple-element.44) | copy-start | bytes 196612
  18.0 12.4 %collective-permute-start.7 = (bf16[4,128,256]{2,1,0:T(8,128)(2,1)S(1)}, bf16[4,128,256]{2,1,0:T(8,128)(2,1)S(1)}, u32[]{:S(2)}, u32[]{:S(2)}) collective-permute-start(bf16[4,128,256]{2,1,0:T(8,128)(2,1)S(1)} %pad_maximum_fusion.1.refs_4_), channel_id=1, source_target_pairs={{0,192},{16,208},{32,224},{48,240},{64,0},{80,16},{96,32},{112,48}... | collective-permute-start | bytes 786440 | tf_op jit(solution)/shard_map/ppermute | solution.py:25
  20.8 9.6 %collective-permute-start.8 = (bf16[4,128,256]{2,1,0:T(8,128)(2,1)S(1)}, bf16[4,128,256]{2,1,0:T(8,128)(2,1)S(1)}, u32[]{:S(2)}, u32[]{:S(2)}) collective-permute-start(bf16[4,128,256]{2,1,0:T(8,128)(2,1)S(1)} %pad_maximum_fusion.1.refs_4_), channel_id=1, source_target_pairs={{0,64},{16,80},{32,96},{48,112},{64,128},{80,144},{96,160},{112,17... | collective-permute-start | bytes 786440 | tf_op jit(solution)/shard_map/ppermute | solution.py:25
  20.8 5.4 %collective-permute-start.5 = (bf16[2,128,256]{2,1,0:T(8,128)(2,1)S(1)}, bf16[2,128,256]{2,1,0:T(8,128)(2,1)S(1)}, u32[]{:S(2)}, u32[]{:S(2)}) collective-permute-start(bf16[2,128,256]{2,1,0:T(8,128)(2,1)S(1)} %pad_maximum_fusion.2), channel_id=1, source_target_pairs={{0,8},{1,9},{2,10},{3,11},{4,12},{5,13},{6,14},{7,15},{8,0},{9,1},... | collective-permute-start | bytes 393224 | tf_op jit(solution)/shard_map/ppermute | solution.py:25
  23.5 6.7 %collective-permute-start.6 = (bf16[2,128,256]{2,1,0:T(8,128)(2,1)S(1)}, bf16[2,128,256]{2,1,0:T(8,128)(2,1)S(1)}, u32[]{:S(2)}, u32[]{:S(2)}) collective-permute-start(bf16[2,128,256]{2,1,0:T(8,128)(2,1)S(1)} %pad_maximum_fusion.2), channel_id=1, source_target_pairs={{0,4},{1,5},{2,6},{3,7},{4,8},{5,9},{6,10},{7,11},{8,12},{9,13},{1... | collective-permute-start | bytes 393224 | tf_op jit(solution)/shard_map/ppermute | solution.py:25
  23.8 6.4 %collective-permute-start.4 = (bf16[2,128,256]{2,1,0:T(8,128)(2,1)S(1)}, bf16[2,128,256]{2,1,0:T(8,128)(2,1)S(1)}, u32[]{:S(2)}, u32[]{:S(2)}) collective-permute-start(bf16[2,128,256]{2,1,0:T(8,128)(2,1)S(1)} %pad_maximum_fusion.2), channel_id=1, source_target_pairs={{0,12},{1,13},{2,14},{3,15},{4,0},{5,1},{6,2},{7,3},{8,4},{9,5},{1... | collective-permute-start | bytes 393224 | tf_op jit(solution)/shard_map/ppermute | solution.py:25
  30.3 4.6 %collective-permute-start.9 = (bf16[2,4,128,256]{3,2,1,0:T(8,128)(2,1)S(1)}, bf16[2,4,128,256]{3,2,1,0:T(8,128)(2,1)S(1)}, u32[]{:S(2)}, u32[]{:S(2)}) collective-permute-start(bf16[2,4,128,256]{3,2,1,0:T(8,128)(2,1)S(1)} %pad_maximum_fusion), channel_id=1, source_target_pairs={{0,1},{1,0},{2,3},{3,2},{4,5},{5,4},{6,7},{7,6},{8,9},{9,8},{10,11... | collective-permute-start | bytes 1572872 | tf_op jit(solution)/shard_map/ppermute | solution.py:34
  33.0 9.1 %collective-permute-start.10 = (bf16[4,128,256]{2,1,0:T(8,128)(2,1)S(1)}, bf16[4,128,256]{2,1,0:T(8,128)(2,1)S(1)}, u32[]{:S(2)}, u32[]{:S(2)}) collective-permute-start(bf16[4,128,256]{2,1,0:T(8,128)(2,1)S(1)} %pad_maximum_fusion.1.refs_4_), channel_id=1, source_target_pairs={{0,128},{16,144},{32,160},{48,176},{64,192},{80,208},{96,224},{112... | collective-permute-start | bytes 786440 | tf_op jit(solution)/shard_map/ppermute | solution.py:25
  46.3 9.9 %collective-permute-start.13 = (f32[136,512]{1,0:T(8,128)S(1)}, f32[136,512]{1,0:T(8,128)S(1)}, u32[]{:S(2)}, u32[]{:S(2)}) collective-permute-start(f32[136,512]{1,0:T(8,128)S(1)} %shard_map.79), channel_id=1, source_target_pairs={{0,192},{16,208},{32,224},{48,240},{64,0},{80,16},{96,32},{112,48}... | collective-permute-start | bytes 835592 | tf_op jit(solution)/shard_map/ppermute | solution.py:25
  49.4 8.4 %collective-permute-start.12 = (f32[136,512]{1,0:T(8,128)S(1)}, f32[136,512]{1,0:T(8,128)S(1)}, u32[]{:S(2)}, u32[]{:S(2)}) collective-permute-start(f32[136,512]{1,0:T(8,128)S(1)} %shard_map.78), channel_id=1, source_target_pairs={{0,128},{16,144},{32,160},{48,176},{64,192},{80,208},{96,224},{112... | collective-permute-start | bytes 835592 | tf_op jit(solution)/shard_map/ppermute | solution.py:25
  49.4 15.4 %collective-permute-start.11 = (f32[136,512]{1,0:T(8,128)S(1)}, f32[136,512]{1,0:T(8,128)S(1)}, u32[]{:S(2)}, u32[]{:S(2)}) collective-permute-start(f32[136,512]{1,0:T(8,128)S(1)} %shard_map.77), channel_id=1, source_target_pairs={{0,64},{16,80},{32,96},{48,112},{64,128},{80,144},{96,160},{112,17... | collective-permute-start | bytes 835592 | tf_op jit(solution)/shard_map/ppermute | solution.py:25
  54.3 15.7 %collective-permute-start.14 = (f32[2,136,256]{2,1,0:T(8,128)S(1)}, f32[2,136,256]{2,1,0:T(8,128)S(1)}, u32[]{:S(2)}, u32[]{:S(2)}) collective-permute-start(f32[2,136,256]{2,1,0:T(8,128)S(1)} %get-tuple-element.57), channel_id=1, source_target_pairs={{0,1},{1,0},{2,3},{3,2},{4,5},{5,4},{6,7},{7,6},{8,9},{9,8},{10,11... | collective-permute-start | bytes 835592 | tf_op jit(solution)/shard_map/ppermute | solution.py:34
  69.0 2.1 %collective-permute-start.15 = (f32[2,136,256]{2,1,0:T(8,128)S(1)}, f32[2,136,256]{2,1,0:T(8,128)S(1)}, u32[]{:S(2)}, u32[]{:S(2)}) collective-permute-start(f32[2,136,256]{2,1,0:T(8,128)S(1)} %get-tuple-element.63), channel_id=1, source_target_pairs={{0,1},{1,0},{2,3},{3,2},{4,5},{5,4},{6,7},{7,6},{8,9},{9,8},{10,11... | collective-permute-start | bytes 835592 | tf_op jit(solution)/shard_map/ppermute | solution.py:34
  71.2 9.0 %collective-permute-start.16 = (f32[4,136,128]{2,1,0:T(8,128)S(1)}, f32[4,136,128]{2,1,0:T(8,128)S(1)}, u32[]{:S(2)}, u32[]{:S(2)}) collective-permute-start(f32[4,136,128]{2,1,0:T(8,128)S(1)} %get-tuple-element.65), channel_id=1, source_target_pairs={{0,2},{1,3},{2,0},{3,1},{4,6},{5,7},{6,4},{7,5},{8,10},{9,11},{10,... | collective-permute-start | bytes 835592 | tf_op jit(solution)/shard_map/ppermute | solution.py:34
  72.7 11.7 %collective-permute-start.20 = (f32[136,128]{1,0:T(8,128)S(1)}, f32[136,128]{1,0:T(8,128)S(1)}, u32[]{:S(2)}, u32[]{:S(2)}) collective-permute-start(f32[136,128]{1,0:T(8,128)S(1)} %get-tuple-element.77), channel_id=1, source_target_pairs={{0,16},{16,32},{32,48},{48,0},{64,80},{80,96},{96,112},{112,64},{1... | collective-permute-start | bytes 208904 | tf_op jit(solution)/shard_map/ppermute | solution.py:30
  73.1 15.4 %collective-permute-start.21 = (f32[136,128]{1,0:T(8,128)S(1)}, f32[136,128]{1,0:T(8,128)S(1)}, u32[]{:S(2)}, u32[]{:S(2)}) collective-permute-start(f32[136,128]{1,0:T(8,128)S(1)} %get-tuple-element.78), channel_id=1, source_target_pairs={{0,32},{16,48},{32,0},{48,16},{64,96},{80,112},{96,64},{112,80},{1... | collective-permute-start | bytes 208904 | tf_op jit(solution)/shard_map/ppermute | solution.py:30
  77.0 11.5 %collective-permute-start.22 = (f32[136,128]{1,0:T(8,128)S(1)}, f32[136,128]{1,0:T(8,128)S(1)}, u32[]{:S(2)}, u32[]{:S(2)}) collective-permute-start(f32[136,128]{1,0:T(8,128)S(1)} %get-tuple-element.79), channel_id=1, source_target_pairs={{0,48},{16,0},{32,16},{48,32},{64,112},{80,64},{96,80},{112,96},{1... | collective-permute-start | bytes 208904 | tf_op jit(solution)/shard_map/ppermute | solution.py:30
  80.3 9.0 %collective-permute-start.17 = (f32[136,128]{1,0:T(8,128)S(1)}, f32[136,128]{1,0:T(8,128)S(1)}, u32[]{:S(2)}, u32[]{:S(2)}) collective-permute-start(f32[136,128]{1,0:T(8,128)S(1)} %get-tuple-element.67), channel_id=1, source_target_pairs={{0,4},{1,5},{2,6},{3,7},{4,8},{5,9},{6,10},{7,11},{8,12},{9,13},{1... | collective-permute-start | bytes 208904 | tf_op jit(solution)/shard_map/ppermute | solution.py:25
  80.4 8.9 %collective-permute-start.18 = (f32[136,128]{1,0:T(8,128)S(1)}, f32[136,128]{1,0:T(8,128)S(1)}, u32[]{:S(2)}, u32[]{:S(2)}) collective-permute-start(f32[136,128]{1,0:T(8,128)S(1)} %get-tuple-element.68), channel_id=1, source_target_pairs={{0,8},{1,9},{2,10},{3,11},{4,12},{5,13},{6,14},{7,15},{8,0},{9,1},... | collective-permute-start | bytes 208904 | tf_op jit(solution)/shard_map/ppermute | solution.py:25
  84.5 4.8 %collective-permute-start.19 = (f32[136,128]{1,0:T(8,128)S(1)}, f32[136,128]{1,0:T(8,128)S(1)}, u32[]{:S(2)}, u32[]{:S(2)}) collective-permute-start(f32[136,128]{1,0:T(8,128)S(1)} %get-tuple-element.69), channel_id=1, source_target_pairs={{0,12},{1,13},{2,14},{3,15},{4,0},{5,1},{6,2},{7,3},{8,4},{9,5},{1... | collective-permute-start | bytes 208904 | tf_op jit(solution)/shard_map/ppermute | solution.py:25

commit v3 on v2

v3 whole, which is shorter than its diff:
```python
import functools
import math

import jax
import jax.numpy as jnp
from jax import lax
from jax.experimental import pallas as pl
from jax.experimental.pallas import tpu as pltpu
from jax.sharding import PartitionSpec as P

GRID_W = 256
SUB = 4
SHARD = 128
WIDTH = 128
BLOCK = SUB * SHARD
ROWS = WIDTH + 8
AUG = 16
TOTAL_ROW, ACROSS_ROW, DOWN_ROW, PEAK_ROW = 0, 1, 2, 3
VMEM = pl.BlockSpec(memory_space=pltpu.VMEM)
HBM = pl.BlockSpec(memory_space=pltpu.HBM)


def slow_shift(axis, value, step):
    pairs = [(i, ((i // SUB + step) % SUB) * SUB + i % SUB) for i in range(SUB * SUB)]
    return lax.ppermute(value, axis, pairs)


def fast_shift(axis, value, step):
    pairs = [(i, (i // SUB) * SUB + (i % SUB + step) % SUB) for i in range(SUB * SUB)]
    return lax.ppermute(value, axis, pairs)


def fast_swap(axis, value, step):
    return lax.ppermute(value, axis, [(i, i ^ step) for i in range(SUB * SUB)])


def pack_kernel(feat_one, value_one, feat_two, value_two, out, feats, held, sems):
    sources = ((feat_one, value_one), (feat_two, value_two))
    copies = []
    for side, (feat, value) in enumerate(sources):
        copies.append(pltpu.make_async_copy(value, held.at[side], sems.at[2 * side]))
        copies.append(pltpu.make_async_copy(feat, feats.at[side], sems.at[2 * side + 1]))
    for copy in copies:
        copy.start()
    for side in range(2):
        copies[2 * side].wait()
        out[side, 1] = held[side].astype(jnp.float32).T.astype(jnp.bfloat16)
        copies[2 * side + 1].wait()
        out[side, 0] = feats[side]


def piece_coords(start, total):
    across = (start % GRID_W).astype(jnp.float32) / GRID_W
    down = (start // GRID_W).astype(jnp.float32) / (total // GRID_W)
    return across, down


def coord_rows(start, total):
    across, down = piece_coords(start, total)
    sub = lax.broadcasted_iota(jnp.int32, (AUG, SHARD), 0)
    lane = lax.broadcasted_iota(jnp.int32, (AUG, SHARD), 1).astype(jnp.float32) / GRID_W
    rows = jnp.where(sub == DOWN_ROW, down, 0.0)
    rows = jnp.where(sub == ACROSS_ROW, across + lane, rows)
    rows = jnp.where(sub == TOTAL_ROW, 1.0, rows)
    return rows.astype(jnp.bfloat16)


def key_start(side, slow, fast):
    row, col = lax.axis_index("row"), lax.axis_index("col")
    z = (row % SUB + fast) % SUB
    if side == 0:
        y = (row // SUB + slow) % SUB
        return ((col * SUB + y) * SUB + z) * SHARD
    x = (col // SUB + slow) % SUB
    return (((row // SUB * SUB + z) * SUB + x) * SUB + col % SUB) * SHARD


def own_start(side):
    row, col = lax.axis_index("row"), lax.axis_index("col")
    return (row * SUB * SUB + col if side == 0 else col * SUB * SUB + row) * SHARD


def merge(peaks, parts):
    top = peaks[0]
    for peak in peaks[1:]:
        top = jnp.maximum(top, peak)
    whole = None
    for peak, part in zip(peaks, parts):
        term = part * jnp.exp2(peak - top)
        whole = term if whole is None else whole + term
    return top, whole


def with_peak(top, whole):
    sub = lax.broadcasted_iota(jnp.int32, (ROWS - WIDTH, top.shape[1]), 0)
    return jnp.concatenate(
        [whole[:WIDTH], jnp.where(sub == PEAK_ROW, top, whole[WIDTH:])], axis=0
    )


def peak_of(part):
    return part[WIDTH + PEAK_ROW : WIDTH + PEAK_ROW + 1, :]


def merged(parts):
    return with_peak(*merge([peak_of(part) for part in parts], parts))


def attend(scale, query, blocks):
    peaks, parts = [], []
    for keys, values in blocks:
        score = lax.dot_general(
            keys, query, (((1,), (1,)), ((), ())), preferred_element_type=jnp.float32
        ) * scale
        peak = jnp.max(score, axis=0, keepdims=True)
        weight = jnp.exp2(score - peak).astype(jnp.bfloat16)
        parts.append(jnp.dot(values, weight, preferred_element_type=jnp.float32)[:ROWS])
        peaks.append(peak)
    return with_peak(*merge(peaks, parts))


def score_kernel(total, scale, side, first, queries, *refs):
    keys, (out,) = refs[:SUB], refs[SUB:]

    def block_of(slow):
        tiles = keys[slow]
        feats = jnp.concatenate([tiles[2 * fast] for fast in range(SUB)], axis=0)
        values = jnp.concatenate([tiles[2 * fast + 1] for fast in range(SUB)], axis=1)
        extra = [coord_rows(key_start(side, slow, fast), total) for fast in range(SUB)]
        return feats, jnp.concatenate([values, jnp.concatenate(extra, axis=1)], axis=0)

    def step(part, _):
        tiles = [queries[first + part * SUB + piece] for piece in range(SUB)]
        query = jnp.concatenate(tiles, axis=0)
        out[part] = attend(scale, query, [block_of(slow) for slow in range(SUB)])
        return 0

    lax.fori_loop(0, 2, step, 0)


def core_kernel(mine, theirs, *outs):
    for part in range(2):
        whole = merged([mine[part], theirs[part]])
        outs[2 * part][...] = whole[:, : 2 * SHARD]
        outs[2 * part + 1][...] = whole[:, 2 * SHARD :]


def chip_kernel(*refs):
    ins, (keep, send) = refs[: 2 * SUB], refs[2 * SUB :]
    for side in range(2):
        whole = merged([ref[...] for ref in ins[side * SUB : (side + 1) * SUB]])
        keep[side] = whole[:, :SHARD]
        send[side] = whole[:, SHARD:]


def finish_kernel(total, mine, theirs, *outs):
    lane = lax.broadcasted_iota(jnp.int32, (1, SHARD), 1).astype(jnp.float32) / GRID_W
    for side in range(2):
        matched, flow = outs[2 * side], outs[2 * side + 1]
        own_across, own_down = piece_coords(own_start(side), total)
        parts = [mine[side], theirs[side]]
        _, whole = merge([peak_of(part) for part in parts], parts)
        inverse = 1.0 / whole[WIDTH + TOTAL_ROW : WIDTH + TOTAL_ROW + 1, :]
        matched[...] = (whole[:WIDTH] * inverse).T
        across = whole[WIDTH + ACROSS_ROW : WIDTH + ACROSS_ROW + 1, :] * inverse
        down = whole[WIDTH + DOWN_ROW : WIDTH + DOWN_ROW + 1, :] * inverse
        flow[0:1, :] = across - (own_across + lane)
        flow[1:2, :] = down - own_down


def call(kernel, shapes, args, scratch=(), work=0, specs=None, vmem=48 << 20):
    moved = sum(math.prod(a.shape) * a.dtype.itemsize for a in (*args, *shapes))
    return pl.pallas_call(
        kernel,
        out_shape=shapes,
        in_specs=specs or [VMEM] * len(args),
        out_specs=[VMEM] * len(shapes),
        scratch_shapes=list(scratch),
        compiler_params=pltpu.CompilerParams(vmem_limit_bytes=vmem),
        cost_estimate=pl.CostEstimate(
            flops=4 * WIDTH * work, bytes_accessed=moved, transcendentals=work
        ),
    )(*args)


def together(values):
    return lax.optimization_barrier(values)


def f32(*shape):
    return jax.ShapeDtypeStruct(shape, jnp.float32)


def bf16(*shape):
    return jax.ShapeDtypeStruct(shape, jnp.bfloat16)


def body(feat_one, feat_two, value_one, value_two):
    total = feat_one.shape[0] * lax.axis_size("row") * lax.axis_size("col")
    scale = math.log2(math.e) / math.sqrt(WIDTH)
    own, feats = call(
        pack_kernel,
        [bf16(2, 2, SHARD, WIDTH), bf16(2, SHARD, WIDTH)],
        (feat_one, value_one, feat_two, value_two),
        scratch=[
            pltpu.VMEM((2, SHARD, WIDTH), jnp.bfloat16),
            pltpu.SemaphoreType.DMA((4,)),
        ],
        specs=[HBM] * 4,
        vmem=62 << 20,
    )

    pieces = [own] + [fast_shift("row", own, -step) for step in range(1, SUB)]
    partner = fast_swap("col", feats, 2)
    sends = [
        jnp.concatenate([piece[side] for piece in pieces] + [partner[side : side + 1]])
        for side in range(2)
    ]
    sends = together(sends)
    tiles = [
        [send] + [slow_shift(axis, send, -step) for step in range(1, SUB)]
        for axis, send in zip(("col", "row"), sends)
    ]
    tiles = together(tiles)
    queries = jnp.stack(
        [tile[index] for side in tiles for tile in side for index in (0, 2 * SUB)]
    )
    others = fast_swap("col", queries, 1)

    def score(side, queries):
        shapes = [f32(2, ROWS, BLOCK)]
        kernel = functools.partial(score_kernel, total, scale, side, side * 2 * SUB)
        work = 2 * SUB * SHARD * SUB * BLOCK
        return call(kernel, shapes, (queries, *tiles[1 - side]), work=work)[0]

    def core_merge(mine, theirs):
        return call(core_kernel, [f32(ROWS, 2 * SHARD)] * SUB, (mine, theirs))

    def spread(axis, parts):
        return [parts[0]] + [slow_shift(axis, parts[step], step) for step in range(1, SUB)]

    keep_one = score(0, queries)
    others, keep_one = together((others, keep_one))
    send_one = score(0, others)
    theirs_one = fast_swap("col", send_one, 1)
    others, _ = together((others, send_one))
    send_two = score(1, others)
    theirs_two = fast_swap("col", send_two, 1)
    rows = core_merge(keep_one, theirs_one)
    queries, _, rows = together((queries, send_two, rows))
    rows = spread("col", rows)
    keep_two = score(1, queries)
    rows, keep_two = together((rows, keep_two))
    cols = spread("row", core_merge(keep_two, theirs_two))
    keep, send = call(chip_kernel, [f32(2, ROWS, SHARD)] * 2, (*rows, *cols))
    theirs = fast_swap("col", send, 2)
    outs = [f32(SHARD, WIDTH), f32(2, SHARD)] * 2
    return tuple(call(functools.partial(finish_kernel, total), outs, (keep, theirs)))


def solution(mesh):
    return jax.shard_map(
        body,
        mesh=mesh,
        in_specs=(
            P(("row", "col"), None),
            P(("col", "row"), None),
            P(("row", "col"), None),
            P(("col", "row"), None),
        ),
        out_specs=(
            P(("row", "col"), None),
            P(None, ("row", "col")),
            P(("col", "row"), None),
            P(None, ("col", "row")),
        ),
        check_vma=False,
    )
```

time: 91.5 us -> 88.8 us (0.970)
  the two profiles are of different devices: /device:TPU:1 before, /device:TPU:14 now
where the time goes in v3:
time: 88.8 us; the launch traced here: 88.6 us
  waiting for transfers between devices  39.3 us (44%)
  starting transfers between devices  27.7 us (31%)
  Pallas kernels  19.6 us (22%)
  local copies, waits for them, and re-layouts  1.11 us (1%)
    ppermute x12, waiting for transfers between devices, slow_shift(): return lax.ppermute(value, axis, pairs)  24.8 us
    pallas_call x9, Pallas kernels, call(): pl.pallas_call(kernel, out_shape=shapes, in_specs=specs or [VMEM] * len(a...  19.6 us
    ppermute x12, starting transfers between devices, slow_shift(): return lax.ppermute(value, axis, pairs)  14.2 us
    ppermute x3, starting transfers between devices, fast_shift(): return lax.ppermute(value, axis, pairs)  11.4 us
    ppermute x3, waiting for transfers between devices, fast_shift(): return lax.ppermute(value, axis, pairs)  7.84 us
    ppermute x5, waiting for transfers between devices, fast_swap(): return lax.ppermute(value, axis, [(i, i ^ step) for i in range(SUB * SUB)])  6.68 us
    ppermute x5, starting transfers between devices, fast_swap(): return lax.ppermute(value, axis, [(i, i ^ step) for i in range(SUB * SUB)])  2.06 us
  transfers between devices with their start and end apart: 20, of which 13 were waited for; matrix products, arithmetic and copies ran while one was open for 1% of the time, Pallas kernels for 14%

profile of v3, /device:TPU:14, one launch (start us, length us, event | category | flops | bytes accessed | tf_op | source)
XLA Modules:
  0.0 88.6 jit_solution(5518968621144900825)
XLA Ops:
  0.6 1.7 %shard_map.75 = (bf16[2,2,128,128]{3,2,1,0:T(8,128)(2,1)}, bf16[2,128,128]{2,1,0:T(8,128)(2,1)}) custom-call(bf16[128,128]{1,0:T(8,128)(2,1)} %feat_one.1, bf16[128,128]{1,0:T(8,128)(2,1)} %value_one.1, bf16[128,128]{1,0:T(8,128)(2,1)} %feat_two.1, bf16[128,128]{1,0:T(8,128)(2,1)} %value_two.1), custom_call_target="tpu_custom_call" | custom-call | bytes 327680 | tf_op jit(solution)/shard_map/pallas_call | solution.py:173
  2.3 3.3 %collective-permute-start.2 = (bf16[2,2,128,128]{3,2,1,0:T(8,128)(2,1)}, bf16[2,2,128,128]{3,2,1,0:T(8,128)(2,1)S(1)}, u32[]{:S(2)}, u32[]{:S(2)}) collective-permute-start(bf16[2,2,128,128]{3,2,1,0:T(8,128)(2,1)} %get-tuple-element.39), channel_id=1, source_target_pairs={{0,16},{16,32},{32,48},{48,0},{64,80},{80,96},{96,112},{112,64},{1... | collective-permute-start | bytes 393224 | tf_op jit(solution)/shard_map/ppermute | solution.py:30
  5.7 5.4 %collective-permute-start.1 = (bf16[2,2,128,128]{3,2,1,0:T(8,128)(2,1)}, bf16[2,2,128,128]{3,2,1,0:T(8,128)(2,1)S(1)}, u32[]{:S(2)}, u32[]{:S(2)}) collective-permute-start(bf16[2,2,128,128]{3,2,1,0:T(8,128)(2,1)} %get-tuple-element.39), channel_id=1, source_target_pairs={{0,32},{16,48},{32,0},{48,16},{64,96},{80,112},{96,64},{112,80},{1... | collective-permute-start | bytes 393224 | tf_op jit(solution)/shard_map/ppermute | solution.py:30
  11.1 2.7 %collective-permute-start = (bf16[2,2,128,128]{3,2,1,0:T(8,128)(2,1)}, bf16[2,2,128,128]{3,2,1,0:T(8,128)(2,1)S(1)}, u32[]{:S(2)}, u32[]{:S(2)}) collective-permute-start(bf16[2,2,128,128]{3,2,1,0:T(8,128)(2,1)} %get-tuple-element.39), channel_id=1, source_target_pairs={{0,48},{16,0},{32,16},{48,32},{64,112},{80,64},{96,80},{112,96},{1... | collective-permute-start | bytes 393224 | tf_op jit(solution)/shard_map/ppermute | solution.py:30
  13.7 1.0 %collective-permute-start.3 = (bf16[2,128,128]{2,1,0:T(8,128)(2,1)}, bf16[2,128,128]{2,1,0:T(8,128)(2,1)S(1)}, u32[]{:S(2)}, u32[]{:S(2)}) collective-permute-start(bf16[2,128,128]{2,1,0:T(8,128)(2,1)} %get-tuple-element.40), channel_id=1, source_target_pairs={{0,2},{1,3},{2,0},{3,1},{4,6},{5,7},{6,4},{7,5},{8,10},{9,11},{10,... | collective-permute-start | bytes 196616 | tf_op jit(solution)/shard_map/ppermute | solution.py:34
  14.8 0.9 bitcast_dynamic-update-slice_fusion
  15.6 7.8 %collective-permute-done = bf16[2,2,128,128]{3,2,1,0:T(8,128)(2,1)S(1)} collective-permute-done((bf16[2,2,128,128]{3,2,1,0:T(8,128)(2,1)}, bf16[2,2,128,128]{3,2,1,0:T(8,128)(2,1)S(1)}, u32[]{:S(2)}, u32[]{:S(2)}) %collective-permute-start) | collective-permute-done | bytes 131104 | tf_op jit(solution)/shard_map/ppermute | solution.py:30
  23.5 0.0 collective-permute-done.1
  23.5 0.0 collective-permute-done.2
  23.6 1.3 %collective-permute-done.3 = bf16[2,128,128]{2,1,0:T(8,128)(2,1)S(1)} collective-permute-done((bf16[2,128,128]{2,1,0:T(8,128)(2,1)}, bf16[2,128,128]{2,1,0:T(8,128)(2,1)S(1)}, u32[]{:S(2)}, u32[]{:S(2)}) %collective-permute-start.3) | collective-permute-done | bytes 65568 | tf_op jit(solution)/shard_map/ppermute | solution.py:34
  24.9 0.6 collective-permute-start.6
  25.4 2.4 %collective-permute-start.5 = (bf16[9,128,128]{2,1,0:T(8,128)(2,1)S(1)}, bf16[9,128,128]{2,1,0:T(8,128)(2,1)S(1)}, u32[]{:S(2)}, u32[]{:S(2)}) collective-permute-start(bf16[9,128,128]{2,1,0:T(8,128)(2,1)S(1)} %get-tuple-element.43.refs_0_), channel_id=1, source_target_pairs={{0,8},{1,9},{2,10},{3,11},{4,12},{5,13},{6,14},{7,15},{8,0},{9,1},... | collective-permute-start | bytes 884744 | tf_op jit(solution)/shard_map/ppermute | solution.py:25
  27.9 0.0 collective-permute-start.4
  27.9 1.6 %collective-permute-start.9 = (bf16[9,128,128]{2,1,0:T(8,128)(2,1)S(1)}, bf16[9,128,128]{2,1,0:T(8,128)(2,1)S(1)}, u32[]{:S(2)}, u32[]{:S(2)}) collective-permute-start(bf16[9,128,128]{2,1,0:T(8,128)(2,1)S(1)} %get-tuple-element.47.refs_0_), channel_id=1, source_target_pairs={{0,64},{16,80},{32,96},{48,112},{64,128},{80,144},{96,160},{112,17... | collective-permute-start | bytes 884744 | tf_op jit(solution)/shard_map/ppermute | solution.py:25
  29.4 0.9 %collective-permute-start.8 = (bf16[9,128,128]{2,1,0:T(8,128)(2,1)S(1)}, bf16[9,128,128]{2,1,0:T(8,128)(2,1)S(1)}, u32[]{:S(2)}, u32[]{:S(2)}) collective-permute-start(bf16[9,128,128]{2,1,0:T(8,128)(2,1)S(1)} %get-tuple-element.47.refs_0_), channel_id=1, source_target_pairs={{0,128},{16,144},{32,160},{48,176},{64,192},{80,208},{96,224},{112... | collective-permute-start | bytes 884744 | tf_op jit(solution)/shard_map/ppermute | solution.py:25
  30.4 4.5 %collective-permute-done.6.refs_3_ = bf16[9,128,128]{2,1,0:T(8,128)(2,1)S(1)} collective-permute-done((bf16[9,128,128]{2,1,0:T(8,128)(2,1)S(1)}, bf16[9,128,128]{2,1,0:T(8,128)(2,1)S(1)}, u32[]{:S(2)}, u32[]{:S(2)}) %collective-permute-start.6) | collective-permute-done | bytes 294944 | tf_op jit(solution)/shard_map/ppermute | solution.py:25
  34.9 0.4 collective-permute-start.7
  35.3 1.6 %collective-permute-done.5.refs_2_ = bf16[9,128,128]{2,1,0:T(8,128)(2,1)S(1)} collective-permute-done((bf16[9,128,128]{2,1,0:T(8,128)(2,1)S(1)}, bf16[9,128,128]{2,1,0:T(8,128)(2,1)S(1)}, u32[]{:S(2)}, u32[]{:S(2)}) %collective-permute-start.5) | collective-permute-done | bytes 294944 | tf_op jit(solution)/shard_map/ppermute | solution.py:25
  36.9 4.6 %collective-permute-done.4.refs_1_ = bf16[9,128,128]{2,1,0:T(8,128)(2,1)S(1)} collective-permute-done((bf16[9,128,128]{2,1,0:T(8,128)(2,1)S(1)}, bf16[9,128,128]{2,1,0:T(8,128)(2,1)S(1)}, u32[]{:S(2)}, u32[]{:S(2)}) %collective-permute-start.4) | collective-permute-done | bytes 294944 | tf_op jit(solution)/shard_map/ppermute | solution.py:25
  41.5 0.0 collective-permute-done.9.refs_3_
  41.5 0.0 collective-permute-done.8.refs_2_
  41.5 3.4 %collective-permute-done.7.refs_1_ = bf16[9,128,128]{2,1,0:T(8,128)(2,1)S(1)} collective-permute-done((bf16[9,128,128]{2,1,0:T(8,128)(2,1)S(1)}, bf16[9,128,128]{2,1,0:T(8,128)(2,1)S(1)}, u32[]{:S(2)}, u32[]{:S(2)}) %collective-permute-start.7) | collective-permute-done | bytes 294944 | tf_op jit(solution)/shard_map/ppermute | solution.py:25
  45.2 0.1 collective-permute-start.10
  45.3 4.2 %shard_map.76.mine = f32[2,136,512]{2,1,0:T(8,128)S(1)} custom-call(bf16[16,128,128]{2,1,0:T(8,128)(2,1)S(1)} %constant_dynamic-update-slice_fusion.2.queries, bf16[9,128,128]{2,1,0:T(8,128)(2,1)S(1)} %get-tuple-element.47.refs_0_, bf16[9,128,128]{2,1,0:T(8,128)(2,1)S(1)} %collective-permute-done.7.refs_1_, ...), custom_call_target="tpu_custom_call" | custom-call | flops 1073741824 | bytes 2260992 | tf_op jit(solution)/shard_map/pallas_call | solution.py:173
  49.5 0.0 collective-permute-done.10.queries
  49.5 4.2 %shard_map.77 = f32[2,136,512]{2,1,0:T(8,128)S(1)} custom-call(bf16[16,128,128]{2,1,0:T(8,128)(2,1)S(1)} %collective-permute-done.10.queries, bf16[9,128,128]{2,1,0:T(8,128)(2,1)S(1)} %get-tuple-element.47.refs_0_, bf16[9,128,128]{2,1,0:T(8,128)(2,1)S(1)} %collective-permute-done.7.refs_1_, bf16[9,128,128]{2,1,0:T(8,128)(2,1)S(1)} %collective-permute-done.8.refs_2_, ...), custom_call_target="tpu_custom_call" | custom-call | flops 1073741824 | bytes 2260992 | tf_op jit(solution)/shard_map/pallas_call | solution.py:173
  53.7 0.8 collective-permute-start.11
  54.5 4.2 %shard_map.78 = f32[2,136,512]{2,1,0:T(8,128)S(1)} custom-call(bf16[16,128,128]{2,1,0:T(8,128)(2,1)S(1)} %collective-permute-done.10.queries, bf16[9,128,128]{2,1,0:T(8,128)(2,1)S(1)} %get-tuple-element.43.refs_0_, bf16[9,128,128]{2,1,0:T(8,128)(2,1)S(1)} %collective-permute-done.4.refs_1_, bf16[9,128,128]{2,1,0:T(8,128)(2,1)S(1)} %collective-permute-done.5.refs_2_, ...), custom_call_target="tpu_custom_call" | custom-call | flops 1073741824 | bytes 2260992 | tf_op jit(solution)/shard_map/pallas_call | solution.py:173
  58.7 0.1 collective-permute-start.15
  58.8 0.1 shard_map.79
  58.9 3.0 %collective-permute-start.12 = (f32[136,256]{1,0:T(8,128)S(1)}, f32[136,256]{1,0:T(8,128)S(1)}, u32[]{:S(2)}, u32[]{:S(2)}) collective-permute-start(f32[136,256]{1,0:T(8,128)S(1)} %get-tuple-element.59), channel_id=1, source_target_pairs={{0,4},{1,5},{2,6},{3,7},{4,8},{5,9},{6,10},{7,11},{8,12},{9,13},{1... | collective-permute-start | bytes 417800 | tf_op jit(solution)/shard_map/ppermute | solution.py:25
  62.0 0.1 collective-permute-start.13
  62.1 1.3 %collective-permute-start.14 = (f32[136,256]{1,0:T(8,128)S(1)}, f32[136,256]{1,0:T(8,128)S(1)}, u32[]{:S(2)}, u32[]{:S(2)}) collective-permute-start(f32[136,256]{1,0:T(8,128)S(1)} %get-tuple-element.61), channel_id=1, source_target_pairs={{0,12},{1,13},{2,14},{3,15},{4,0},{5,1},{6,2},{7,3},{8,4},{9,5},{1... | collective-permute-start | bytes 417800 | tf_op jit(solution)/shard_map/ppermute | solution.py:25
  63.4 4.2 %shard_map.80.mine = f32[2,136,512]{2,1,0:T(8,128)S(1)} custom-call(bf16[16,128,128]{2,1,0:T(8,128)(2,1)S(1)} %constant_dynamic-update-slice_fusion.2.queries, bf16[9,128,128]{2,1,0:T(8,128)(2,1)S(1)} %get-tuple-element.43.refs_0_, bf16[9,128,128]{2,1,0:T(8,128)(2,1)S(1)} %collective-permute-done.4.refs_1_, ...), custom_call_target="tpu_custom_call" | custom-call | flops 1073741824 | bytes 2260992 | tf_op jit(solution)/shard_map/pallas_call | solution.py:173
  67.6 0.9 %collective-permute-done.12.refs_1_ = f32[136,256]{1,0:T(8,128)S(1)} collective-permute-done((f32[136,256]{1,0:T(8,128)S(1)}, f32[136,256]{1,0:T(8,128)S(1)}, u32[]{:S(2)}, u32[]{:S(2)}) %collective-permute-start.12) | collective-permute-done | bytes 139296 | tf_op jit(solution)/shard_map/ppermute | solution.py:25
  68.5 1.5 %collective-permute-done.13.refs_2_ = f32[136,256]{1,0:T(8,128)S(1)} collective-permute-done((f32[136,256]{1,0:T(8,128)S(1)}, f32[136,256]{1,0:T(8,128)S(1)}, u32[]{:S(2)}, u32[]{:S(2)}) %collective-permute-start.13) | collective-permute-done | bytes 139296 | tf_op jit(solution)/shard_map/ppermute | solution.py:25
  70.0 2.0 %collective-permute-done.14.refs_3_ = f32[136,256]{1,0:T(8,128)S(1)} collective-permute-done((f32[136,256]{1,0:T(8,128)S(1)}, f32[136,256]{1,0:T(8,128)S(1)}, u32[]{:S(2)}, u32[]{:S(2)}) %collective-permute-start.14) | collective-permute-done | bytes 139296 | tf_op jit(solution)/shard_map/ppermute | solution.py:25
  72.1 0.1 shard_map.81
  72.2 0.7 collective-permute-start.16
  72.9 1.6 %collective-permute-start.17 = (f32[136,256]{1,0:T(8,128)S(1)}, f32[136,256]{1,0:T(8,128)S(1)}, u32[]{:S(2)}, u32[]{:S(2)}) collective-permute-start(f32[136,256]{1,0:T(8,128)S(1)} %get-tuple-element.70), channel_id=1, source_target_pairs={{0,128},{16,144},{32,160},{48,176},{64,192},{80,208},{96,224},{112... | collective-permute-start | bytes 417800 | tf_op jit(solution)/shard_map/ppermute | solution.py:25
  74.4 1.6 %collective-permute-start.18 = (f32[136,256]{1,0:T(8,128)S(1)}, f32[136,256]{1,0:T(8,128)S(1)}, u32[]{:S(2)}, u32[]{:S(2)}) collective-permute-start(f32[136,256]{1,0:T(8,128)S(1)} %get-tuple-element.71), channel_id=1, source_target_pairs={{0,192},{16,208},{32,224},{48,240},{64,0},{80,16},{96,32},{112,48}... | collective-permute-start | bytes 417800 | tf_op jit(solution)/shard_map/ppermute | solution.py:25
  76.0 2.8 %collective-permute-done.16.refs_5_ = f32[136,256]{1,0:T(8,128)S(1)} collective-permute-done((f32[136,256]{1,0:T(8,128)S(1)}, f32[136,256]{1,0:T(8,128)S(1)}, u32[]{:S(2)}, u32[]{:S(2)}) %collective-permute-start.16) | collective-permute-done | bytes 139296 | tf_op jit(solution)/shard_map/ppermute | solution.py:25
  78.8 2.2 %collective-permute-done.17.refs_6_ = f32[136,256]{1,0:T(8,128)S(1)} collective-permute-done((f32[136,256]{1,0:T(8,128)S(1)}, f32[136,256]{1,0:T(8,128)S(1)}, u32[]{:S(2)}, u32[]{:S(2)}) %collective-permute-start.17) | collective-permute-done | bytes 139296 | tf_op jit(solution)/shard_map/ppermute | solution.py:25
  81.0 1.3 %collective-permute-done.18.refs_7_ = f32[136,256]{1,0:T(8,128)S(1)} collective-permute-done((f32[136,256]{1,0:T(8,128)S(1)}, f32[136,256]{1,0:T(8,128)S(1)}, u32[]{:S(2)}, u32[]{:S(2)}) %collective-permute-start.18) | collective-permute-done | bytes 139296 | tf_op jit(solution)/shard_map/ppermute | solution.py:25
  82.3 0.1 shard_map.82
  82.4 0.1 collective-permute-start.19
  82.5 5.4 %collective-permute-done.19.theirs = f32[2,136,128]{2,1,0:T(8,128)S(1)} collective-permute-done((f32[2,136,128]{2,1,0:T(8,128)S(1)}, f32[2,136,128]{2,1,0:T(8,128)S(1)}, u32[]{:S(2)}, u32[]{:S(2)}) %collective-permute-start.19) | collective-permute-done | bytes 139296 | tf_op jit(solution)/shard_map/ppermute | solution.py:34
  87.9 0.8 shard_map.83
  (22 shorter events, 0.2 us)
Async XLA Ops:
  2.3 21.2 %collective-permute-start.2 = (bf16[2,2,128,128]{3,2,1,0:T(8,128)(2,1)}, bf16[2,2,128,128]{3,2,1,0:T(8,128)(2,1)S(1)}, u32[]{:S(2)}, u32[]{:S(2)}) collective-permute-start(bf16[2,2,128,128]{3,2,1,0:T(8,128)(2,1)} %get-tuple-element.39), channel_id=1, source_target_pairs={{0,16},{16,32},{32,48},{48,0},{64,80},{80,96},{96,112},{112,64},{1... | collective-permute-start | bytes 393224 | tf_op jit(solution)/shard_map/ppermute | solution.py:30
  5.7 17.8 %collective-permute-start.1 = (bf16[2,2,128,128]{3,2,1,0:T(8,128)(2,1)}, bf16[2,2,128,128]{3,2,1,0:T(8,128)(2,1)S(1)}, u32[]{:S(2)}, u32[]{:S(2)}) collective-permute-start(bf16[2,2,128,128]{3,2,1,0:T(8,128)(2,1)} %get-tuple-element.39), channel_id=1, source_target_pairs={{0,32},{16,48},{32,0},{48,16},{64,96},{80,112},{96,64},{112,80},{1... | collective-permute-start | bytes 393224 | tf_op jit(solution)/shard_map/ppermute | solution.py:30
  11.1 12.4 %collective-permute-start = (bf16[2,2,128,128]{3,2,1,0:T(8,128)(2,1)}, bf16[2,2,128,128]{3,2,1,0:T(8,128)(2,1)S(1)}, u32[]{:S(2)}, u32[]{:S(2)}) collective-permute-start(bf16[2,2,128,128]{3,2,1,0:T(8,128)(2,1)} %get-tuple-element.39), channel_id=1, source_target_pairs={{0,48},{16,0},{32,16},{48,32},{64,112},{80,64},{96,80},{112,96},{1... | collective-permute-start | bytes 393224 | tf_op jit(solution)/shard_map/ppermute | solution.py:30
  13.7 11.1 %collective-permute-start.3 = (bf16[2,128,128]{2,1,0:T(8,128)(2,1)}, bf16[2,128,128]{2,1,0:T(8,128)(2,1)S(1)}, u32[]{:S(2)}, u32[]{:S(2)}) collective-permute-start(bf16[2,128,128]{2,1,0:T(8,128)(2,1)} %get-tuple-element.40), channel_id=1, source_target_pairs={{0,2},{1,3},{2,0},{3,1},{4,6},{5,7},{6,4},{7,5},{8,10},{9,11},{10,... | collective-permute-start | bytes 196616 | tf_op jit(solution)/shard_map/ppermute | solution.py:34
  24.9 10.0 %collective-permute-start.6 = (bf16[9,128,128]{2,1,0:T(8,128)(2,1)S(1)}, bf16[9,128,128]{2,1,0:T(8,128)(2,1)S(1)}, u32[]{:S(2)}, u32[]{:S(2)}) collective-permute-start(bf16[9,128,128]{2,1,0:T(8,128)(2,1)S(1)} %get-tuple-element.43.refs_0_), channel_id=1, source_target_pairs={{0,4},{1,5},{2,6},{3,7},{4,8},{5,9},{6,10},{7,11},{8,12},{9,13},{1... | collective-permute-start | bytes 884744 | tf_op jit(solution)/shard_map/ppermute | solution.py:25
  25.4 11.5 %collective-permute-start.5 = (bf16[9,128,128]{2,1,0:T(8,128)(2,1)S(1)}, bf16[9,128,128]{2,1,0:T(8,128)(2,1)S(1)}, u32[]{:S(2)}, u32[]{:S(2)}) collective-permute-start(bf16[9,128,128]{2,1,0:T(8,128)(2,1)S(1)} %get-tuple-element.43.refs_0_), channel_id=1, source_target_pairs={{0,8},{1,9},{2,10},{3,11},{4,12},{5,13},{6,14},{7,15},{8,0},{9,1},... | collective-permute-start | bytes 884744 | tf_op jit(solution)/shard_map/ppermute | solution.py:25
  27.9 13.7 %collective-permute-start.4 = (bf16[9,128,128]{2,1,0:T(8,128)(2,1)S(1)}, bf16[9,128,128]{2,1,0:T(8,128)(2,1)S(1)}, u32[]{:S(2)}, u32[]{:S(2)}) collective-permute-start(bf16[9,128,128]{2,1,0:T(8,128)(2,1)S(1)} %get-tuple-element.43.refs_0_), channel_id=1, source_target_pairs={{0,12},{1,13},{2,14},{3,15},{4,0},{5,1},{6,2},{7,3},{8,4},{9,5},{1... | collective-permute-start | bytes 884744 | tf_op jit(solution)/shard_map/ppermute | solution.py:25
  27.9 13.7 %collective-permute-start.9 = (bf16[9,128,128]{2,1,0:T(8,128)(2,1)S(1)}, bf16[9,128,128]{2,1,0:T(8,128)(2,1)S(1)}, u32[]{:S(2)}, u32[]{:S(2)}) collective-permute-start(bf16[9,128,128]{2,1,0:T(8,128)(2,1)S(1)} %get-tuple-element.47.refs_0_), channel_id=1, source_target_pairs={{0,64},{16,80},{32,96},{48,112},{64,128},{80,144},{96,160},{112,17... | collective-permute-start | bytes 884744 | tf_op jit(solution)/shard_map/ppermute | solution.py:25
  29.4 12.1 %collective-permute-start.8 = (bf16[9,128,128]{2,1,0:T(8,128)(2,1)S(1)}, bf16[9,128,128]{2,1,0:T(8,128)(2,1)S(1)}, u32[]{:S(2)}, u32[]{:S(2)}) collective-permute-start(bf16[9,128,128]{2,1,0:T(8,128)(2,1)S(1)} %get-tuple-element.47.refs_0_), channel_id=1, source_target_pairs={{0,128},{16,144},{32,160},{48,176},{64,192},{80,208},{96,224},{112... | collective-permute-start | bytes 884744 | tf_op jit(solution)/shard_map/ppermute | solution.py:25
  34.9 10.1 %collective-permute-start.7 = (bf16[9,128,128]{2,1,0:T(8,128)(2,1)S(1)}, bf16[9,128,128]{2,1,0:T(8,128)(2,1)S(1)}, u32[]{:S(2)}, u32[]{:S(2)}) collective-permute-start(bf16[9,128,128]{2,1,0:T(8,128)(2,1)S(1)} %get-tuple-element.47.refs_0_), channel_id=1, source_target_pairs={{0,192},{16,208},{32,224},{48,240},{64,0},{80,16},{96,32},{112,48}... | collective-permute-start | bytes 884744 | tf_op jit(solution)/shard_map/ppermute | solution.py:25
  45.2 4.3 %collective-permute-start.10 = (bf16[16,128,128]{2,1,0:T(8,128)(2,1)S(1)}, bf16[16,128,128]{2,1,0:T(8,128)(2,1)S(1)}, u32[]{:S(2)}, u32[]{:S(2)}) collective-permute-start(bf16[16,128,128]{2,1,0:T(8,128)(2,1)S(1)} %constant_dynamic-update-slice_fusion.2.queries), channel_id=1, source_target_pairs={{0,1},{1,0},{2,3},{3,2},{4,5},{5,4},{6,7},{7,6},{8,9},{9,8},{10,11... | collective-permute-start | bytes 1572872 | tf_op jit(solution)/shard_map/ppermute | solution.py:34
  53.7 5.1 %collective-permute-start.11 = (f32[2,136,512]{2,1,0:T(8,128)S(1)}, f32[2,136,512]{2,1,0:T(8,128)S(1)}, u32[]{:S(2)}, u32[]{:S(2)}) collective-permute-start(f32[2,136,512]{2,1,0:T(8,128)S(1)} %shard_map.77), channel_id=1, source_target_pairs={{0,1},{1,0},{2,3},{3,2},{4,5},{5,4},{6,7},{7,6},{8,9},{9,8},{10,11... | collective-permute-start | bytes 1671176 | tf_op jit(solution)/shard_map/ppermute | solution.py:34
  58.7 13.3 %collective-permute-start.15 = (f32[2,136,512]{2,1,0:T(8,128)S(1)}, f32[2,136,512]{2,1,0:T(8,128)S(1)}, u32[]{:S(2)}, u32[]{:S(2)}) collective-permute-start(f32[2,136,512]{2,1,0:T(8,128)S(1)} %shard_map.78), channel_id=1, source_target_pairs={{0,1},{1,0},{2,3},{3,2},{4,5},{5,4},{6,7},{7,6},{8,9},{9,8},{10,11... | collective-permute-start | bytes 1671176 | tf_op jit(solution)/shard_map/ppermute | solution.py:34
  58.9 9.6 %collective-permute-start.12 = (f32[136,256]{1,0:T(8,128)S(1)}, f32[136,256]{1,0:T(8,128)S(1)}, u32[]{:S(2)}, u32[]{:S(2)}) collective-permute-start(f32[136,256]{1,0:T(8,128)S(1)} %get-tuple-element.59), channel_id=1, source_target_pairs={{0,4},{1,5},{2,6},{3,7},{4,8},{5,9},{6,10},{7,11},{8,12},{9,13},{1... | collective-permute-start | bytes 417800 | tf_op jit(solution)/shard_map/ppermute | solution.py:25
  62.0 8.1 %collective-permute-start.13 = (f32[136,256]{1,0:T(8,128)S(1)}, f32[136,256]{1,0:T(8,128)S(1)}, u32[]{:S(2)}, u32[]{:S(2)}) collective-permute-start(f32[136,256]{1,0:T(8,128)S(1)} %get-tuple-element.60), channel_id=1, source_target_pairs={{0,8},{1,9},{2,10},{3,11},{4,12},{5,13},{6,14},{7,15},{8,0},{9,1},... | collective-permute-start | bytes 417800 | tf_op jit(solution)/shard_map/ppermute | solution.py:25
  62.1 10.0 %collective-permute-start.14 = (f32[136,256]{1,0:T(8,128)S(1)}, f32[136,256]{1,0:T(8,128)S(1)}, u32[]{:S(2)}, u32[]{:S(2)}) collective-permute-start(f32[136,256]{1,0:T(8,128)S(1)} %get-tuple-element.61), channel_id=1, source_target_pairs={{0,12},{1,13},{2,14},{3,15},{4,0},{5,1},{6,2},{7,3},{8,4},{9,5},{1... | collective-permute-start | bytes 417800 | tf_op jit(solution)/shard_map/ppermute | solution.py:25
  72.2 6.6 %collective-permute-start.16 = (f32[136,256]{1,0:T(8,128)S(1)}, f32[136,256]{1,0:T(8,128)S(1)}, u32[]{:S(2)}, u32[]{:S(2)}) collective-permute-start(f32[136,256]{1,0:T(8,128)S(1)} %get-tuple-element.69), channel_id=1, source_target_pairs={{0,64},{16,80},{32,96},{48,112},{64,128},{80,144},{96,160},{112,17... | collective-permute-start | bytes 417800 | tf_op jit(solution)/shard_map/ppermute | solution.py:25
  72.9 8.1 %collective-permute-start.17 = (f32[136,256]{1,0:T(8,128)S(1)}, f32[136,256]{1,0:T(8,128)S(1)}, u32[]{:S(2)}, u32[]{:S(2)}) collective-permute-start(f32[136,256]{1,0:T(8,128)S(1)} %get-tuple-element.70), channel_id=1, source_target_pairs={{0,128},{16,144},{32,160},{48,176},{64,192},{80,208},{96,224},{112... | collective-permute-start | bytes 417800 | tf_op jit(solution)/shard_map/ppermute | solution.py:25
  74.4 7.8 %collective-permute-start.18 = (f32[136,256]{1,0:T(8,128)S(1)}, f32[136,256]{1,0:T(8,128)S(1)}, u32[]{:S(2)}, u32[]{:S(2)}) collective-permute-start(f32[136,256]{1,0:T(8,128)S(1)} %get-tuple-element.71), channel_id=1, source_target_pairs={{0,192},{16,208},{32,224},{48,240},{64,0},{80,16},{96,32},{112,48}... | collective-permute-start | bytes 417800 | tf_op jit(solution)/shard_map/ppermute | solution.py:25
  82.4 5.5 %collective-permute-start.19 = (f32[2,136,128]{2,1,0:T(8,128)S(1)}, f32[2,136,128]{2,1,0:T(8,128)S(1)}, u32[]{:S(2)}, u32[]{:S(2)}) collective-permute-start(f32[2,136,128]{2,1,0:T(8,128)S(1)} %get-tuple-element.73), channel_id=1, source_target_pairs={{0,2},{1,3},{2,0},{3,1},{4,6},{5,7},{6,4},{7,5},{8,10},{9,11},{10,... | collective-permute-start | bytes 417800 | tf_op jit(solution)/shard_map/ppermute | solution.py:34

commit v4 on v3

--- a/solution.py
+++ b/solution.py
@@ -34,19 +34,20 @@
     return lax.ppermute(value, axis, [(i, i ^ step) for i in range(SUB * SUB)])
 
 
-def pack_kernel(feat_one, value_one, feat_two, value_two, out, feats, held, sems):
-    sources = ((feat_one, value_one), (feat_two, value_two))
+def pack_kernel(feat_one, value_one, feat_two, value_two, both, feats, held, sems):
     copies = []
-    for side, (feat, value) in enumerate(sources):
-        copies.append(pltpu.make_async_copy(value, held.at[side], sems.at[2 * side]))
-        copies.append(pltpu.make_async_copy(feat, feats.at[side], sems.at[2 * side + 1]))
+    for side, value in enumerate((value_one, value_two)):
+        copies.append(pltpu.make_async_copy(value, held.at[side], sems.at[side]))
+    for side, feat in enumerate((feat_one, feat_two)):
+        copies.append(pltpu.make_async_copy(feat, feats.at[side], sems.at[2 + side]))
     for copy in copies:
         copy.start()
     for side in range(2):
-        copies[2 * side].wait()
-        out[side, 1] = held[side].astype(jnp.float32).T.astype(jnp.bfloat16)
-        copies[2 * side + 1].wait()
-        out[side, 0] = feats[side]
+        copies[side].wait()
+        both[side, 1] = held[side].astype(jnp.float32).T.astype(jnp.bfloat16)
+    for side in range(2):
+        copies[2 + side].wait()
+        both[side, 0] = feats[side]
 
 
 def piece_coords(start, total):
@@ -106,8 +107,8 @@
     return with_peak(*merge([peak_of(part) for part in parts], parts))
 
 
-def attend(scale, query, blocks):
-    peaks, parts = [], []
+def attend(scale, query, blocks, carry):
+    peaks, parts = [peak_of(part) for part in carry], list(carry)
     for keys, values in blocks:
         score = lax.dot_general(
             keys, query, (((1,), (1,)), ((), ())), preferred_element_type=jnp.float32
@@ -119,20 +120,26 @@
     return with_peak(*merge(peaks, parts))
 
 
-def score_kernel(total, scale, side, first, queries, *refs):
-    keys, (out,) = refs[:SUB], refs[SUB:]
-
-    def block_of(slow):
-        tiles = keys[slow]
-        feats = jnp.concatenate([tiles[2 * fast] for fast in range(SUB)], axis=0)
-        values = jnp.concatenate([tiles[2 * fast + 1] for fast in range(SUB)], axis=1)
-        extra = [coord_rows(key_start(side, slow, fast), total) for fast in range(SUB)]
+def score_kernel(total, scale, side, fasts, carried, queries, *refs):
+    keys, refs = refs[:SUB], refs[SUB:]
+    out = refs[-1]
+
+    def block_of(index, fast):
+        feats = jnp.concatenate([key[2 * index] for key in keys], axis=0)
+        values = jnp.concatenate([key[2 * index + 1] for key in keys], axis=1)
+        extra = [coord_rows(key_start(side, slow, fast), total) for slow in range(SUB)]
         return feats, jnp.concatenate([values, jnp.concatenate(extra, axis=1)], axis=0)
 
     def step(part, _):
-        tiles = [queries[first + part * SUB + piece] for piece in range(SUB)]
+        tiles = [
+            queries[(half * 2 + side) * SUB + part * 2 + slow]
+            for slow in range(2)
+            for half in range(2)
+        ]
         query = jnp.concatenate(tiles, axis=0)
-        out[part] = attend(scale, query, [block_of(slow) for slow in range(SUB)])
+        blocks = [block_of(index, fast) for index, fast in enumerate(fasts)]
+        carry = [refs[0][part]] if carried else []
+        out[part] = attend(scale, query, blocks, carry)
         return 0
 
     lax.fori_loop(0, 2, step, 0)
@@ -198,7 +205,7 @@
 def body(feat_one, feat_two, value_one, value_two):
     total = feat_one.shape[0] * lax.axis_size("row") * lax.axis_size("col")
     scale = math.log2(math.e) / math.sqrt(WIDTH)
-    own, feats = call(
+    both, feats = call(
         pack_kernel,
         [bf16(2, 2, SHARD, WIDTH), bf16(2, SHARD, WIDTH)],
         (feat_one, value_one, feat_two, value_two),
@@ -210,28 +217,30 @@
         vmem=62 << 20,
     )
 
-    pieces = [own] + [fast_shift("row", own, -step) for step in range(1, SUB)]
+    def gathered(axis, value):
+        return [value] + [slow_shift(axis, value, -step) for step in range(1, SUB)]
+
     partner = fast_swap("col", feats, 2)
-    sends = [
-        jnp.concatenate([piece[side] for piece in pieces] + [partner[side : side + 1]])
-        for side in range(2)
-    ]
-    sends = together(sends)
-    tiles = [
-        [send] + [slow_shift(axis, send, -step) for step in range(1, SUB)]
-        for axis, send in zip(("col", "row"), sends)
-    ]
-    tiles = together(tiles)
-    queries = jnp.stack(
-        [tile[index] for side in tiles for tile in side for index in (0, 2 * SUB)]
-    )
-    others = fast_swap("col", queries, 1)
-
-    def score(side, queries):
-        shapes = [f32(2, ROWS, BLOCK)]
-        kernel = functools.partial(score_kernel, total, scale, side, side * 2 * SUB)
-        work = 2 * SUB * SHARD * SUB * BLOCK
-        return call(kernel, shapes, (queries, *tiles[1 - side]), work=work)[0]
+    others = [fast_shift("row", both, -step) for step in range(1, SUB)]
+    own = [jnp.concatenate([both[side], partner[side : side + 1]]) for side in range(2)]
+    near = [gathered("col", own[0]), gathered("row", own[1])]
+    sends = [jnp.concatenate([piece[side] for piece in others]) for side in range(2)]
+    near, sends = together((near, sends))
+    far = [gathered("col", sends[0]), gathered("row", sends[1])]
+    queries = jnp.stack([tile[at] for at in (0, 2) for side in near for tile in side])
+    partners = fast_swap("col", queries, 1)
+
+    def score(side, queries, keys, fasts, carry=()):
+        kernel = functools.partial(score_kernel, total, scale, side, fasts, len(carry))
+        work = 2 * SUB * SHARD * SUB * SHARD * len(fasts)
+        args = (queries, *keys[1 - side], *carry)
+        return call(kernel, [f32(2, ROWS, BLOCK)], args, work=work)[0]
+
+    rest = tuple(range(1, SUB))
+    early = [score(side, queries, near, (0,)) for side in range(2)]
+    partners, early = together((partners, early))
+    early_send = [score(side, partners, near, (0,)) for side in range(2)]
+    far[1], early_send = together((far[1], early_send))
 
     def core_merge(mine, theirs):
         return call(core_kernel, [f32(ROWS, 2 * SHARD)] * SUB, (mine, theirs))
@@ -239,17 +248,17 @@
     def spread(axis, parts):
         return [parts[0]] + [slow_shift(axis, parts[step], step) for step in range(1, SUB)]
 
-    keep_one = score(0, queries)
-    others, keep_one = together((others, keep_one))
-    send_one = score(0, others)
+    send_one = score(0, partners, far, rest, (early_send[0],))
     theirs_one = fast_swap("col", send_one, 1)
-    others, _ = together((others, send_one))
-    send_two = score(1, others)
+    queries, _ = together((queries, send_one))
+    keep_one = score(0, queries, far, rest, (early[0],))
+    partners, keep_one = together((partners, keep_one))
+    send_two = score(1, partners, far, rest, (early_send[1],))
     theirs_two = fast_swap("col", send_two, 1)
     rows = core_merge(keep_one, theirs_one)
     queries, _, rows = together((queries, send_two, rows))
     rows = spread("col", rows)
-    keep_two = score(1, queries)
+    keep_two = score(1, queries, far, rest, (early[1],))
     rows, keep_two = together((rows, keep_two))
     cols = spread("row", core_merge(keep_two, theirs_two))
     keep, send = call(chip_kernel, [f32(2, ROWS, SHARD)] * 2, (*rows, *cols))

time: 88.8 us -> 92.3 us (1.039)
  the two profiles are of different devices: /device:TPU:14 before, /device:TPU:10 now
where the time goes in v4:
time: 92.3 us; the launch traced here: 92.1 us
  starting transfers between devices  41.7 us (45%)
  waiting for transfers between devices  27.3 us (30%)
  Pallas kernels  20.9 us (23%)
  local copies, waits for them, and re-layouts  1.07 us (1%)
  between operations  0.96 us (1%)
    ppermute x18, starting transfers between devices, slow_shift(): return lax.ppermute(value, axis, pairs)  28.5 us
    pallas_call x13, Pallas kernels, call(): pl.pallas_call(kernel, out_shape=shapes, in_specs=specs or [VMEM] * len(a...  20.9 us
    ppermute x5, waiting for transfers between devices, fast_swap(): return lax.ppermute(value, axis, [(i, i ^ step) for i in range(SUB * SUB)])  14.8 us
    ppermute x18, waiting for transfers between devices, slow_shift(): return lax.ppermute(value, axis, pairs)  12.4 us
    ppermute x3, starting transfers between devices, fast_shift(): return lax.ppermute(value, axis, pairs)  11.4 us
    ppermute x5, starting transfers between devices, fast_swap(): return lax.ppermute(value, axis, [(i, i ^ step) for i in range(SUB * SUB)])  1.88 us
  transfers between devices with their start and end apart: 26, of which 10 were waited for; matrix products, arithmetic and copies ran while one was open for 1% of the time, Pallas kernels for 20%

profile of v4, /device:TPU:10, one launch (start us, length us, event | category | flops | bytes accessed | tf_op | source)
XLA Modules:
  0.0 92.1 jit_solution(8814044749919161751)
XLA Ops:
  0.6 1.7 %shard_map.75 = (bf16[2,2,128,128]{3,2,1,0:T(8,128)(2,1)}, bf16[2,128,128]{2,1,0:T(8,128)(2,1)}) custom-call(bf16[128,128]{1,0:T(8,128)(2,1)} %feat_one.1, bf16[128,128]{1,0:T(8,128)(2,1)} %value_one.1, bf16[128,128]{1,0:T(8,128)(2,1)} %feat_two.1, bf16[128,128]{1,0:T(8,128)(2,1)} %value_two.1), custom_call_target="tpu_custom_call" | custom-call | bytes 327680 | tf_op jit(solution)/shard_map/pallas_call | solution.py:180
  2.3 3.3 %collective-permute-start.9 = (bf16[2,2,128,128]{3,2,1,0:T(8,128)(2,1)}, bf16[2,2,128,128]{3,2,1,0:T(8,128)(2,1)S(1)}, u32[]{:S(2)}, u32[]{:S(2)}) collective-permute-start(bf16[2,2,128,128]{3,2,1,0:T(8,128)(2,1)} %get-tuple-element.48), channel_id=1, source_target_pairs={{0,16},{16,32},{32,48},{48,0},{64,80},{80,96},{96,112},{112,64},{1... | collective-permute-start | bytes 393224 | tf_op jit(solution)/shard_map/ppermute | solution.py:30
  5.7 5.4 %collective-permute-start.8 = (bf16[2,2,128,128]{3,2,1,0:T(8,128)(2,1)}, bf16[2,2,128,128]{3,2,1,0:T(8,128)(2,1)S(1)}, u32[]{:S(2)}, u32[]{:S(2)}) collective-permute-start(bf16[2,2,128,128]{3,2,1,0:T(8,128)(2,1)} %get-tuple-element.48), channel_id=1, source_target_pairs={{0,32},{16,48},{32,0},{48,16},{64,96},{80,112},{96,64},{112,80},{1... | collective-permute-start | bytes 393224 | tf_op jit(solution)/shard_map/ppermute | solution.py:30
  11.0 2.7 %collective-permute-start.7 = (bf16[2,2,128,128]{3,2,1,0:T(8,128)(2,1)}, bf16[2,2,128,128]{3,2,1,0:T(8,128)(2,1)S(1)}, u32[]{:S(2)}, u32[]{:S(2)}) collective-permute-start(bf16[2,2,128,128]{3,2,1,0:T(8,128)(2,1)} %get-tuple-element.48), channel_id=1, source_target_pairs={{0,48},{16,0},{32,16},{48,32},{64,112},{80,64},{96,80},{112,96},{1... | collective-permute-start | bytes 393224 | tf_op jit(solution)/shard_map/ppermute | solution.py:30
  13.7 1.0 %collective-permute-start = (bf16[2,128,128]{2,1,0:T(8,128)(2,1)}, bf16[2,128,128]{2,1,0:T(8,128)(2,1)S(1)}, u32[]{:S(2)}, u32[]{:S(2)}) collective-permute-start(bf16[2,128,128]{2,1,0:T(8,128)(2,1)} %get-tuple-element.49), channel_id=1, source_target_pairs={{0,2},{1,3},{2,0},{3,1},{4,6},{5,7},{6,4},{7,5},{8,10},{9,11},{10,... | collective-permute-start | bytes 196616 | tf_op jit(solution)/shard_map/ppermute | solution.py:34
  14.7 0.9 slice_bitcast_fusion.6
  15.6 9.2 %collective-permute-done = bf16[2,128,128]{2,1,0:T(8,128)(2,1)S(1)} collective-permute-done((bf16[2,128,128]{2,1,0:T(8,128)(2,1)}, bf16[2,128,128]{2,1,0:T(8,128)(2,1)S(1)}, u32[]{:S(2)}, u32[]{:S(2)}) %collective-permute-start) | collective-permute-done | bytes 65568 | tf_op jit(solution)/shard_map/ppermute | solution.py:34
  24.9 0.6 collective-permute-start.1
  25.5 2.4 %collective-permute-start.2 = (bf16[3,128,128]{2,1,0:T(8,128)(2,1)S(1)}, bf16[3,128,128]{2,1,0:T(8,128)(2,1)S(1)}, u32[]{:S(2)}, u32[]{:S(2)}) collective-permute-start(bf16[3,128,128]{2,1,0:T(8,128)(2,1)S(1)} %pad_maximum_fusion.2.refs_0_), channel_id=1, source_target_pairs={{0,8},{1,9},{2,10},{3,11},{4,12},{5,13},{6,14},{7,15},{8,0},{9,1},... | collective-permute-start | bytes 294920 | tf_op jit(solution)/shard_map/ppermute | solution.py:25
  27.9 1.9 %collective-permute-start.3 = (bf16[3,128,128]{2,1,0:T(8,128)(2,1)S(1)}, bf16[3,128,128]{2,1,0:T(8,128)(2,1)S(1)}, u32[]{:S(2)}, u32[]{:S(2)}) collective-permute-start(bf16[3,128,128]{2,1,0:T(8,128)(2,1)S(1)} %pad_maximum_fusion.2.refs_0_), channel_id=1, source_target_pairs={{0,4},{1,5},{2,6},{3,7},{4,8},{5,9},{6,10},{7,11},{8,12},{9,13},{1... | collective-permute-start | bytes 294920 | tf_op jit(solution)/shard_map/ppermute | solution.py:25
  29.8 0.5 collective-permute-start.4
  30.4 2.7 %collective-permute-start.5 = (bf16[3,128,128]{2,1,0:T(8,128)(2,1)S(1)}, bf16[3,128,128]{2,1,0:T(8,128)(2,1)S(1)}, u32[]{:S(2)}, u32[]{:S(2)}) collective-permute-start(bf16[3,128,128]{2,1,0:T(8,128)(2,1)S(1)} %pad_maximum_fusion.3.refs_0_), channel_id=1, source_target_pairs={{0,128},{16,144},{32,160},{48,176},{64,192},{80,208},{96,224},{112... | collective-permute-start | bytes 294920 | tf_op jit(solution)/shard_map/ppermute | solution.py:25
  33.1 2.0 %collective-permute-start.6 = (bf16[3,128,128]{2,1,0:T(8,128)(2,1)S(1)}, bf16[3,128,128]{2,1,0:T(8,128)(2,1)S(1)}, u32[]{:S(2)}, u32[]{:S(2)}) collective-permute-start(bf16[3,128,128]{2,1,0:T(8,128)(2,1)S(1)} %pad_maximum_fusion.3.refs_0_), channel_id=1, source_target_pairs={{0,64},{16,80},{32,96},{48,112},{64,128},{80,144},{96,160},{112,17... | collective-permute-start | bytes 294920 | tf_op jit(solution)/shard_map/ppermute | solution.py:25
  35.1 0.3 collective-permute-done.4.refs_1_
  35.5 1.1 %collective-permute-done.5.refs_2_ = bf16[3,128,128]{2,1,0:T(8,128)(2,1)S(1)} collective-permute-done((bf16[3,128,128]{2,1,0:T(8,128)(2,1)S(1)}, bf16[3,128,128]{2,1,0:T(8,128)(2,1)S(1)}, u32[]{:S(2)}, u32[]{:S(2)}) %collective-permute-start.5) | collective-permute-done | bytes 98336 | tf_op jit(solution)/shard_map/ppermute | solution.py:25
  36.6 1.2 %collective-permute-done.6.refs_3_ = bf16[3,128,128]{2,1,0:T(8,128)(2,1)S(1)} collective-permute-done((bf16[3,128,128]{2,1,0:T(8,128)(2,1)S(1)}, bf16[3,128,128]{2,1,0:T(8,128)(2,1)S(1)}, u32[]{:S(2)}, u32[]{:S(2)}) %collective-permute-start.6) | collective-permute-done | bytes 98336 | tf_op jit(solution)/shard_map/ppermute | solution.py:25
  38.0 0.1 collective-permute-start.10
  38.1 3.0 %collective-permute-start.11 = (bf16[6,128,128]{2,1,0:T(8,128)(2,1)S(1)}, bf16[6,128,128]{2,1,0:T(8,128)(2,1)S(1)}, u32[]{:S(2)}, u32[]{:S(2)}) collective-permute-start(bf16[6,128,128]{2,1,0:T(8,128)(2,1)S(1)} %get-tuple-element.60.refs_0_), channel_id=1, source_target_pairs={{0,192},{16,208},{32,224},{48,240},{64,0},{80,16},{96,32},{112,48}... | collective-permute-start | bytes 589832 | tf_op jit(solution)/shard_map/ppermute | solution.py:25
  41.1 0.5 collective-permute-start.12
  41.5 1.6 %collective-permute-start.13 = (bf16[6,128,128]{2,1,0:T(8,128)(2,1)S(1)}, bf16[6,128,128]{2,1,0:T(8,128)(2,1)S(1)}, u32[]{:S(2)}, u32[]{:S(2)}) collective-permute-start(bf16[6,128,128]{2,1,0:T(8,128)(2,1)S(1)} %get-tuple-element.60.refs_0_), channel_id=1, source_target_pairs={{0,64},{16,80},{32,96},{48,112},{64,128},{80,144},{96,160},{112,17... | collective-permute-start | bytes 589832 | tf_op jit(solution)/shard_map/ppermute | solution.py:25
  43.1 0.2 collective-permute-start.14
  43.3 1.3 %shard_map.76.refs_4_ = f32[2,136,512]{2,1,0:T(8,128)S(1)} custom-call(bf16[16,128,128]{2,1,0:T(8,128)(2,1)S(1)} %constant_dynamic-update-slice_fusion.queries, bf16[3,128,128]{2,1,0:T(8,128)(2,1)S(1)} %pad_maximum_fusion.3.refs_0_, bf16[3,128,128]{2,1,0:T(8,128)(2,1)S(1)} %collective-permute-done.4.refs_1_, ...), custom_call_target="tpu_custom_call" | custom-call | flops 268435456 | bytes 1474560 | tf_op jit(solution)/shard_map/pallas_call | solution.py:180
  44.6 1.3 %shard_map.77.refs_4_ = f32[2,136,512]{2,1,0:T(8,128)S(1)} custom-call(bf16[16,128,128]{2,1,0:T(8,128)(2,1)S(1)} %constant_dynamic-update-slice_fusion.queries, bf16[3,128,128]{2,1,0:T(8,128)(2,1)S(1)} %pad_maximum_fusion.2.refs_0_, bf16[3,128,128]{2,1,0:T(8,128)(2,1)S(1)} %collective-permute-done.1.refs_1_, ...), custom_call_target="tpu_custom_call" | custom-call | flops 268435456 | bytes 1474560 | tf_op jit(solution)/shard_map/pallas_call | solution.py:180
  45.9 1.5 %collective-permute-start.15 = (bf16[6,128,128]{2,1,0:T(8,128)(2,1)S(1)}, bf16[6,128,128]{2,1,0:T(8,128)(2,1)S(1)}, u32[]{:S(2)}, u32[]{:S(2)}) collective-permute-start(bf16[6,128,128]{2,1,0:T(8,128)(2,1)S(1)} %get-tuple-element.68.refs_0_), channel_id=1, source_target_pairs={{0,8},{1,9},{2,10},{3,11},{4,12},{5,13},{6,14},{7,15},{8,0},{9,1},... | collective-permute-start | bytes 589832 | tf_op jit(solution)/shard_map/ppermute | solution.py:25
  47.3 2.6 %collective-permute-start.16 = (bf16[6,128,128]{2,1,0:T(8,128)(2,1)S(1)}, bf16[6,128,128]{2,1,0:T(8,128)(2,1)S(1)}, u32[]{:S(2)}, u32[]{:S(2)}) collective-permute-start(bf16[6,128,128]{2,1,0:T(8,128)(2,1)S(1)} %get-tuple-element.68.refs_0_), channel_id=1, source_target_pairs={{0,4},{1,5},{2,6},{3,7},{4,8},{5,9},{6,10},{7,11},{8,12},{9,13},{1... | collective-permute-start | bytes 589832 | tf_op jit(solution)/shard_map/ppermute | solution.py:25
  50.0 1.3 %shard_map.78.refs_4_ = f32[2,136,512]{2,1,0:T(8,128)S(1)} custom-call(bf16[16,128,128]{2,1,0:T(8,128)(2,1)S(1)} %collective-permute-done.10.queries, bf16[3,128,128]{2,1,0:T(8,128)(2,1)S(1)} %pad_maximum_fusion.3.refs_0_, bf16[3,128,128]{2,1,0:T(8,128)(2,1)S(1)} %collective-permute-done.4.refs_1_, bf16[3,128,128]{2,1,0:T(8,128)(2,1)S(1)} %collective-permute-done.5.refs_2_, ...), custom_call_target="tpu_custom_call" | custom-call | flops 268435456 | bytes 1474560 | tf_op jit(solution)/shard_map/pallas_call | solution.py:180
  51.2 1.3 %shard_map.79.refs_4_ = f32[2,136,512]{2,1,0:T(8,128)S(1)} custom-call(bf16[16,128,128]{2,1,0:T(8,128)(2,1)S(1)} %collective-permute-done.10.queries, bf16[3,128,128]{2,1,0:T(8,128)(2,1)S(1)} %pad_maximum_fusion.2.refs_0_, bf16[3,128,128]{2,1,0:T(8,128)(2,1)S(1)} %collective-permute-done.1.refs_1_, bf16[3,128,128]{2,1,0:T(8,128)(2,1)S(1)} %collective-permute-done.2.refs_2_, ...), custom_call_target="tpu_custom_call" | custom-call | flops 268435456 | bytes 1474560 | tf_op jit(solution)/shard_map/pallas_call | solution.py:180
  52.5 3.3 %shard_map.80 = f32[2,136,512]{2,1,0:T(8,128)S(1)} custom-call(bf16[16,128,128]{2,1,0:T(8,128)(2,1)S(1)} %collective-permute-done.10.queries, bf16[6,128,128]{2,1,0:T(8,128)(2,1)S(1)} %get-tuple-element.60.refs_0_, bf16[6,128,128]{2,1,0:T(8,128)(2,1)S(1)} %collective-permute-done.11.refs_1_, bf16[6,128,128]{2,1,0:T(8,128)(2,1)S(1)} %collective-permute-done.12.refs_2_, ...), custom_call_target="tpu_custom_call" | custom-call | flops 805306368 | bytes 2424832 | tf_op jit(solution)/shard_map/pallas_call | solution.py:180
  55.8 0.1 collective-permute-start.17
  55.9 3.3 %shard_map.81.mine = f32[2,136,512]{2,1,0:T(8,128)S(1)} custom-call(bf16[16,128,128]{2,1,0:T(8,128)(2,1)S(1)} %constant_dynamic-update-slice_fusion.queries, bf16[6,128,128]{2,1,0:T(8,128)(2,1)S(1)} %get-tuple-element.60.refs_0_, bf16[6,128,128]{2,1,0:T(8,128)(2,1)S(1)} %collective-permute-done.11.refs_1_, ...), custom_call_target="tpu_custom_call" | custom-call | flops 805306368 | bytes 2424832 | tf_op jit(solution)/shard_map/pallas_call | solution.py:180
  59.2 3.3 %shard_map.82 = f32[2,136,512]{2,1,0:T(8,128)S(1)} custom-call(bf16[16,128,128]{2,1,0:T(8,128)(2,1)S(1)} %collective-permute-done.10.queries, bf16[6,128,128]{2,1,0:T(8,128)(2,1)S(1)} %get-tuple-element.68.refs_0_, bf16[6,128,128]{2,1,0:T(8,128)(2,1)S(1)} %collective-permute-done.14.refs_1_, bf16[6,128,128]{2,1,0:T(8,128)(2,1)S(1)} %collective-permute-done.15.refs_2_, ...), custom_call_target="tpu_custom_call" | custom-call | flops 805306368 | bytes 2424832 | tf_op jit(solution)/shard_map/pallas_call | solution.py:180
  62.5 0.6 collective-permute-start.21
  63.2 0.2 collective-permute-start.18
  63.4 2.6 %collective-permute-start.19 = (f32[136,256]{1,0:T(8,128)S(1)}, f32[136,256]{1,0:T(8,128)S(1)}, u32[]{:S(2)}, u32[]{:S(2)}) collective-permute-start(f32[136,256]{1,0:T(8,128)S(1)} %get-tuple-element.77), channel_id=1, source_target_pairs={{0,8},{1,9},{2,10},{3,11},{4,12},{5,13},{6,14},{7,15},{8,0},{9,1},... | collective-permute-start | bytes 417800 | tf_op jit(solution)/shard_map/ppermute | solution.py:25
  66.0 1.9 %collective-permute-start.20 = (f32[136,256]{1,0:T(8,128)S(1)}, f32[136,256]{1,0:T(8,128)S(1)}, u32[]{:S(2)}, u32[]{:S(2)}) collective-permute-start(f32[136,256]{1,0:T(8,128)S(1)} %get-tuple-element.78), channel_id=1, source_target_pairs={{0,12},{1,13},{2,14},{3,15},{4,0},{5,1},{6,2},{7,3},{8,4},{9,5},{1... | collective-permute-start | bytes 417800 | tf_op jit(solution)/shard_map/ppermute | solution.py:25
  67.9 3.3 %shard_map.84.mine = f32[2,136,512]{2,1,0:T(8,128)S(1)} custom-call(bf16[16,128,128]{2,1,0:T(8,128)(2,1)S(1)} %constant_dynamic-update-slice_fusion.queries, bf16[6,128,128]{2,1,0:T(8,128)(2,1)S(1)} %get-tuple-element.68.refs_0_, bf16[6,128,128]{2,1,0:T(8,128)(2,1)S(1)} %collective-permute-done.14.refs_1_, ...), custom_call_target="tpu_custom_call" | custom-call | flops 805306368 | bytes 2424832 | tf_op jit(solution)/shard_map/pallas_call | solution.py:180
  71.2 0.3 collective-permute-done.19.refs_2_
  71.5 2.1 %collective-permute-done.20.refs_3_ = f32[136,256]{1,0:T(8,128)S(1)} collective-permute-done((f32[136,256]{1,0:T(8,128)S(1)}, f32[136,256]{1,0:T(8,128)S(1)}, u32[]{:S(2)}, u32[]{:S(2)}) %collective-permute-start.20) | collective-permute-done | bytes 139296 | tf_op jit(solution)/shard_map/ppermute | solution.py:25
  73.6 2.1 %collective-permute-start.22 = (f32[136,256]{1,0:T(8,128)S(1)}, f32[136,256]{1,0:T(8,128)S(1)}, u32[]{:S(2)}, u32[]{:S(2)}) collective-permute-start(f32[136,256]{1,0:T(8,128)S(1)} %get-tuple-element.87), channel_id=1, source_target_pairs={{0,64},{16,80},{32,96},{48,112},{64,128},{80,144},{96,160},{112,17... | collective-permute-start | bytes 417800 | tf_op jit(solution)/shard_map/ppermute | solution.py:25
  75.7 1.9 %collective-permute-start.23 = (f32[136,256]{1,0:T(8,128)S(1)}, f32[136,256]{1,0:T(8,128)S(1)}, u32[]{:S(2)}, u32[]{:S(2)}) collective-permute-start(f32[136,256]{1,0:T(8,128)S(1)} %get-tuple-element.88), channel_id=1, source_target_pairs={{0,128},{16,144},{32,160},{48,176},{64,192},{80,208},{96,224},{112... | collective-permute-start | bytes 417800 | tf_op jit(solution)/shard_map/ppermute | solution.py:25
  77.5 0.5 collective-permute-start.24
  78.0 3.8 %collective-permute-done.22.refs_5_ = f32[136,256]{1,0:T(8,128)S(1)} collective-permute-done((f32[136,256]{1,0:T(8,128)S(1)}, f32[136,256]{1,0:T(8,128)S(1)}, u32[]{:S(2)}, u32[]{:S(2)}) %collective-permute-start.22) | collective-permute-done | bytes 139296 | tf_op jit(solution)/shard_map/ppermute | solution.py:25
  81.8 2.0 %collective-permute-done.23.refs_6_ = f32[136,256]{1,0:T(8,128)S(1)} collective-permute-done((f32[136,256]{1,0:T(8,128)S(1)}, f32[136,256]{1,0:T(8,128)S(1)}, u32[]{:S(2)}, u32[]{:S(2)}) %collective-permute-start.23) | collective-permute-done | bytes 139296 | tf_op jit(solution)/shard_map/ppermute | solution.py:25
  83.8 1.7 %collective-permute-done.24.refs_7_ = f32[136,256]{1,0:T(8,128)S(1)} collective-permute-done((f32[136,256]{1,0:T(8,128)S(1)}, f32[136,256]{1,0:T(8,128)S(1)}, u32[]{:S(2)}, u32[]{:S(2)}) %collective-permute-start.24) | collective-permute-done | bytes 139296 | tf_op jit(solution)/shard_map/ppermute | solution.py:25
  85.5 0.1 shard_map.86
  85.6 0.1 collective-permute-start.25
  85.7 5.6 %collective-permute-done.25.theirs = f32[2,136,128]{2,1,0:T(8,128)S(1)} collective-permute-done((f32[2,136,128]{2,1,0:T(8,128)S(1)}, f32[2,136,128]{2,1,0:T(8,128)S(1)}, u32[]{:S(2)}, u32[]{:S(2)}) %collective-permute-start.25) | collective-permute-done | bytes 139296 | tf_op jit(solution)/shard_map/ppermute | solution.py:34
  91.3 0.8 shard_map.87
  (41 shorter events, 0.5 us)
Async XLA Ops:
  2.3 25.6 %collective-permute-start.9 = (bf16[2,2,128,128]{3,2,1,0:T(8,128)(2,1)}, bf16[2,2,128,128]{3,2,1,0:T(8,128)(2,1)S(1)}, u32[]{:S(2)}, u32[]{:S(2)}) collective-permute-start(bf16[2,2,128,128]{3,2,1,0:T(8,128)(2,1)} %get-tuple-element.48), channel_id=1, source_target_pairs={{0,16},{16,32},{32,48},{48,0},{64,80},{80,96},{96,112},{112,64},{1... | collective-permute-start | bytes 393224 | tf_op jit(solution)/shard_map/ppermute | solution.py:30
  5.7 24.2 %collective-permute-start.8 = (bf16[2,2,128,128]{3,2,1,0:T(8,128)(2,1)}, bf16[2,2,128,128]{3,2,1,0:T(8,128)(2,1)S(1)}, u32[]{:S(2)}, u32[]{:S(2)}) collective-permute-start(bf16[2,2,128,128]{3,2,1,0:T(8,128)(2,1)} %get-tuple-element.48), channel_id=1, source_target_pairs={{0,32},{16,48},{32,0},{48,16},{64,96},{80,112},{96,64},{112,80},{1... | collective-permute-start | bytes 393224 | tf_op jit(solution)/shard_map/ppermute | solution.py:30
  11.0 19.3 %collective-permute-start.7 = (bf16[2,2,128,128]{3,2,1,0:T(8,128)(2,1)}, bf16[2,2,128,128]{3,2,1,0:T(8,128)(2,1)S(1)}, u32[]{:S(2)}, u32[]{:S(2)}) collective-permute-start(bf16[2,2,128,128]{3,2,1,0:T(8,128)(2,1)} %get-tuple-element.48), channel_id=1, source_target_pairs={{0,48},{16,0},{32,16},{48,32},{64,112},{80,64},{96,80},{112,96},{1... | collective-permute-start | bytes 393224 | tf_op jit(solution)/shard_map/ppermute | solution.py:30
  13.7 11.1 %collective-permute-start = (bf16[2,128,128]{2,1,0:T(8,128)(2,1)}, bf16[2,128,128]{2,1,0:T(8,128)(2,1)S(1)}, u32[]{:S(2)}, u32[]{:S(2)}) collective-permute-start(bf16[2,128,128]{2,1,0:T(8,128)(2,1)} %get-tuple-element.49), channel_id=1, source_target_pairs={{0,2},{1,3},{2,0},{3,1},{4,6},{5,7},{6,4},{7,5},{8,10},{9,11},{10,... | collective-permute-start | bytes 196616 | tf_op jit(solution)/shard_map/ppermute | solution.py:34
  24.9 8.2 %collective-permute-start.1 = (bf16[3,128,128]{2,1,0:T(8,128)(2,1)S(1)}, bf16[3,128,128]{2,1,0:T(8,128)(2,1)S(1)}, u32[]{:S(2)}, u32[]{:S(2)}) collective-permute-start(bf16[3,128,128]{2,1,0:T(8,128)(2,1)S(1)} %pad_maximum_fusion.2.refs_0_), channel_id=1, source_target_pairs={{0,12},{1,13},{2,14},{3,15},{4,0},{5,1},{6,2},{7,3},{8,4},{9,5},{1... | collective-permute-start | bytes 294920 | tf_op jit(solution)/shard_map/ppermute | solution.py:25
  25.5 9.6 %collective-permute-start.2 = (bf16[3,128,128]{2,1,0:T(8,128)(2,1)S(1)}, bf16[3,128,128]{2,1,0:T(8,128)(2,1)S(1)}, u32[]{:S(2)}, u32[]{:S(2)}) collective-permute-start(bf16[3,128,128]{2,1,0:T(8,128)(2,1)S(1)} %pad_maximum_fusion.2.refs_0_), channel_id=1, source_target_pairs={{0,8},{1,9},{2,10},{3,11},{4,12},{5,13},{6,14},{7,15},{8,0},{9,1},... | collective-permute-start | bytes 294920 | tf_op jit(solution)/shard_map/ppermute | solution.py:25
  27.9 7.2 %collective-permute-start.3 = (bf16[3,128,128]{2,1,0:T(8,128)(2,1)S(1)}, bf16[3,128,128]{2,1,0:T(8,128)(2,1)S(1)}, u32[]{:S(2)}, u32[]{:S(2)}) collective-permute-start(bf16[3,128,128]{2,1,0:T(8,128)(2,1)S(1)} %pad_maximum_fusion.2.refs_0_), channel_id=1, source_target_pairs={{0,4},{1,5},{2,6},{3,7},{4,8},{5,9},{6,10},{7,11},{8,12},{9,13},{1... | collective-permute-start | bytes 294920 | tf_op jit(solution)/shard_map/ppermute | solution.py:25
  29.8 5.6 %collective-permute-start.4 = (bf16[3,128,128]{2,1,0:T(8,128)(2,1)S(1)}, bf16[3,128,128]{2,1,0:T(8,128)(2,1)S(1)}, u32[]{:S(2)}, u32[]{:S(2)}) collective-permute-start(bf16[3,128,128]{2,1,0:T(8,128)(2,1)S(1)} %pad_maximum_fusion.3.refs_0_), channel_id=1, source_target_pairs={{0,192},{16,208},{32,224},{48,240},{64,0},{80,16},{96,32},{112,48}... | collective-permute-start | bytes 294920 | tf_op jit(solution)/shard_map/ppermute | solution.py:25
  30.4 6.2 %collective-permute-start.5 = (bf16[3,128,128]{2,1,0:T(8,128)(2,1)S(1)}, bf16[3,128,128]{2,1,0:T(8,128)(2,1)S(1)}, u32[]{:S(2)}, u32[]{:S(2)}) collective-permute-start(bf16[3,128,128]{2,1,0:T(8,128)(2,1)S(1)} %pad_maximum_fusion.3.refs_0_), channel_id=1, source_target_pairs={{0,128},{16,144},{32,160},{48,176},{64,192},{80,208},{96,224},{112... | collective-permute-start | bytes 294920 | tf_op jit(solution)/shard_map/ppermute | solution.py:25
  33.1 4.7 %collective-permute-start.6 = (bf16[3,128,128]{2,1,0:T(8,128)(2,1)S(1)}, bf16[3,128,128]{2,1,0:T(8,128)(2,1)S(1)}, u32[]{:S(2)}, u32[]{:S(2)}) collective-permute-start(bf16[3,128,128]{2,1,0:T(8,128)(2,1)S(1)} %pad_maximum_fusion.3.refs_0_), channel_id=1, source_target_pairs={{0,64},{16,80},{32,96},{48,112},{64,128},{80,144},{96,160},{112,17... | collective-permute-start | bytes 294920 | tf_op jit(solution)/shard_map/ppermute | solution.py:25
  38.0 7.9 %collective-permute-start.10 = (bf16[16,128,128]{2,1,0:T(8,128)(2,1)S(1)}, bf16[16,128,128]{2,1,0:T(8,128)(2,1)S(1)}, u32[]{:S(2)}, u32[]{:S(2)}) collective-permute-start(bf16[16,128,128]{2,1,0:T(8,128)(2,1)S(1)} %constant_dynamic-update-slice_fusion.queries), channel_id=1, source_target_pairs={{0,1},{1,0},{2,3},{3,2},{4,5},{5,4},{6,7},{7,6},{8,9},{9,8},{10,11... | collective-permute-start | bytes 1572872 | tf_op jit(solution)/shard_map/ppermute | solution.py:34
  38.1 9.2 %collective-permute-start.11 = (bf16[6,128,128]{2,1,0:T(8,128)(2,1)S(1)}, bf16[6,128,128]{2,1,0:T(8,128)(2,1)S(1)}, u32[]{:S(2)}, u32[]{:S(2)}) collective-permute-start(bf16[6,128,128]{2,1,0:T(8,128)(2,1)S(1)} %get-tuple-element.60.refs_0_), channel_id=1, source_target_pairs={{0,192},{16,208},{32,224},{48,240},{64,0},{80,16},{96,32},{112,48}... | collective-permute-start | bytes 589832 | tf_op jit(solution)/shard_map/ppermute | solution.py:25
  41.1 11.4 %collective-permute-start.12 = (bf16[6,128,128]{2,1,0:T(8,128)(2,1)S(1)}, bf16[6,128,128]{2,1,0:T(8,128)(2,1)S(1)}, u32[]{:S(2)}, u32[]{:S(2)}) collective-permute-start(bf16[6,128,128]{2,1,0:T(8,128)(2,1)S(1)} %get-tuple-element.60.refs_0_), channel_id=1, source_target_pairs={{0,128},{16,144},{32,160},{48,176},{64,192},{80,208},{96,224},{112... | collective-permute-start | bytes 589832 | tf_op jit(solution)/shard_map/ppermute | solution.py:25
  41.5 11.0 %collective-permute-start.13 = (bf16[6,128,128]{2,1,0:T(8,128)(2,1)S(1)}, bf16[6,128,128]{2,1,0:T(8,128)(2,1)S(1)}, u32[]{:S(2)}, u32[]{:S(2)}) collective-permute-start(bf16[6,128,128]{2,1,0:T(8,128)(2,1)S(1)} %get-tuple-element.60.refs_0_), channel_id=1, source_target_pairs={{0,64},{16,80},{32,96},{48,112},{64,128},{80,144},{96,160},{112,17... | collective-permute-start | bytes 589832 | tf_op jit(solution)/shard_map/ppermute | solution.py:25
  43.1 16.1 %collective-permute-start.14 = (bf16[6,128,128]{2,1,0:T(8,128)(2,1)S(1)}, bf16[6,128,128]{2,1,0:T(8,128)(2,1)S(1)}, u32[]{:S(2)}, u32[]{:S(2)}) collective-permute-start(bf16[6,128,128]{2,1,0:T(8,128)(2,1)S(1)} %get-tuple-element.68.refs_0_), channel_id=1, source_target_pairs={{0,12},{1,13},{2,14},{3,15},{4,0},{5,1},{6,2},{7,3},{8,4},{9,5},{1... | collective-permute-start | bytes 589832 | tf_op jit(solution)/shard_map/ppermute | solution.py:25
  45.9 13.4 %collective-permute-start.15 = (bf16[6,128,128]{2,1,0:T(8,128)(2,1)S(1)}, bf16[6,128,128]{2,1,0:T(8,128)(2,1)S(1)}, u32[]{:S(2)}, u32[]{:S(2)}) collective-permute-start(bf16[6,128,128]{2,1,0:T(8,128)(2,1)S(1)} %get-tuple-element.68.refs_0_), channel_id=1, source_target_pairs={{0,8},{1,9},{2,10},{3,11},{4,12},{5,13},{6,14},{7,15},{8,0},{9,1},... | collective-permute-start | bytes 589832 | tf_op jit(solution)/shard_map/ppermute | solution.py:25
  47.3 11.9 %collective-permute-start.16 = (bf16[6,128,128]{2,1,0:T(8,128)(2,1)S(1)}, bf16[6,128,128]{2,1,0:T(8,128)(2,1)S(1)}, u32[]{:S(2)}, u32[]{:S(2)}) collective-permute-start(bf16[6,128,128]{2,1,0:T(8,128)(2,1)S(1)} %get-tuple-element.68.refs_0_), channel_id=1, source_target_pairs={{0,4},{1,5},{2,6},{3,7},{4,8},{5,9},{6,10},{7,11},{8,12},{9,13},{1... | collective-permute-start | bytes 589832 | tf_op jit(solution)/shard_map/ppermute | solution.py:25
  55.8 7.3 %collective-permute-start.17 = (f32[2,136,512]{2,1,0:T(8,128)S(1)}, f32[2,136,512]{2,1,0:T(8,128)S(1)}, u32[]{:S(2)}, u32[]{:S(2)}) collective-permute-start(f32[2,136,512]{2,1,0:T(8,128)S(1)} %shard_map.80), channel_id=1, source_target_pairs={{0,1},{1,0},{2,3},{3,2},{4,5},{5,4},{6,7},{7,6},{8,9},{9,8},{10,11... | collective-permute-start | bytes 1671176 | tf_op jit(solution)/shard_map/ppermute | solution.py:34
  62.5 11.0 %collective-permute-start.21 = (f32[2,136,512]{2,1,0:T(8,128)S(1)}, f32[2,136,512]{2,1,0:T(8,128)S(1)}, u32[]{:S(2)}, u32[]{:S(2)}) collective-permute-start(f32[2,136,512]{2,1,0:T(8,128)S(1)} %shard_map.82), channel_id=1, source_target_pairs={{0,1},{1,0},{2,3},{3,2},{4,5},{5,4},{6,7},{7,6},{8,9},{9,8},{10,11... | collective-permute-start | bytes 1671176 | tf_op jit(solution)/shard_map/ppermute | solution.py:34
  63.2 8.0 %collective-permute-start.18 = (f32[136,256]{1,0:T(8,128)S(1)}, f32[136,256]{1,0:T(8,128)S(1)}, u32[]{:S(2)}, u32[]{:S(2)}) collective-permute-start(f32[136,256]{1,0:T(8,128)S(1)} %get-tuple-element.76), channel_id=1, source_target_pairs={{0,4},{1,5},{2,6},{3,7},{4,8},{5,9},{6,10},{7,11},{8,12},{9,13},{1... | collective-permute-start | bytes 417800 | tf_op jit(solution)/shard_map/ppermute | solution.py:25
  63.4 8.0 %collective-permute-start.19 = (f32[136,256]{1,0:T(8,128)S(1)}, f32[136,256]{1,0:T(8,128)S(1)}, u32[]{:S(2)}, u32[]{:S(2)}) collective-permute-start(f32[136,256]{1,0:T(8,128)S(1)} %get-tuple-element.77), channel_id=1, source_target_pairs={{0,8},{1,9},{2,10},{3,11},{4,12},{5,13},{6,14},{7,15},{8,0},{9,1},... | collective-permute-start | bytes 417800 | tf_op jit(solution)/shard_map/ppermute | solution.py:25
  66.0 7.5 %collective-permute-start.20 = (f32[136,256]{1,0:T(8,128)S(1)}, f32[136,256]{1,0:T(8,128)S(1)}, u32[]{:S(2)}, u32[]{:S(2)}) collective-permute-start(f32[136,256]{1,0:T(8,128)S(1)} %get-tuple-element.78), channel_id=1, source_target_pairs={{0,12},{1,13},{2,14},{3,15},{4,0},{5,1},{6,2},{7,3},{8,4},{9,5},{1... | collective-permute-start | bytes 417800 | tf_op jit(solution)/shard_map/ppermute | solution.py:25
  73.6 8.2 %collective-permute-start.22 = (f32[136,256]{1,0:T(8,128)S(1)}, f32[136,256]{1,0:T(8,128)S(1)}, u32[]{:S(2)}, u32[]{:S(2)}) collective-permute-start(f32[136,256]{1,0:T(8,128)S(1)} %get-tuple-element.87), channel_id=1, source_target_pairs={{0,64},{16,80},{32,96},{48,112},{64,128},{80,144},{96,160},{112,17... | collective-permute-start | bytes 417800 | tf_op jit(solution)/shard_map/ppermute | solution.py:25
  75.7 8.1 %collective-permute-start.23 = (f32[136,256]{1,0:T(8,128)S(1)}, f32[136,256]{1,0:T(8,128)S(1)}, u32[]{:S(2)}, u32[]{:S(2)}) collective-permute-start(f32[136,256]{1,0:T(8,128)S(1)} %get-tuple-element.88), channel_id=1, source_target_pairs={{0,128},{16,144},{32,160},{48,176},{64,192},{80,208},{96,224},{112... | collective-permute-start | bytes 417800 | tf_op jit(solution)/shard_map/ppermute | solution.py:25
  77.5 7.9 %collective-permute-start.24 = (f32[136,256]{1,0:T(8,128)S(1)}, f32[136,256]{1,0:T(8,128)S(1)}, u32[]{:S(2)}, u32[]{:S(2)}) collective-permute-start(f32[136,256]{1,0:T(8,128)S(1)} %get-tuple-element.89), channel_id=1, source_target_pairs={{0,192},{16,208},{32,224},{48,240},{64,0},{80,16},{96,32},{112,48}... | collective-permute-start | bytes 417800 | tf_op jit(solution)/shard_map/ppermute | solution.py:25
  85.6 5.7 %collective-permute-start.25 = (f32[2,136,128]{2,1,0:T(8,128)S(1)}, f32[2,136,128]{2,1,0:T(8,128)S(1)}, u32[]{:S(2)}, u32[]{:S(2)}) collective-permute-start(f32[2,136,128]{2,1,0:T(8,128)S(1)} %get-tuple-element.91), channel_id=1, source_target_pairs={{0,2},{1,3},{2,0},{3,1},{4,6},{5,7},{6,4},{7,5},{8,10},{9,11},{10,... | collective-permute-start | bytes 417800 | tf_op jit(solution)/shard_map/ppermute | solution.py:34

commit v5 on v3

--- a/solution.py
+++ b/solution.py
@@ -106,21 +106,33 @@
     return with_peak(*merge([peak_of(part) for part in parts], parts))
 
 
-def attend(scale, query, blocks):
-    peaks, parts = [], []
-    for keys, values in blocks:
-        score = lax.dot_general(
-            keys, query, (((1,), (1,)), ((), ())), preferred_element_type=jnp.float32
-        ) * scale
+def attend(scale, queries, blocks):
+    steps = [(tile, block) for tile in range(len(queries)) for block in range(len(blocks))]
+
+    def raw(tile, block):
+        return lax.dot_general(
+            blocks[block][0],
+            queries[tile],
+            (((1,), (1,)), ((), ())),
+            preferred_element_type=jnp.float32,
+        )
+
+    peaks, parts = [[] for _ in queries], [[] for _ in queries]
+    ahead = raw(*steps[0])
+    for at, (tile, block) in enumerate(steps):
+        score = ahead * scale
+        if at + 1 < len(steps):
+            ahead = raw(*steps[at + 1])
         peak = jnp.max(score, axis=0, keepdims=True)
         weight = jnp.exp2(score - peak).astype(jnp.bfloat16)
-        parts.append(jnp.dot(values, weight, preferred_element_type=jnp.float32)[:ROWS])
-        peaks.append(peak)
-    return with_peak(*merge(peaks, parts))
-
-
-def score_kernel(total, scale, side, first, queries, *refs):
-    keys, (out,) = refs[:SUB], refs[SUB:]
+        part = jnp.dot(blocks[block][1], weight, preferred_element_type=jnp.float32)
+        parts[tile].append(part[:ROWS])
+        peaks[tile].append(peak)
+    return [with_peak(*merge(*pair)) for pair in zip(peaks, parts)]
+
+
+def score_kernel(total, scale, side, halves, queries, *refs):
+    keys, outs = refs[:SUB], refs[SUB:]
 
     def block_of(slow):
         tiles = keys[slow]
@@ -129,20 +141,24 @@
         extra = [coord_rows(key_start(side, slow, fast), total) for fast in range(SUB)]
         return feats, jnp.concatenate([values, jnp.concatenate(extra, axis=1)], axis=0)
 
-    def step(part, _):
-        tiles = [queries[first + part * SUB + piece] for piece in range(SUB)]
-        query = jnp.concatenate(tiles, axis=0)
-        out[part] = attend(scale, query, [block_of(slow) for slow in range(SUB)])
-        return 0
-
-    lax.fori_loop(0, 2, step, 0)
-
-
-def core_kernel(mine, theirs, *outs):
-    for part in range(2):
-        whole = merged([mine[part], theirs[part]])
-        outs[2 * part][...] = whole[:, : 2 * SHARD]
-        outs[2 * part + 1][...] = whole[:, 2 * SHARD :]
+    blocks = [block_of(slow) for slow in range(SUB)]
+    tiles = [
+        jnp.concatenate(
+            [queries[(side * 2 + half) * SUB + piece] for piece in range(SUB)], axis=0
+        )
+        for half in halves
+    ]
+    for index, whole in enumerate(attend(scale, tiles, blocks)):
+        outs[0][index] = whole
+
+
+def core_kernel(halves, *refs):
+    (theirs, *mine), outs = refs[: -2 * len(halves)], refs[-2 * len(halves) :]
+    for index, half in enumerate(halves):
+        own = mine[0][index]
+        whole = merged([own, theirs[half]])
+        outs[2 * index][...] = whole[:, : 2 * SHARD]
+        outs[2 * index + 1][...] = whole[:, 2 * SHARD :]
 
 
 def chip_kernel(*refs):
@@ -227,31 +243,39 @@
     )
     others = fast_swap("col", queries, 1)
 
-    def score(side, queries):
-        shapes = [f32(2, ROWS, BLOCK)]
-        kernel = functools.partial(score_kernel, total, scale, side, side * 2 * SUB)
-        work = 2 * SUB * SHARD * SUB * BLOCK
+    def score(side, queries, *halves):
+        shapes = [f32(len(halves), ROWS, BLOCK)]
+        kernel = functools.partial(score_kernel, total, scale, side, halves)
+        work = len(halves) * SUB * SHARD * SUB * BLOCK
         return call(kernel, shapes, (queries, *tiles[1 - side]), work=work)[0]
 
-    def core_merge(mine, theirs):
-        return call(core_kernel, [f32(ROWS, 2 * SHARD)] * SUB, (mine, theirs))
-
-    def spread(axis, parts):
-        return [parts[0]] + [slow_shift(axis, parts[step], step) for step in range(1, SUB)]
-
-    keep_one = score(0, queries)
+    def core_merge(mine, theirs, *halves):
+        shapes = [f32(ROWS, 2 * SHARD)] * (2 * len(halves))
+        return call(functools.partial(core_kernel, halves), shapes, (theirs, mine))
+
+    def spread(axis, parts, first=0):
+        return [
+            slow_shift(axis, part, first + step) if first + step else part
+            for step, part in enumerate(parts)
+        ]
+
+    keep_one = score(0, queries, 0, 1)
     others, keep_one = together((others, keep_one))
-    send_one = score(0, others)
+    send_one = score(0, others, 0, 1)
     theirs_one = fast_swap("col", send_one, 1)
     others, _ = together((others, send_one))
-    send_two = score(1, others)
+    send_two = score(1, others, 0, 1)
     theirs_two = fast_swap("col", send_two, 1)
-    rows = core_merge(keep_one, theirs_one)
+    rows = core_merge(keep_one, theirs_one, 0, 1)
     queries, _, rows = together((queries, send_two, rows))
     rows = spread("col", rows)
-    keep_two = score(1, queries)
-    rows, keep_two = together((rows, keep_two))
-    cols = spread("row", core_merge(keep_two, theirs_two))
+    far_two = score(1, queries, 1)
+    far_cols = core_merge(far_two, theirs_two, 1)
+    queries, far_cols = together((queries, far_cols))
+    far_cols = spread("row", far_cols, 2)
+    near_two = score(1, queries, 0)
+    rows, near_two = together((rows, near_two))
+    cols = spread("row", core_merge(near_two, theirs_two, 0)) + far_cols
     keep, send = call(chip_kernel, [f32(2, ROWS, SHARD)] * 2, (*rows, *cols))
     theirs = fast_swap("col", send, 2)
     outs = [f32(SHARD, WIDTH), f32(2, SHARD)] * 2

time: 88.8 us -> 80.8 us (0.910)
  the two profiles are of different devices: /device:TPU:14 before, /device:TPU:4 now
where the time goes in v5:
time: 80.8 us; the launch traced here: 80.6 us
  starting transfers between devices  34.7 us (43%)
  waiting for transfers between devices  29.4 us (36%)
  Pallas kernels  14.4 us (18%)
  local copies, waits for them, and re-layouts  1.11 us (1%)
  between operations  0.9 us (1%)
    ppermute x12, starting transfers between devices, slow_shift(): return lax.ppermute(value, axis, pairs)  21.2 us
    ppermute x12, waiting for transfers between devices, slow_shift(): return lax.ppermute(value, axis, pairs)  15.2 us
    pallas_call x11, Pallas kernels, call(): pl.pallas_call(kernel, out_shape=shapes, in_specs=specs or [VMEM] * len(a...  14.4 us
    ppermute x3, starting transfers between devices, fast_shift(): return lax.ppermute(value, axis, pairs)  11.4 us
    ppermute x3, waiting for transfers between devices, fast_shift(): return lax.ppermute(value, axis, pairs)  7.84 us
    ppermute x5, waiting for transfers between devices, fast_swap(): return lax.ppermute(value, axis, [(i, i ^ step) for i in range(SUB * SUB)])  6.36 us
    ppermute x5, starting transfers between devices, fast_swap(): return lax.ppermute(value, axis, [(i, i ^ step) for i in range(SUB * SUB)])  2.08 us
  transfers between devices with their start and end apart: 20, of which 10 were waited for; matrix products, arithmetic and copies ran while one was open for 1% of the time, Pallas kernels for 11%

profile of v5, /device:TPU:4, one launch (start us, length us, event | category | flops | bytes accessed | tf_op | source)
XLA Modules:
  0.0 80.6 jit_solution(15531699209338540326)
XLA Ops:
  0.6 1.7 %shard_map.75 = (bf16[2,2,128,128]{3,2,1,0:T(8,128)(2,1)}, bf16[2,128,128]{2,1,0:T(8,128)(2,1)}) custom-call(bf16[128,128]{1,0:T(8,128)(2,1)} %feat_one.1, bf16[128,128]{1,0:T(8,128)(2,1)} %value_one.1, bf16[128,128]{1,0:T(8,128)(2,1)} %feat_two.1, bf16[128,128]{1,0:T(8,128)(2,1)} %value_two.1), custom_call_target="tpu_custom_call" | custom-call | bytes 327680 | tf_op jit(solution)/shard_map/pallas_call | solution.py:189
  2.3 3.3 %collective-permute-start.2 = (bf16[2,2,128,128]{3,2,1,0:T(8,128)(2,1)}, bf16[2,2,128,128]{3,2,1,0:T(8,128)(2,1)S(1)}, u32[]{:S(2)}, u32[]{:S(2)}) collective-permute-start(bf16[2,2,128,128]{3,2,1,0:T(8,128)(2,1)} %get-tuple-element.42), channel_id=1, source_target_pairs={{0,16},{16,32},{32,48},{48,0},{64,80},{80,96},{96,112},{112,64},{1... | collective-permute-start | bytes 393224 | tf_op jit(solution)/shard_map/ppermute | solution.py:30
  5.7 5.4 %collective-permute-start.1 = (bf16[2,2,128,128]{3,2,1,0:T(8,128)(2,1)}, bf16[2,2,128,128]{3,2,1,0:T(8,128)(2,1)S(1)}, u32[]{:S(2)}, u32[]{:S(2)}) collective-permute-start(bf16[2,2,128,128]{3,2,1,0:T(8,128)(2,1)} %get-tuple-element.42), channel_id=1, source_target_pairs={{0,32},{16,48},{32,0},{48,16},{64,96},{80,112},{96,64},{112,80},{1... | collective-permute-start | bytes 393224 | tf_op jit(solution)/shard_map/ppermute | solution.py:30
  11.1 2.7 %collective-permute-start = (bf16[2,2,128,128]{3,2,1,0:T(8,128)(2,1)}, bf16[2,2,128,128]{3,2,1,0:T(8,128)(2,1)S(1)}, u32[]{:S(2)}, u32[]{:S(2)}) collective-permute-start(bf16[2,2,128,128]{3,2,1,0:T(8,128)(2,1)} %get-tuple-element.42), channel_id=1, source_target_pairs={{0,48},{16,0},{32,16},{48,32},{64,112},{80,64},{96,80},{112,96},{1... | collective-permute-start | bytes 393224 | tf_op jit(solution)/shard_map/ppermute | solution.py:30
  13.7 1.0 %collective-permute-start.3 = (bf16[2,128,128]{2,1,0:T(8,128)(2,1)}, bf16[2,128,128]{2,1,0:T(8,128)(2,1)S(1)}, u32[]{:S(2)}, u32[]{:S(2)}) collective-permute-start(bf16[2,128,128]{2,1,0:T(8,128)(2,1)} %get-tuple-element.43), channel_id=1, source_target_pairs={{0,2},{1,3},{2,0},{3,1},{4,6},{5,7},{6,4},{7,5},{8,10},{9,11},{10,... | collective-permute-start | bytes 196616 | tf_op jit(solution)/shard_map/ppermute | solution.py:34
  14.7 0.9 %bitcast_dynamic-update-slice_fusion = (bf16[9,128,128]{2,1,0:T(8,128)(2,1)S(1)}, bf16[9,128,128]{2,1,0:T(8,128)(2,1)S(1)}) fusion(bf16[2,2,128,128]{3,2,1,0:T(8,128)(2,1)} %get-tuple-element.42), kind=kLoop, calls=%fused_computation.12 | loop fusion | bytes 262144
  15.6 7.8 %collective-permute-done = bf16[2,2,128,128]{3,2,1,0:T(8,128)(2,1)S(1)} collective-permute-done((bf16[2,2,128,128]{3,2,1,0:T(8,128)(2,1)}, bf16[2,2,128,128]{3,2,1,0:T(8,128)(2,1)S(1)}, u32[]{:S(2)}, u32[]{:S(2)}) %collective-permute-start) | collective-permute-done | bytes 131104 | tf_op jit(solution)/shard_map/ppermute | solution.py:30
  23.5 0.0 collective-permute-done.1
  23.5 0.0 collective-permute-done.2
  23.6 1.3 %collective-permute-done.3 = bf16[2,128,128]{2,1,0:T(8,128)(2,1)S(1)} collective-permute-done((bf16[2,128,128]{2,1,0:T(8,128)(2,1)}, bf16[2,128,128]{2,1,0:T(8,128)(2,1)S(1)}, u32[]{:S(2)}, u32[]{:S(2)}) %collective-permute-start.3) | collective-permute-done | bytes 65568 | tf_op jit(solution)/shard_map/ppermute | solution.py:34
  24.9 1.3 %collective-permute-start.6 = (bf16[9,128,128]{2,1,0:T(8,128)(2,1)S(1)}, bf16[9,128,128]{2,1,0:T(8,128)(2,1)S(1)}, u32[]{:S(2)}, u32[]{:S(2)}) collective-permute-start(bf16[9,128,128]{2,1,0:T(8,128)(2,1)S(1)} %get-tuple-element.46.refs_0_), channel_id=1, source_target_pairs={{0,4},{1,5},{2,6},{3,7},{4,8},{5,9},{6,10},{7,11},{8,12},{9,13},{1... | collective-permute-start | bytes 884744 | tf_op jit(solution)/shard_map/ppermute | solution.py:25
  26.2 0.8 collective-permute-start.5
  27.0 1.1 %collective-permute-start.4 = (bf16[9,128,128]{2,1,0:T(8,128)(2,1)S(1)}, bf16[9,128,128]{2,1,0:T(8,128)(2,1)S(1)}, u32[]{:S(2)}, u32[]{:S(2)}) collective-permute-start(bf16[9,128,128]{2,1,0:T(8,128)(2,1)S(1)} %get-tuple-element.46.refs_0_), channel_id=1, source_target_pairs={{0,12},{1,13},{2,14},{3,15},{4,0},{5,1},{6,2},{7,3},{8,4},{9,5},{1... | collective-permute-start | bytes 884744 | tf_op jit(solution)/shard_map/ppermute | solution.py:25
  28.1 1.6 %collective-permute-start.9 = (bf16[9,128,128]{2,1,0:T(8,128)(2,1)S(1)}, bf16[9,128,128]{2,1,0:T(8,128)(2,1)S(1)}, u32[]{:S(2)}, u32[]{:S(2)}) collective-permute-start(bf16[9,128,128]{2,1,0:T(8,128)(2,1)S(1)} %get-tuple-element.50.refs_0_), channel_id=1, source_target_pairs={{0,64},{16,80},{32,96},{48,112},{64,128},{80,144},{96,160},{112,17... | collective-permute-start | bytes 884744 | tf_op jit(solution)/shard_map/ppermute | solution.py:25
  29.7 2.9 %collective-permute-start.8 = (bf16[9,128,128]{2,1,0:T(8,128)(2,1)S(1)}, bf16[9,128,128]{2,1,0:T(8,128)(2,1)S(1)}, u32[]{:S(2)}, u32[]{:S(2)}) collective-permute-start(bf16[9,128,128]{2,1,0:T(8,128)(2,1)S(1)} %get-tuple-element.50.refs_0_), channel_id=1, source_target_pairs={{0,128},{16,144},{32,160},{48,176},{64,192},{80,208},{96,224},{112... | collective-permute-start | bytes 884744 | tf_op jit(solution)/shard_map/ppermute | solution.py:25
  32.6 2.3 %collective-permute-done.6.refs_3_ = bf16[9,128,128]{2,1,0:T(8,128)(2,1)S(1)} collective-permute-done((bf16[9,128,128]{2,1,0:T(8,128)(2,1)S(1)}, bf16[9,128,128]{2,1,0:T(8,128)(2,1)S(1)}, u32[]{:S(2)}, u32[]{:S(2)}) %collective-permute-start.6) | collective-permute-done | bytes 294944 | tf_op jit(solution)/shard_map/ppermute | solution.py:25
  34.9 3.0 %collective-permute-start.7 = (bf16[9,128,128]{2,1,0:T(8,128)(2,1)S(1)}, bf16[9,128,128]{2,1,0:T(8,128)(2,1)S(1)}, u32[]{:S(2)}, u32[]{:S(2)}) collective-permute-start(bf16[9,128,128]{2,1,0:T(8,128)(2,1)S(1)} %get-tuple-element.50.refs_0_), channel_id=1, source_target_pairs={{0,192},{16,208},{32,224},{48,240},{64,0},{80,16},{96,32},{112,48}... | collective-permute-start | bytes 884744 | tf_op jit(solution)/shard_map/ppermute | solution.py:25
  37.9 1.9 %collective-permute-done.5.refs_2_ = bf16[9,128,128]{2,1,0:T(8,128)(2,1)S(1)} collective-permute-done((bf16[9,128,128]{2,1,0:T(8,128)(2,1)S(1)}, bf16[9,128,128]{2,1,0:T(8,128)(2,1)S(1)}, u32[]{:S(2)}, u32[]{:S(2)}) %collective-permute-start.5) | collective-permute-done | bytes 294944 | tf_op jit(solution)/shard_map/ppermute | solution.py:25
  39.8 1.8 %collective-permute-done.4.refs_1_ = bf16[9,128,128]{2,1,0:T(8,128)(2,1)S(1)} collective-permute-done((bf16[9,128,128]{2,1,0:T(8,128)(2,1)S(1)}, bf16[9,128,128]{2,1,0:T(8,128)(2,1)S(1)}, u32[]{:S(2)}, u32[]{:S(2)}) %collective-permute-start.4) | collective-permute-done | bytes 294944 | tf_op jit(solution)/shard_map/ppermute | solution.py:25
  41.6 0.0 collective-permute-done.9.refs_3_
  41.6 2.9 %collective-permute-done.8.refs_2_ = bf16[9,128,128]{2,1,0:T(8,128)(2,1)S(1)} collective-permute-done((bf16[9,128,128]{2,1,0:T(8,128)(2,1)S(1)}, bf16[9,128,128]{2,1,0:T(8,128)(2,1)S(1)}, u32[]{:S(2)}, u32[]{:S(2)}) %collective-permute-start.8) | collective-permute-done | bytes 294944 | tf_op jit(solution)/shard_map/ppermute | solution.py:25
  44.6 0.0 collective-permute-done.7.refs_1_
  44.8 0.3 collective-permute-start.10
  45.1 2.8 %shard_map.76.refs_1_ = f32[2,136,512]{2,1,0:T(8,128)S(1)} custom-call(bf16[16,128,128]{2,1,0:T(8,128)(2,1)S(1)} %constant_dynamic-update-slice_fusion.2.queries, bf16[9,128,128]{2,1,0:T(8,128)(2,1)S(1)} %get-tuple-element.50.refs_0_, bf16[9,128,128]{2,1,0:T(8,128)(2,1)S(1)} %collective-permute-done.7.refs_1_, ...), custom_call_target="tpu_custom_call" | custom-call | flops 1073741824 | bytes 2260992 | tf_op jit(solution)/shard_map/pallas_call | solution.py:189
  47.9 0.0 collective-permute-done.10.queries
  47.9 2.8 %shard_map.77 = f32[2,136,512]{2,1,0:T(8,128)S(1)} custom-call(bf16[16,128,128]{2,1,0:T(8,128)(2,1)S(1)} %collective-permute-done.10.queries, bf16[9,128,128]{2,1,0:T(8,128)(2,1)S(1)} %get-tuple-element.50.refs_0_, bf16[9,128,128]{2,1,0:T(8,128)(2,1)S(1)} %collective-permute-done.7.refs_1_, bf16[9,128,128]{2,1,0:T(8,128)(2,1)S(1)} %collective-permute-done.8.refs_2_, ...), custom_call_target="tpu_custom_call" | custom-call | flops 1073741824 | bytes 2260992 | tf_op jit(solution)/shard_map/pallas_call | solution.py:189
  50.7 0.6 collective-permute-start.11
  51.3 2.8 %shard_map.78 = f32[2,136,512]{2,1,0:T(8,128)S(1)} custom-call(bf16[16,128,128]{2,1,0:T(8,128)(2,1)S(1)} %collective-permute-done.10.queries, bf16[9,128,128]{2,1,0:T(8,128)(2,1)S(1)} %get-tuple-element.46.refs_0_, bf16[9,128,128]{2,1,0:T(8,128)(2,1)S(1)} %collective-permute-done.4.refs_1_, bf16[9,128,128]{2,1,0:T(8,128)(2,1)S(1)} %collective-permute-done.5.refs_2_, ...), custom_call_target="tpu_custom_call" | custom-call | flops 1073741824 | bytes 2260992 | tf_op jit(solution)/shard_map/pallas_call | solution.py:189
  54.1 0.1 collective-permute-start.15
  54.2 0.1 shard_map.79
  54.3 1.3 %collective-permute-start.12 = (f32[136,256]{1,0:T(8,128)S(1)}, f32[136,256]{1,0:T(8,128)S(1)}, u32[]{:S(2)}, u32[]{:S(2)}) collective-permute-start(f32[136,256]{1,0:T(8,128)S(1)} %get-tuple-element.62), channel_id=1, source_target_pairs={{0,4},{1,5},{2,6},{3,7},{4,8},{5,9},{6,10},{7,11},{8,12},{9,13},{1... | collective-permute-start | bytes 417800 | tf_op jit(solution)/shard_map/ppermute | solution.py:25
  55.6 2.4 %collective-permute-start.13 = (f32[136,256]{1,0:T(8,128)S(1)}, f32[136,256]{1,0:T(8,128)S(1)}, u32[]{:S(2)}, u32[]{:S(2)}) collective-permute-start(f32[136,256]{1,0:T(8,128)S(1)} %get-tuple-element.63), channel_id=1, source_target_pairs={{0,8},{1,9},{2,10},{3,11},{4,12},{5,13},{6,14},{7,15},{8,0},{9,1},... | collective-permute-start | bytes 417800 | tf_op jit(solution)/shard_map/ppermute | solution.py:25
  58.0 2.0 %collective-permute-start.14 = (f32[136,256]{1,0:T(8,128)S(1)}, f32[136,256]{1,0:T(8,128)S(1)}, u32[]{:S(2)}, u32[]{:S(2)}) collective-permute-start(f32[136,256]{1,0:T(8,128)S(1)} %get-tuple-element.64), channel_id=1, source_target_pairs={{0,12},{1,13},{2,14},{3,15},{4,0},{5,1},{6,2},{7,3},{8,4},{9,5},{1... | collective-permute-start | bytes 417800 | tf_op jit(solution)/shard_map/ppermute | solution.py:25
  60.1 1.6 %shard_map.80.refs_1_ = f32[1,136,512]{2,1,0:T(8,128)S(1)} custom-call(bf16[16,128,128]{2,1,0:T(8,128)(2,1)S(1)} %constant_dynamic-update-slice_fusion.2.queries, bf16[9,128,128]{2,1,0:T(8,128)(2,1)S(1)} %get-tuple-element.46.refs_0_, bf16[9,128,128]{2,1,0:T(8,128)(2,1)S(1)} %collective-permute-done.4.refs_1_, ...), custom_call_target="tpu_custom_call" | custom-call | flops 536870912 | bytes 1982464 | tf_op jit(solution)/shard_map/pallas_call | solution.py:189
  61.7 0.0 collective-permute-done.15.refs_0_
  61.8 2.7 %collective-permute-start.17 = (f32[136,256]{1,0:T(8,128)S(1)}, f32[136,256]{1,0:T(8,128)S(1)}, u32[]{:S(2)}, u32[]{:S(2)}) collective-permute-start(f32[136,256]{1,0:T(8,128)S(1)} %get-tuple-element.76), channel_id=1, source_target_pairs={{0,128},{16,144},{32,160},{48,176},{64,192},{80,208},{96,224},{112... | collective-permute-start | bytes 417800 | tf_op jit(solution)/shard_map/ppermute | solution.py:25
  64.4 2.0 %collective-permute-start.18 = (f32[136,256]{1,0:T(8,128)S(1)}, f32[136,256]{1,0:T(8,128)S(1)}, u32[]{:S(2)}, u32[]{:S(2)}) collective-permute-start(f32[136,256]{1,0:T(8,128)S(1)} %get-tuple-element.77), channel_id=1, source_target_pairs={{0,192},{16,208},{32,224},{48,240},{64,0},{80,16},{96,32},{112,48}... | collective-permute-start | bytes 417800 | tf_op jit(solution)/shard_map/ppermute | solution.py:25
  66.4 1.6 %shard_map.82.refs_1_ = f32[1,136,512]{2,1,0:T(8,128)S(1)} custom-call(bf16[16,128,128]{2,1,0:T(8,128)(2,1)S(1)} %constant_dynamic-update-slice_fusion.2.queries, bf16[9,128,128]{2,1,0:T(8,128)(2,1)S(1)} %get-tuple-element.46.refs_0_, bf16[9,128,128]{2,1,0:T(8,128)(2,1)S(1)} %collective-permute-done.4.refs_1_, ...), custom_call_target="tpu_custom_call" | custom-call | flops 536870912 | bytes 1982464 | tf_op jit(solution)/shard_map/pallas_call | solution.py:189
  68.1 0.0 collective-permute-done.13.refs_2_
  68.1 0.0 collective-permute-done.14.refs_3_
  68.2 0.1 collective-permute-start.16
  68.3 0.3 collective-permute-done.17.refs_6_
  68.6 2.4 %collective-permute-done.18.refs_7_ = f32[136,256]{1,0:T(8,128)S(1)} collective-permute-done((f32[136,256]{1,0:T(8,128)S(1)}, f32[136,256]{1,0:T(8,128)S(1)}, u32[]{:S(2)}, u32[]{:S(2)}) %collective-permute-start.18) | collective-permute-done | bytes 139296 | tf_op jit(solution)/shard_map/ppermute | solution.py:25
  71.0 3.6 %collective-permute-done.16.refs_5_ = f32[136,256]{1,0:T(8,128)S(1)} collective-permute-done((f32[136,256]{1,0:T(8,128)S(1)}, f32[136,256]{1,0:T(8,128)S(1)}, u32[]{:S(2)}, u32[]{:S(2)}) %collective-permute-start.16) | collective-permute-done | bytes 139296 | tf_op jit(solution)/shard_map/ppermute | solution.py:25
  74.5 0.1 shard_map.84
  74.6 0.1 collective-permute-start.19
  74.7 5.0 %collective-permute-done.19.theirs = f32[2,136,128]{2,1,0:T(8,128)S(1)} collective-permute-done((f32[2,136,128]{2,1,0:T(8,128)S(1)}, f32[2,136,128]{2,1,0:T(8,128)S(1)}, u32[]{:S(2)}, u32[]{:S(2)}) %collective-permute-start.19) | collective-permute-done | bytes 139296 | tf_op jit(solution)/shard_map/ppermute | solution.py:34
  79.8 0.8 shard_map.85
  (24 shorter events, 0.3 us)
Async XLA Ops:
  2.3 21.2 %collective-permute-start.2 = (bf16[2,2,128,128]{3,2,1,0:T(8,128)(2,1)}, bf16[2,2,128,128]{3,2,1,0:T(8,128)(2,1)S(1)}, u32[]{:S(2)}, u32[]{:S(2)}) collective-permute-start(bf16[2,2,128,128]{3,2,1,0:T(8,128)(2,1)} %get-tuple-element.42), channel_id=1, source_target_pairs={{0,16},{16,32},{32,48},{48,0},{64,80},{80,96},{96,112},{112,64},{1... | collective-permute-start | bytes 393224 | tf_op jit(solution)/shard_map/ppermute | solution.py:30
  5.7 17.8 %collective-permute-start.1 = (bf16[2,2,128,128]{3,2,1,0:T(8,128)(2,1)}, bf16[2,2,128,128]{3,2,1,0:T(8,128)(2,1)S(1)}, u32[]{:S(2)}, u32[]{:S(2)}) collective-permute-start(bf16[2,2,128,128]{3,2,1,0:T(8,128)(2,1)} %get-tuple-element.42), channel_id=1, source_target_pairs={{0,32},{16,48},{32,0},{48,16},{64,96},{80,112},{96,64},{112,80},{1... | collective-permute-start | bytes 393224 | tf_op jit(solution)/shard_map/ppermute | solution.py:30
  11.1 12.4 %collective-permute-start = (bf16[2,2,128,128]{3,2,1,0:T(8,128)(2,1)}, bf16[2,2,128,128]{3,2,1,0:T(8,128)(2,1)S(1)}, u32[]{:S(2)}, u32[]{:S(2)}) collective-permute-start(bf16[2,2,128,128]{3,2,1,0:T(8,128)(2,1)} %get-tuple-element.42), channel_id=1, source_target_pairs={{0,48},{16,0},{32,16},{48,32},{64,112},{80,64},{96,80},{112,96},{1... | collective-permute-start | bytes 393224 | tf_op jit(solution)/shard_map/ppermute | solution.py:30
  13.7 11.1 %collective-permute-start.3 = (bf16[2,128,128]{2,1,0:T(8,128)(2,1)}, bf16[2,128,128]{2,1,0:T(8,128)(2,1)S(1)}, u32[]{:S(2)}, u32[]{:S(2)}) collective-permute-start(bf16[2,128,128]{2,1,0:T(8,128)(2,1)} %get-tuple-element.43), channel_id=1, source_target_pairs={{0,2},{1,3},{2,0},{3,1},{4,6},{5,7},{6,4},{7,5},{8,10},{9,11},{10,... | collective-permute-start | bytes 196616 | tf_op jit(solution)/shard_map/ppermute | solution.py:34
  24.9 10.0 %collective-permute-start.6 = (bf16[9,128,128]{2,1,0:T(8,128)(2,1)S(1)}, bf16[9,128,128]{2,1,0:T(8,128)(2,1)S(1)}, u32[]{:S(2)}, u32[]{:S(2)}) collective-permute-start(bf16[9,128,128]{2,1,0:T(8,128)(2,1)S(1)} %get-tuple-element.46.refs_0_), channel_id=1, source_target_pairs={{0,4},{1,5},{2,6},{3,7},{4,8},{5,9},{6,10},{7,11},{8,12},{9,13},{1... | collective-permute-start | bytes 884744 | tf_op jit(solution)/shard_map/ppermute | solution.py:25
  26.2 13.7 %collective-permute-start.5 = (bf16[9,128,128]{2,1,0:T(8,128)(2,1)S(1)}, bf16[9,128,128]{2,1,0:T(8,128)(2,1)S(1)}, u32[]{:S(2)}, u32[]{:S(2)}) collective-permute-start(bf16[9,128,128]{2,1,0:T(8,128)(2,1)S(1)} %get-tuple-element.46.refs_0_), channel_id=1, source_target_pairs={{0,8},{1,9},{2,10},{3,11},{4,12},{5,13},{6,14},{7,15},{8,0},{9,1},... | collective-permute-start | bytes 884744 | tf_op jit(solution)/shard_map/ppermute | solution.py:25
  27.0 14.7 %collective-permute-start.4 = (bf16[9,128,128]{2,1,0:T(8,128)(2,1)S(1)}, bf16[9,128,128]{2,1,0:T(8,128)(2,1)S(1)}, u32[]{:S(2)}, u32[]{:S(2)}) collective-permute-start(bf16[9,128,128]{2,1,0:T(8,128)(2,1)S(1)} %get-tuple-element.46.refs_0_), channel_id=1, source_target_pairs={{0,12},{1,13},{2,14},{3,15},{4,0},{5,1},{6,2},{7,3},{8,4},{9,5},{1... | collective-permute-start | bytes 884744 | tf_op jit(solution)/shard_map/ppermute | solution.py:25
  28.1 13.6 %collective-permute-start.9 = (bf16[9,128,128]{2,1,0:T(8,128)(2,1)S(1)}, bf16[9,128,128]{2,1,0:T(8,128)(2,1)S(1)}, u32[]{:S(2)}, u32[]{:S(2)}) collective-permute-start(bf16[9,128,128]{2,1,0:T(8,128)(2,1)S(1)} %get-tuple-element.50.refs_0_), channel_id=1, source_target_pairs={{0,64},{16,80},{32,96},{48,112},{64,128},{80,144},{96,160},{112,17... | collective-permute-start | bytes 884744 | tf_op jit(solution)/shard_map/ppermute | solution.py:25
  29.7 14.9 %collective-permute-start.8 = (bf16[9,128,128]{2,1,0:T(8,128)(2,1)S(1)}, bf16[9,128,128]{2,1,0:T(8,128)(2,1)S(1)}, u32[]{:S(2)}, u32[]{:S(2)}) collective-permute-start(bf16[9,128,128]{2,1,0:T(8,128)(2,1)S(1)} %get-tuple-element.50.refs_0_), channel_id=1, source_target_pairs={{0,128},{16,144},{32,160},{48,176},{64,192},{80,208},{96,224},{112... | collective-permute-start | bytes 884744 | tf_op jit(solution)/shard_map/ppermute | solution.py:25
  34.9 9.7 %collective-permute-start.7 = (bf16[9,128,128]{2,1,0:T(8,128)(2,1)S(1)}, bf16[9,128,128]{2,1,0:T(8,128)(2,1)S(1)}, u32[]{:S(2)}, u32[]{:S(2)}) collective-permute-start(bf16[9,128,128]{2,1,0:T(8,128)(2,1)S(1)} %get-tuple-element.50.refs_0_), channel_id=1, source_target_pairs={{0,192},{16,208},{32,224},{48,240},{64,0},{80,16},{96,32},{112,48}... | collective-permute-start | bytes 884744 | tf_op jit(solution)/shard_map/ppermute | solution.py:25
  44.8 3.1 %collective-permute-start.10 = (bf16[16,128,128]{2,1,0:T(8,128)(2,1)S(1)}, bf16[16,128,128]{2,1,0:T(8,128)(2,1)S(1)}, u32[]{:S(2)}, u32[]{:S(2)}) collective-permute-start(bf16[16,128,128]{2,1,0:T(8,128)(2,1)S(1)} %constant_dynamic-update-slice_fusion.2.queries), channel_id=1, source_target_pairs={{0,1},{1,0},{2,3},{3,2},{4,5},{5,4},{6,7},{7,6},{8,9},{9,8},{10,11... | collective-permute-start | bytes 1572872 | tf_op jit(solution)/shard_map/ppermute | solution.py:34
  50.7 3.5 %collective-permute-start.11 = (f32[2,136,512]{2,1,0:T(8,128)S(1)}, f32[2,136,512]{2,1,0:T(8,128)S(1)}, u32[]{:S(2)}, u32[]{:S(2)}) collective-permute-start(f32[2,136,512]{2,1,0:T(8,128)S(1)} %shard_map.77), channel_id=1, source_target_pairs={{0,1},{1,0},{2,3},{3,2},{4,5},{5,4},{6,7},{7,6},{8,9},{9,8},{10,11... | collective-permute-start | bytes 1671176 | tf_op jit(solution)/shard_map/ppermute | solution.py:34
  54.1 7.6 %collective-permute-start.15 = (f32[2,136,512]{2,1,0:T(8,128)S(1)}, f32[2,136,512]{2,1,0:T(8,128)S(1)}, u32[]{:S(2)}, u32[]{:S(2)}) collective-permute-start(f32[2,136,512]{2,1,0:T(8,128)S(1)} %shard_map.78), channel_id=1, source_target_pairs={{0,1},{1,0},{2,3},{3,2},{4,5},{5,4},{6,7},{7,6},{8,9},{9,8},{10,11... | collective-permute-start | bytes 1671176 | tf_op jit(solution)/shard_map/ppermute | solution.py:34
  54.3 13.7 %collective-permute-start.12 = (f32[136,256]{1,0:T(8,128)S(1)}, f32[136,256]{1,0:T(8,128)S(1)}, u32[]{:S(2)}, u32[]{:S(2)}) collective-permute-start(f32[136,256]{1,0:T(8,128)S(1)} %get-tuple-element.62), channel_id=1, source_target_pairs={{0,4},{1,5},{2,6},{3,7},{4,8},{5,9},{6,10},{7,11},{8,12},{9,13},{1... | collective-permute-start | bytes 417800 | tf_op jit(solution)/shard_map/ppermute | solution.py:25
  55.6 12.4 %collective-permute-start.13 = (f32[136,256]{1,0:T(8,128)S(1)}, f32[136,256]{1,0:T(8,128)S(1)}, u32[]{:S(2)}, u32[]{:S(2)}) collective-permute-start(f32[136,256]{1,0:T(8,128)S(1)} %get-tuple-element.63), channel_id=1, source_target_pairs={{0,8},{1,9},{2,10},{3,11},{4,12},{5,13},{6,14},{7,15},{8,0},{9,1},... | collective-permute-start | bytes 417800 | tf_op jit(solution)/shard_map/ppermute | solution.py:25
  58.0 10.1 %collective-permute-start.14 = (f32[136,256]{1,0:T(8,128)S(1)}, f32[136,256]{1,0:T(8,128)S(1)}, u32[]{:S(2)}, u32[]{:S(2)}) collective-permute-start(f32[136,256]{1,0:T(8,128)S(1)} %get-tuple-element.64), channel_id=1, source_target_pairs={{0,12},{1,13},{2,14},{3,15},{4,0},{5,1},{6,2},{7,3},{8,4},{9,5},{1... | collective-permute-start | bytes 417800 | tf_op jit(solution)/shard_map/ppermute | solution.py:25
  61.8 6.8 %collective-permute-start.17 = (f32[136,256]{1,0:T(8,128)S(1)}, f32[136,256]{1,0:T(8,128)S(1)}, u32[]{:S(2)}, u32[]{:S(2)}) collective-permute-start(f32[136,256]{1,0:T(8,128)S(1)} %get-tuple-element.76), channel_id=1, source_target_pairs={{0,128},{16,144},{32,160},{48,176},{64,192},{80,208},{96,224},{112... | collective-permute-start | bytes 417800 | tf_op jit(solution)/shard_map/ppermute | solution.py:25
  64.4 6.5 %collective-permute-start.18 = (f32[136,256]{1,0:T(8,128)S(1)}, f32[136,256]{1,0:T(8,128)S(1)}, u32[]{:S(2)}, u32[]{:S(2)}) collective-permute-start(f32[136,256]{1,0:T(8,128)S(1)} %get-tuple-element.77), channel_id=1, source_target_pairs={{0,192},{16,208},{32,224},{48,240},{64,0},{80,16},{96,32},{112,48}... | collective-permute-start | bytes 417800 | tf_op jit(solution)/shard_map/ppermute | solution.py:25
  68.2 6.3 %collective-permute-start.16 = (f32[136,256]{1,0:T(8,128)S(1)}, f32[136,256]{1,0:T(8,128)S(1)}, u32[]{:S(2)}, u32[]{:S(2)}) collective-permute-start(f32[136,256]{1,0:T(8,128)S(1)} %get-tuple-element.75), channel_id=1, source_target_pairs={{0,64},{16,80},{32,96},{48,112},{64,128},{80,144},{96,160},{112,17... | collective-permute-start | bytes 417800 | tf_op jit(solution)/shard_map/ppermute | solution.py:25
  74.6 5.1 %collective-permute-start.19 = (f32[2,136,128]{2,1,0:T(8,128)S(1)}, f32[2,136,128]{2,1,0:T(8,128)S(1)}, u32[]{:S(2)}, u32[]{:S(2)}) collective-permute-start(f32[2,136,128]{2,1,0:T(8,128)S(1)} %get-tuple-element.79), channel_id=1, source_target_pairs={{0,2},{1,3},{2,0},{3,1},{4,6},{5,7},{6,4},{7,5},{8,10},{9,11},{10,... | collective-permute-start | bytes 417800 | tf_op jit(solution)/shard_map/ppermute | solution.py:34

commit v6 on v2

--- a/solution.py
+++ b/solution.py
@@ -113,17 +113,29 @@
     return with_peak(*merge([peak_of(part) for part in parts], parts))
 
 
-def attend(scale, query, blocks):
-    peaks, parts = [], []
-    for keys, values in blocks:
-        score = lax.dot_general(
-            keys, query, (((1,), (1,)), ((), ())), preferred_element_type=jnp.float32
-        ) * scale
+def attend(scale, queries, blocks):
+    steps = [(tile, block) for tile in range(len(queries)) for block in range(len(blocks))]
+
+    def raw(tile, block):
+        return lax.dot_general(
+            blocks[block][0],
+            queries[tile],
+            (((1,), (1,)), ((), ())),
+            preferred_element_type=jnp.float32,
+        )
+
+    peaks, parts = [[] for _ in queries], [[] for _ in queries]
+    ahead = raw(*steps[0])
+    for at, (tile, block) in enumerate(steps):
+        score = ahead * scale
+        if at + 1 < len(steps):
+            ahead = raw(*steps[at + 1])
         peak = jnp.max(score, axis=0, keepdims=True)
         weight = jnp.exp2(score - peak).astype(jnp.bfloat16)
-        parts.append(jnp.dot(values, weight, preferred_element_type=jnp.float32)[:ROWS])
-        peaks.append(peak)
-    return with_peak(*merge(peaks, parts))
+        part = jnp.dot(blocks[block][1], weight, preferred_element_type=jnp.float32)
+        parts[tile].append(part[:ROWS])
+        peaks[tile].append(peak)
+    return [with_peak(*merge(*pair)) for pair in zip(peaks, parts)]
 
 
 def one_block(ones, slow, total):
@@ -143,35 +155,44 @@
 def col_kernel(total, scale, *refs):
     ones, two, out = refs[:SUB], refs[SUB], refs[SUB + 1]
     query = jnp.concatenate([two[piece, :, :WIDTH] for piece in range(SUB)], axis=0)
-    out[...] = attend(scale, query, [one_block(ones, slow, total) for slow in range(SUB)])
-
-
-def row_kernel(total, scale, first, *refs):
-    ones, twos, (keep, send) = refs[:SUB], refs[SUB : 2 * SUB], refs[2 * SUB :]
-
-    def step(slow, _):
-        query = jnp.concatenate([ref[first + slow, :, :WIDTH] for ref in ones], axis=0)
-        blocks = [two_block(two, block, total) for block, two in enumerate(twos)]
-        whole = attend(scale, query, blocks)
-        keep[slow] = whole[:, : BLOCK // 2]
-        send[slow] = whole[:, BLOCK // 2 :]
-        return 0
-
-    lax.fori_loop(0, keep.shape[0], step, 0)
-
-
-def halve_kernel(mine, theirs, mine_b, theirs_b, keep, send):
-    half = SUB // 2
-    for slow in range(half):
-        for first, one, two in ((0, mine, theirs), (half, mine_b, theirs_b)):
-            whole = merged([one[slow], two[slow]])
-            keep[first + slow] = whole[:, :SHARD]
-            send[first + slow] = whole[:, SHARD:]
-
-
-def pair_kernel(mine, theirs, *outs):
-    for slow in range(SUB):
-        outs[slow][...] = merged([mine[slow], theirs[slow]])
+    blocks = [one_block(ones, slow, total) for slow in range(SUB)]
+    (out[...],) = attend(scale, [query], blocks)
+
+
+def row_kernel(total, scale, halves, *refs):
+    ones, twos, outs = refs[:SUB], refs[SUB : 2 * SUB], refs[2 * SUB :]
+    tiles = [
+        jnp.concatenate(
+            [
+                ones[2 * core + high][slow, :, :WIDTH]
+                for slow in (2 * half, 2 * half + 1)
+                for high in range(2)
+            ],
+            axis=0,
+        )
+        for core, half in halves
+    ]
+    blocks = [two_block(two, block, total) for block, two in enumerate(twos)]
+    wholes = attend(scale, tiles, blocks)
+    for out in outs:
+        for index in range(out.shape[0]):
+            out[index] = wholes.pop(0)
+
+
+def core_kernel(halves, *refs):
+    (theirs, *mine), outs = refs[: -2 * len(halves)], refs[-2 * len(halves) :]
+    for index, half in enumerate(halves):
+        own = mine[0][index]
+        whole = merged([own, theirs[half]])
+        outs[2 * index][...] = whole[:, : 2 * SHARD]
+        outs[2 * index + 1][...] = whole[:, 2 * SHARD :]
+
+
+def chip_kernel(*refs):
+    ins, (keep, send) = refs[:SUB], refs[SUB:]
+    whole = merged([ref[...] for ref in ins])
+    keep[...] = whole[:, :SHARD]
+    send[...] = whole[:, SHARD:]
 
 
 def block_kernel(*refs):
@@ -182,7 +203,7 @@
 
 
 def finish_kernel(total, own_start, *refs):
-    ins, (matched, flow) = refs[:SUB], refs[SUB:]
+    ins, (matched, flow) = refs[:-2], refs[-2:]
     own_across, own_down = piece_coords(own_start(), total)
     lane = lax.broadcasted_iota(jnp.int32, (1, SHARD), 1).astype(jnp.float32) / GRID_W
     parts = [ref[...] for ref in ins]
@@ -216,6 +237,10 @@
 
 def f32(*shape):
     return jax.ShapeDtypeStruct(shape, jnp.float32)
+
+
+def bf16(*shape):
+    return jax.ShapeDtypeStruct(shape, jnp.bfloat16)
 
 
 def body(feat_one, feat_two, value_one, value_two):
@@ -247,8 +272,20 @@
     def col_scores(*refs):
         col_kernel(total, scale, *refs)
 
-    def row_scores_of(first):
-        return functools.partial(row_kernel, total, scale, first)
+    def row_scores(ones, halves, weight, *counts):
+        shapes = [f32(count, ROWS, BLOCK) for count in counts]
+        kernel = functools.partial(row_kernel, total, scale, halves)
+        return call(kernel, shapes, (*ones, *twos), work=weight * work)
+
+    def core_merge(mine, theirs, *halves):
+        shapes = [f32(ROWS, 2 * SHARD)] * (2 * len(halves))
+        return call(functools.partial(core_kernel, halves), shapes, (theirs, mine))
+
+    def spread(axis, parts, first=0):
+        return [
+            slow_shift(axis, part, first + step) if first + step else part
+            for step, part in enumerate(parts)
+        ]
 
     def finish_one(*refs):
         finish_kernel(total, lambda: start_one(0, 0, 0), *refs)
@@ -262,26 +299,22 @@
         if step == 2:
             twos[2], _ = together((twos[2], cols[0]))
         (cols[step],) = call(col_scores, [f32(ROWS, BLOCK)], (*ones, twos[step]), work=work)
-    ones, _ = together((ones, cols))
-    cols = [cols[0]] + [slow_shift("row", cols[step], step) for step in range(1, SUB)]
-    half = SUB // 2
-    shapes = [f32(half, ROWS, BLOCK // 2)] * 2
-    keep, send = call(row_scores_of(0), shapes, (*ones, *twos), work=half * work)
-    theirs = fast_swap("col", send, 1)
-    ones, cols, keep = together((ones, cols, keep))
-    keep_b, send_b = call(row_scores_of(half), shapes, (*ones, *twos), work=half * work)
-    theirs_b = fast_swap("col", send_b, 1)
+    ones, cols = together((ones, cols))
+    cols = spread("row", cols)
+    send_one, far_one = row_scores(ones, ((1, 0), (1, 1), (0, 1)), 3, 2, 1)
+    theirs_one = fast_swap("col", send_one, 1)
+    far_rows = core_merge(far_one, theirs_one, 1)
+    far_rows = spread("col", far_rows, 2)
     cols = call(block_kernel, [f32(ROWS, SHARD)] * SUB, cols)
+    ones, _, cols = together((ones, far_one, cols))
     cols = [cols[0]] + [fast_shift("row", cols[step], step) for step in range(1, SUB)]
-    keep, send = call(
-        halve_kernel, [f32(SUB, ROWS, SHARD)] * 2, (keep, theirs, keep_b, theirs_b)
-    )
+    (near_one,) = row_scores(ones, ((0, 0),), 40, 1)
+    rows = spread("col", core_merge(near_one, theirs_one, 0)) + far_rows
+    keep, send = call(chip_kernel, [f32(ROWS, SHARD)] * 2, rows)
     theirs = fast_swap("col", send, 2)
-    rows = call(pair_kernel, [f32(ROWS, SHARD)] * SUB, (keep, theirs))
-    rows = [rows[0]] + [slow_shift("col", rows[step], step) for step in range(1, SUB)]
     outs = [f32(SHARD, WIDTH), f32(2, SHARD)]
     matched_two, flow_two = call(finish_two, outs, cols)
-    matched_one, flow_one = call(finish_one, outs, rows)
+    matched_one, flow_one = call(finish_one, outs, (keep, theirs))
     return matched_one, flow_one, matched_two, flow_two
 
 

time: 91.5 us -> 83.1 us (0.908)
  Pallas kernels: 20.3 us -> 15.5 us
  starting transfers between devices: 45.7 us -> 42.8 us
    pallas_call x12 -> x13, Pallas kernels: 20.3 us -> 15.5 us  [call(): pl.pallas_call(kernel, out_shape=shapes, in_specs=specs or [VMEM] * len(a...]
    ppermute x12, starting transfers between devices: 20.4 us -> 16.9 us  [slow_shift(): return lax.ppermute(value, axis, pairs)]
    ppermute x6, starting transfers between devices: 15.8 us -> 17.1 us  [fast_shift(): return lax.ppermute(value, axis, pairs)]
    ppermute x12, waiting for transfers between devices: 15.5 us -> 14.3 us  [slow_shift(): return lax.ppermute(value, axis, pairs)]
    ppermute x5 -> x4, starting transfers between devices: 9.52 us -> 8.76 us  [fast_swap(): return lax.ppermute(value, axis, [(i, i ^ step) for i in range(SUB * SUB)])]
    ppermute x5 -> x4, waiting for transfers between devices: 1.19 us -> 1.86 us  [fast_swap(): return lax.ppermute(value, axis, [(i, i ^ step) for i in range(SUB * SUB)])]
  transfers between devices with their start and end apart: 23 -> 22, of which waited for: 8 -> 11; matrix products, arithmetic and copies ran while one was open for 1% -> 1% of each run, Pallas kernels for 15% -> 10%
where the time goes in v6:
time: 83.1 us; the launch traced here: 81.8 us
  starting transfers between devices  42.8 us (52%)
  waiting for transfers between devices  21.7 us (26%)
  Pallas kernels  15.5 us (19%)
  other arithmetic  0.99 us (1%)
    ppermute x6, starting transfers between devices, fast_shift(): return lax.ppermute(value, axis, pairs)  17.1 us
    ppermute x12, starting transfers between devices, slow_shift(): return lax.ppermute(value, axis, pairs)  16.9 us
    pallas_call x13, Pallas kernels, call(): pl.pallas_call(kernel, out_shape=shapes, in_specs=specs or [VMEM] * len(a...  15.5 us
    ppermute x12, waiting for transfers between devices, slow_shift(): return lax.ppermute(value, axis, pairs)  14.3 us
    ppermute x4, starting transfers between devices, fast_swap(): return lax.ppermute(value, axis, [(i, i ^ step) for i in range(SUB * SUB)])  8.76 us
    ppermute x6, waiting for transfers between devices, fast_shift(): return lax.ppermute(value, axis, pairs)  5.53 us
    ppermute x4, waiting for transfers between devices, fast_swap(): return lax.ppermute(value, axis, [(i, i ^ step) for i in range(SUB * SUB)])  1.86 us
  transfers between devices with their start and end apart: 22, of which 11 were waited for; matrix products, arithmetic and copies ran while one was open for 1% of the time, Pallas kernels for 10%

profile of v6, /device:TPU:1, one launch (start us, length us, event | category | flops | bytes accessed | tf_op | source)
XLA Modules:
  0.0 81.8 jit_solution(4176228866811062099)
XLA Ops:
  0.6 1.7 %shard_map.75 = (bf16[128,256]{1,0:T(8,128)(2,1)}, bf16[128,256]{1,0:T(8,128)(2,1)}) custom-call(bf16[128,128]{1,0:T(8,128)(2,1)} %feat_one.1, bf16[128,128]{1,0:T(8,128)(2,1)} %value_one.1, bf16[128,128]{1,0:T(8,128)(2,1)} %feat_two.1, bf16[128,128]{1,0:T(8,128)(2,1)} %value_two.1), custom_call_target="tpu_custom_call" | custom-call | bytes 262144 | tf_op jit(solution)/shard_map/pallas_call | solution.py:221
  2.3 2.6 %collective-permute-start = (bf16[128,256]{1,0:T(8,128)(2,1)}, bf16[128,256]{1,0:T(8,128)(2,1)S(1)}, u32[]{:S(2)}, u32[]{:S(2)}) collective-permute-start(bf16[128,256]{1,0:T(8,128)(2,1)} %get-tuple-element.44), channel_id=1, source_target_pairs={{0,2},{1,3},{2,0},{3,1},{4,6},{5,7},{6,4},{7,5},{8,10},{9,11},{10,... | collective-permute-start | bytes 196616 | tf_op jit(solution)/shard_map/ppermute | solution.py:34
  4.9 3.0 %collective-permute-start.3 = (bf16[128,256]{1,0:T(8,128)(2,1)}, bf16[128,256]{1,0:T(8,128)(2,1)S(1)}, u32[]{:S(2)}, u32[]{:S(2)}) collective-permute-start(bf16[128,256]{1,0:T(8,128)(2,1)} %get-tuple-element.45), channel_id=1, source_target_pairs={{0,16},{16,32},{32,48},{48,0},{64,80},{80,96},{96,112},{112,64},{1... | collective-permute-start | bytes 196616 | tf_op jit(solution)/shard_map/ppermute | solution.py:30
  7.9 4.2 %collective-permute-start.2 = (bf16[128,256]{1,0:T(8,128)(2,1)}, bf16[128,256]{1,0:T(8,128)(2,1)S(1)}, u32[]{:S(2)}, u32[]{:S(2)}) collective-permute-start(bf16[128,256]{1,0:T(8,128)(2,1)} %get-tuple-element.45), channel_id=1, source_target_pairs={{0,32},{16,48},{32,0},{48,16},{64,96},{80,112},{96,64},{112,80},{1... | collective-permute-start | bytes 196616 | tf_op jit(solution)/shard_map/ppermute | solution.py:30
  12.1 2.4 %collective-permute-start.1 = (bf16[128,256]{1,0:T(8,128)(2,1)}, bf16[128,256]{1,0:T(8,128)(2,1)S(1)}, u32[]{:S(2)}, u32[]{:S(2)}) collective-permute-start(bf16[128,256]{1,0:T(8,128)(2,1)} %get-tuple-element.45), channel_id=1, source_target_pairs={{0,48},{16,0},{32,16},{48,32},{64,112},{80,64},{96,80},{112,96},{1... | collective-permute-start | bytes 196616 | tf_op jit(solution)/shard_map/ppermute | solution.py:30
  14.5 0.9 %pad_maximum_fusion.2 = bf16[2,128,256]{2,1,0:T(8,128)(2,1)S(1)} fusion(bf16[1,128,256]{2,1,0:T(8,128)(2,1)S(1)} %bitcast.29, bf16[1,128,256]{2,1,0:T(8,128)(2,1)} %bitcast.28), kind=kLoop, calls=%fused_computation.6 | loop fusion | flops 65536 | bytes 262144 | tf_op jit(solution)/shard_map/stack | solution.py:264
  15.4 1.9 %collective-permute-done.2 = bf16[128,256]{1,0:T(8,128)(2,1)S(1)} collective-permute-done((bf16[128,256]{1,0:T(8,128)(2,1)}, bf16[128,256]{1,0:T(8,128)(2,1)S(1)}, u32[]{:S(2)}, u32[]{:S(2)}) %collective-permute-start.2) | collective-permute-done | bytes 65568 | tf_op jit(solution)/shard_map/ppermute | solution.py:30
  17.3 1.0 %collective-permute-done.1 = bf16[128,256]{1,0:T(8,128)(2,1)S(1)} collective-permute-done((bf16[128,256]{1,0:T(8,128)(2,1)}, bf16[128,256]{1,0:T(8,128)(2,1)S(1)}, u32[]{:S(2)}, u32[]{:S(2)}) %collective-permute-start.1) | collective-permute-done | bytes 65568 | tf_op jit(solution)/shard_map/ppermute | solution.py:30
  18.3 1.4 %collective-permute-start.8 = (bf16[4,128,256]{2,1,0:T(8,128)(2,1)S(1)}, bf16[4,128,256]{2,1,0:T(8,128)(2,1)S(1)}, u32[]{:S(2)}, u32[]{:S(2)}) collective-permute-start(bf16[4,128,256]{2,1,0:T(8,128)(2,1)S(1)} %pad_maximum_fusion.1.refs_4_), channel_id=1, source_target_pairs={{0,64},{16,80},{32,96},{48,112},{64,128},{80,144},{96,160},{112,17... | collective-permute-start | bytes 786440 | tf_op jit(solution)/shard_map/ppermute | solution.py:25
  19.7 1.5 %collective-permute-start.7 = (bf16[4,128,256]{2,1,0:T(8,128)(2,1)S(1)}, bf16[4,128,256]{2,1,0:T(8,128)(2,1)S(1)}, u32[]{:S(2)}, u32[]{:S(2)}) collective-permute-start(bf16[4,128,256]{2,1,0:T(8,128)(2,1)S(1)} %pad_maximum_fusion.1.refs_4_), channel_id=1, source_target_pairs={{0,192},{16,208},{32,224},{48,240},{64,0},{80,16},{96,32},{112,48}... | collective-permute-start | bytes 786440 | tf_op jit(solution)/shard_map/ppermute | solution.py:25
  21.2 1.2 %collective-permute-start.6 = (bf16[2,128,256]{2,1,0:T(8,128)(2,1)S(1)}, bf16[2,128,256]{2,1,0:T(8,128)(2,1)S(1)}, u32[]{:S(2)}, u32[]{:S(2)}) collective-permute-start(bf16[2,128,256]{2,1,0:T(8,128)(2,1)S(1)} %pad_maximum_fusion.2), channel_id=1, source_target_pairs={{0,4},{1,5},{2,6},{3,7},{4,8},{5,9},{6,10},{7,11},{8,12},{9,13},{1... | collective-permute-start | bytes 393224 | tf_op jit(solution)/shard_map/ppermute | solution.py:25
  22.5 2.5 %collective-permute-start.5 = (bf16[2,128,256]{2,1,0:T(8,128)(2,1)S(1)}, bf16[2,128,256]{2,1,0:T(8,128)(2,1)S(1)}, u32[]{:S(2)}, u32[]{:S(2)}) collective-permute-start(bf16[2,128,256]{2,1,0:T(8,128)(2,1)S(1)} %pad_maximum_fusion.2), channel_id=1, source_target_pairs={{0,8},{1,9},{2,10},{3,11},{4,12},{5,13},{6,14},{7,15},{8,0},{9,1},... | collective-permute-start | bytes 393224 | tf_op jit(solution)/shard_map/ppermute | solution.py:25
  24.9 1.2 %collective-permute-start.4 = (bf16[2,128,256]{2,1,0:T(8,128)(2,1)S(1)}, bf16[2,128,256]{2,1,0:T(8,128)(2,1)S(1)}, u32[]{:S(2)}, u32[]{:S(2)}) collective-permute-start(bf16[2,128,256]{2,1,0:T(8,128)(2,1)S(1)} %pad_maximum_fusion.2), channel_id=1, source_target_pairs={{0,12},{1,13},{2,14},{3,15},{4,0},{5,1},{6,2},{7,3},{8,4},{9,5},{1... | collective-permute-start | bytes 393224 | tf_op jit(solution)/shard_map/ppermute | solution.py:25
  26.1 0.5 collective-permute-done.6
  26.6 2.2 %collective-permute-done.5 = bf16[2,128,256]{2,1,0:T(8,128)(2,1)S(1)} collective-permute-done((bf16[2,128,256]{2,1,0:T(8,128)(2,1)S(1)}, bf16[2,128,256]{2,1,0:T(8,128)(2,1)S(1)}, u32[]{:S(2)}, u32[]{:S(2)}) %collective-permute-start.5) | collective-permute-done | bytes 131104 | tf_op jit(solution)/shard_map/ppermute | solution.py:25
  28.8 0.6 collective-permute-done.4
  29.3 0.1 pad_maximum_fusion
  29.4 0.0 collective-permute-done.7.refs_4_.refs_5_
  29.4 3.4 %collective-permute-start.9 = (bf16[2,4,128,256]{3,2,1,0:T(8,128)(2,1)S(1)}, bf16[2,4,128,256]{3,2,1,0:T(8,128)(2,1)S(1)}, u32[]{:S(2)}, u32[]{:S(2)}) collective-permute-start(bf16[2,4,128,256]{3,2,1,0:T(8,128)(2,1)S(1)} %pad_maximum_fusion), channel_id=1, source_target_pairs={{0,1},{1,0},{2,3},{3,2},{4,5},{5,4},{6,7},{7,6},{8,9},{9,8},{10,11... | collective-permute-start | bytes 1572872 | tf_op jit(solution)/shard_map/ppermute | solution.py:34
  32.8 1.7 %collective-permute-start.10 = (bf16[4,128,256]{2,1,0:T(8,128)(2,1)S(1)}, bf16[4,128,256]{2,1,0:T(8,128)(2,1)S(1)}, u32[]{:S(2)}, u32[]{:S(2)}) collective-permute-start(bf16[4,128,256]{2,1,0:T(8,128)(2,1)S(1)} %pad_maximum_fusion.1.refs_4_), channel_id=1, source_target_pairs={{0,128},{16,144},{32,160},{48,176},{64,192},{80,208},{96,224},{112... | collective-permute-start | bytes 786440 | tf_op jit(solution)/shard_map/ppermute | solution.py:25
  34.6 0.0 collective-permute-done.9
  34.6 1.6 %shard_map.76.refs_0_ = f32[136,512]{1,0:T(8,128)S(1)} custom-call(bf16[4,128,256]{2,1,0:T(8,128)(2,1)S(1)} %get-tuple-element.66.refs_0_, bf16[4,128,256]{2,1,0:T(8,128)(2,1)S(1)} %get-tuple-element.67.refs_1_, bf16[4,128,256]{2,1,0:T(8,128)(2,1)S(1)} %get-tuple-element.68.refs_2_, bf16[4,128,256]{2,1,0:T(8,128)(2,1)S(1)} %get-tuple-element.69.refs_3_, ...), custom_call_target="tpu_custom_call" | custom-call | flops 536870912 | bytes 1589248 | tf_op jit(solution)/shard_map/pallas_call | solution.py:221
  36.2 5.7 %collective-permute-done.10.refs_4_.refs_6_ = bf16[4,128,256]{2,1,0:T(8,128)(2,1)S(1)} collective-permute-done((bf16[4,128,256]{2,1,0:T(8,128)(2,1)S(1)}, bf16[4,128,256]{2,1,0:T(8,128)(2,1)S(1)}, u32[]{:S(2)}, u32[]{:S(2)}) %collective-permute-start.10) | collective-permute-done | bytes 262176 | tf_op jit(solution)/shard_map/ppermute | solution.py:25
  42.0 1.6 %shard_map.78 = f32[136,512]{1,0:T(8,128)S(1)} custom-call(bf16[4,128,256]{2,1,0:T(8,128)(2,1)S(1)} %get-tuple-element.66.refs_0_, bf16[4,128,256]{2,1,0:T(8,128)(2,1)S(1)} %get-tuple-element.67.refs_1_, bf16[4,128,256]{2,1,0:T(8,128)(2,1)S(1)} %get-tuple-element.68.refs_2_, bf16[4,128,256]{2,1,0:T(8,128)(2,1)S(1)} %get-tuple-element.69.refs_3_, ...), custom_call_target="tpu_custom_call" | custom-call | flops 536870912 | bytes 1589248 | tf_op jit(solution)/shard_map/pallas_call | solution.py:221
  43.6 1.6 %shard_map.79 = f32[136,512]{1,0:T(8,128)S(1)} custom-call(bf16[4,128,256]{2,1,0:T(8,128)(2,1)S(1)} %get-tuple-element.66.refs_0_, bf16[4,128,256]{2,1,0:T(8,128)(2,1)S(1)} %get-tuple-element.67.refs_1_, bf16[4,128,256]{2,1,0:T(8,128)(2,1)S(1)} %get-tuple-element.68.refs_2_, bf16[4,128,256]{2,1,0:T(8,128)(2,1)S(1)} %get-tuple-element.69.refs_3_, ...), custom_call_target="tpu_custom_call" | custom-call | flops 536870912 | bytes 1589248 | tf_op jit(solution)/shard_map/pallas_call | solution.py:221
  45.2 1.6 %shard_map.77 = f32[136,512]{1,0:T(8,128)S(1)} custom-call(bf16[4,128,256]{2,1,0:T(8,128)(2,1)S(1)} %get-tuple-element.66.refs_0_, bf16[4,128,256]{2,1,0:T(8,128)(2,1)S(1)} %get-tuple-element.67.refs_1_, bf16[4,128,256]{2,1,0:T(8,128)(2,1)S(1)} %get-tuple-element.68.refs_2_, bf16[4,128,256]{2,1,0:T(8,128)(2,1)S(1)} %get-tuple-element.69.refs_3_, ...), custom_call_target="tpu_custom_call" | custom-call | flops 536870912 | bytes 1589248 | tf_op jit(solution)/shard_map/pallas_call | solution.py:221
  46.8 0.2 collective-permute-start.12
  47.0 2.6 %collective-permute-start.13 = (f32[136,512]{1,0:T(8,128)S(1)}, f32[136,512]{1,0:T(8,128)S(1)}, u32[]{:S(2)}, u32[]{:S(2)}) collective-permute-start(f32[136,512]{1,0:T(8,128)S(1)} %shard_map.78), channel_id=1, source_target_pairs={{0,128},{16,144},{32,160},{48,176},{64,192},{80,208},{96,224},{112... | collective-permute-start | bytes 835592 | tf_op jit(solution)/shard_map/ppermute | solution.py:25
  49.6 1.1 %collective-permute-start.14 = (f32[136,512]{1,0:T(8,128)S(1)}, f32[136,512]{1,0:T(8,128)S(1)}, u32[]{:S(2)}, u32[]{:S(2)}) collective-permute-start(f32[136,512]{1,0:T(8,128)S(1)} %shard_map.79), channel_id=1, source_target_pairs={{0,192},{16,208},{32,224},{48,240},{64,0},{80,16},{96,32},{112,48}... | collective-permute-start | bytes 835592 | tf_op jit(solution)/shard_map/ppermute | solution.py:25
  50.6 4.0 %shard_map.80 = (f32[2,136,512]{2,1,0:T(8,128)S(1)}, f32[1,136,512]{2,1,0:T(8,128)S(1)}) custom-call(bf16[4,128,256]{2,1,0:T(8,128)(2,1)S(1)} %get-tuple-element.66.refs_0_, bf16[4,128,256]{2,1,0:T(8,128)(2,1)S(1)} %get-tuple-element.67.refs_1_, bf16[4,128,256]{2,1,0:T(8,128)(2,1)S(1)} %get-tuple-element.68.refs_2_, ...), custom_call_target="tpu_custom_call" | custom-call | flops 1610612736 | bytes 2932736 | tf_op jit(solution)/shard_map/pallas_call | solution.py:221
  54.6 2.2 %collective-permute-start.11 = (f32[2,136,512]{2,1,0:T(8,128)S(1)}, f32[2,136,512]{2,1,0:T(8,128)S(1)}, u32[]{:S(2)}, u32[]{:S(2)}) collective-permute-start(f32[2,136,512]{2,1,0:T(8,128)S(1)} %get-tuple-element.56), channel_id=1, source_target_pairs={{0,1},{1,0},{2,3},{3,2},{4,5},{5,4},{6,7},{7,6},{8,9},{9,8},{10,11... | collective-permute-start | bytes 1671176 | tf_op jit(solution)/shard_map/ppermute | solution.py:34
  56.9 4.3 %collective-permute-done.13.refs_2_ = f32[136,512]{1,0:T(8,128)S(1)} collective-permute-done((f32[136,512]{1,0:T(8,128)S(1)}, f32[136,512]{1,0:T(8,128)S(1)}, u32[]{:S(2)}, u32[]{:S(2)}) %collective-permute-start.13) | collective-permute-done | bytes 278560 | tf_op jit(solution)/shard_map/ppermute | solution.py:25
  61.1 1.1 %collective-permute-done.14.refs_3_ = f32[136,512]{1,0:T(8,128)S(1)} collective-permute-done((f32[136,512]{1,0:T(8,128)S(1)}, f32[136,512]{1,0:T(8,128)S(1)}, u32[]{:S(2)}, u32[]{:S(2)}) %collective-permute-start.14) | collective-permute-done | bytes 278560 | tf_op jit(solution)/shard_map/ppermute | solution.py:25
  62.2 0.1 shard_map.81
  62.3 1.6 %shard_map.82.refs_1_ = f32[1,136,512]{2,1,0:T(8,128)S(1)} custom-call(bf16[4,128,256]{2,1,0:T(8,128)(2,1)S(1)} %get-tuple-element.66.refs_0_, bf16[4,128,256]{2,1,0:T(8,128)(2,1)S(1)} %get-tuple-element.67.refs_1_, bf16[4,128,256]{2,1,0:T(8,128)(2,1)S(1)} %get-tuple-element.68.refs_2_, bf16[4,128,256]{2,1,0:T(8,128)(2,1)S(1)} %get-tuple-element.69.refs_3_, ...), custom_call_target="tpu_custom_call" | custom-call | flops 21474836480 | bytes 2375680 | tf_op jit(solution)/shard_map/pallas_call | solution.py:221
  64.0 2.1 %collective-permute-start.16 = (f32[136,256]{1,0:T(8,128)S(1)}, f32[136,256]{1,0:T(8,128)S(1)}, u32[]{:S(2)}, u32[]{:S(2)}) collective-permute-start(f32[136,256]{1,0:T(8,128)S(1)} %get-tuple-element.72), channel_id=1, source_target_pairs={{0,8},{1,9},{2,10},{3,11},{4,12},{5,13},{6,14},{7,15},{8,0},{9,1},... | collective-permute-start | bytes 417800 | tf_op jit(solution)/shard_map/ppermute | solution.py:25
  66.1 1.4 %collective-permute-start.17 = (f32[136,256]{1,0:T(8,128)S(1)}, f32[136,256]{1,0:T(8,128)S(1)}, u32[]{:S(2)}, u32[]{:S(2)}) collective-permute-start(f32[136,256]{1,0:T(8,128)S(1)} %get-tuple-element.73), channel_id=1, source_target_pairs={{0,12},{1,13},{2,14},{3,15},{4,0},{5,1},{6,2},{7,3},{8,4},{9,5},{1... | collective-permute-start | bytes 417800 | tf_op jit(solution)/shard_map/ppermute | solution.py:25
  67.5 0.2 collective-permute-start.15
  67.7 1.8 %collective-permute-start.19 = (f32[136,128]{1,0:T(8,128)S(1)}, f32[136,128]{1,0:T(8,128)S(1)}, u32[]{:S(2)}, u32[]{:S(2)}) collective-permute-start(f32[136,128]{1,0:T(8,128)S(1)} %get-tuple-element.79), channel_id=1, source_target_pairs={{0,16},{16,32},{32,48},{48,0},{64,80},{80,96},{96,112},{112,64},{1... | collective-permute-start | bytes 208904 | tf_op jit(solution)/shard_map/ppermute | solution.py:30
  69.5 3.4 %collective-permute-start.20 = (f32[136,128]{1,0:T(8,128)S(1)}, f32[136,128]{1,0:T(8,128)S(1)}, u32[]{:S(2)}, u32[]{:S(2)}) collective-permute-start(f32[136,128]{1,0:T(8,128)S(1)} %get-tuple-element.80), channel_id=1, source_target_pairs={{0,32},{16,48},{32,0},{48,16},{64,96},{80,112},{96,64},{112,80},{1... | collective-permute-start | bytes 208904 | tf_op jit(solution)/shard_map/ppermute | solution.py:30
  72.8 2.4 %collective-permute-start.21 = (f32[136,128]{1,0:T(8,128)S(1)}, f32[136,128]{1,0:T(8,128)S(1)}, u32[]{:S(2)}, u32[]{:S(2)}) collective-permute-start(f32[136,128]{1,0:T(8,128)S(1)} %get-tuple-element.81), channel_id=1, source_target_pairs={{0,48},{16,0},{32,16},{48,32},{64,112},{80,64},{96,80},{112,96},{1... | collective-permute-start | bytes 208904 | tf_op jit(solution)/shard_map/ppermute | solution.py:30
  75.2 0.1 shard_map.85
  75.3 0.6 collective-permute-start.18
  75.9 0.9 %collective-permute-done.20.refs_2_ = f32[136,128]{1,0:T(8,128)S(1)} collective-permute-done((f32[136,128]{1,0:T(8,128)S(1)}, f32[136,128]{1,0:T(8,128)S(1)}, u32[]{:S(2)}, u32[]{:S(2)}) %collective-permute-start.20) | collective-permute-done | bytes 69664 | tf_op jit(solution)/shard_map/ppermute | solution.py:30
  76.8 1.7 %collective-permute-done.21.refs_3_ = f32[136,128]{1,0:T(8,128)S(1)} collective-permute-done((f32[136,128]{1,0:T(8,128)S(1)}, f32[136,128]{1,0:T(8,128)S(1)}, u32[]{:S(2)}, u32[]{:S(2)}) %collective-permute-start.21) | collective-permute-done | bytes 69664 | tf_op jit(solution)/shard_map/ppermute | solution.py:30
  78.5 0.8 shard_map.87
  79.2 1.9 %collective-permute-done.18.refs_1_ = f32[136,128]{1,0:T(8,128)S(1)} collective-permute-done((f32[136,128]{1,0:T(8,128)S(1)}, f32[136,128]{1,0:T(8,128)S(1)}, u32[]{:S(2)}, u32[]{:S(2)}) %collective-permute-start.18) | collective-permute-done | bytes 69664 | tf_op jit(solution)/shard_map/ppermute | solution.py:34
  81.1 0.8 shard_map.86
  (16 shorter events, 0.2 us)
Async XLA Ops:
  2.3 12.1 %collective-permute-start = (bf16[128,256]{1,0:T(8,128)(2,1)}, bf16[128,256]{1,0:T(8,128)(2,1)S(1)}, u32[]{:S(2)}, u32[]{:S(2)}) collective-permute-start(bf16[128,256]{1,0:T(8,128)(2,1)} %get-tuple-element.44), channel_id=1, source_target_pairs={{0,2},{1,3},{2,0},{3,1},{4,6},{5,7},{6,4},{7,5},{8,10},{9,11},{10,... | collective-permute-start | bytes 196616 | tf_op jit(solution)/shard_map/ppermute | solution.py:34
  4.9 10.5 %collective-permute-start.3 = (bf16[128,256]{1,0:T(8,128)(2,1)}, bf16[128,256]{1,0:T(8,128)(2,1)S(1)}, u32[]{:S(2)}, u32[]{:S(2)}) collective-permute-start(bf16[128,256]{1,0:T(8,128)(2,1)} %get-tuple-element.45), channel_id=1, source_target_pairs={{0,16},{16,32},{32,48},{48,0},{64,80},{80,96},{96,112},{112,64},{1... | collective-permute-start | bytes 196616 | tf_op jit(solution)/shard_map/ppermute | solution.py:30
  7.9 9.4 %collective-permute-start.2 = (bf16[128,256]{1,0:T(8,128)(2,1)}, bf16[128,256]{1,0:T(8,128)(2,1)S(1)}, u32[]{:S(2)}, u32[]{:S(2)}) collective-permute-start(bf16[128,256]{1,0:T(8,128)(2,1)} %get-tuple-element.45), channel_id=1, source_target_pairs={{0,32},{16,48},{32,0},{48,16},{64,96},{80,112},{96,64},{112,80},{1... | collective-permute-start | bytes 196616 | tf_op jit(solution)/shard_map/ppermute | solution.py:30
  12.1 6.2 %collective-permute-start.1 = (bf16[128,256]{1,0:T(8,128)(2,1)}, bf16[128,256]{1,0:T(8,128)(2,1)S(1)}, u32[]{:S(2)}, u32[]{:S(2)}) collective-permute-start(bf16[128,256]{1,0:T(8,128)(2,1)} %get-tuple-element.45), channel_id=1, source_target_pairs={{0,48},{16,0},{32,16},{48,32},{64,112},{80,64},{96,80},{112,96},{1... | collective-permute-start | bytes 196616 | tf_op jit(solution)/shard_map/ppermute | solution.py:30
  14.5 3.8 %copy-start = (bf16[128,256]{1,0:T(8,128)(2,1)S(1)}, bf16[128,256]{1,0:T(8,128)(2,1)}, u32[]{:S(2)}) copy-start(bf16[128,256]{1,0:T(8,128)(2,1)} %get-tuple-element.45) | copy-start | bytes 196612
  18.3 11.1 %collective-permute-start.8 = (bf16[4,128,256]{2,1,0:T(8,128)(2,1)S(1)}, bf16[4,128,256]{2,1,0:T(8,128)(2,1)S(1)}, u32[]{:S(2)}, u32[]{:S(2)}) collective-permute-start(bf16[4,128,256]{2,1,0:T(8,128)(2,1)S(1)} %pad_maximum_fusion.1.refs_4_), channel_id=1, source_target_pairs={{0,64},{16,80},{32,96},{48,112},{64,128},{80,144},{96,160},{112,17... | collective-permute-start | bytes 786440 | tf_op jit(solution)/shard_map/ppermute | solution.py:25
  19.7 9.7 %collective-permute-start.7 = (bf16[4,128,256]{2,1,0:T(8,128)(2,1)S(1)}, bf16[4,128,256]{2,1,0:T(8,128)(2,1)S(1)}, u32[]{:S(2)}, u32[]{:S(2)}) collective-permute-start(bf16[4,128,256]{2,1,0:T(8,128)(2,1)S(1)} %pad_maximum_fusion.1.refs_4_), channel_id=1, source_target_pairs={{0,192},{16,208},{32,224},{48,240},{64,0},{80,16},{96,32},{112,48}... | collective-permute-start | bytes 786440 | tf_op jit(solution)/shard_map/ppermute | solution.py:25
  21.2 5.3 %collective-permute-start.6 = (bf16[2,128,256]{2,1,0:T(8,128)(2,1)S(1)}, bf16[2,128,256]{2,1,0:T(8,128)(2,1)S(1)}, u32[]{:S(2)}, u32[]{:S(2)}) collective-permute-start(bf16[2,128,256]{2,1,0:T(8,128)(2,1)S(1)} %pad_maximum_fusion.2), channel_id=1, source_target_pairs={{0,4},{1,5},{2,6},{3,7},{4,8},{5,9},{6,10},{7,11},{8,12},{9,13},{1... | collective-permute-start | bytes 393224 | tf_op jit(solution)/shard_map/ppermute | solution.py:25
  22.5 6.3 %collective-permute-start.5 = (bf16[2,128,256]{2,1,0:T(8,128)(2,1)S(1)}, bf16[2,128,256]{2,1,0:T(8,128)(2,1)S(1)}, u32[]{:S(2)}, u32[]{:S(2)}) collective-permute-start(bf16[2,128,256]{2,1,0:T(8,128)(2,1)S(1)} %pad_maximum_fusion.2), channel_id=1, source_target_pairs={{0,8},{1,9},{2,10},{3,11},{4,12},{5,13},{6,14},{7,15},{8,0},{9,1},... | collective-permute-start | bytes 393224 | tf_op jit(solution)/shard_map/ppermute | solution.py:25
  24.9 4.4 %collective-permute-start.4 = (bf16[2,128,256]{2,1,0:T(8,128)(2,1)S(1)}, bf16[2,128,256]{2,1,0:T(8,128)(2,1)S(1)}, u32[]{:S(2)}, u32[]{:S(2)}) collective-permute-start(bf16[2,128,256]{2,1,0:T(8,128)(2,1)S(1)} %pad_maximum_fusion.2), channel_id=1, source_target_pairs={{0,12},{1,13},{2,14},{3,15},{4,0},{5,1},{6,2},{7,3},{8,4},{9,5},{1... | collective-permute-start | bytes 393224 | tf_op jit(solution)/shard_map/ppermute | solution.py:25
  29.4 5.2 %collective-permute-start.9 = (bf16[2,4,128,256]{3,2,1,0:T(8,128)(2,1)S(1)}, bf16[2,4,128,256]{3,2,1,0:T(8,128)(2,1)S(1)}, u32[]{:S(2)}, u32[]{:S(2)}) collective-permute-start(bf16[2,4,128,256]{3,2,1,0:T(8,128)(2,1)S(1)} %pad_maximum_fusion), channel_id=1, source_target_pairs={{0,1},{1,0},{2,3},{3,2},{4,5},{5,4},{6,7},{7,6},{8,9},{9,8},{10,11... | collective-permute-start | bytes 1572872 | tf_op jit(solution)/shard_map/ppermute | solution.py:34
  32.8 9.1 %collective-permute-start.10 = (bf16[4,128,256]{2,1,0:T(8,128)(2,1)S(1)}, bf16[4,128,256]{2,1,0:T(8,128)(2,1)S(1)}, u32[]{:S(2)}, u32[]{:S(2)}) collective-permute-start(bf16[4,128,256]{2,1,0:T(8,128)(2,1)S(1)} %pad_maximum_fusion.1.refs_4_), channel_id=1, source_target_pairs={{0,128},{16,144},{32,160},{48,176},{64,192},{80,208},{96,224},{112... | collective-permute-start | bytes 786440 | tf_op jit(solution)/shard_map/ppermute | solution.py:25
  46.8 10.1 %collective-permute-start.12 = (f32[136,512]{1,0:T(8,128)S(1)}, f32[136,512]{1,0:T(8,128)S(1)}, u32[]{:S(2)}, u32[]{:S(2)}) collective-permute-start(f32[136,512]{1,0:T(8,128)S(1)} %shard_map.77), channel_id=1, source_target_pairs={{0,64},{16,80},{32,96},{48,112},{64,128},{80,144},{96,160},{112,17... | collective-permute-start | bytes 835592 | tf_op jit(solution)/shard_map/ppermute | solution.py:25
  47.0 14.2 %collective-permute-start.13 = (f32[136,512]{1,0:T(8,128)S(1)}, f32[136,512]{1,0:T(8,128)S(1)}, u32[]{:S(2)}, u32[]{:S(2)}) collective-permute-start(f32[136,512]{1,0:T(8,128)S(1)} %shard_map.78), channel_id=1, source_target_pairs={{0,128},{16,144},{32,160},{48,176},{64,192},{80,208},{96,224},{112... | collective-permute-start | bytes 835592 | tf_op jit(solution)/shard_map/ppermute | solution.py:25
  49.6 12.6 %collective-permute-start.14 = (f32[136,512]{1,0:T(8,128)S(1)}, f32[136,512]{1,0:T(8,128)S(1)}, u32[]{:S(2)}, u32[]{:S(2)}) collective-permute-start(f32[136,512]{1,0:T(8,128)S(1)} %shard_map.79), channel_id=1, source_target_pairs={{0,192},{16,208},{32,224},{48,240},{64,0},{80,16},{96,32},{112,48}... | collective-permute-start | bytes 835592 | tf_op jit(solution)/shard_map/ppermute | solution.py:25
  54.6 9.3 %collective-permute-start.11 = (f32[2,136,512]{2,1,0:T(8,128)S(1)}, f32[2,136,512]{2,1,0:T(8,128)S(1)}, u32[]{:S(2)}, u32[]{:S(2)}) collective-permute-start(f32[2,136,512]{2,1,0:T(8,128)S(1)} %get-tuple-element.56), channel_id=1, source_target_pairs={{0,1},{1,0},{2,3},{3,2},{4,5},{5,4},{6,7},{7,6},{8,9},{9,8},{10,11... | collective-permute-start | bytes 1671176 | tf_op jit(solution)/shard_map/ppermute | solution.py:34
  64.0 8.9 %collective-permute-start.16 = (f32[136,256]{1,0:T(8,128)S(1)}, f32[136,256]{1,0:T(8,128)S(1)}, u32[]{:S(2)}, u32[]{:S(2)}) collective-permute-start(f32[136,256]{1,0:T(8,128)S(1)} %get-tuple-element.72), channel_id=1, source_target_pairs={{0,8},{1,9},{2,10},{3,11},{4,12},{5,13},{6,14},{7,15},{8,0},{9,1},... | collective-permute-start | bytes 417800 | tf_op jit(solution)/shard_map/ppermute | solution.py:25
  66.1 9.1 %collective-permute-start.17 = (f32[136,256]{1,0:T(8,128)S(1)}, f32[136,256]{1,0:T(8,128)S(1)}, u32[]{:S(2)}, u32[]{:S(2)}) collective-permute-start(f32[136,256]{1,0:T(8,128)S(1)} %get-tuple-element.73), channel_id=1, source_target_pairs={{0,12},{1,13},{2,14},{3,15},{4,0},{5,1},{6,2},{7,3},{8,4},{9,5},{1... | collective-permute-start | bytes 417800 | tf_op jit(solution)/shard_map/ppermute | solution.py:25
  67.5 7.7 %collective-permute-start.15 = (f32[136,256]{1,0:T(8,128)S(1)}, f32[136,256]{1,0:T(8,128)S(1)}, u32[]{:S(2)}, u32[]{:S(2)}) collective-permute-start(f32[136,256]{1,0:T(8,128)S(1)} %get-tuple-element.71), channel_id=1, source_target_pairs={{0,4},{1,5},{2,6},{3,7},{4,8},{5,9},{6,10},{7,11},{8,12},{9,13},{1... | collective-permute-start | bytes 417800 | tf_op jit(solution)/shard_map/ppermute | solution.py:25
  67.7 8.2 %collective-permute-start.19 = (f32[136,128]{1,0:T(8,128)S(1)}, f32[136,128]{1,0:T(8,128)S(1)}, u32[]{:S(2)}, u32[]{:S(2)}) collective-permute-start(f32[136,128]{1,0:T(8,128)S(1)} %get-tuple-element.79), channel_id=1, source_target_pairs={{0,16},{16,32},{32,48},{48,0},{64,80},{80,96},{96,112},{112,64},{1... | collective-permute-start | bytes 208904 | tf_op jit(solution)/shard_map/ppermute | solution.py:30
  69.5 7.3 %collective-permute-start.20 = (f32[136,128]{1,0:T(8,128)S(1)}, f32[136,128]{1,0:T(8,128)S(1)}, u32[]{:S(2)}, u32[]{:S(2)}) collective-permute-start(f32[136,128]{1,0:T(8,128)S(1)} %get-tuple-element.80), channel_id=1, source_target_pairs={{0,32},{16,48},{32,0},{48,16},{64,96},{80,112},{96,64},{112,80},{1... | collective-permute-start | bytes 208904 | tf_op jit(solution)/shard_map/ppermute | solution.py:30
  72.8 5.6 %collective-permute-start.21 = (f32[136,128]{1,0:T(8,128)S(1)}, f32[136,128]{1,0:T(8,128)S(1)}, u32[]{:S(2)}, u32[]{:S(2)}) collective-permute-start(f32[136,128]{1,0:T(8,128)S(1)} %get-tuple-element.81), channel_id=1, source_target_pairs={{0,48},{16,0},{32,16},{48,32},{64,112},{80,64},{96,80},{112,96},{1... | collective-permute-start | bytes 208904 | tf_op jit(solution)/shard_map/ppermute | solution.py:30
  75.3 5.8 %collective-permute-start.18 = (f32[136,128]{1,0:T(8,128)S(1)}, f32[136,128]{1,0:T(8,128)S(1)}, u32[]{:S(2)}, u32[]{:S(2)}) collective-permute-start(f32[136,128]{1,0:T(8,128)S(1)} %get-tuple-element.75), channel_id=1, source_target_pairs={{0,2},{1,3},{2,0},{3,1},{4,6},{5,7},{6,4},{7,5},{8,10},{9,11},{10,... | collective-permute-start | bytes 208904 | tf_op jit(solution)/shard_map/ppermute | solution.py:34

commit v7 on v6

--- a/solution.py
+++ b/solution.py
@@ -263,9 +263,8 @@
     one = [own_one, fast_swap("col", own_one, 2)]
     one, two = together((jnp.stack(one), jnp.stack(two)))
     one = [one] + [slow_shift("col", one, -step) for step in range(1, SUB)]
-    near, far = slow_shift("row", two, -1), slow_shift("row", two, 1)
-    one, near, far = together((jnp.stack(one, axis=1), near, far))
-    twos = [two, near, slow_shift("row", two, -2), far]
+    twos = [two] + [slow_shift("row", two, -step) for step in range(1, SUB)]
+    one, twos = together((jnp.stack(one, axis=1), twos))
     other = fast_swap("col", one, 1)
     ones = [one[0], one[1], other[0], other[1]]
 
@@ -295,11 +294,9 @@
 
     work = BLOCK * BLOCK * SUB
     cols = [None] * SUB
-    for step in (0, 1, 3, 2):
-        if step == 2:
-            twos[2], _ = together((twos[2], cols[0]))
+    for step in (1, 3, 2, 0):
         (cols[step],) = call(col_scores, [f32(ROWS, BLOCK)], (*ones, twos[step]), work=work)
-    ones, cols = together((ones, cols))
+    ones, _ = together((ones, cols))
     cols = spread("row", cols)
     send_one, far_one = row_scores(ones, ((1, 0), (1, 1), (0, 1)), 3, 2, 1)
     theirs_one = fast_swap("col", send_one, 1)

time: 83.1 us -> 79.3 us (0.954)
  the two profiles are of different devices: /device:TPU:1 before, /device:TPU:8 now
where the time goes in v7:
time: 79.3 us; the launch traced here: 79.1 us
  starting transfers between devices  41.3 us (52%)
  waiting for transfers between devices  20.4 us (26%)
  Pallas kernels  15.5 us (20%)
  other arithmetic  0.99 us (1%)
  between operations  0.81 us (1%)
    ppermute x12, starting transfers between devices, slow_shift(): return lax.ppermute(value, axis, pairs)  20.3 us
    ppermute x6, starting transfers between devices, fast_shift(): return lax.ppermute(value, axis, pairs)  18.9 us
    pallas_call x13, Pallas kernels, call(): pl.pallas_call(kernel, out_shape=shapes, in_specs=specs or [VMEM] * len(a...  15.5 us
    ppermute x12, waiting for transfers between devices, slow_shift(): return lax.ppermute(value, axis, pairs)  12 us
    ppermute x6, waiting for transfers between devices, fast_shift(): return lax.ppermute(value, axis, pairs)  6.19 us
    ppermute x4, starting transfers between devices, fast_swap(): return lax.ppermute(value, axis, [(i, i ^ step) for i in range(SUB * SUB)])  2.19 us
    ppermute x4, waiting for transfers between devices, fast_swap(): return lax.ppermute(value, axis, [(i, i ^ step) for i in range(SUB * SUB)])  2.15 us
  transfers between devices with their start and end apart: 22, of which 11 were waited for; matrix products, arithmetic and copies ran while one was open for 1% of the time, Pallas kernels for 10%

profile of v7, /device:TPU:8, one launch (start us, length us, event | category | flops | bytes accessed | tf_op | source)
XLA Modules:
  0.0 79.1 jit_solution(826920002485059908)
XLA Ops:
  0.6 1.7 %shard_map.75 = (bf16[128,256]{1,0:T(8,128)(2,1)}, bf16[128,256]{1,0:T(8,128)(2,1)}) custom-call(bf16[128,128]{1,0:T(8,128)(2,1)} %feat_one.1, bf16[128,128]{1,0:T(8,128)(2,1)} %value_one.1, bf16[128,128]{1,0:T(8,128)(2,1)} %feat_two.1, bf16[128,128]{1,0:T(8,128)(2,1)} %value_two.1), custom_call_target="tpu_custom_call" | custom-call | bytes 262144 | tf_op jit(solution)/shard_map/pallas_call | solution.py:221
  2.3 2.0 %collective-permute-start = (bf16[128,256]{1,0:T(8,128)(2,1)}, bf16[128,256]{1,0:T(8,128)(2,1)S(1)}, u32[]{:S(2)}, u32[]{:S(2)}) collective-permute-start(bf16[128,256]{1,0:T(8,128)(2,1)} %get-tuple-element.41), channel_id=1, source_target_pairs={{0,2},{1,3},{2,0},{3,1},{4,6},{5,7},{6,4},{7,5},{8,10},{9,11},{10,... | collective-permute-start | bytes 196616 | tf_op jit(solution)/shard_map/ppermute | solution.py:34
  4.3 3.3 %collective-permute-start.3 = (bf16[128,256]{1,0:T(8,128)(2,1)}, bf16[128,256]{1,0:T(8,128)(2,1)S(1)}, u32[]{:S(2)}, u32[]{:S(2)}) collective-permute-start(bf16[128,256]{1,0:T(8,128)(2,1)} %get-tuple-element.42), channel_id=1, source_target_pairs={{0,16},{16,32},{32,48},{48,0},{64,80},{80,96},{96,112},{112,64},{1... | collective-permute-start | bytes 196616 | tf_op jit(solution)/shard_map/ppermute | solution.py:30
  7.6 4.5 %collective-permute-start.2 = (bf16[128,256]{1,0:T(8,128)(2,1)}, bf16[128,256]{1,0:T(8,128)(2,1)S(1)}, u32[]{:S(2)}, u32[]{:S(2)}) collective-permute-start(bf16[128,256]{1,0:T(8,128)(2,1)} %get-tuple-element.42), channel_id=1, source_target_pairs={{0,32},{16,48},{32,0},{48,16},{64,96},{80,112},{96,64},{112,80},{1... | collective-permute-start | bytes 196616 | tf_op jit(solution)/shard_map/ppermute | solution.py:30
  12.1 2.7 %collective-permute-start.1 = (bf16[128,256]{1,0:T(8,128)(2,1)}, bf16[128,256]{1,0:T(8,128)(2,1)S(1)}, u32[]{:S(2)}, u32[]{:S(2)}) collective-permute-start(bf16[128,256]{1,0:T(8,128)(2,1)} %get-tuple-element.42), channel_id=1, source_target_pairs={{0,48},{16,0},{32,16},{48,32},{64,112},{80,64},{96,80},{112,96},{1... | collective-permute-start | bytes 196616 | tf_op jit(solution)/shard_map/ppermute | solution.py:30
  14.8 0.0 collective-permute-done
  14.8 0.9 %pad_maximum_fusion.2 = bf16[2,128,256]{2,1,0:T(8,128)(2,1)S(1)} fusion(bf16[1,128,256]{2,1,0:T(8,128)(2,1)S(1)} %bitcast.29, bf16[1,128,256]{2,1,0:T(8,128)(2,1)} %bitcast.28), kind=kLoop, calls=%fused_computation.6 | loop fusion | flops 65536 | bytes 262144 | tf_op jit(solution)/shard_map/stack | solution.py:264
  15.7 2.4 %collective-permute-done.2 = bf16[128,256]{1,0:T(8,128)(2,1)S(1)} collective-permute-done((bf16[128,256]{1,0:T(8,128)(2,1)}, bf16[128,256]{1,0:T(8,128)(2,1)S(1)}, u32[]{:S(2)}, u32[]{:S(2)}) %collective-permute-start.2) | collective-permute-done | bytes 65568 | tf_op jit(solution)/shard_map/ppermute | solution.py:30
  18.0 0.6 collective-permute-done.1
  18.6 1.6 %collective-permute-start.6 = (bf16[2,128,256]{2,1,0:T(8,128)(2,1)S(1)}, bf16[2,128,256]{2,1,0:T(8,128)(2,1)S(1)}, u32[]{:S(2)}, u32[]{:S(2)}) collective-permute-start(bf16[2,128,256]{2,1,0:T(8,128)(2,1)S(1)} %pad_maximum_fusion.2), channel_id=1, source_target_pairs={{0,4},{1,5},{2,6},{3,7},{4,8},{5,9},{6,10},{7,11},{8,12},{9,13},{1... | collective-permute-start | bytes 393224 | tf_op jit(solution)/shard_map/ppermute | solution.py:25
  20.2 1.6 %collective-permute-start.9 = (bf16[4,128,256]{2,1,0:T(8,128)(2,1)S(1)}, bf16[4,128,256]{2,1,0:T(8,128)(2,1)S(1)}, u32[]{:S(2)}, u32[]{:S(2)}) collective-permute-start(bf16[4,128,256]{2,1,0:T(8,128)(2,1)S(1)} %pad_maximum_fusion.1.refs_4_), channel_id=1, source_target_pairs={{0,64},{16,80},{32,96},{48,112},{64,128},{80,144},{96,160},{112,17... | collective-permute-start | bytes 786440 | tf_op jit(solution)/shard_map/ppermute | solution.py:25
  21.8 0.9 %collective-permute-start.8 = (bf16[4,128,256]{2,1,0:T(8,128)(2,1)S(1)}, bf16[4,128,256]{2,1,0:T(8,128)(2,1)S(1)}, u32[]{:S(2)}, u32[]{:S(2)}) collective-permute-start(bf16[4,128,256]{2,1,0:T(8,128)(2,1)S(1)} %pad_maximum_fusion.1.refs_4_), channel_id=1, source_target_pairs={{0,128},{16,144},{32,160},{48,176},{64,192},{80,208},{96,224},{112... | collective-permute-start | bytes 786440 | tf_op jit(solution)/shard_map/ppermute | solution.py:25
  22.7 2.4 %collective-permute-start.7 = (bf16[4,128,256]{2,1,0:T(8,128)(2,1)S(1)}, bf16[4,128,256]{2,1,0:T(8,128)(2,1)S(1)}, u32[]{:S(2)}, u32[]{:S(2)}) collective-permute-start(bf16[4,128,256]{2,1,0:T(8,128)(2,1)S(1)} %pad_maximum_fusion.1.refs_4_), channel_id=1, source_target_pairs={{0,192},{16,208},{32,224},{48,240},{64,0},{80,16},{96,32},{112,48}... | collective-permute-start | bytes 786440 | tf_op jit(solution)/shard_map/ppermute | solution.py:25
  25.1 2.7 %collective-permute-start.5 = (bf16[2,128,256]{2,1,0:T(8,128)(2,1)S(1)}, bf16[2,128,256]{2,1,0:T(8,128)(2,1)S(1)}, u32[]{:S(2)}, u32[]{:S(2)}) collective-permute-start(bf16[2,128,256]{2,1,0:T(8,128)(2,1)S(1)} %pad_maximum_fusion.2), channel_id=1, source_target_pairs={{0,8},{1,9},{2,10},{3,11},{4,12},{5,13},{6,14},{7,15},{8,0},{9,1},... | collective-permute-start | bytes 393224 | tf_op jit(solution)/shard_map/ppermute | solution.py:25
  27.9 1.4 %collective-permute-start.4 = (bf16[2,128,256]{2,1,0:T(8,128)(2,1)S(1)}, bf16[2,128,256]{2,1,0:T(8,128)(2,1)S(1)}, u32[]{:S(2)}, u32[]{:S(2)}) collective-permute-start(bf16[2,128,256]{2,1,0:T(8,128)(2,1)S(1)} %pad_maximum_fusion.2), channel_id=1, source_target_pairs={{0,12},{1,13},{2,14},{3,15},{4,0},{5,1},{6,2},{7,3},{8,4},{9,5},{1... | collective-permute-start | bytes 393224 | tf_op jit(solution)/shard_map/ppermute | solution.py:25
  29.3 2.3 %collective-permute-done.5 = bf16[2,128,256]{2,1,0:T(8,128)(2,1)S(1)} collective-permute-done((bf16[2,128,256]{2,1,0:T(8,128)(2,1)S(1)}, bf16[2,128,256]{2,1,0:T(8,128)(2,1)S(1)}, u32[]{:S(2)}, u32[]{:S(2)}) %collective-permute-start.5) | collective-permute-done | bytes 131104 | tf_op jit(solution)/shard_map/ppermute | solution.py:25
  31.6 1.2 %collective-permute-done.4 = bf16[2,128,256]{2,1,0:T(8,128)(2,1)S(1)} collective-permute-done((bf16[2,128,256]{2,1,0:T(8,128)(2,1)S(1)}, bf16[2,128,256]{2,1,0:T(8,128)(2,1)S(1)}, u32[]{:S(2)}, u32[]{:S(2)}) %collective-permute-start.4) | collective-permute-done | bytes 131104 | tf_op jit(solution)/shard_map/ppermute | solution.py:25
  32.8 0.1 pad_maximum_fusion
  32.9 0.0 collective-permute-done.8.refs_4_.refs_6_
  32.9 1.5 %collective-permute-done.7.refs_4_.refs_5_ = bf16[4,128,256]{2,1,0:T(8,128)(2,1)S(1)} collective-permute-done((bf16[4,128,256]{2,1,0:T(8,128)(2,1)S(1)}, bf16[4,128,256]{2,1,0:T(8,128)(2,1)S(1)}, u32[]{:S(2)}, u32[]{:S(2)}) %collective-permute-start.7) | collective-permute-done | bytes 262176 | tf_op jit(solution)/shard_map/ppermute | solution.py:25
  34.5 1.9 %collective-permute-done.10 = bf16[2,4,128,256]{3,2,1,0:T(8,128)(2,1)S(1)} collective-permute-done((bf16[2,4,128,256]{3,2,1,0:T(8,128)(2,1)S(1)}, bf16[2,4,128,256]{3,2,1,0:T(8,128)(2,1)S(1)}, u32[]{:S(2)}, u32[]{:S(2)}) %collective-permute-start.10) | collective-permute-done | bytes 524320 | tf_op jit(solution)/shard_map/ppermute | solution.py:34
  36.4 1.6 %shard_map.79 = f32[136,512]{1,0:T(8,128)S(1)} custom-call(bf16[4,128,256]{2,1,0:T(8,128)(2,1)S(1)} %get-tuple-element.60.refs_0_, bf16[4,128,256]{2,1,0:T(8,128)(2,1)S(1)} %get-tuple-element.61.refs_1_, bf16[4,128,256]{2,1,0:T(8,128)(2,1)S(1)} %get-tuple-element.62.refs_2_, bf16[4,128,256]{2,1,0:T(8,128)(2,1)S(1)} %get-tuple-element.63.refs_3_, ...), custom_call_target="tpu_custom_call" | custom-call | flops 536870912 | bytes 1589248 | tf_op jit(solution)/shard_map/pallas_call | solution.py:221
  38.0 1.6 %shard_map.78 = f32[136,512]{1,0:T(8,128)S(1)} custom-call(bf16[4,128,256]{2,1,0:T(8,128)(2,1)S(1)} %get-tuple-element.60.refs_0_, bf16[4,128,256]{2,1,0:T(8,128)(2,1)S(1)} %get-tuple-element.61.refs_1_, bf16[4,128,256]{2,1,0:T(8,128)(2,1)S(1)} %get-tuple-element.62.refs_2_, bf16[4,128,256]{2,1,0:T(8,128)(2,1)S(1)} %get-tuple-element.63.refs_3_, ...), custom_call_target="tpu_custom_call" | custom-call | flops 536870912 | bytes 1589248 | tf_op jit(solution)/shard_map/pallas_call | solution.py:221
  39.7 1.6 %shard_map.77 = f32[136,512]{1,0:T(8,128)S(1)} custom-call(bf16[4,128,256]{2,1,0:T(8,128)(2,1)S(1)} %get-tuple-element.60.refs_0_, bf16[4,128,256]{2,1,0:T(8,128)(2,1)S(1)} %get-tuple-element.61.refs_1_, bf16[4,128,256]{2,1,0:T(8,128)(2,1)S(1)} %get-tuple-element.62.refs_2_, bf16[4,128,256]{2,1,0:T(8,128)(2,1)S(1)} %get-tuple-element.63.refs_3_, ...), custom_call_target="tpu_custom_call" | custom-call | flops 536870912 | bytes 1589248 | tf_op jit(solution)/shard_map/pallas_call | solution.py:221
  41.3 1.6 %collective-permute-start.12 = (f32[136,512]{1,0:T(8,128)S(1)}, f32[136,512]{1,0:T(8,128)S(1)}, u32[]{:S(2)}, u32[]{:S(2)}) collective-permute-start(f32[136,512]{1,0:T(8,128)S(1)} %shard_map.77), channel_id=1, source_target_pairs={{0,64},{16,80},{32,96},{48,112},{64,128},{80,144},{96,160},{112,17... | collective-permute-start | bytes 835592 | tf_op jit(solution)/shard_map/ppermute | solution.py:25
  42.9 1.6 %collective-permute-start.13 = (f32[136,512]{1,0:T(8,128)S(1)}, f32[136,512]{1,0:T(8,128)S(1)}, u32[]{:S(2)}, u32[]{:S(2)}) collective-permute-start(f32[136,512]{1,0:T(8,128)S(1)} %shard_map.78), channel_id=1, source_target_pairs={{0,128},{16,144},{32,160},{48,176},{64,192},{80,208},{96,224},{112... | collective-permute-start | bytes 835592 | tf_op jit(solution)/shard_map/ppermute | solution.py:25
  44.5 1.5 %collective-permute-start.14 = (f32[136,512]{1,0:T(8,128)S(1)}, f32[136,512]{1,0:T(8,128)S(1)}, u32[]{:S(2)}, u32[]{:S(2)}) collective-permute-start(f32[136,512]{1,0:T(8,128)S(1)} %shard_map.79), channel_id=1, source_target_pairs={{0,192},{16,208},{32,224},{48,240},{64,0},{80,16},{96,32},{112,48}... | collective-permute-start | bytes 835592 | tf_op jit(solution)/shard_map/ppermute | solution.py:25
  45.9 1.6 %shard_map.76.refs_0_ = f32[136,512]{1,0:T(8,128)S(1)} custom-call(bf16[4,128,256]{2,1,0:T(8,128)(2,1)S(1)} %get-tuple-element.60.refs_0_, bf16[4,128,256]{2,1,0:T(8,128)(2,1)S(1)} %get-tuple-element.61.refs_1_, bf16[4,128,256]{2,1,0:T(8,128)(2,1)S(1)} %get-tuple-element.62.refs_2_, bf16[4,128,256]{2,1,0:T(8,128)(2,1)S(1)} %get-tuple-element.63.refs_3_, ...), custom_call_target="tpu_custom_call" | custom-call | flops 536870912 | bytes 1589248 | tf_op jit(solution)/shard_map/pallas_call | solution.py:221
  47.6 4.0 %shard_map.80 = (f32[2,136,512]{2,1,0:T(8,128)S(1)}, f32[1,136,512]{2,1,0:T(8,128)S(1)}) custom-call(bf16[4,128,256]{2,1,0:T(8,128)(2,1)S(1)} %get-tuple-element.60.refs_0_, bf16[4,128,256]{2,1,0:T(8,128)(2,1)S(1)} %get-tuple-element.61.refs_1_, bf16[4,128,256]{2,1,0:T(8,128)(2,1)S(1)} %get-tuple-element.62.refs_2_, ...), custom_call_target="tpu_custom_call" | custom-call | flops 1610612736 | bytes 2932736 | tf_op jit(solution)/shard_map/pallas_call | solution.py:221
  51.6 0.1 collective-permute-start.11
  51.7 2.3 %collective-permute-done.13.refs_2_ = f32[136,512]{1,0:T(8,128)S(1)} collective-permute-done((f32[136,512]{1,0:T(8,128)S(1)}, f32[136,512]{1,0:T(8,128)S(1)}, u32[]{:S(2)}, u32[]{:S(2)}) %collective-permute-start.13) | collective-permute-done | bytes 278560 | tf_op jit(solution)/shard_map/ppermute | solution.py:25
  54.0 4.6 %collective-permute-done.14.refs_3_ = f32[136,512]{1,0:T(8,128)S(1)} collective-permute-done((f32[136,512]{1,0:T(8,128)S(1)}, f32[136,512]{1,0:T(8,128)S(1)}, u32[]{:S(2)}, u32[]{:S(2)}) %collective-permute-start.14) | collective-permute-done | bytes 278560 | tf_op jit(solution)/shard_map/ppermute | solution.py:25
  58.6 0.1 shard_map.81
  58.7 1.6 %shard_map.82.refs_1_ = f32[1,136,512]{2,1,0:T(8,128)S(1)} custom-call(bf16[4,128,256]{2,1,0:T(8,128)(2,1)S(1)} %get-tuple-element.60.refs_0_, bf16[4,128,256]{2,1,0:T(8,128)(2,1)S(1)} %get-tuple-element.61.refs_1_, bf16[4,128,256]{2,1,0:T(8,128)(2,1)S(1)} %get-tuple-element.62.refs_2_, bf16[4,128,256]{2,1,0:T(8,128)(2,1)S(1)} %get-tuple-element.63.refs_3_, ...), custom_call_target="tpu_custom_call" | custom-call | flops 21474836480 | bytes 2375680 | tf_op jit(solution)/shard_map/pallas_call | solution.py:221
  60.3 0.0 collective-permute-done.11.refs_0_
  60.4 2.8 %collective-permute-start.16 = (f32[136,256]{1,0:T(8,128)S(1)}, f32[136,256]{1,0:T(8,128)S(1)}, u32[]{:S(2)}, u32[]{:S(2)}) collective-permute-start(f32[136,256]{1,0:T(8,128)S(1)} %get-tuple-element.66), channel_id=1, source_target_pairs={{0,8},{1,9},{2,10},{3,11},{4,12},{5,13},{6,14},{7,15},{8,0},{9,1},... | collective-permute-start | bytes 417800 | tf_op jit(solution)/shard_map/ppermute | solution.py:25
  63.2 1.4 %collective-permute-start.17 = (f32[136,256]{1,0:T(8,128)S(1)}, f32[136,256]{1,0:T(8,128)S(1)}, u32[]{:S(2)}, u32[]{:S(2)}) collective-permute-start(f32[136,256]{1,0:T(8,128)S(1)} %get-tuple-element.67), channel_id=1, source_target_pairs={{0,12},{1,13},{2,14},{3,15},{4,0},{5,1},{6,2},{7,3},{8,4},{9,5},{1... | collective-permute-start | bytes 417800 | tf_op jit(solution)/shard_map/ppermute | solution.py:25
  64.7 0.7 collective-permute-start.15
  65.4 0.8 %collective-permute-start.19 = (f32[136,128]{1,0:T(8,128)S(1)}, f32[136,128]{1,0:T(8,128)S(1)}, u32[]{:S(2)}, u32[]{:S(2)}) collective-permute-start(f32[136,128]{1,0:T(8,128)S(1)} %get-tuple-element.73), channel_id=1, source_target_pairs={{0,16},{16,32},{32,48},{48,0},{64,80},{80,96},{96,112},{112,64},{1... | collective-permute-start | bytes 208904 | tf_op jit(solution)/shard_map/ppermute | solution.py:30
  66.2 4.8 %collective-permute-start.20 = (f32[136,128]{1,0:T(8,128)S(1)}, f32[136,128]{1,0:T(8,128)S(1)}, u32[]{:S(2)}, u32[]{:S(2)}) collective-permute-start(f32[136,128]{1,0:T(8,128)S(1)} %get-tuple-element.74), channel_id=1, source_target_pairs={{0,32},{16,48},{32,0},{48,16},{64,96},{80,112},{96,64},{112,80},{1... | collective-permute-start | bytes 208904 | tf_op jit(solution)/shard_map/ppermute | solution.py:30
  71.0 2.9 %collective-permute-start.21 = (f32[136,128]{1,0:T(8,128)S(1)}, f32[136,128]{1,0:T(8,128)S(1)}, u32[]{:S(2)}, u32[]{:S(2)}) collective-permute-start(f32[136,128]{1,0:T(8,128)S(1)} %get-tuple-element.75), channel_id=1, source_target_pairs={{0,48},{16,0},{32,16},{48,32},{64,112},{80,64},{96,80},{112,96},{1... | collective-permute-start | bytes 208904 | tf_op jit(solution)/shard_map/ppermute | solution.py:30
  73.8 0.1 shard_map.85
  73.9 0.1 collective-permute-start.18
  74.0 2.1 %collective-permute-done.20.refs_2_ = f32[136,128]{1,0:T(8,128)S(1)} collective-permute-done((f32[136,128]{1,0:T(8,128)S(1)}, f32[136,128]{1,0:T(8,128)S(1)}, u32[]{:S(2)}, u32[]{:S(2)}) %collective-permute-start.20) | collective-permute-done | bytes 69664 | tf_op jit(solution)/shard_map/ppermute | solution.py:30
  76.2 1.1 %collective-permute-done.21.refs_3_ = f32[136,128]{1,0:T(8,128)S(1)} collective-permute-done((f32[136,128]{1,0:T(8,128)S(1)}, f32[136,128]{1,0:T(8,128)S(1)}, u32[]{:S(2)}, u32[]{:S(2)}) %collective-permute-start.21) | collective-permute-done | bytes 69664 | tf_op jit(solution)/shard_map/ppermute | solution.py:30
  77.3 0.8 shard_map.87
  78.0 0.3 collective-permute-done.18.refs_1_
  78.3 0.8 shard_map.86
  (16 shorter events, 0.2 us)
Async XLA Ops:
  2.3 12.4 %collective-permute-start = (bf16[128,256]{1,0:T(8,128)(2,1)}, bf16[128,256]{1,0:T(8,128)(2,1)S(1)}, u32[]{:S(2)}, u32[]{:S(2)}) collective-permute-start(bf16[128,256]{1,0:T(8,128)(2,1)} %get-tuple-element.41), channel_id=1, source_target_pairs={{0,2},{1,3},{2,0},{3,1},{4,6},{5,7},{6,4},{7,5},{8,10},{9,11},{10,... | collective-permute-start | bytes 196616 | tf_op jit(solution)/shard_map/ppermute | solution.py:34
  4.3 11.3 %collective-permute-start.3 = (bf16[128,256]{1,0:T(8,128)(2,1)}, bf16[128,256]{1,0:T(8,128)(2,1)S(1)}, u32[]{:S(2)}, u32[]{:S(2)}) collective-permute-start(bf16[128,256]{1,0:T(8,128)(2,1)} %get-tuple-element.42), channel_id=1, source_target_pairs={{0,16},{16,32},{32,48},{48,0},{64,80},{80,96},{96,112},{112,64},{1... | collective-permute-start | bytes 196616 | tf_op jit(solution)/shard_map/ppermute | solution.py:30
  7.6 10.4 %collective-permute-start.2 = (bf16[128,256]{1,0:T(8,128)(2,1)}, bf16[128,256]{1,0:T(8,128)(2,1)S(1)}, u32[]{:S(2)}, u32[]{:S(2)}) collective-permute-start(bf16[128,256]{1,0:T(8,128)(2,1)} %get-tuple-element.42), channel_id=1, source_target_pairs={{0,32},{16,48},{32,0},{48,16},{64,96},{80,112},{96,64},{112,80},{1... | collective-permute-start | bytes 196616 | tf_op jit(solution)/shard_map/ppermute | solution.py:30
  12.1 6.5 %collective-permute-start.1 = (bf16[128,256]{1,0:T(8,128)(2,1)}, bf16[128,256]{1,0:T(8,128)(2,1)S(1)}, u32[]{:S(2)}, u32[]{:S(2)}) collective-permute-start(bf16[128,256]{1,0:T(8,128)(2,1)} %get-tuple-element.42), channel_id=1, source_target_pairs={{0,48},{16,0},{32,16},{48,32},{64,112},{80,64},{96,80},{112,96},{1... | collective-permute-start | bytes 196616 | tf_op jit(solution)/shard_map/ppermute | solution.py:30
  14.8 3.8 %copy-start = (bf16[128,256]{1,0:T(8,128)(2,1)S(1)}, bf16[128,256]{1,0:T(8,128)(2,1)}, u32[]{:S(2)}) copy-start(bf16[128,256]{1,0:T(8,128)(2,1)} %get-tuple-element.42) | copy-start | bytes 196612
  18.6 9.2 %collective-permute-start.6 = (bf16[2,128,256]{2,1,0:T(8,128)(2,1)S(1)}, bf16[2,128,256]{2,1,0:T(8,128)(2,1)S(1)}, u32[]{:S(2)}, u32[]{:S(2)}) collective-permute-start(bf16[2,128,256]{2,1,0:T(8,128)(2,1)S(1)} %pad_maximum_fusion.2), channel_id=1, source_target_pairs={{0,4},{1,5},{2,6},{3,7},{4,8},{5,9},{6,10},{7,11},{8,12},{9,13},{1... | collective-permute-start | bytes 393224 | tf_op jit(solution)/shard_map/ppermute | solution.py:25
  20.2 12.7 %collective-permute-start.9 = (bf16[4,128,256]{2,1,0:T(8,128)(2,1)S(1)}, bf16[4,128,256]{2,1,0:T(8,128)(2,1)S(1)}, u32[]{:S(2)}, u32[]{:S(2)}) collective-permute-start(bf16[4,128,256]{2,1,0:T(8,128)(2,1)S(1)} %pad_maximum_fusion.1.refs_4_), channel_id=1, source_target_pairs={{0,64},{16,80},{32,96},{48,112},{64,128},{80,144},{96,160},{112,17... | collective-permute-start | bytes 786440 | tf_op jit(solution)/shard_map/ppermute | solution.py:25
  21.8 11.1 %collective-permute-start.8 = (bf16[4,128,256]{2,1,0:T(8,128)(2,1)S(1)}, bf16[4,128,256]{2,1,0:T(8,128)(2,1)S(1)}, u32[]{:S(2)}, u32[]{:S(2)}) collective-permute-start(bf16[4,128,256]{2,1,0:T(8,128)(2,1)S(1)} %pad_maximum_fusion.1.refs_4_), channel_id=1, source_target_pairs={{0,128},{16,144},{32,160},{48,176},{64,192},{80,208},{96,224},{112... | collective-permute-start | bytes 786440 | tf_op jit(solution)/shard_map/ppermute | solution.py:25
  22.7 11.8 %collective-permute-start.7 = (bf16[4,128,256]{2,1,0:T(8,128)(2,1)S(1)}, bf16[4,128,256]{2,1,0:T(8,128)(2,1)S(1)}, u32[]{:S(2)}, u32[]{:S(2)}) collective-permute-start(bf16[4,128,256]{2,1,0:T(8,128)(2,1)S(1)} %pad_maximum_fusion.1.refs_4_), channel_id=1, source_target_pairs={{0,192},{16,208},{32,224},{48,240},{64,0},{80,16},{96,32},{112,48}... | collective-permute-start | bytes 786440 | tf_op jit(solution)/shard_map/ppermute | solution.py:25
  25.1 6.5 %collective-permute-start.5 = (bf16[2,128,256]{2,1,0:T(8,128)(2,1)S(1)}, bf16[2,128,256]{2,1,0:T(8,128)(2,1)S(1)}, u32[]{:S(2)}, u32[]{:S(2)}) collective-permute-start(bf16[2,128,256]{2,1,0:T(8,128)(2,1)S(1)} %pad_maximum_fusion.2), channel_id=1, source_target_pairs={{0,8},{1,9},{2,10},{3,11},{4,12},{5,13},{6,14},{7,15},{8,0},{9,1},... | collective-permute-start | bytes 393224 | tf_op jit(solution)/shard_map/ppermute | solution.py:25
  27.9 5.0 %collective-permute-start.4 = (bf16[2,128,256]{2,1,0:T(8,128)(2,1)S(1)}, bf16[2,128,256]{2,1,0:T(8,128)(2,1)S(1)}, u32[]{:S(2)}, u32[]{:S(2)}) collective-permute-start(bf16[2,128,256]{2,1,0:T(8,128)(2,1)S(1)} %pad_maximum_fusion.2), channel_id=1, source_target_pairs={{0,12},{1,13},{2,14},{3,15},{4,0},{5,1},{6,2},{7,3},{8,4},{9,5},{1... | collective-permute-start | bytes 393224 | tf_op jit(solution)/shard_map/ppermute | solution.py:25
  34.5 1.9 %collective-permute-start.10 = (bf16[2,4,128,256]{3,2,1,0:T(8,128)(2,1)S(1)}, bf16[2,4,128,256]{3,2,1,0:T(8,128)(2,1)S(1)}, u32[]{:S(2)}, u32[]{:S(2)}) collective-permute-start(bf16[2,4,128,256]{3,2,1,0:T(8,128)(2,1)S(1)} %pad_maximum_fusion), channel_id=1, source_target_pairs={{0,1},{1,0},{2,3},{3,2},{4,5},{5,4},{6,7},{7,6},{8,9},{9,8},{10,11... | collective-permute-start | bytes 1572872 | tf_op jit(solution)/shard_map/ppermute | solution.py:34
  41.3 10.4 %collective-permute-start.12 = (f32[136,512]{1,0:T(8,128)S(1)}, f32[136,512]{1,0:T(8,128)S(1)}, u32[]{:S(2)}, u32[]{:S(2)}) collective-permute-start(f32[136,512]{1,0:T(8,128)S(1)} %shard_map.77), channel_id=1, source_target_pairs={{0,64},{16,80},{32,96},{48,112},{64,128},{80,144},{96,160},{112,17... | collective-permute-start | bytes 835592 | tf_op jit(solution)/shard_map/ppermute | solution.py:25
  42.9 11.0 %collective-permute-start.13 = (f32[136,512]{1,0:T(8,128)S(1)}, f32[136,512]{1,0:T(8,128)S(1)}, u32[]{:S(2)}, u32[]{:S(2)}) collective-permute-start(f32[136,512]{1,0:T(8,128)S(1)} %shard_map.78), channel_id=1, source_target_pairs={{0,128},{16,144},{32,160},{48,176},{64,192},{80,208},{96,224},{112... | collective-permute-start | bytes 835592 | tf_op jit(solution)/shard_map/ppermute | solution.py:25
  44.5 14.1 %collective-permute-start.14 = (f32[136,512]{1,0:T(8,128)S(1)}, f32[136,512]{1,0:T(8,128)S(1)}, u32[]{:S(2)}, u32[]{:S(2)}) collective-permute-start(f32[136,512]{1,0:T(8,128)S(1)} %shard_map.79), channel_id=1, source_target_pairs={{0,192},{16,208},{32,224},{48,240},{64,0},{80,16},{96,32},{112,48}... | collective-permute-start | bytes 835592 | tf_op jit(solution)/shard_map/ppermute | solution.py:25
  51.6 8.8 %collective-permute-start.11 = (f32[2,136,512]{2,1,0:T(8,128)S(1)}, f32[2,136,512]{2,1,0:T(8,128)S(1)}, u32[]{:S(2)}, u32[]{:S(2)}) collective-permute-start(f32[2,136,512]{2,1,0:T(8,128)S(1)} %get-tuple-element.54), channel_id=1, source_target_pairs={{0,1},{1,0},{2,3},{3,2},{4,5},{5,4},{6,7},{7,6},{8,9},{9,8},{10,11... | collective-permute-start | bytes 1671176 | tf_op jit(solution)/shard_map/ppermute | solution.py:34
  60.4 10.6 %collective-permute-start.16 = (f32[136,256]{1,0:T(8,128)S(1)}, f32[136,256]{1,0:T(8,128)S(1)}, u32[]{:S(2)}, u32[]{:S(2)}) collective-permute-start(f32[136,256]{1,0:T(8,128)S(1)} %get-tuple-element.66), channel_id=1, source_target_pairs={{0,8},{1,9},{2,10},{3,11},{4,12},{5,13},{6,14},{7,15},{8,0},{9,1},... | collective-permute-start | bytes 417800 | tf_op jit(solution)/shard_map/ppermute | solution.py:25
  63.2 10.6 %collective-permute-start.17 = (f32[136,256]{1,0:T(8,128)S(1)}, f32[136,256]{1,0:T(8,128)S(1)}, u32[]{:S(2)}, u32[]{:S(2)}) collective-permute-start(f32[136,256]{1,0:T(8,128)S(1)} %get-tuple-element.67), channel_id=1, source_target_pairs={{0,12},{1,13},{2,14},{3,15},{4,0},{5,1},{6,2},{7,3},{8,4},{9,5},{1... | collective-permute-start | bytes 417800 | tf_op jit(solution)/shard_map/ppermute | solution.py:25
  64.7 9.1 %collective-permute-start.15 = (f32[136,256]{1,0:T(8,128)S(1)}, f32[136,256]{1,0:T(8,128)S(1)}, u32[]{:S(2)}, u32[]{:S(2)}) collective-permute-start(f32[136,256]{1,0:T(8,128)S(1)} %get-tuple-element.65), channel_id=1, source_target_pairs={{0,4},{1,5},{2,6},{3,7},{4,8},{5,9},{6,10},{7,11},{8,12},{9,13},{1... | collective-permute-start | bytes 417800 | tf_op jit(solution)/shard_map/ppermute | solution.py:25
  65.4 8.6 %collective-permute-start.19 = (f32[136,128]{1,0:T(8,128)S(1)}, f32[136,128]{1,0:T(8,128)S(1)}, u32[]{:S(2)}, u32[]{:S(2)}) collective-permute-start(f32[136,128]{1,0:T(8,128)S(1)} %get-tuple-element.73), channel_id=1, source_target_pairs={{0,16},{16,32},{32,48},{48,0},{64,80},{80,96},{96,112},{112,64},{1... | collective-permute-start | bytes 208904 | tf_op jit(solution)/shard_map/ppermute | solution.py:30
  66.2 10.0 %collective-permute-start.20 = (f32[136,128]{1,0:T(8,128)S(1)}, f32[136,128]{1,0:T(8,128)S(1)}, u32[]{:S(2)}, u32[]{:S(2)}) collective-permute-start(f32[136,128]{1,0:T(8,128)S(1)} %get-tuple-element.74), channel_id=1, source_target_pairs={{0,32},{16,48},{32,0},{48,16},{64,96},{80,112},{96,64},{112,80},{1... | collective-permute-start | bytes 208904 | tf_op jit(solution)/shard_map/ppermute | solution.py:30
  71.0 6.3 %collective-permute-start.21 = (f32[136,128]{1,0:T(8,128)S(1)}, f32[136,128]{1,0:T(8,128)S(1)}, u32[]{:S(2)}, u32[]{:S(2)}) collective-permute-start(f32[136,128]{1,0:T(8,128)S(1)} %get-tuple-element.75), channel_id=1, source_target_pairs={{0,48},{16,0},{32,16},{48,32},{64,112},{80,64},{96,80},{112,96},{1... | collective-permute-start | bytes 208904 | tf_op jit(solution)/shard_map/ppermute | solution.py:30
  73.9 4.4 %collective-permute-start.18 = (f32[136,128]{1,0:T(8,128)S(1)}, f32[136,128]{1,0:T(8,128)S(1)}, u32[]{:S(2)}, u32[]{:S(2)}) collective-permute-start(f32[136,128]{1,0:T(8,128)S(1)} %get-tuple-element.69), channel_id=1, source_target_pairs={{0,2},{1,3},{2,0},{3,1},{4,6},{5,7},{6,4},{7,5},{8,10},{9,11},{10,... | collective-permute-start | bytes 208904 | tf_op jit(solution)/shard_map/ppermute | solution.py:34

commit v8 on v7

--- a/solution.py
+++ b/solution.py
@@ -160,7 +160,7 @@
 
 
 def row_kernel(total, scale, halves, *refs):
-    ones, twos, outs = refs[:SUB], refs[SUB : 2 * SUB], refs[2 * SUB :]
+    ones, twos, outs = refs[:2], refs[2 : 2 + SUB], refs[2 + SUB :]
     tiles = [
         jnp.concatenate(
             [
@@ -202,18 +202,20 @@
         outs[piece][...] = merged([ref[:, span] for ref in ins])
 
 
-def finish_kernel(total, own_start, *refs):
-    ins, (matched, flow) = refs[:-2], refs[-2:]
-    own_across, own_down = piece_coords(own_start(), total)
+def finish_kernel(total, *refs):
+    ins, outs = refs[:-4], refs[-4:]
     lane = lax.broadcasted_iota(jnp.int32, (1, SHARD), 1).astype(jnp.float32) / GRID_W
-    parts = [ref[...] for ref in ins]
-    _, whole = merge([peak_of(part) for part in parts], parts)
-    inverse = 1.0 / whole[WIDTH + TOTAL_ROW : WIDTH + TOTAL_ROW + 1, :]
-    matched[...] = (whole[:WIDTH] * inverse).T
-    across = whole[WIDTH + ACROSS_ROW : WIDTH + ACROSS_ROW + 1, :] * inverse
-    down = whole[WIDTH + DOWN_ROW : WIDTH + DOWN_ROW + 1, :] * inverse
-    flow[0:1, :] = across - (own_across + lane)
-    flow[1:2, :] = down - own_down
+    for side, start in enumerate((start_one(0, 0, 0), start_two(0, 0))):
+        matched, flow = outs[2 * side], outs[2 * side + 1]
+        own_across, own_down = piece_coords(start, total)
+        parts = [ref[...] for ref in (ins[2:] if side else ins[:2])]
+        _, whole = merge([peak_of(part) for part in parts], parts)
+        inverse = 1.0 / whole[WIDTH + TOTAL_ROW : WIDTH + TOTAL_ROW + 1, :]
+        matched[...] = (whole[:WIDTH] * inverse).T
+        across = whole[WIDTH + ACROSS_ROW : WIDTH + ACROSS_ROW + 1, :] * inverse
+        down = whole[WIDTH + DOWN_ROW : WIDTH + DOWN_ROW + 1, :] * inverse
+        flow[0:1, :] = across - (own_across + lane)
+        flow[1:2, :] = down - own_down
 
 
 def call(kernel, shapes, args, scratch=(), work=0, specs=None, vmem=48 << 20):
@@ -271,7 +273,7 @@
     def col_scores(*refs):
         col_kernel(total, scale, *refs)
 
-    def row_scores(ones, halves, weight, *counts):
+    def row_scores(ones, twos, halves, weight, *counts):
         shapes = [f32(count, ROWS, BLOCK) for count in counts]
         kernel = functools.partial(row_kernel, total, scale, halves)
         return call(kernel, shapes, (*ones, *twos), work=weight * work)
@@ -286,33 +288,22 @@
             for step, part in enumerate(parts)
         ]
 
-    def finish_one(*refs):
-        finish_kernel(total, lambda: start_one(0, 0, 0), *refs)
-
-    def finish_two(*refs):
-        finish_kernel(total, lambda: start_two(0, 0), *refs)
-
     work = BLOCK * BLOCK * SUB
     cols = [None] * SUB
+    (keep_one,) = row_scores(ones[:2], twos, ((0, 0), (0, 1)), 2, 2)
+    (send_one,) = row_scores(ones[2:], twos, ((0, 0), (0, 1)), 2, 2)
+    theirs_one = fast_swap("col", send_one, 1)
+    ones, _ = together((ones, send_one))
     for step in (1, 3, 2, 0):
         (cols[step],) = call(col_scores, [f32(ROWS, BLOCK)], (*ones, twos[step]), work=work)
-    ones, _ = together((ones, cols))
     cols = spread("row", cols)
-    send_one, far_one = row_scores(ones, ((1, 0), (1, 1), (0, 1)), 3, 2, 1)
-    theirs_one = fast_swap("col", send_one, 1)
-    far_rows = core_merge(far_one, theirs_one, 1)
-    far_rows = spread("col", far_rows, 2)
-    cols = call(block_kernel, [f32(ROWS, SHARD)] * SUB, cols)
-    ones, _, cols = together((ones, far_one, cols))
+    rows = spread("col", core_merge(keep_one, theirs_one, 0, 1))
+    cols = call(block_kernel, [f32(ROWS, SHARD)] * SUB, cols, work=4 * work)
     cols = [cols[0]] + [fast_shift("row", cols[step], step) for step in range(1, SUB)]
-    (near_one,) = row_scores(ones, ((0, 0),), 40, 1)
-    rows = spread("col", core_merge(near_one, theirs_one, 0)) + far_rows
     keep, send = call(chip_kernel, [f32(ROWS, SHARD)] * 2, rows)
     theirs = fast_swap("col", send, 2)
-    outs = [f32(SHARD, WIDTH), f32(2, SHARD)]
-    matched_two, flow_two = call(finish_two, outs, cols)
-    matched_one, flow_one = call(finish_one, outs, (keep, theirs))
-    return matched_one, flow_one, matched_two, flow_two
+    outs = [f32(SHARD, WIDTH), f32(2, SHARD)] * 2
+    return tuple(call(functools.partial(finish_kernel, total), outs, (keep, theirs, *cols)))
 
 
 def solution(mesh):

time: 79.3 us -> 76.7 us (0.967)
  the two profiles are of different devices: /device:TPU:8 before, /device:TPU:1 now
where the time goes in v8:
time: 76.7 us; the launch traced here: 76.2 us
  starting transfers between devices  42.6 us (56%)
  waiting for transfers between devices  17.1 us (22%)
  Pallas kernels  14.8 us (19%)
  other arithmetic  0.99 us (1%)
  between operations  0.77 us (1%)
    ppermute x12, starting transfers between devices, slow_shift(): return lax.ppermute(value, axis, pairs)  19 us
    ppermute x6, starting transfers between devices, fast_shift(): return lax.ppermute(value, axis, pairs)  17.3 us
    pallas_call x11, Pallas kernels, call(): pl.pallas_call(kernel, out_shape=shapes, in_specs=specs or [VMEM] * len(a...  14.8 us
    ppermute x6, waiting for transfers between devices, fast_shift(): return lax.ppermute(value, axis, pairs)  7.91 us
    ppermute x12, waiting for transfers between devices, slow_shift(): return lax.ppermute(value, axis, pairs)  7.25 us
    ppermute x4, starting transfers between devices, fast_swap(): return lax.ppermute(value, axis, [(i, i ^ step) for i in range(SUB * SUB)])  6.31 us
    ppermute x4, waiting for transfers between devices, fast_swap(): return lax.ppermute(value, axis, [(i, i ^ step) for i in range(SUB * SUB)])  1.93 us
  transfers between devices with their start and end apart: 22, of which 10 were waited for; matrix products, arithmetic and copies ran while one was open for 1% of the time, Pallas kernels for 12%

profile of v8, /device:TPU:1, one launch (start us, length us, event | category | flops | bytes accessed | tf_op | source)
XLA Modules:
  0.0 76.2 jit_solution(13790636883519448920)
XLA Ops:
  0.6 1.7 %shard_map.75 = (bf16[128,256]{1,0:T(8,128)(2,1)}, bf16[128,256]{1,0:T(8,128)(2,1)}) custom-call(bf16[128,128]{1,0:T(8,128)(2,1)} %feat_one.1, bf16[128,128]{1,0:T(8,128)(2,1)} %value_one.1, bf16[128,128]{1,0:T(8,128)(2,1)} %feat_two.1, bf16[128,128]{1,0:T(8,128)(2,1)} %value_two.1), custom_call_target="tpu_custom_call" | custom-call | bytes 262144 | tf_op jit(solution)/shard_map/pallas_call | solution.py:223
  2.3 2.6 %collective-permute-start = (bf16[128,256]{1,0:T(8,128)(2,1)}, bf16[128,256]{1,0:T(8,128)(2,1)S(1)}, u32[]{:S(2)}, u32[]{:S(2)}) collective-permute-start(bf16[128,256]{1,0:T(8,128)(2,1)} %get-tuple-element.27), channel_id=1, source_target_pairs={{0,2},{1,3},{2,0},{3,1},{4,6},{5,7},{6,4},{7,5},{8,10},{9,11},{10,... | collective-permute-start | bytes 196616 | tf_op jit(solution)/shard_map/ppermute | solution.py:34
  4.9 3.0 %collective-permute-start.3 = (bf16[128,256]{1,0:T(8,128)(2,1)}, bf16[128,256]{1,0:T(8,128)(2,1)S(1)}, u32[]{:S(2)}, u32[]{:S(2)}) collective-permute-start(bf16[128,256]{1,0:T(8,128)(2,1)} %get-tuple-element.28), channel_id=1, source_target_pairs={{0,16},{16,32},{32,48},{48,0},{64,80},{80,96},{96,112},{112,64},{1... | collective-permute-start | bytes 196616 | tf_op jit(solution)/shard_map/ppermute | solution.py:30
  7.9 4.2 %collective-permute-start.2 = (bf16[128,256]{1,0:T(8,128)(2,1)}, bf16[128,256]{1,0:T(8,128)(2,1)S(1)}, u32[]{:S(2)}, u32[]{:S(2)}) collective-permute-start(bf16[128,256]{1,0:T(8,128)(2,1)} %get-tuple-element.28), channel_id=1, source_target_pairs={{0,32},{16,48},{32,0},{48,16},{64,96},{80,112},{96,64},{112,80},{1... | collective-permute-start | bytes 196616 | tf_op jit(solution)/shard_map/ppermute | solution.py:30
  12.1 2.4 %collective-permute-start.1 = (bf16[128,256]{1,0:T(8,128)(2,1)}, bf16[128,256]{1,0:T(8,128)(2,1)S(1)}, u32[]{:S(2)}, u32[]{:S(2)}) collective-permute-start(bf16[128,256]{1,0:T(8,128)(2,1)} %get-tuple-element.28), channel_id=1, source_target_pairs={{0,48},{16,0},{32,16},{48,32},{64,112},{80,64},{96,80},{112,96},{1... | collective-permute-start | bytes 196616 | tf_op jit(solution)/shard_map/ppermute | solution.py:30
  14.5 0.9 %pad_maximum_fusion.2 = bf16[2,128,256]{2,1,0:T(8,128)(2,1)S(1)} fusion(bf16[1,128,256]{2,1,0:T(8,128)(2,1)S(1)} %bitcast.29, bf16[1,128,256]{2,1,0:T(8,128)(2,1)} %bitcast.28), kind=kLoop, calls=%fused_computation.6 | loop fusion | flops 65536 | bytes 262144 | tf_op jit(solution)/shard_map/stack | solution.py:266
  15.4 1.9 %collective-permute-done.2 = bf16[128,256]{1,0:T(8,128)(2,1)S(1)} collective-permute-done((bf16[128,256]{1,0:T(8,128)(2,1)}, bf16[128,256]{1,0:T(8,128)(2,1)S(1)}, u32[]{:S(2)}, u32[]{:S(2)}) %collective-permute-start.2) | collective-permute-done | bytes 65568 | tf_op jit(solution)/shard_map/ppermute | solution.py:30
  17.3 1.0 %collective-permute-done.1 = bf16[128,256]{1,0:T(8,128)(2,1)S(1)} collective-permute-done((bf16[128,256]{1,0:T(8,128)(2,1)}, bf16[128,256]{1,0:T(8,128)(2,1)S(1)}, u32[]{:S(2)}, u32[]{:S(2)}) %collective-permute-start.1) | collective-permute-done | bytes 65568 | tf_op jit(solution)/shard_map/ppermute | solution.py:30
  18.3 1.3 %collective-permute-start.6 = (bf16[2,128,256]{2,1,0:T(8,128)(2,1)S(1)}, bf16[2,128,256]{2,1,0:T(8,128)(2,1)S(1)}, u32[]{:S(2)}, u32[]{:S(2)}) collective-permute-start(bf16[2,128,256]{2,1,0:T(8,128)(2,1)S(1)} %pad_maximum_fusion.2), channel_id=1, source_target_pairs={{0,4},{1,5},{2,6},{3,7},{4,8},{5,9},{6,10},{7,11},{8,12},{9,13},{1... | collective-permute-start | bytes 393224 | tf_op jit(solution)/shard_map/ppermute | solution.py:25
  19.6 1.3 %collective-permute-start.9 = (bf16[4,128,256]{2,1,0:T(8,128)(2,1)S(1)}, bf16[4,128,256]{2,1,0:T(8,128)(2,1)S(1)}, u32[]{:S(2)}, u32[]{:S(2)}) collective-permute-start(bf16[4,128,256]{2,1,0:T(8,128)(2,1)S(1)} %pad_maximum_fusion.1.refs_2_.refs_4_), channel_id=1, source_target_pairs={{0,64},{16,80},{32,96},{48,112},{64,128},{80,144},{96,160},{112,17... | collective-permute-start | bytes 786440 | tf_op jit(solution)/shard_map/ppermute | solution.py:25
  20.9 2.6 %collective-permute-start.8 = (bf16[4,128,256]{2,1,0:T(8,128)(2,1)S(1)}, bf16[4,128,256]{2,1,0:T(8,128)(2,1)S(1)}, u32[]{:S(2)}, u32[]{:S(2)}) collective-permute-start(bf16[4,128,256]{2,1,0:T(8,128)(2,1)S(1)} %pad_maximum_fusion.1.refs_2_.refs_4_), channel_id=1, source_target_pairs={{0,128},{16,144},{32,160},{48,176},{64,192},{80,208},{96,224},{112... | collective-permute-start | bytes 786440 | tf_op jit(solution)/shard_map/ppermute | solution.py:25
  23.5 1.1 %collective-permute-start.7 = (bf16[4,128,256]{2,1,0:T(8,128)(2,1)S(1)}, bf16[4,128,256]{2,1,0:T(8,128)(2,1)S(1)}, u32[]{:S(2)}, u32[]{:S(2)}) collective-permute-start(bf16[4,128,256]{2,1,0:T(8,128)(2,1)S(1)} %pad_maximum_fusion.1.refs_2_.refs_4_), channel_id=1, source_target_pairs={{0,192},{16,208},{32,224},{48,240},{64,0},{80,16},{96,32},{112,48}... | collective-permute-start | bytes 786440 | tf_op jit(solution)/shard_map/ppermute | solution.py:25
  24.6 2.5 %collective-permute-start.5 = (bf16[2,128,256]{2,1,0:T(8,128)(2,1)S(1)}, bf16[2,128,256]{2,1,0:T(8,128)(2,1)S(1)}, u32[]{:S(2)}, u32[]{:S(2)}) collective-permute-start(bf16[2,128,256]{2,1,0:T(8,128)(2,1)S(1)} %pad_maximum_fusion.2), channel_id=1, source_target_pairs={{0,8},{1,9},{2,10},{3,11},{4,12},{5,13},{6,14},{7,15},{8,0},{9,1},... | collective-permute-start | bytes 393224 | tf_op jit(solution)/shard_map/ppermute | solution.py:25
  27.1 1.2 %collective-permute-start.4 = (bf16[2,128,256]{2,1,0:T(8,128)(2,1)S(1)}, bf16[2,128,256]{2,1,0:T(8,128)(2,1)S(1)}, u32[]{:S(2)}, u32[]{:S(2)}) collective-permute-start(bf16[2,128,256]{2,1,0:T(8,128)(2,1)S(1)} %pad_maximum_fusion.2), channel_id=1, source_target_pairs={{0,12},{1,13},{2,14},{3,15},{4,0},{5,1},{6,2},{7,3},{8,4},{9,5},{1... | collective-permute-start | bytes 393224 | tf_op jit(solution)/shard_map/ppermute | solution.py:25
  28.2 1.7 %collective-permute-done.5 = bf16[2,128,256]{2,1,0:T(8,128)(2,1)S(1)} collective-permute-done((bf16[2,128,256]{2,1,0:T(8,128)(2,1)S(1)}, bf16[2,128,256]{2,1,0:T(8,128)(2,1)S(1)}, u32[]{:S(2)}, u32[]{:S(2)}) %collective-permute-start.5) | collective-permute-done | bytes 131104 | tf_op jit(solution)/shard_map/ppermute | solution.py:25
  29.9 0.9 %collective-permute-done.4 = bf16[2,128,256]{2,1,0:T(8,128)(2,1)S(1)} collective-permute-done((bf16[2,128,256]{2,1,0:T(8,128)(2,1)S(1)}, bf16[2,128,256]{2,1,0:T(8,128)(2,1)S(1)}, u32[]{:S(2)}, u32[]{:S(2)}) %collective-permute-start.4) | collective-permute-done | bytes 131104 | tf_op jit(solution)/shard_map/ppermute | solution.py:25
  30.9 0.1 pad_maximum_fusion
  31.0 2.4 %collective-permute-done.8.refs_4_ = bf16[4,128,256]{2,1,0:T(8,128)(2,1)S(1)} collective-permute-done((bf16[4,128,256]{2,1,0:T(8,128)(2,1)S(1)}, bf16[4,128,256]{2,1,0:T(8,128)(2,1)S(1)}, u32[]{:S(2)}, u32[]{:S(2)}) %collective-permute-start.8) | collective-permute-done | bytes 262176 | tf_op jit(solution)/shard_map/ppermute | solution.py:25
  33.4 3.0 %collective-permute-start.10 = (bf16[2,4,128,256]{3,2,1,0:T(8,128)(2,1)S(1)}, bf16[2,4,128,256]{3,2,1,0:T(8,128)(2,1)S(1)}, u32[]{:S(2)}, u32[]{:S(2)}) collective-permute-start(bf16[2,4,128,256]{3,2,1,0:T(8,128)(2,1)S(1)} %pad_maximum_fusion), channel_id=1, source_target_pairs={{0,1},{1,0},{2,3},{3,2},{4,5},{5,4},{6,7},{7,6},{8,9},{9,8},{10,11... | collective-permute-start | bytes 1572872 | tf_op jit(solution)/shard_map/ppermute | solution.py:34
  36.4 1.5 %collective-permute-done.10 = bf16[2,4,128,256]{3,2,1,0:T(8,128)(2,1)S(1)} collective-permute-done((bf16[2,4,128,256]{3,2,1,0:T(8,128)(2,1)S(1)}, bf16[2,4,128,256]{3,2,1,0:T(8,128)(2,1)S(1)}, u32[]{:S(2)}, u32[]{:S(2)}) %collective-permute-start.10) | collective-permute-done | bytes 524320 | tf_op jit(solution)/shard_map/ppermute | solution.py:34
  38.0 2.8 %shard_map.76 = f32[2,136,512]{2,1,0:T(8,128)S(1)} custom-call(bf16[4,128,256]{2,1,0:T(8,128)(2,1)S(1)} %get-tuple-element.44.refs_0_.refs_2_, bf16[4,128,256]{2,1,0:T(8,128)(2,1)S(1)} %get-tuple-element.45.refs_1_.refs_3_, bf16[4,128,256]{2,1,0:T(8,128)(2,1)S(1)} %pad_maximum_fusion.1.refs_2_.refs_4_, ...), custom_call_target="tpu_custom_call" | custom-call | flops 1073741824 | bytes 2129920 | tf_op jit(solution)/shard_map/pallas_call | solution.py:223
  40.8 0.6 collective-permute-start.11
  41.5 1.6 %shard_map.81 = f32[136,512]{1,0:T(8,128)S(1)} custom-call(bf16[4,128,256]{2,1,0:T(8,128)(2,1)S(1)} %get-tuple-element.42.refs_0_, bf16[4,128,256]{2,1,0:T(8,128)(2,1)S(1)} %get-tuple-element.43.refs_1_, bf16[4,128,256]{2,1,0:T(8,128)(2,1)S(1)} %get-tuple-element.44.refs_0_.refs_2_, bf16[4,128,256]{2,1,0:T(8,128)(2,1)S(1)} %get-tuple-element.45.refs_1_.refs_3_, ...), custom_call_target="tpu_custom_call" | custom-call | flops 536870912 | bytes 1589248 | tf_op jit(solution)/shard_map/pallas_call | solution.py:223
  43.1 0.9 %collective-permute-start.16 = (f32[136,512]{1,0:T(8,128)S(1)}, f32[136,512]{1,0:T(8,128)S(1)}, u32[]{:S(2)}, u32[]{:S(2)}) collective-permute-start(f32[136,512]{1,0:T(8,128)S(1)} %shard_map.81), channel_id=1, source_target_pairs={{0,64},{16,80},{32,96},{48,112},{64,128},{80,144},{96,160},{112,17... | collective-permute-start | bytes 835592 | tf_op jit(solution)/shard_map/ppermute | solution.py:25
  44.0 1.6 %shard_map.83 = f32[136,512]{1,0:T(8,128)S(1)} custom-call(bf16[4,128,256]{2,1,0:T(8,128)(2,1)S(1)} %get-tuple-element.42.refs_0_, bf16[4,128,256]{2,1,0:T(8,128)(2,1)S(1)} %get-tuple-element.43.refs_1_, bf16[4,128,256]{2,1,0:T(8,128)(2,1)S(1)} %get-tuple-element.44.refs_0_.refs_2_, bf16[4,128,256]{2,1,0:T(8,128)(2,1)S(1)} %get-tuple-element.45.refs_1_.refs_3_, ...), custom_call_target="tpu_custom_call" | custom-call | flops 536870912 | bytes 1589248 | tf_op jit(solution)/shard_map/pallas_call | solution.py:223
  45.6 1.6 %shard_map.82 = f32[136,512]{1,0:T(8,128)S(1)} custom-call(bf16[4,128,256]{2,1,0:T(8,128)(2,1)S(1)} %get-tuple-element.42.refs_0_, bf16[4,128,256]{2,1,0:T(8,128)(2,1)S(1)} %get-tuple-element.43.refs_1_, bf16[4,128,256]{2,1,0:T(8,128)(2,1)S(1)} %get-tuple-element.44.refs_0_.refs_2_, bf16[4,128,256]{2,1,0:T(8,128)(2,1)S(1)} %get-tuple-element.45.refs_1_.refs_3_, ...), custom_call_target="tpu_custom_call" | custom-call | flops 536870912 | bytes 1589248 | tf_op jit(solution)/shard_map/pallas_call | solution.py:223
  47.3 2.2 %collective-permute-start.17 = (f32[136,512]{1,0:T(8,128)S(1)}, f32[136,512]{1,0:T(8,128)S(1)}, u32[]{:S(2)}, u32[]{:S(2)}) collective-permute-start(f32[136,512]{1,0:T(8,128)S(1)} %shard_map.82), channel_id=1, source_target_pairs={{0,128},{16,144},{32,160},{48,176},{64,192},{80,208},{96,224},{112... | collective-permute-start | bytes 835592 | tf_op jit(solution)/shard_map/ppermute | solution.py:25
  49.5 1.4 %collective-permute-start.18 = (f32[136,512]{1,0:T(8,128)S(1)}, f32[136,512]{1,0:T(8,128)S(1)}, u32[]{:S(2)}, u32[]{:S(2)}) collective-permute-start(f32[136,512]{1,0:T(8,128)S(1)} %shard_map.83), channel_id=1, source_target_pairs={{0,192},{16,208},{32,224},{48,240},{64,0},{80,16},{96,32},{112,48}... | collective-permute-start | bytes 835592 | tf_op jit(solution)/shard_map/ppermute | solution.py:25
  50.8 2.8 %shard_map.77.refs_1_ = f32[2,136,512]{2,1,0:T(8,128)S(1)} custom-call(bf16[4,128,256]{2,1,0:T(8,128)(2,1)S(1)} %get-tuple-element.42.refs_0_, bf16[4,128,256]{2,1,0:T(8,128)(2,1)S(1)} %get-tuple-element.43.refs_1_, bf16[4,128,256]{2,1,0:T(8,128)(2,1)S(1)} %pad_maximum_fusion.1.refs_2_.refs_4_, ...), custom_call_target="tpu_custom_call" | custom-call | flops 1073741824 | bytes 2129920 | tf_op jit(solution)/shard_map/pallas_call | solution.py:223
  53.6 1.6 %shard_map.80.refs_0_ = f32[136,512]{1,0:T(8,128)S(1)} custom-call(bf16[4,128,256]{2,1,0:T(8,128)(2,1)S(1)} %get-tuple-element.42.refs_0_, bf16[4,128,256]{2,1,0:T(8,128)(2,1)S(1)} %get-tuple-element.43.refs_1_, bf16[4,128,256]{2,1,0:T(8,128)(2,1)S(1)} %get-tuple-element.44.refs_0_.refs_2_, bf16[4,128,256]{2,1,0:T(8,128)(2,1)S(1)} %get-tuple-element.45.refs_1_.refs_3_, ...), custom_call_target="tpu_custom_call" | custom-call | flops 536870912 | bytes 1589248 | tf_op jit(solution)/shard_map/pallas_call | solution.py:223
  55.2 0.0 collective-permute-done.11.refs_0_
  55.2 0.1 shard_map.78
  55.3 1.3 %collective-permute-start.12 = (f32[136,256]{1,0:T(8,128)S(1)}, f32[136,256]{1,0:T(8,128)S(1)}, u32[]{:S(2)}, u32[]{:S(2)}) collective-permute-start(f32[136,256]{1,0:T(8,128)S(1)} %get-tuple-element.37), channel_id=1, source_target_pairs={{0,4},{1,5},{2,6},{3,7},{4,8},{5,9},{6,10},{7,11},{8,12},{9,13},{1... | collective-permute-start | bytes 417800 | tf_op jit(solution)/shard_map/ppermute | solution.py:25
  56.6 1.4 %collective-permute-start.13 = (f32[136,256]{1,0:T(8,128)S(1)}, f32[136,256]{1,0:T(8,128)S(1)}, u32[]{:S(2)}, u32[]{:S(2)}) collective-permute-start(f32[136,256]{1,0:T(8,128)S(1)} %get-tuple-element.38), channel_id=1, source_target_pairs={{0,8},{1,9},{2,10},{3,11},{4,12},{5,13},{6,14},{7,15},{8,0},{9,1},... | collective-permute-start | bytes 417800 | tf_op jit(solution)/shard_map/ppermute | solution.py:25
  58.1 1.9 %collective-permute-start.14 = (f32[136,256]{1,0:T(8,128)S(1)}, f32[136,256]{1,0:T(8,128)S(1)}, u32[]{:S(2)}, u32[]{:S(2)}) collective-permute-start(f32[136,256]{1,0:T(8,128)S(1)} %get-tuple-element.39), channel_id=1, source_target_pairs={{0,12},{1,13},{2,14},{3,15},{4,0},{5,1},{6,2},{7,3},{8,4},{9,5},{1... | collective-permute-start | bytes 417800 | tf_op jit(solution)/shard_map/ppermute | solution.py:25
  60.0 0.0 collective-permute-done.17.refs_2_
  60.0 2.1 %collective-permute-done.18.refs_3_ = f32[136,512]{1,0:T(8,128)S(1)} collective-permute-done((f32[136,512]{1,0:T(8,128)S(1)}, f32[136,512]{1,0:T(8,128)S(1)}, u32[]{:S(2)}, u32[]{:S(2)}) %collective-permute-start.18) | collective-permute-done | bytes 278560 | tf_op jit(solution)/shard_map/ppermute | solution.py:25
  62.1 0.1 shard_map.84
  62.2 0.8 %collective-permute-start.19 = (f32[136,128]{1,0:T(8,128)S(1)}, f32[136,128]{1,0:T(8,128)S(1)}, u32[]{:S(2)}, u32[]{:S(2)}) collective-permute-start(f32[136,128]{1,0:T(8,128)S(1)} %get-tuple-element.47), channel_id=1, source_target_pairs={{0,16},{16,32},{32,48},{48,0},{64,80},{80,96},{96,112},{112,64},{1... | collective-permute-start | bytes 208904 | tf_op jit(solution)/shard_map/ppermute | solution.py:30
  63.1 4.3 %collective-permute-start.20 = (f32[136,128]{1,0:T(8,128)S(1)}, f32[136,128]{1,0:T(8,128)S(1)}, u32[]{:S(2)}, u32[]{:S(2)}) collective-permute-start(f32[136,128]{1,0:T(8,128)S(1)} %get-tuple-element.48), channel_id=1, source_target_pairs={{0,32},{16,48},{32,0},{48,16},{64,96},{80,112},{96,64},{112,80},{1... | collective-permute-start | bytes 208904 | tf_op jit(solution)/shard_map/ppermute | solution.py:30
  67.3 0.0 collective-permute-done.12.refs_1_
  67.3 2.6 %collective-permute-start.21 = (f32[136,128]{1,0:T(8,128)S(1)}, f32[136,128]{1,0:T(8,128)S(1)}, u32[]{:S(2)}, u32[]{:S(2)}) collective-permute-start(f32[136,128]{1,0:T(8,128)S(1)} %get-tuple-element.49), channel_id=1, source_target_pairs={{0,48},{16,0},{32,16},{48,32},{64,112},{80,64},{96,80},{112,96},{1... | collective-permute-start | bytes 208904 | tf_op jit(solution)/shard_map/ppermute | solution.py:30
  69.9 0.1 shard_map.79
  70.0 0.1 collective-permute-start.15
  70.1 1.1 %collective-permute-done.20.refs_4_ = f32[136,128]{1,0:T(8,128)S(1)} collective-permute-done((f32[136,128]{1,0:T(8,128)S(1)}, f32[136,128]{1,0:T(8,128)S(1)}, u32[]{:S(2)}, u32[]{:S(2)}) %collective-permute-start.20) | collective-permute-done | bytes 69664 | tf_op jit(solution)/shard_map/ppermute | solution.py:30
  71.2 3.9 %collective-permute-done.21.refs_5_ = f32[136,128]{1,0:T(8,128)S(1)} collective-permute-done((f32[136,128]{1,0:T(8,128)S(1)}, f32[136,128]{1,0:T(8,128)S(1)}, u32[]{:S(2)}, u32[]{:S(2)}) %collective-permute-start.21) | collective-permute-done | bytes 69664 | tf_op jit(solution)/shard_map/ppermute | solution.py:30
  75.1 0.4 collective-permute-done.15.refs_1_
  75.5 0.8 %shard_map.85 = (f32[128,128]{1,0:T(8,128)}, f32[2,128]{1,0:T(2,128)}, f32[128,128]{1,0:T(8,128)}, f32[2,128]{1,0:T(2,128)}) custom-call(f32[136,128]{1,0:T(8,128)S(1)} %get-tuple-element.40.refs_0_, f32[136,128]{1,0:T(8,128)S(1)} %collective-permute-done.15.refs_1_, f32[136,128]{1,0:T(8,128)S(1)} %get-tuple-element.46.refs_2_, ...), custom_call_target="tpu_custom_call" | custom-call | bytes 550912 | tf_op jit(solution)/shard_map/pallas_call | solution.py:223
  (14 shorter events, 0.1 us)
Async XLA Ops:
  2.3 12.1 %collective-permute-start = (bf16[128,256]{1,0:T(8,128)(2,1)}, bf16[128,256]{1,0:T(8,128)(2,1)S(1)}, u32[]{:S(2)}, u32[]{:S(2)}) collective-permute-start(bf16[128,256]{1,0:T(8,128)(2,1)} %get-tuple-element.27), channel_id=1, source_target_pairs={{0,2},{1,3},{2,0},{3,1},{4,6},{5,7},{6,4},{7,5},{8,10},{9,11},{10,... | collective-permute-start | bytes 196616 | tf_op jit(solution)/shard_map/ppermute | solution.py:34
  4.9 10.5 %collective-permute-start.3 = (bf16[128,256]{1,0:T(8,128)(2,1)}, bf16[128,256]{1,0:T(8,128)(2,1)S(1)}, u32[]{:S(2)}, u32[]{:S(2)}) collective-permute-start(bf16[128,256]{1,0:T(8,128)(2,1)} %get-tuple-element.28), channel_id=1, source_target_pairs={{0,16},{16,32},{32,48},{48,0},{64,80},{80,96},{96,112},{112,64},{1... | collective-permute-start | bytes 196616 | tf_op jit(solution)/shard_map/ppermute | solution.py:30
  7.9 9.4 %collective-permute-start.2 = (bf16[128,256]{1,0:T(8,128)(2,1)}, bf16[128,256]{1,0:T(8,128)(2,1)S(1)}, u32[]{:S(2)}, u32[]{:S(2)}) collective-permute-start(bf16[128,256]{1,0:T(8,128)(2,1)} %get-tuple-element.28), channel_id=1, source_target_pairs={{0,32},{16,48},{32,0},{48,16},{64,96},{80,112},{96,64},{112,80},{1... | collective-permute-start | bytes 196616 | tf_op jit(solution)/shard_map/ppermute | solution.py:30
  12.1 6.2 %collective-permute-start.1 = (bf16[128,256]{1,0:T(8,128)(2,1)}, bf16[128,256]{1,0:T(8,128)(2,1)S(1)}, u32[]{:S(2)}, u32[]{:S(2)}) collective-permute-start(bf16[128,256]{1,0:T(8,128)(2,1)} %get-tuple-element.28), channel_id=1, source_target_pairs={{0,48},{16,0},{32,16},{48,32},{64,112},{80,64},{96,80},{112,96},{1... | collective-permute-start | bytes 196616 | tf_op jit(solution)/shard_map/ppermute | solution.py:30
  14.5 3.8 %copy-start = (bf16[128,256]{1,0:T(8,128)(2,1)S(1)}, bf16[128,256]{1,0:T(8,128)(2,1)}, u32[]{:S(2)}) copy-start(bf16[128,256]{1,0:T(8,128)(2,1)} %get-tuple-element.28) | copy-start | bytes 196612
  18.3 8.7 %collective-permute-start.6 = (bf16[2,128,256]{2,1,0:T(8,128)(2,1)S(1)}, bf16[2,128,256]{2,1,0:T(8,128)(2,1)S(1)}, u32[]{:S(2)}, u32[]{:S(2)}) collective-permute-start(bf16[2,128,256]{2,1,0:T(8,128)(2,1)S(1)} %pad_maximum_fusion.2), channel_id=1, source_target_pairs={{0,4},{1,5},{2,6},{3,7},{4,8},{5,9},{6,10},{7,11},{8,12},{9,13},{1... | collective-permute-start | bytes 393224 | tf_op jit(solution)/shard_map/ppermute | solution.py:25
  19.6 11.3 %collective-permute-start.9 = (bf16[4,128,256]{2,1,0:T(8,128)(2,1)S(1)}, bf16[4,128,256]{2,1,0:T(8,128)(2,1)S(1)}, u32[]{:S(2)}, u32[]{:S(2)}) collective-permute-start(bf16[4,128,256]{2,1,0:T(8,128)(2,1)S(1)} %pad_maximum_fusion.1.refs_2_.refs_4_), channel_id=1, source_target_pairs={{0,64},{16,80},{32,96},{48,112},{64,128},{80,144},{96,160},{112,17... | collective-permute-start | bytes 786440 | tf_op jit(solution)/shard_map/ppermute | solution.py:25
  20.9 12.5 %collective-permute-start.8 = (bf16[4,128,256]{2,1,0:T(8,128)(2,1)S(1)}, bf16[4,128,256]{2,1,0:T(8,128)(2,1)S(1)}, u32[]{:S(2)}, u32[]{:S(2)}) collective-permute-start(bf16[4,128,256]{2,1,0:T(8,128)(2,1)S(1)} %pad_maximum_fusion.1.refs_2_.refs_4_), channel_id=1, source_target_pairs={{0,128},{16,144},{32,160},{48,176},{64,192},{80,208},{96,224},{112... | collective-permute-start | bytes 786440 | tf_op jit(solution)/shard_map/ppermute | solution.py:25
  23.5 9.9 %collective-permute-start.7 = (bf16[4,128,256]{2,1,0:T(8,128)(2,1)S(1)}, bf16[4,128,256]{2,1,0:T(8,128)(2,1)S(1)}, u32[]{:S(2)}, u32[]{:S(2)}) collective-permute-start(bf16[4,128,256]{2,1,0:T(8,128)(2,1)S(1)} %pad_maximum_fusion.1.refs_2_.refs_4_), channel_id=1, source_target_pairs={{0,192},{16,208},{32,224},{48,240},{64,0},{80,16},{96,32},{112,48}... | collective-permute-start | bytes 786440 | tf_op jit(solution)/shard_map/ppermute | solution.py:25
  24.6 5.3 %collective-permute-start.5 = (bf16[2,128,256]{2,1,0:T(8,128)(2,1)S(1)}, bf16[2,128,256]{2,1,0:T(8,128)(2,1)S(1)}, u32[]{:S(2)}, u32[]{:S(2)}) collective-permute-start(bf16[2,128,256]{2,1,0:T(8,128)(2,1)S(1)} %pad_maximum_fusion.2), channel_id=1, source_target_pairs={{0,8},{1,9},{2,10},{3,11},{4,12},{5,13},{6,14},{7,15},{8,0},{9,1},... | collective-permute-start | bytes 393224 | tf_op jit(solution)/shard_map/ppermute | solution.py:25
  27.1 3.8 %collective-permute-start.4 = (bf16[2,128,256]{2,1,0:T(8,128)(2,1)S(1)}, bf16[2,128,256]{2,1,0:T(8,128)(2,1)S(1)}, u32[]{:S(2)}, u32[]{:S(2)}) collective-permute-start(bf16[2,128,256]{2,1,0:T(8,128)(2,1)S(1)} %pad_maximum_fusion.2), channel_id=1, source_target_pairs={{0,12},{1,13},{2,14},{3,15},{4,0},{5,1},{6,2},{7,3},{8,4},{9,5},{1... | collective-permute-start | bytes 393224 | tf_op jit(solution)/shard_map/ppermute | solution.py:25
  33.4 4.5 %collective-permute-start.10 = (bf16[2,4,128,256]{3,2,1,0:T(8,128)(2,1)S(1)}, bf16[2,4,128,256]{3,2,1,0:T(8,128)(2,1)S(1)}, u32[]{:S(2)}, u32[]{:S(2)}) collective-permute-start(bf16[2,4,128,256]{3,2,1,0:T(8,128)(2,1)S(1)} %pad_maximum_fusion), channel_id=1, source_target_pairs={{0,1},{1,0},{2,3},{3,2},{4,5},{5,4},{6,7},{7,6},{8,9},{9,8},{10,11... | collective-permute-start | bytes 1572872 | tf_op jit(solution)/shard_map/ppermute | solution.py:34
  40.8 14.5 %collective-permute-start.11 = (f32[2,136,512]{2,1,0:T(8,128)S(1)}, f32[2,136,512]{2,1,0:T(8,128)S(1)}, u32[]{:S(2)}, u32[]{:S(2)}) collective-permute-start(f32[2,136,512]{2,1,0:T(8,128)S(1)} %shard_map.76), channel_id=1, source_target_pairs={{0,1},{1,0},{2,3},{3,2},{4,5},{5,4},{6,7},{7,6},{8,9},{9,8},{10,11... | collective-permute-start | bytes 1671176 | tf_op jit(solution)/shard_map/ppermute | solution.py:34
  43.1 15.0 %collective-permute-start.16 = (f32[136,512]{1,0:T(8,128)S(1)}, f32[136,512]{1,0:T(8,128)S(1)}, u32[]{:S(2)}, u32[]{:S(2)}) collective-permute-start(f32[136,512]{1,0:T(8,128)S(1)} %shard_map.81), channel_id=1, source_target_pairs={{0,64},{16,80},{32,96},{48,112},{64,128},{80,144},{96,160},{112,17... | collective-permute-start | bytes 835592 | tf_op jit(solution)/shard_map/ppermute | solution.py:25
  47.3 12.7 %collective-permute-start.17 = (f32[136,512]{1,0:T(8,128)S(1)}, f32[136,512]{1,0:T(8,128)S(1)}, u32[]{:S(2)}, u32[]{:S(2)}) collective-permute-start(f32[136,512]{1,0:T(8,128)S(1)} %shard_map.82), channel_id=1, source_target_pairs={{0,128},{16,144},{32,160},{48,176},{64,192},{80,208},{96,224},{112... | collective-permute-start | bytes 835592 | tf_op jit(solution)/shard_map/ppermute | solution.py:25
  49.5 12.6 %collective-permute-start.18 = (f32[136,512]{1,0:T(8,128)S(1)}, f32[136,512]{1,0:T(8,128)S(1)}, u32[]{:S(2)}, u32[]{:S(2)}) collective-permute-start(f32[136,512]{1,0:T(8,128)S(1)} %shard_map.83), channel_id=1, source_target_pairs={{0,192},{16,208},{32,224},{48,240},{64,0},{80,16},{96,32},{112,48}... | collective-permute-start | bytes 835592 | tf_op jit(solution)/shard_map/ppermute | solution.py:25
  55.3 12.0 %collective-permute-start.12 = (f32[136,256]{1,0:T(8,128)S(1)}, f32[136,256]{1,0:T(8,128)S(1)}, u32[]{:S(2)}, u32[]{:S(2)}) collective-permute-start(f32[136,256]{1,0:T(8,128)S(1)} %get-tuple-element.37), channel_id=1, source_target_pairs={{0,4},{1,5},{2,6},{3,7},{4,8},{5,9},{6,10},{7,11},{8,12},{9,13},{1... | collective-permute-start | bytes 417800 | tf_op jit(solution)/shard_map/ppermute | solution.py:25
  56.6 13.2 %collective-permute-start.13 = (f32[136,256]{1,0:T(8,128)S(1)}, f32[136,256]{1,0:T(8,128)S(1)}, u32[]{:S(2)}, u32[]{:S(2)}) collective-permute-start(f32[136,256]{1,0:T(8,128)S(1)} %get-tuple-element.38), channel_id=1, source_target_pairs={{0,8},{1,9},{2,10},{3,11},{4,12},{5,13},{6,14},{7,15},{8,0},{9,1},... | collective-permute-start | bytes 417800 | tf_op jit(solution)/shard_map/ppermute | solution.py:25
  58.1 11.8 %collective-permute-start.14 = (f32[136,256]{1,0:T(8,128)S(1)}, f32[136,256]{1,0:T(8,128)S(1)}, u32[]{:S(2)}, u32[]{:S(2)}) collective-permute-start(f32[136,256]{1,0:T(8,128)S(1)} %get-tuple-element.39), channel_id=1, source_target_pairs={{0,12},{1,13},{2,14},{3,15},{4,0},{5,1},{6,2},{7,3},{8,4},{9,5},{1... | collective-permute-start | bytes 417800 | tf_op jit(solution)/shard_map/ppermute | solution.py:25
  62.2 7.9 %collective-permute-start.19 = (f32[136,128]{1,0:T(8,128)S(1)}, f32[136,128]{1,0:T(8,128)S(1)}, u32[]{:S(2)}, u32[]{:S(2)}) collective-permute-start(f32[136,128]{1,0:T(8,128)S(1)} %get-tuple-element.47), channel_id=1, source_target_pairs={{0,16},{16,32},{32,48},{48,0},{64,80},{80,96},{96,112},{112,64},{1... | collective-permute-start | bytes 208904 | tf_op jit(solution)/shard_map/ppermute | solution.py:30
  63.1 8.2 %collective-permute-start.20 = (f32[136,128]{1,0:T(8,128)S(1)}, f32[136,128]{1,0:T(8,128)S(1)}, u32[]{:S(2)}, u32[]{:S(2)}) collective-permute-start(f32[136,128]{1,0:T(8,128)S(1)} %get-tuple-element.48), channel_id=1, source_target_pairs={{0,32},{16,48},{32,0},{48,16},{64,96},{80,112},{96,64},{112,80},{1... | collective-permute-start | bytes 208904 | tf_op jit(solution)/shard_map/ppermute | solution.py:30
  67.3 7.8 %collective-permute-start.21 = (f32[136,128]{1,0:T(8,128)S(1)}, f32[136,128]{1,0:T(8,128)S(1)}, u32[]{:S(2)}, u32[]{:S(2)}) collective-permute-start(f32[136,128]{1,0:T(8,128)S(1)} %get-tuple-element.49), channel_id=1, source_target_pairs={{0,48},{16,0},{32,16},{48,32},{64,112},{80,64},{96,80},{112,96},{1... | collective-permute-start | bytes 208904 | tf_op jit(solution)/shard_map/ppermute | solution.py:30
  70.0 5.5 %collective-permute-start.15 = (f32[136,128]{1,0:T(8,128)S(1)}, f32[136,128]{1,0:T(8,128)S(1)}, u32[]{:S(2)}, u32[]{:S(2)}) collective-permute-start(f32[136,128]{1,0:T(8,128)S(1)} %get-tuple-element.41), channel_id=1, source_target_pairs={{0,2},{1,3},{2,0},{3,1},{4,6},{5,7},{6,4},{7,5},{8,10},{9,11},{10,... | collective-permute-start | bytes 208904 | tf_op jit(solution)/shard_map/ppermute | solution.py:34

commit v9 on v8

--- a/solution.py
+++ b/solution.py
@@ -152,11 +152,14 @@
     )
 
 
-def col_kernel(total, scale, *refs):
-    ones, two, out = refs[:SUB], refs[SUB], refs[SUB + 1]
-    query = jnp.concatenate([two[piece, :, :WIDTH] for piece in range(SUB)], axis=0)
+def col_kernel(total, scale, count, *refs):
+    ones, twos, outs = refs[:SUB], refs[SUB : SUB + count], refs[SUB + count :]
+    tiles = [
+        jnp.concatenate([two[piece, :, :WIDTH] for piece in range(SUB)], axis=0) for two in twos
+    ]
     blocks = [one_block(ones, slow, total) for slow in range(SUB)]
-    (out[...],) = attend(scale, [query], blocks)
+    for out, whole in zip(outs, attend(scale, tiles, blocks)):
+        out[...] = whole
 
 
 def row_kernel(total, scale, halves, *refs):
@@ -270,8 +273,10 @@
     other = fast_swap("col", one, 1)
     ones = [one[0], one[1], other[0], other[1]]
 
-    def col_scores(*refs):
-        col_kernel(total, scale, *refs)
+    def col_scores(*steps):
+        kernel = functools.partial(col_kernel, total, scale, len(steps))
+        args = (*ones, *(twos[step] for step in steps))
+        return call(kernel, [f32(ROWS, BLOCK)] * len(steps), args, work=len(steps) * work)
 
     def row_scores(ones, twos, halves, weight, *counts):
         shapes = [f32(count, ROWS, BLOCK) for count in counts]
@@ -290,16 +295,18 @@
 
     work = BLOCK * BLOCK * SUB
     cols = [None] * SUB
-    (keep_one,) = row_scores(ones[:2], twos, ((0, 0), (0, 1)), 2, 2)
+    mine = ones[:2]
+    cols[2], cols[3], cols[1] = col_scores(2, 3, 1)
+    ones, far = together((ones, cols[1:]))
+    (cols[0],) = col_scores(0)
+    cols = spread("row", [cols[0], *far])
     (send_one,) = row_scores(ones[2:], twos, ((0, 0), (0, 1)), 2, 2)
     theirs_one = fast_swap("col", send_one, 1)
-    ones, _ = together((ones, send_one))
-    for step in (1, 3, 2, 0):
-        (cols[step],) = call(col_scores, [f32(ROWS, BLOCK)], (*ones, twos[step]), work=work)
-    cols = spread("row", cols)
+    (keep_one,) = row_scores(ones[:2], twos, ((0, 0), (0, 1)), 2, 2)
+    cols = call(block_kernel, [f32(ROWS, SHARD)] * SUB, cols, work=40 * work)
+    theirs_one, cols = together((theirs_one, cols))
+    cols = [cols[0]] + [fast_shift("row", cols[step], step) for step in range(1, SUB)]
     rows = spread("col", core_merge(keep_one, theirs_one, 0, 1))
-    cols = call(block_kernel, [f32(ROWS, SHARD)] * SUB, cols, work=4 * work)
-    cols = [cols[0]] + [fast_shift("row", cols[step], step) for step in range(1, SUB)]
     keep, send = call(chip_kernel, [f32(ROWS, SHARD)] * 2, rows)
     theirs = fast_swap("col", send, 2)
     outs = [f32(SHARD, WIDTH), f32(2, SHARD)] * 2

time: 76.7 us -> 79.5 us (1.037); the launches traced: 76.2 us -> 78 us
  waiting for transfers between devices: 17.1 us -> 24.5 us
  starting transfers between devices: 42.6 us -> 37.7 us
  Pallas kernels: 14.8 us -> 13.9 us
    ppermute x12, waiting for transfers between devices: 7.25 us -> 15.1 us  [slow_shift(): return lax.ppermute(value, axis, pairs)]
    ppermute x12, starting transfers between devices: 19 us -> 15.1 us  [slow_shift(): return lax.ppermute(value, axis, pairs)]
    ppermute x6, waiting for transfers between devices: 7.91 us -> 6.22 us  [fast_shift(): return lax.ppermute(value, axis, pairs)]
    ppermute x4, waiting for transfers between devices: 1.93 us -> 3.21 us  [fast_swap(): return lax.ppermute(value, axis, [(i, i ^ step) for i in range(SUB * SUB)])]
    ppermute x4, starting transfers between devices: 6.31 us -> 5.11 us  [fast_swap(): return lax.ppermute(value, axis, [(i, i ^ step) for i in range(SUB * SUB)])]
    pallas_call x11 -> x9, Pallas kernels: 14.8 us -> 13.9 us  [call(): pl.pallas_call(kernel, out_shape=shapes, in_specs=specs or [VMEM] * len(a...]
  transfers between devices with their start and end apart: 22 -> 22, of which waited for: 10 -> 11; matrix products, arithmetic and copies ran while one was open for 1% -> 1% of each run, Pallas kernels for 12% -> 9%
where the time goes in v9:
time: 79.5 us; the launch traced here: 78 us
  starting transfers between devices  37.7 us (47%)
  waiting for transfers between devices  24.5 us (31%)
  Pallas kernels  13.9 us (17%)
  other arithmetic  0.99 us (1%)
    ppermute x6, starting transfers between devices, fast_shift(): return lax.ppermute(value, axis, pairs)  17.5 us
    ppermute x12, waiting for transfers between devices, slow_shift(): return lax.ppermute(value, axis, pairs)  15.1 us
    ppermute x12, starting transfers between devices, slow_shift(): return lax.ppermute(value, axis, pairs)  15.1 us
    pallas_call x9, Pallas kernels, call(): pl.pallas_call(kernel, out_shape=shapes, in_specs=specs or [VMEM] * len(a...  13.9 us
    ppermute x6, waiting for transfers between devices, fast_shift(): return lax.ppermute(value, axis, pairs)  6.22 us
    ppermute x4, starting transfers between devices, fast_swap(): return lax.ppermute(value, axis, [(i, i ^ step) for i in range(SUB * SUB)])  5.11 us
    ppermute x4, waiting for transfers between devices, fast_swap(): return lax.ppermute(value, axis, [(i, i ^ step) for i in range(SUB * SUB)])  3.21 us
  transfers between devices with their start and end apart: 22, of which 11 were waited for; matrix products, arithmetic and copies ran while one was open for 1% of the time, Pallas kernels for 9%

profile of v9, /device:TPU:1, one launch (start us, length us, event | category | flops | bytes accessed | tf_op | source)
XLA Modules:
  0.0 78.0 jit_solution(3150382596073990305)
XLA Ops:
  0.6 1.7 %shard_map.75 = (bf16[128,256]{1,0:T(8,128)(2,1)}, bf16[128,256]{1,0:T(8,128)(2,1)}) custom-call(bf16[128,128]{1,0:T(8,128)(2,1)} %feat_one.1, bf16[128,128]{1,0:T(8,128)(2,1)} %value_one.1, bf16[128,128]{1,0:T(8,128)(2,1)} %feat_two.1, bf16[128,128]{1,0:T(8,128)(2,1)} %value_two.1), custom_call_target="tpu_custom_call" | custom-call | bytes 262144 | tf_op jit(solution)/shard_map/pallas_call | solution.py:226
  2.3 2.6 %collective-permute-start = (bf16[128,256]{1,0:T(8,128)(2,1)}, bf16[128,256]{1,0:T(8,128)(2,1)S(1)}, u32[]{:S(2)}, u32[]{:S(2)}) collective-permute-start(bf16[128,256]{1,0:T(8,128)(2,1)} %get-tuple-element.38), channel_id=1, source_target_pairs={{0,2},{1,3},{2,0},{3,1},{4,6},{5,7},{6,4},{7,5},{8,10},{9,11},{10,... | collective-permute-start | bytes 196616 | tf_op jit(solution)/shard_map/ppermute | solution.py:34
  4.9 5.1 %collective-permute-start.1 = (bf16[128,256]{1,0:T(8,128)(2,1)}, bf16[128,256]{1,0:T(8,128)(2,1)S(1)}, u32[]{:S(2)}, u32[]{:S(2)}) collective-permute-start(bf16[128,256]{1,0:T(8,128)(2,1)} %get-tuple-element.39), channel_id=1, source_target_pairs={{0,48},{16,0},{32,16},{48,32},{64,112},{80,64},{96,80},{112,96},{1... | collective-permute-start | bytes 196616 | tf_op jit(solution)/shard_map/ppermute | solution.py:30
  10.0 1.2 %collective-permute-start.2 = (bf16[128,256]{1,0:T(8,128)(2,1)}, bf16[128,256]{1,0:T(8,128)(2,1)S(1)}, u32[]{:S(2)}, u32[]{:S(2)}) collective-permute-start(bf16[128,256]{1,0:T(8,128)(2,1)} %get-tuple-element.39), channel_id=1, source_target_pairs={{0,32},{16,48},{32,0},{48,16},{64,96},{80,112},{96,64},{112,80},{1... | collective-permute-start | bytes 196616 | tf_op jit(solution)/shard_map/ppermute | solution.py:30
  11.2 2.1 %collective-permute-start.3 = (bf16[128,256]{1,0:T(8,128)(2,1)}, bf16[128,256]{1,0:T(8,128)(2,1)S(1)}, u32[]{:S(2)}, u32[]{:S(2)}) collective-permute-start(bf16[128,256]{1,0:T(8,128)(2,1)} %get-tuple-element.39), channel_id=1, source_target_pairs={{0,16},{16,32},{32,48},{48,0},{64,80},{80,96},{96,112},{112,64},{1... | collective-permute-start | bytes 196616 | tf_op jit(solution)/shard_map/ppermute | solution.py:30
  13.3 0.0 collective-permute-done
  13.3 0.9 %pad_maximum_fusion.2 = bf16[2,128,256]{2,1,0:T(8,128)(2,1)S(1)} fusion(bf16[1,128,256]{2,1,0:T(8,128)(2,1)S(1)} %bitcast.29, bf16[1,128,256]{2,1,0:T(8,128)(2,1)} %bitcast.28), kind=kLoop, calls=%fused_computation.6 | loop fusion | flops 65536 | bytes 262144 | tf_op jit(solution)/shard_map/stack | solution.py:269
  14.1 0.0 collective-permute-done.1
  14.2 3.3 %collective-permute-done.2 = bf16[128,256]{1,0:T(8,128)(2,1)S(1)} collective-permute-done((bf16[128,256]{1,0:T(8,128)(2,1)}, bf16[128,256]{1,0:T(8,128)(2,1)S(1)}, u32[]{:S(2)}, u32[]{:S(2)}) %collective-permute-start.2) | collective-permute-done | bytes 65568 | tf_op jit(solution)/shard_map/ppermute | solution.py:30
  17.5 0.4 collective-permute-done.3
  18.0 2.8 %collective-permute-start.5 = (bf16[2,128,256]{2,1,0:T(8,128)(2,1)S(1)}, bf16[2,128,256]{2,1,0:T(8,128)(2,1)S(1)}, u32[]{:S(2)}, u32[]{:S(2)}) collective-permute-start(bf16[2,128,256]{2,1,0:T(8,128)(2,1)S(1)} %pad_maximum_fusion.2), channel_id=1, source_target_pairs={{0,8},{1,9},{2,10},{3,11},{4,12},{5,13},{6,14},{7,15},{8,0},{9,1},... | collective-permute-start | bytes 393224 | tf_op jit(solution)/shard_map/ppermute | solution.py:25
  20.8 2.7 %collective-permute-start.7 = (bf16[4,128,256]{2,1,0:T(8,128)(2,1)S(1)}, bf16[4,128,256]{2,1,0:T(8,128)(2,1)S(1)}, u32[]{:S(2)}, u32[]{:S(2)}) collective-permute-start(bf16[4,128,256]{2,1,0:T(8,128)(2,1)S(1)} %pad_maximum_fusion.1.refs_2_.refs_4_), channel_id=1, source_target_pairs={{0,192},{16,208},{32,224},{48,240},{64,0},{80,16},{96,32},{112,48}... | collective-permute-start | bytes 786440 | tf_op jit(solution)/shard_map/ppermute | solution.py:25
  23.5 0.3 collective-permute-start.8
  23.9 0.7 collective-permute-start.9
  24.6 0.3 collective-permute-start.6
  24.9 2.4 %collective-permute-start.4 = (bf16[2,128,256]{2,1,0:T(8,128)(2,1)S(1)}, bf16[2,128,256]{2,1,0:T(8,128)(2,1)S(1)}, u32[]{:S(2)}, u32[]{:S(2)}) collective-permute-start(bf16[2,128,256]{2,1,0:T(8,128)(2,1)S(1)} %pad_maximum_fusion.2), channel_id=1, source_target_pairs={{0,12},{1,13},{2,14},{3,15},{4,0},{5,1},{6,2},{7,3},{8,4},{9,5},{1... | collective-permute-start | bytes 393224 | tf_op jit(solution)/shard_map/ppermute | solution.py:25
  27.2 2.3 %collective-permute-done.6 = bf16[2,128,256]{2,1,0:T(8,128)(2,1)S(1)} collective-permute-done((bf16[2,128,256]{2,1,0:T(8,128)(2,1)S(1)}, bf16[2,128,256]{2,1,0:T(8,128)(2,1)S(1)}, u32[]{:S(2)}, u32[]{:S(2)}) %collective-permute-start.6) | collective-permute-done | bytes 131104 | tf_op jit(solution)/shard_map/ppermute | solution.py:25
  29.6 0.1 pad_maximum_fusion
  29.7 0.3 collective-permute-done.7.refs_6_.refs_3_
  29.9 0.4 collective-permute-done.8.refs_4_
  30.4 7.6 %collective-permute-done.9.refs_5_ = bf16[4,128,256]{2,1,0:T(8,128)(2,1)S(1)} collective-permute-done((bf16[4,128,256]{2,1,0:T(8,128)(2,1)S(1)}, bf16[4,128,256]{2,1,0:T(8,128)(2,1)S(1)}, u32[]{:S(2)}, u32[]{:S(2)}) %collective-permute-start.9) | collective-permute-done | bytes 262176 | tf_op jit(solution)/shard_map/ppermute | solution.py:25
  37.9 1.4 %collective-permute-start.10 = (bf16[2,4,128,256]{3,2,1,0:T(8,128)(2,1)S(1)}, bf16[2,4,128,256]{3,2,1,0:T(8,128)(2,1)S(1)}, u32[]{:S(2)}, u32[]{:S(2)}) collective-permute-start(bf16[2,4,128,256]{3,2,1,0:T(8,128)(2,1)S(1)} %pad_maximum_fusion), channel_id=1, source_target_pairs={{0,1},{1,0},{2,3},{3,2},{4,5},{5,4},{6,7},{7,6},{8,9},{9,8},{10,11... | collective-permute-start | bytes 1572872 | tf_op jit(solution)/shard_map/ppermute | solution.py:34
  39.4 1.5 %collective-permute-done.10 = bf16[2,4,128,256]{3,2,1,0:T(8,128)(2,1)S(1)} collective-permute-done((bf16[2,4,128,256]{3,2,1,0:T(8,128)(2,1)S(1)}, bf16[2,4,128,256]{3,2,1,0:T(8,128)(2,1)S(1)}, u32[]{:S(2)}, u32[]{:S(2)}) %collective-permute-start.10) | collective-permute-done | bytes 524320 | tf_op jit(solution)/shard_map/ppermute | solution.py:34
  40.9 4.0 %shard_map.76 = (f32[136,512]{1,0:T(8,128)S(1)}, f32[136,512]{1,0:T(8,128)S(1)}, f32[136,512]{1,0:T(8,128)S(1)}) custom-call(bf16[4,128,256]{2,1,0:T(8,128)(2,1)S(1)} %get-tuple-element.52.refs_0_, bf16[4,128,256]{2,1,0:T(8,128)(2,1)S(1)} %get-tuple-element.53.refs_1_, bf16[4,128,256]{2,1,0:T(8,128)(2,1)S(1)} %get-tuple-element.49.refs_2_.refs_0_, ...), custom_call_target="tpu_custom_call" | custom-call | flops 1610612736 | bytes 2670592 | tf_op jit(solution)/shard_map/pallas_call | solution.py:226
  44.9 0.3 collective-permute-start.12
  45.2 1.5 %collective-permute-start.13 = (f32[136,512]{1,0:T(8,128)S(1)}, f32[136,512]{1,0:T(8,128)S(1)}, u32[]{:S(2)}, u32[]{:S(2)}) collective-permute-start(f32[136,512]{1,0:T(8,128)S(1)} %get-tuple-element.55), channel_id=1, source_target_pairs={{0,128},{16,144},{32,160},{48,176},{64,192},{80,208},{96,224},{112... | collective-permute-start | bytes 835592 | tf_op jit(solution)/shard_map/ppermute | solution.py:25
  46.7 1.2 %collective-permute-start.14 = (f32[136,512]{1,0:T(8,128)S(1)}, f32[136,512]{1,0:T(8,128)S(1)}, u32[]{:S(2)}, u32[]{:S(2)}) collective-permute-start(f32[136,512]{1,0:T(8,128)S(1)} %get-tuple-element.56), channel_id=1, source_target_pairs={{0,192},{16,208},{32,224},{48,240},{64,0},{80,16},{96,32},{112,48}... | collective-permute-start | bytes 835592 | tf_op jit(solution)/shard_map/ppermute | solution.py:25
  47.8 2.8 %shard_map.77 = f32[2,136,512]{2,1,0:T(8,128)S(1)} custom-call(bf16[4,128,256]{2,1,0:T(8,128)(2,1)S(1)} %get-tuple-element.49.refs_2_.refs_0_, bf16[4,128,256]{2,1,0:T(8,128)(2,1)S(1)} %get-tuple-element.50.refs_3_.refs_1_, bf16[4,128,256]{2,1,0:T(8,128)(2,1)S(1)} %pad_maximum_fusion.1.refs_2_.refs_4_, ...), custom_call_target="tpu_custom_call" | custom-call | flops 1073741824 | bytes 2129920 | tf_op jit(solution)/shard_map/pallas_call | solution.py:226
  50.6 1.0 %collective-permute-start.11 = (f32[2,136,512]{2,1,0:T(8,128)S(1)}, f32[2,136,512]{2,1,0:T(8,128)S(1)}, u32[]{:S(2)}, u32[]{:S(2)}) collective-permute-start(f32[2,136,512]{2,1,0:T(8,128)S(1)} %shard_map.77), channel_id=1, source_target_pairs={{0,1},{1,0},{2,3},{3,2},{4,5},{5,4},{6,7},{7,6},{8,9},{9,8},{10,11... | collective-permute-start | bytes 1671176 | tf_op jit(solution)/shard_map/ppermute | solution.py:34
  51.7 1.6 %shard_map.78.refs_0_ = f32[136,512]{1,0:T(8,128)S(1)} custom-call(bf16[4,128,256]{2,1,0:T(8,128)(2,1)S(1)} %get-tuple-element.52.refs_0_, bf16[4,128,256]{2,1,0:T(8,128)(2,1)S(1)} %get-tuple-element.53.refs_1_, bf16[4,128,256]{2,1,0:T(8,128)(2,1)S(1)} %get-tuple-element.49.refs_2_.refs_0_, bf16[4,128,256]{2,1,0:T(8,128)(2,1)S(1)} %get-tuple-element.50.refs_3_.refs_1_, ...), custom_call_target="tpu_custom_call" | custom-call | flops 536870912 | bytes 1589248 | tf_op jit(solution)/shard_map/pallas_call | solution.py:226
  53.3 2.8 %shard_map.80.refs_1_ = f32[2,136,512]{2,1,0:T(8,128)S(1)} custom-call(bf16[4,128,256]{2,1,0:T(8,128)(2,1)S(1)} %get-tuple-element.52.refs_0_, bf16[4,128,256]{2,1,0:T(8,128)(2,1)S(1)} %get-tuple-element.53.refs_1_, bf16[4,128,256]{2,1,0:T(8,128)(2,1)S(1)} %pad_maximum_fusion.1.refs_2_.refs_4_, ...), custom_call_target="tpu_custom_call" | custom-call | flops 1073741824 | bytes 2129920 | tf_op jit(solution)/shard_map/pallas_call | solution.py:226
  56.1 4.1 %collective-permute-done.12.refs_1_ = f32[136,512]{1,0:T(8,128)S(1)} collective-permute-done((f32[136,512]{1,0:T(8,128)S(1)}, f32[136,512]{1,0:T(8,128)S(1)}, u32[]{:S(2)}, u32[]{:S(2)}) %collective-permute-start.12) | collective-permute-done | bytes 278560 | tf_op jit(solution)/shard_map/ppermute | solution.py:25
  60.2 0.0 collective-permute-done.13.refs_2_
  60.2 0.3 collective-permute-done.14.refs_3_
  60.6 0.1 shard_map.79
  60.7 0.0 collective-permute-done.11.refs_0_
  60.7 0.1 shard_map.81
  60.8 0.4 collective-permute-start.15
  61.2 1.7 %collective-permute-start.16 = (f32[136,256]{1,0:T(8,128)S(1)}, f32[136,256]{1,0:T(8,128)S(1)}, u32[]{:S(2)}, u32[]{:S(2)}) collective-permute-start(f32[136,256]{1,0:T(8,128)S(1)} %get-tuple-element.64), channel_id=1, source_target_pairs={{0,8},{1,9},{2,10},{3,11},{4,12},{5,13},{6,14},{7,15},{8,0},{9,1},... | collective-permute-start | bytes 417800 | tf_op jit(solution)/shard_map/ppermute | solution.py:25
  62.9 0.8 collective-permute-start.17
  63.7 0.9 %collective-permute-start.19 = (f32[136,128]{1,0:T(8,128)S(1)}, f32[136,128]{1,0:T(8,128)S(1)}, u32[]{:S(2)}, u32[]{:S(2)}) collective-permute-start(f32[136,128]{1,0:T(8,128)S(1)} %get-tuple-element.69), channel_id=1, source_target_pairs={{0,16},{16,32},{32,48},{48,0},{64,80},{80,96},{96,112},{112,64},{1... | collective-permute-start | bytes 208904 | tf_op jit(solution)/shard_map/ppermute | solution.py:30
  64.6 4.7 %collective-permute-start.20 = (f32[136,128]{1,0:T(8,128)S(1)}, f32[136,128]{1,0:T(8,128)S(1)}, u32[]{:S(2)}, u32[]{:S(2)}) collective-permute-start(f32[136,128]{1,0:T(8,128)S(1)} %get-tuple-element.70), channel_id=1, source_target_pairs={{0,32},{16,48},{32,0},{48,16},{64,96},{80,112},{96,64},{112,80},{1... | collective-permute-start | bytes 208904 | tf_op jit(solution)/shard_map/ppermute | solution.py:30
  69.3 3.6 %collective-permute-start.21 = (f32[136,128]{1,0:T(8,128)S(1)}, f32[136,128]{1,0:T(8,128)S(1)}, u32[]{:S(2)}, u32[]{:S(2)}) collective-permute-start(f32[136,128]{1,0:T(8,128)S(1)} %get-tuple-element.71), channel_id=1, source_target_pairs={{0,48},{16,0},{32,16},{48,32},{64,112},{80,64},{96,80},{112,96},{1... | collective-permute-start | bytes 208904 | tf_op jit(solution)/shard_map/ppermute | solution.py:30
  72.9 0.1 shard_map.82
  72.9 0.1 collective-permute-start.18
  73.1 2.5 %collective-permute-done.21.refs_5_ = f32[136,128]{1,0:T(8,128)S(1)} collective-permute-done((f32[136,128]{1,0:T(8,128)S(1)}, f32[136,128]{1,0:T(8,128)S(1)}, u32[]{:S(2)}, u32[]{:S(2)}) %collective-permute-start.21) | collective-permute-done | bytes 69664 | tf_op jit(solution)/shard_map/ppermute | solution.py:30
  75.5 1.7 %collective-permute-done.18.refs_1_ = f32[136,128]{1,0:T(8,128)S(1)} collective-permute-done((f32[136,128]{1,0:T(8,128)S(1)}, f32[136,128]{1,0:T(8,128)S(1)}, u32[]{:S(2)}, u32[]{:S(2)}) %collective-permute-start.18) | collective-permute-done | bytes 69664 | tf_op jit(solution)/shard_map/ppermute | solution.py:34
  77.2 0.8 %shard_map.83 = (f32[128,128]{1,0:T(8,128)}, f32[2,128]{1,0:T(2,128)}, f32[128,128]{1,0:T(8,128)}, f32[2,128]{1,0:T(2,128)}) custom-call(f32[136,128]{1,0:T(8,128)S(1)} %get-tuple-element.66.refs_0_, f32[136,128]{1,0:T(8,128)S(1)} %collective-permute-done.18.refs_1_, f32[136,128]{1,0:T(8,128)S(1)} %get-tuple-element.68.refs_2_, ...), custom_call_target="tpu_custom_call" | custom-call | bytes 550912 | tf_op jit(solution)/shard_map/pallas_call | solution.py:226
  (12 shorter events, 0.1 us)
Async XLA Ops:
  2.3 10.9 %collective-permute-start = (bf16[128,256]{1,0:T(8,128)(2,1)}, bf16[128,256]{1,0:T(8,128)(2,1)S(1)}, u32[]{:S(2)}, u32[]{:S(2)}) collective-permute-start(bf16[128,256]{1,0:T(8,128)(2,1)} %get-tuple-element.38), channel_id=1, source_target_pairs={{0,2},{1,3},{2,0},{3,1},{4,6},{5,7},{6,4},{7,5},{8,10},{9,11},{10,... | collective-permute-start | bytes 196616 | tf_op jit(solution)/shard_map/ppermute | solution.py:34
  4.9 9.3 %collective-permute-start.1 = (bf16[128,256]{1,0:T(8,128)(2,1)}, bf16[128,256]{1,0:T(8,128)(2,1)S(1)}, u32[]{:S(2)}, u32[]{:S(2)}) collective-permute-start(bf16[128,256]{1,0:T(8,128)(2,1)} %get-tuple-element.39), channel_id=1, source_target_pairs={{0,48},{16,0},{32,16},{48,32},{64,112},{80,64},{96,80},{112,96},{1... | collective-permute-start | bytes 196616 | tf_op jit(solution)/shard_map/ppermute | solution.py:30
  10.0 7.5 %collective-permute-start.2 = (bf16[128,256]{1,0:T(8,128)(2,1)}, bf16[128,256]{1,0:T(8,128)(2,1)S(1)}, u32[]{:S(2)}, u32[]{:S(2)}) collective-permute-start(bf16[128,256]{1,0:T(8,128)(2,1)} %get-tuple-element.39), channel_id=1, source_target_pairs={{0,32},{16,48},{32,0},{48,16},{64,96},{80,112},{96,64},{112,80},{1... | collective-permute-start | bytes 196616 | tf_op jit(solution)/shard_map/ppermute | solution.py:30
  11.2 6.8 %collective-permute-start.3 = (bf16[128,256]{1,0:T(8,128)(2,1)}, bf16[128,256]{1,0:T(8,128)(2,1)S(1)}, u32[]{:S(2)}, u32[]{:S(2)}) collective-permute-start(bf16[128,256]{1,0:T(8,128)(2,1)} %get-tuple-element.39), channel_id=1, source_target_pairs={{0,16},{16,32},{32,48},{48,0},{64,80},{80,96},{96,112},{112,64},{1... | collective-permute-start | bytes 196616 | tf_op jit(solution)/shard_map/ppermute | solution.py:30
  13.3 4.7 %copy-start = (bf16[128,256]{1,0:T(8,128)(2,1)S(1)}, bf16[128,256]{1,0:T(8,128)(2,1)}, u32[]{:S(2)}) copy-start(bf16[128,256]{1,0:T(8,128)(2,1)} %get-tuple-element.39) | copy-start | bytes 196612
  18.0 6.9 %collective-permute-start.5 = (bf16[2,128,256]{2,1,0:T(8,128)(2,1)S(1)}, bf16[2,128,256]{2,1,0:T(8,128)(2,1)S(1)}, u32[]{:S(2)}, u32[]{:S(2)}) collective-permute-start(bf16[2,128,256]{2,1,0:T(8,128)(2,1)S(1)} %pad_maximum_fusion.2), channel_id=1, source_target_pairs={{0,8},{1,9},{2,10},{3,11},{4,12},{5,13},{6,14},{7,15},{8,0},{9,1},... | collective-permute-start | bytes 393224 | tf_op jit(solution)/shard_map/ppermute | solution.py:25
  20.8 9.1 %collective-permute-start.7 = (bf16[4,128,256]{2,1,0:T(8,128)(2,1)S(1)}, bf16[4,128,256]{2,1,0:T(8,128)(2,1)S(1)}, u32[]{:S(2)}, u32[]{:S(2)}) collective-permute-start(bf16[4,128,256]{2,1,0:T(8,128)(2,1)S(1)} %pad_maximum_fusion.1.refs_2_.refs_4_), channel_id=1, source_target_pairs={{0,192},{16,208},{32,224},{48,240},{64,0},{80,16},{96,32},{112,48}... | collective-permute-start | bytes 786440 | tf_op jit(solution)/shard_map/ppermute | solution.py:25
  23.5 6.8 %collective-permute-start.8 = (bf16[4,128,256]{2,1,0:T(8,128)(2,1)S(1)}, bf16[4,128,256]{2,1,0:T(8,128)(2,1)S(1)}, u32[]{:S(2)}, u32[]{:S(2)}) collective-permute-start(bf16[4,128,256]{2,1,0:T(8,128)(2,1)S(1)} %pad_maximum_fusion.1.refs_2_.refs_4_), channel_id=1, source_target_pairs={{0,128},{16,144},{32,160},{48,176},{64,192},{80,208},{96,224},{112... | collective-permute-start | bytes 786440 | tf_op jit(solution)/shard_map/ppermute | solution.py:25
  23.9 14.1 %collective-permute-start.9 = (bf16[4,128,256]{2,1,0:T(8,128)(2,1)S(1)}, bf16[4,128,256]{2,1,0:T(8,128)(2,1)S(1)}, u32[]{:S(2)}, u32[]{:S(2)}) collective-permute-start(bf16[4,128,256]{2,1,0:T(8,128)(2,1)S(1)} %pad_maximum_fusion.1.refs_2_.refs_4_), channel_id=1, source_target_pairs={{0,64},{16,80},{32,96},{48,112},{64,128},{80,144},{96,160},{112,17... | collective-permute-start | bytes 786440 | tf_op jit(solution)/shard_map/ppermute | solution.py:25
  24.6 5.0 %collective-permute-start.6 = (bf16[2,128,256]{2,1,0:T(8,128)(2,1)S(1)}, bf16[2,128,256]{2,1,0:T(8,128)(2,1)S(1)}, u32[]{:S(2)}, u32[]{:S(2)}) collective-permute-start(bf16[2,128,256]{2,1,0:T(8,128)(2,1)S(1)} %pad_maximum_fusion.2), channel_id=1, source_target_pairs={{0,4},{1,5},{2,6},{3,7},{4,8},{5,9},{6,10},{7,11},{8,12},{9,13},{1... | collective-permute-start | bytes 393224 | tf_op jit(solution)/shard_map/ppermute | solution.py:25
  24.9 4.7 %collective-permute-start.4 = (bf16[2,128,256]{2,1,0:T(8,128)(2,1)S(1)}, bf16[2,128,256]{2,1,0:T(8,128)(2,1)S(1)}, u32[]{:S(2)}, u32[]{:S(2)}) collective-permute-start(bf16[2,128,256]{2,1,0:T(8,128)(2,1)S(1)} %pad_maximum_fusion.2), channel_id=1, source_target_pairs={{0,12},{1,13},{2,14},{3,15},{4,0},{5,1},{6,2},{7,3},{8,4},{9,5},{1... | collective-permute-start | bytes 393224 | tf_op jit(solution)/shard_map/ppermute | solution.py:25
  37.9 3.0 %collective-permute-start.10 = (bf16[2,4,128,256]{3,2,1,0:T(8,128)(2,1)S(1)}, bf16[2,4,128,256]{3,2,1,0:T(8,128)(2,1)S(1)}, u32[]{:S(2)}, u32[]{:S(2)}) collective-permute-start(bf16[2,4,128,256]{3,2,1,0:T(8,128)(2,1)S(1)} %pad_maximum_fusion), channel_id=1, source_target_pairs={{0,1},{1,0},{2,3},{3,2},{4,5},{5,4},{6,7},{7,6},{8,9},{9,8},{10,11... | collective-permute-start | bytes 1572872 | tf_op jit(solution)/shard_map/ppermute | solution.py:34
  44.9 15.3 %collective-permute-start.12 = (f32[136,512]{1,0:T(8,128)S(1)}, f32[136,512]{1,0:T(8,128)S(1)}, u32[]{:S(2)}, u32[]{:S(2)}) collective-permute-start(f32[136,512]{1,0:T(8,128)S(1)} %get-tuple-element.54), channel_id=1, source_target_pairs={{0,64},{16,80},{32,96},{48,112},{64,128},{80,144},{96,160},{112,17... | collective-permute-start | bytes 835592 | tf_op jit(solution)/shard_map/ppermute | solution.py:25
  45.2 15.0 %collective-permute-start.13 = (f32[136,512]{1,0:T(8,128)S(1)}, f32[136,512]{1,0:T(8,128)S(1)}, u32[]{:S(2)}, u32[]{:S(2)}) collective-permute-start(f32[136,512]{1,0:T(8,128)S(1)} %get-tuple-element.55), channel_id=1, source_target_pairs={{0,128},{16,144},{32,160},{48,176},{64,192},{80,208},{96,224},{112... | collective-permute-start | bytes 835592 | tf_op jit(solution)/shard_map/ppermute | solution.py:25
  46.7 13.9 %collective-permute-start.14 = (f32[136,512]{1,0:T(8,128)S(1)}, f32[136,512]{1,0:T(8,128)S(1)}, u32[]{:S(2)}, u32[]{:S(2)}) collective-permute-start(f32[136,512]{1,0:T(8,128)S(1)} %get-tuple-element.56), channel_id=1, source_target_pairs={{0,192},{16,208},{32,224},{48,240},{64,0},{80,16},{96,32},{112,48}... | collective-permute-start | bytes 835592 | tf_op jit(solution)/shard_map/ppermute | solution.py:25
  50.6 10.1 %collective-permute-start.11 = (f32[2,136,512]{2,1,0:T(8,128)S(1)}, f32[2,136,512]{2,1,0:T(8,128)S(1)}, u32[]{:S(2)}, u32[]{:S(2)}) collective-permute-start(f32[2,136,512]{2,1,0:T(8,128)S(1)} %shard_map.77), channel_id=1, source_target_pairs={{0,1},{1,0},{2,3},{3,2},{4,5},{5,4},{6,7},{7,6},{8,9},{9,8},{10,11... | collective-permute-start | bytes 1671176 | tf_op jit(solution)/shard_map/ppermute | solution.py:34
  60.8 8.5 %collective-permute-start.15 = (f32[136,256]{1,0:T(8,128)S(1)}, f32[136,256]{1,0:T(8,128)S(1)}, u32[]{:S(2)}, u32[]{:S(2)}) collective-permute-start(f32[136,256]{1,0:T(8,128)S(1)} %get-tuple-element.63), channel_id=1, source_target_pairs={{0,4},{1,5},{2,6},{3,7},{4,8},{5,9},{6,10},{7,11},{8,12},{9,13},{1... | collective-permute-start | bytes 417800 | tf_op jit(solution)/shard_map/ppermute | solution.py:25
  61.2 11.7 %collective-permute-start.16 = (f32[136,256]{1,0:T(8,128)S(1)}, f32[136,256]{1,0:T(8,128)S(1)}, u32[]{:S(2)}, u32[]{:S(2)}) collective-permute-start(f32[136,256]{1,0:T(8,128)S(1)} %get-tuple-element.64), channel_id=1, source_target_pairs={{0,8},{1,9},{2,10},{3,11},{4,12},{5,13},{6,14},{7,15},{8,0},{9,1},... | collective-permute-start | bytes 417800 | tf_op jit(solution)/shard_map/ppermute | solution.py:25
  62.9 9.9 %collective-permute-start.17 = (f32[136,256]{1,0:T(8,128)S(1)}, f32[136,256]{1,0:T(8,128)S(1)}, u32[]{:S(2)}, u32[]{:S(2)}) collective-permute-start(f32[136,256]{1,0:T(8,128)S(1)} %get-tuple-element.65), channel_id=1, source_target_pairs={{0,12},{1,13},{2,14},{3,15},{4,0},{5,1},{6,2},{7,3},{8,4},{9,5},{1... | collective-permute-start | bytes 417800 | tf_op jit(solution)/shard_map/ppermute | solution.py:25
  63.7 9.4 %collective-permute-start.19 = (f32[136,128]{1,0:T(8,128)S(1)}, f32[136,128]{1,0:T(8,128)S(1)}, u32[]{:S(2)}, u32[]{:S(2)}) collective-permute-start(f32[136,128]{1,0:T(8,128)S(1)} %get-tuple-element.69), channel_id=1, source_target_pairs={{0,16},{16,32},{32,48},{48,0},{64,80},{80,96},{96,112},{112,64},{1... | collective-permute-start | bytes 208904 | tf_op jit(solution)/shard_map/ppermute | solution.py:30
  64.6 8.5 %collective-permute-start.20 = (f32[136,128]{1,0:T(8,128)S(1)}, f32[136,128]{1,0:T(8,128)S(1)}, u32[]{:S(2)}, u32[]{:S(2)}) collective-permute-start(f32[136,128]{1,0:T(8,128)S(1)} %get-tuple-element.70), channel_id=1, source_target_pairs={{0,32},{16,48},{32,0},{48,16},{64,96},{80,112},{96,64},{112,80},{1... | collective-permute-start | bytes 208904 | tf_op jit(solution)/shard_map/ppermute | solution.py:30
  69.3 6.2 %collective-permute-start.21 = (f32[136,128]{1,0:T(8,128)S(1)}, f32[136,128]{1,0:T(8,128)S(1)}, u32[]{:S(2)}, u32[]{:S(2)}) collective-permute-start(f32[136,128]{1,0:T(8,128)S(1)} %get-tuple-element.71), channel_id=1, source_target_pairs={{0,48},{16,0},{32,16},{48,32},{64,112},{80,64},{96,80},{112,96},{1... | collective-permute-start | bytes 208904 | tf_op jit(solution)/shard_map/ppermute | solution.py:30
  72.9 4.3 %collective-permute-start.18 = (f32[136,128]{1,0:T(8,128)S(1)}, f32[136,128]{1,0:T(8,128)S(1)}, u32[]{:S(2)}, u32[]{:S(2)}) collective-permute-start(f32[136,128]{1,0:T(8,128)S(1)} %get-tuple-element.67), channel_id=1, source_target_pairs={{0,2},{1,3},{2,0},{3,1},{4,6},{5,7},{6,4},{7,5},{8,10},{9,11},{10,... | collective-permute-start | bytes 208904 | tf_op jit(solution)/shard_map/ppermute | solution.py:34

commit v10 on v9

--- a/solution.py
+++ b/solution.py
@@ -66,9 +66,9 @@
     return rows.astype(jnp.bfloat16)
 
 
-def block_of(pieces, starts, total):
-    keys = jnp.concatenate([piece[:, :WIDTH] for piece in pieces], axis=0)
-    values = jnp.concatenate([piece[:, WIDTH:] for piece in pieces], axis=1)
+def block_of(keys, values, starts, total):
+    keys = jnp.concatenate(keys, axis=0)
+    values = jnp.concatenate(values, axis=1)
     extra = jnp.concatenate([coord_rows(start, total) for start in starts], axis=1)
     return keys, jnp.concatenate([values, extra], axis=0)
 
@@ -141,12 +141,14 @@
 def one_block(ones, slow, total):
     pieces = [ones[low * 2 + high][slow] for low in range(2) for high in range(2)]
     starts = [start_one(slow, high, low) for low in range(2) for high in range(2)]
-    return block_of(pieces, starts, total)
-
-
-def two_block(two, slow, total):
+    keys, values = [p[:, :WIDTH] for p in pieces], [p[:, WIDTH:] for p in pieces]
+    return block_of(keys, values, starts, total)
+
+
+def two_block(two, vals, slow, total):
     return block_of(
         [two[piece] for piece in range(SUB)],
+        [vals[piece] for piece in range(SUB)],
         [start_two(slow, piece) for piece in range(SUB)],
         total,
     )
@@ -155,7 +157,7 @@
 def col_kernel(total, scale, count, *refs):
     ones, twos, outs = refs[:SUB], refs[SUB : SUB + count], refs[SUB + count :]
     tiles = [
-        jnp.concatenate([two[piece, :, :WIDTH] for piece in range(SUB)], axis=0) for two in twos
+        jnp.concatenate([two[piece] for piece in range(SUB)], axis=0) for two in twos
     ]
     blocks = [one_block(ones, slow, total) for slow in range(SUB)]
     for out, whole in zip(outs, attend(scale, tiles, blocks)):
@@ -163,7 +165,7 @@
 
 
 def row_kernel(total, scale, halves, *refs):
-    ones, twos, outs = refs[:2], refs[2 : 2 + SUB], refs[2 + SUB :]
+    ones, twos, outs = refs[:2], refs[2 : 2 + 2 * SUB], refs[2 + 2 * SUB :]
     tiles = [
         jnp.concatenate(
             [
@@ -175,7 +177,7 @@
         )
         for core, half in halves
     ]
-    blocks = [two_block(two, block, total) for block, two in enumerate(twos)]
+    blocks = [two_block(twos[at], twos[SUB + at], at, total) for at in range(SUB)]
     wholes = attend(scale, tiles, blocks)
     for out in outs:
         for index in range(out.shape[0]):
@@ -250,6 +252,7 @@
 
 def body(feat_one, feat_two, value_one, value_two):
     total = feat_one.shape[0] * lax.axis_size("row") * lax.axis_size("col")
+    order = (2, 3, 1)
     scale = math.log2(math.e) / math.sqrt(WIDTH)
     packed = jax.ShapeDtypeStruct((SHARD, 2 * WIDTH), jnp.bfloat16)
     own_one, own_two = call(
@@ -268,9 +271,13 @@
     one = [own_one, fast_swap("col", own_one, 2)]
     one, two = together((jnp.stack(one), jnp.stack(two)))
     one = [one] + [slow_shift("col", one, -step) for step in range(1, SUB)]
-    twos = [two] + [slow_shift("row", two, -step) for step in range(1, SUB)]
-    one, twos = together((jnp.stack(one, axis=1), twos))
+    vals = two[:, :, WIDTH:]
+    twos = [two[:, :, :WIDTH]]
+    twos += [slow_shift("row", twos[0], -step) for step in order]
+    one, twos, vals = together((jnp.stack(one, axis=1), twos, vals))
+    twos = [twos[0]] + [twos[1 + order.index(step)] for step in range(1, SUB)]
     other = fast_swap("col", one, 1)
+    vals = [vals] + [slow_shift("row", vals, -step) for step in range(1, SUB)]
     ones = [one[0], one[1], other[0], other[1]]
 
     def col_scores(*steps):
@@ -281,7 +288,7 @@
     def row_scores(ones, twos, halves, weight, *counts):
         shapes = [f32(count, ROWS, BLOCK) for count in counts]
         kernel = functools.partial(row_kernel, total, scale, halves)
-        return call(kernel, shapes, (*ones, *twos), work=weight * work)
+        return call(kernel, shapes, (*ones, *twos, *vals), work=weight * work)
 
     def core_merge(mine, theirs, *halves):
         shapes = [f32(ROWS, 2 * SHARD)] * (2 * len(halves))

time: 79.5 us -> 79.2 us (level); the launches traced: 78 us -> 79 us
  starting transfers between devices: 37.7 us -> 45.9 us
  waiting for transfers between devices: 24.5 us -> 17.3 us
    ppermute x12 -> x15, starting transfers between devices: 15.1 us -> 22.1 us  [slow_shift(): return lax.ppermute(value, axis, pairs)]
    ppermute x12 -> x15, waiting for transfers between devices: 15.1 us -> 8.82 us  [slow_shift(): return lax.ppermute(value, axis, pairs)]
    ppermute x4, starting transfers between devices: 5.11 us -> 8.8 us  [fast_swap(): return lax.ppermute(value, axis, [(i, i ^ step) for i in range(SUB * SUB)])]
    ppermute x6, starting transfers between devices: 17.5 us -> 15 us  [fast_shift(): return lax.ppermute(value, axis, pairs)]
    ppermute x6, waiting for transfers between devices: 6.22 us -> 5.03 us  [fast_shift(): return lax.ppermute(value, axis, pairs)]
  transfers between devices with their start and end apart: 22 -> 25, of which waited for: 11 -> 7; matrix products, arithmetic and copies ran while one was open for 1% -> 1% of each run, Pallas kernels for 9% -> 14%
where the time goes in v10:
time: 79.2 us; the launch traced here: 79 us
  starting transfers between devices  45.9 us (58%)
  waiting for transfers between devices  17.3 us (22%)
  Pallas kernels  13.9 us (18%)
  other arithmetic  0.99 us (1%)
    ppermute x15, starting transfers between devices, slow_shift(): return lax.ppermute(value, axis, pairs)  22.1 us
    ppermute x6, starting transfers between devices, fast_shift(): return lax.ppermute(value, axis, pairs)  15 us
    pallas_call x9, Pallas kernels, call(): pl.pallas_call(kernel, out_shape=shapes, in_specs=specs or [VMEM] * len(a...  13.9 us
    ppermute x15, waiting for transfers between devices, slow_shift(): return lax.ppermute(value, axis, pairs)  8.82 us
    ppermute x4, starting transfers between devices, fast_swap(): return lax.ppermute(value, axis, [(i, i ^ step) for i in range(SUB * SUB)])  8.8 us
    ppermute x6, waiting for transfers between devices, fast_shift(): return lax.ppermute(value, axis, pairs)  5.03 us
    ppermute x4, waiting for transfers between devices, fast_swap(): return lax.ppermute(value, axis, [(i, i ^ step) for i in range(SUB * SUB)])  3.45 us
  transfers between devices with their start and end apart: 25, of which 7 were waited for; matrix products, arithmetic and copies ran while one was open for 1% of the time, Pallas kernels for 14%

profile of v10, /device:TPU:1, one launch (start us, length us, event | category | flops | bytes accessed | tf_op | source)
XLA Modules:
  0.0 79.0 jit_solution(10245092908663665731)
XLA Ops:
  0.6 1.7 %shard_map.75 = (bf16[128,256]{1,0:T(8,128)(2,1)}, bf16[128,256]{1,0:T(8,128)(2,1)}) custom-call(bf16[128,128]{1,0:T(8,128)(2,1)} %feat_one.1, bf16[128,128]{1,0:T(8,128)(2,1)} %value_one.1, bf16[128,128]{1,0:T(8,128)(2,1)} %feat_two.1, bf16[128,128]{1,0:T(8,128)(2,1)} %value_two.1), custom_call_target="tpu_custom_call" | custom-call | bytes 262144 | tf_op jit(solution)/shard_map/pallas_call | solution.py:228
  2.3 2.6 %collective-permute-start = (bf16[128,256]{1,0:T(8,128)(2,1)}, bf16[128,256]{1,0:T(8,128)(2,1)S(1)}, u32[]{:S(2)}, u32[]{:S(2)}) collective-permute-start(bf16[128,256]{1,0:T(8,128)(2,1)} %get-tuple-element.39), channel_id=1, source_target_pairs={{0,2},{1,3},{2,0},{3,1},{4,6},{5,7},{6,4},{7,5},{8,10},{9,11},{10,... | collective-permute-start | bytes 196616 | tf_op jit(solution)/shard_map/ppermute | solution.py:34
  4.9 5.1 %collective-permute-start.1 = (bf16[128,256]{1,0:T(8,128)(2,1)}, bf16[128,256]{1,0:T(8,128)(2,1)S(1)}, u32[]{:S(2)}, u32[]{:S(2)}) collective-permute-start(bf16[128,256]{1,0:T(8,128)(2,1)} %get-tuple-element.40), channel_id=1, source_target_pairs={{0,48},{16,0},{32,16},{48,32},{64,112},{80,64},{96,80},{112,96},{1... | collective-permute-start | bytes 196616 | tf_op jit(solution)/shard_map/ppermute | solution.py:30
  10.0 1.2 %collective-permute-start.2 = (bf16[128,256]{1,0:T(8,128)(2,1)}, bf16[128,256]{1,0:T(8,128)(2,1)S(1)}, u32[]{:S(2)}, u32[]{:S(2)}) collective-permute-start(bf16[128,256]{1,0:T(8,128)(2,1)} %get-tuple-element.40), channel_id=1, source_target_pairs={{0,32},{16,48},{32,0},{48,16},{64,96},{80,112},{96,64},{112,80},{1... | collective-permute-start | bytes 196616 | tf_op jit(solution)/shard_map/ppermute | solution.py:30
  11.2 2.1 %collective-permute-start.3 = (bf16[128,256]{1,0:T(8,128)(2,1)}, bf16[128,256]{1,0:T(8,128)(2,1)S(1)}, u32[]{:S(2)}, u32[]{:S(2)}) collective-permute-start(bf16[128,256]{1,0:T(8,128)(2,1)} %get-tuple-element.40), channel_id=1, source_target_pairs={{0,16},{16,32},{32,48},{48,0},{64,80},{80,96},{96,112},{112,64},{1... | collective-permute-start | bytes 196616 | tf_op jit(solution)/shard_map/ppermute | solution.py:30
  13.3 0.9 %pad_maximum_fusion.2 = bf16[2,128,256]{2,1,0:T(8,128)(2,1)S(1)} fusion(bf16[1,128,256]{2,1,0:T(8,128)(2,1)S(1)} %bitcast.29, bf16[1,128,256]{2,1,0:T(8,128)(2,1)} %bitcast.28), kind=kLoop, calls=%fused_computation.6 | loop fusion | flops 65536 | bytes 262144 | tf_op jit(solution)/shard_map/stack | solution.py:272
  14.1 0.0 collective-permute-done.1
  14.2 3.3 %collective-permute-done.2 = bf16[128,256]{1,0:T(8,128)(2,1)S(1)} collective-permute-done((bf16[128,256]{1,0:T(8,128)(2,1)}, bf16[128,256]{1,0:T(8,128)(2,1)S(1)}, u32[]{:S(2)}, u32[]{:S(2)}) %collective-permute-start.2) | collective-permute-done | bytes 65568 | tf_op jit(solution)/shard_map/ppermute | solution.py:30
  17.5 0.4 collective-permute-done.3
  18.0 2.8 %collective-permute-start.5 = (bf16[2,128,256]{2,1,0:T(8,128)(2,1)S(1)}, bf16[2,128,256]{2,1,0:T(8,128)(2,1)S(1)}, u32[]{:S(2)}, u32[]{:S(2)}) collective-permute-start(bf16[2,128,256]{2,1,0:T(8,128)(2,1)S(1)} %pad_maximum_fusion.2), channel_id=1, source_target_pairs={{0,8},{1,9},{2,10},{3,11},{4,12},{5,13},{6,14},{7,15},{8,0},{9,1},... | collective-permute-start | bytes 393224 | tf_op jit(solution)/shard_map/ppermute | solution.py:25
  20.8 0.3 collective-permute-start.6
  21.1 2.4 %collective-permute-start.4 = (bf16[2,128,256]{2,1,0:T(8,128)(2,1)S(1)}, bf16[2,128,256]{2,1,0:T(8,128)(2,1)S(1)}, u32[]{:S(2)}, u32[]{:S(2)}) collective-permute-start(bf16[2,128,256]{2,1,0:T(8,128)(2,1)S(1)} %pad_maximum_fusion.2), channel_id=1, source_target_pairs={{0,12},{1,13},{2,14},{3,15},{4,0},{5,1},{6,2},{7,3},{8,4},{9,5},{1... | collective-permute-start | bytes 393224 | tf_op jit(solution)/shard_map/ppermute | solution.py:25
  23.5 3.0 %collective-permute-start.7 = (bf16[4,128,128]{2,1,0:T(8,128)(2,1)S(1)}, bf16[4,128,128]{2,1,0:T(8,128)(2,1)S(1)}, u32[]{:S(2)}, u32[]{:S(2)}) collective-permute-start(bf16[4,128,128]{2,1,0:T(8,128)(2,1)S(1)} %get-tuple-element.52.refs_2_.refs_4_), channel_id=1, source_target_pairs={{0,128},{16,144},{32,160},{48,176},{64,192},{80,208},{96,224},{112... | collective-permute-start | bytes 393224 | tf_op jit(solution)/shard_map/ppermute | solution.py:25
  26.5 0.4 collective-permute-start.8
  26.9 0.0 collective-permute-done.5
  26.9 2.3 %collective-permute-start.9 = (bf16[4,128,128]{2,1,0:T(8,128)(2,1)S(1)}, bf16[4,128,128]{2,1,0:T(8,128)(2,1)S(1)}, u32[]{:S(2)}, u32[]{:S(2)}) collective-permute-start(bf16[4,128,128]{2,1,0:T(8,128)(2,1)S(1)} %get-tuple-element.52.refs_2_.refs_4_), channel_id=1, source_target_pairs={{0,192},{16,208},{32,224},{48,240},{64,0},{80,16},{96,32},{112,48}... | collective-permute-start | bytes 393224 | tf_op jit(solution)/shard_map/ppermute | solution.py:25
  29.2 0.0 collective-permute-done.6
  29.2 0.0 collective-permute-done.4
  29.2 0.1 pad_maximum_fusion
  29.3 0.0 collective-permute-done.7.refs_4_
  29.3 3.8 %collective-permute-done.8.refs_5_ = bf16[4,128,128]{2,1,0:T(8,128)(2,1)S(1)} collective-permute-done((bf16[4,128,128]{2,1,0:T(8,128)(2,1)S(1)}, bf16[4,128,128]{2,1,0:T(8,128)(2,1)S(1)}, u32[]{:S(2)}, u32[]{:S(2)}) %collective-permute-start.8) | collective-permute-done | bytes 131104 | tf_op jit(solution)/shard_map/ppermute | solution.py:25
  33.1 3.3 %collective-permute-start.10 = (bf16[2,4,128,256]{3,2,1,0:T(8,128)(2,1)S(1)}, bf16[2,4,128,256]{3,2,1,0:T(8,128)(2,1)S(1)}, u32[]{:S(2)}, u32[]{:S(2)}) collective-permute-start(bf16[2,4,128,256]{3,2,1,0:T(8,128)(2,1)S(1)} %pad_maximum_fusion), channel_id=1, source_target_pairs={{0,1},{1,0},{2,3},{3,2},{4,5},{5,4},{6,7},{7,6},{8,9},{9,8},{10,11... | collective-permute-start | bytes 1572872 | tf_op jit(solution)/shard_map/ppermute | solution.py:34
  36.4 3.0 %collective-permute-start.11 = (bf16[4,128,128]{2,1,0:T(8,128)(2,1)S(1)}, bf16[4,128,128]{2,1,0:T(8,128)(2,1)S(1)}, u32[]{:S(2)}, u32[]{:S(2)}) collective-permute-start(bf16[4,128,128]{2,1,0:T(8,128)(2,1)S(1)} %get-tuple-element.53.refs_6_), channel_id=1, source_target_pairs={{0,192},{16,208},{32,224},{48,240},{64,0},{80,16},{96,32},{112,48}... | collective-permute-start | bytes 393224 | tf_op jit(solution)/shard_map/ppermute | solution.py:25
  39.3 0.0 collective-permute-start.12
  39.3 0.6 collective-permute-start.13
  40.0 4.0 %shard_map.76 = (f32[136,512]{1,0:T(8,128)S(1)}, f32[136,512]{1,0:T(8,128)S(1)}, f32[136,512]{1,0:T(8,128)S(1)}) custom-call(bf16[4,128,256]{2,1,0:T(8,128)(2,1)S(1)} %get-tuple-element.54.refs_0_, bf16[4,128,256]{2,1,0:T(8,128)(2,1)S(1)} %get-tuple-element.55.refs_1_, bf16[4,128,256]{2,1,0:T(8,128)(2,1)S(1)} %get-tuple-element.50.refs_2_.refs_0_, ...), custom_call_target="tpu_custom_call" | custom-call | flops 1610612736 | bytes 2277376 | tf_op jit(solution)/shard_map/pallas_call | solution.py:228
  44.0 2.1 %collective-permute-start.15 = (f32[136,512]{1,0:T(8,128)S(1)}, f32[136,512]{1,0:T(8,128)S(1)}, u32[]{:S(2)}, u32[]{:S(2)}) collective-permute-start(f32[136,512]{1,0:T(8,128)S(1)} %get-tuple-element.56), channel_id=1, source_target_pairs={{0,64},{16,80},{32,96},{48,112},{64,128},{80,144},{96,160},{112,17... | collective-permute-start | bytes 835592 | tf_op jit(solution)/shard_map/ppermute | solution.py:25
  46.1 1.2 %collective-permute-start.16 = (f32[136,512]{1,0:T(8,128)S(1)}, f32[136,512]{1,0:T(8,128)S(1)}, u32[]{:S(2)}, u32[]{:S(2)}) collective-permute-start(f32[136,512]{1,0:T(8,128)S(1)} %get-tuple-element.57), channel_id=1, source_target_pairs={{0,128},{16,144},{32,160},{48,176},{64,192},{80,208},{96,224},{112... | collective-permute-start | bytes 835592 | tf_op jit(solution)/shard_map/ppermute | solution.py:25
  47.3 1.3 %collective-permute-start.17 = (f32[136,512]{1,0:T(8,128)S(1)}, f32[136,512]{1,0:T(8,128)S(1)}, u32[]{:S(2)}, u32[]{:S(2)}) collective-permute-start(f32[136,512]{1,0:T(8,128)S(1)} %get-tuple-element.58), channel_id=1, source_target_pairs={{0,192},{16,208},{32,224},{48,240},{64,0},{80,16},{96,32},{112,48}... | collective-permute-start | bytes 835592 | tf_op jit(solution)/shard_map/ppermute | solution.py:25
  48.6 2.8 %shard_map.77 = f32[2,136,512]{2,1,0:T(8,128)S(1)} custom-call(bf16[4,128,256]{2,1,0:T(8,128)(2,1)S(1)} %get-tuple-element.50.refs_2_.refs_0_, bf16[4,128,256]{2,1,0:T(8,128)(2,1)S(1)} %get-tuple-element.51.refs_3_.refs_1_, bf16[4,128,128]{2,1,0:T(8,128)(2,1)S(1)} %get-tuple-element.52.refs_2_.refs_4_, ...), custom_call_target="tpu_custom_call" | custom-call | flops 1073741824 | bytes 2129920 | tf_op jit(solution)/shard_map/pallas_call | solution.py:228
  51.4 1.7 %collective-permute-start.14 = (f32[2,136,512]{2,1,0:T(8,128)S(1)}, f32[2,136,512]{2,1,0:T(8,128)S(1)}, u32[]{:S(2)}, u32[]{:S(2)}) collective-permute-start(f32[2,136,512]{2,1,0:T(8,128)S(1)} %shard_map.77), channel_id=1, source_target_pairs={{0,1},{1,0},{2,3},{3,2},{4,5},{5,4},{6,7},{7,6},{8,9},{9,8},{10,11... | collective-permute-start | bytes 1671176 | tf_op jit(solution)/shard_map/ppermute | solution.py:34
  53.1 1.6 %shard_map.78.refs_0_ = f32[136,512]{1,0:T(8,128)S(1)} custom-call(bf16[4,128,256]{2,1,0:T(8,128)(2,1)S(1)} %get-tuple-element.54.refs_0_, bf16[4,128,256]{2,1,0:T(8,128)(2,1)S(1)} %get-tuple-element.55.refs_1_, bf16[4,128,256]{2,1,0:T(8,128)(2,1)S(1)} %get-tuple-element.50.refs_2_.refs_0_, bf16[4,128,256]{2,1,0:T(8,128)(2,1)S(1)} %get-tuple-element.51.refs_3_.refs_1_, ...), custom_call_target="tpu_custom_call" | custom-call | flops 536870912 | bytes 1458176 | tf_op jit(solution)/shard_map/pallas_call | solution.py:228
  54.7 2.8 %shard_map.80.refs_1_ = f32[2,136,512]{2,1,0:T(8,128)S(1)} custom-call(bf16[4,128,256]{2,1,0:T(8,128)(2,1)S(1)} %get-tuple-element.54.refs_0_, bf16[4,128,256]{2,1,0:T(8,128)(2,1)S(1)} %get-tuple-element.55.refs_1_, bf16[4,128,128]{2,1,0:T(8,128)(2,1)S(1)} %get-tuple-element.52.refs_2_.refs_4_, ...), custom_call_target="tpu_custom_call" | custom-call | flops 1073741824 | bytes 2129920 | tf_op jit(solution)/shard_map/pallas_call | solution.py:228
  57.5 3.0 %collective-permute-done.16.refs_2_ = f32[136,512]{1,0:T(8,128)S(1)} collective-permute-done((f32[136,512]{1,0:T(8,128)S(1)}, f32[136,512]{1,0:T(8,128)S(1)}, u32[]{:S(2)}, u32[]{:S(2)}) %collective-permute-start.16) | collective-permute-done | bytes 278560 | tf_op jit(solution)/shard_map/ppermute | solution.py:25
  60.6 0.1 shard_map.79
  60.7 0.1 shard_map.81
  60.8 0.1 collective-permute-start.18
  60.9 0.9 %collective-permute-start.19 = (f32[136,256]{1,0:T(8,128)S(1)}, f32[136,256]{1,0:T(8,128)S(1)}, u32[]{:S(2)}, u32[]{:S(2)}) collective-permute-start(f32[136,256]{1,0:T(8,128)S(1)} %get-tuple-element.66), channel_id=1, source_target_pairs={{0,8},{1,9},{2,10},{3,11},{4,12},{5,13},{6,14},{7,15},{8,0},{9,1},... | collective-permute-start | bytes 417800 | tf_op jit(solution)/shard_map/ppermute | solution.py:25
  61.8 1.8 %collective-permute-start.20 = (f32[136,256]{1,0:T(8,128)S(1)}, f32[136,256]{1,0:T(8,128)S(1)}, u32[]{:S(2)}, u32[]{:S(2)}) collective-permute-start(f32[136,256]{1,0:T(8,128)S(1)} %get-tuple-element.67), channel_id=1, source_target_pairs={{0,12},{1,13},{2,14},{3,15},{4,0},{5,1},{6,2},{7,3},{8,4},{9,5},{1... | collective-permute-start | bytes 417800 | tf_op jit(solution)/shard_map/ppermute | solution.py:25
  63.6 0.0 collective-permute-start.22
  63.6 4.3 %collective-permute-start.23 = (f32[136,128]{1,0:T(8,128)S(1)}, f32[136,128]{1,0:T(8,128)S(1)}, u32[]{:S(2)}, u32[]{:S(2)}) collective-permute-start(f32[136,128]{1,0:T(8,128)S(1)} %get-tuple-element.72), channel_id=1, source_target_pairs={{0,32},{16,48},{32,0},{48,16},{64,96},{80,112},{96,64},{112,80},{1... | collective-permute-start | bytes 208904 | tf_op jit(solution)/shard_map/ppermute | solution.py:30
  67.9 1.9 %collective-permute-done.18.refs_1_ = f32[136,256]{1,0:T(8,128)S(1)} collective-permute-done((f32[136,256]{1,0:T(8,128)S(1)}, f32[136,256]{1,0:T(8,128)S(1)}, u32[]{:S(2)}, u32[]{:S(2)}) %collective-permute-start.18) | collective-permute-done | bytes 139296 | tf_op jit(solution)/shard_map/ppermute | solution.py:25
  69.8 2.3 %collective-permute-start.24 = (f32[136,128]{1,0:T(8,128)S(1)}, f32[136,128]{1,0:T(8,128)S(1)}, u32[]{:S(2)}, u32[]{:S(2)}) collective-permute-start(f32[136,128]{1,0:T(8,128)S(1)} %get-tuple-element.73), channel_id=1, source_target_pairs={{0,48},{16,0},{32,16},{48,32},{64,112},{80,64},{96,80},{112,96},{1... | collective-permute-start | bytes 208904 | tf_op jit(solution)/shard_map/ppermute | solution.py:30
  72.1 0.1 shard_map.82
  72.2 1.3 %collective-permute-start.21 = (f32[136,128]{1,0:T(8,128)S(1)}, f32[136,128]{1,0:T(8,128)S(1)}, u32[]{:S(2)}, u32[]{:S(2)}) collective-permute-start(f32[136,128]{1,0:T(8,128)S(1)} %get-tuple-element.69), channel_id=1, source_target_pairs={{0,2},{1,3},{2,0},{3,1},{4,6},{5,7},{6,4},{7,5},{8,10},{9,11},{10,... | collective-permute-start | bytes 208904 | tf_op jit(solution)/shard_map/ppermute | solution.py:34
  73.5 1.3 %collective-permute-done.24.refs_5_ = f32[136,128]{1,0:T(8,128)S(1)} collective-permute-done((f32[136,128]{1,0:T(8,128)S(1)}, f32[136,128]{1,0:T(8,128)S(1)}, u32[]{:S(2)}, u32[]{:S(2)}) %collective-permute-start.24) | collective-permute-done | bytes 69664 | tf_op jit(solution)/shard_map/ppermute | solution.py:30
  74.7 3.4 %collective-permute-done.21.refs_1_ = f32[136,128]{1,0:T(8,128)S(1)} collective-permute-done((f32[136,128]{1,0:T(8,128)S(1)}, f32[136,128]{1,0:T(8,128)S(1)}, u32[]{:S(2)}, u32[]{:S(2)}) %collective-permute-start.21) | collective-permute-done | bytes 69664 | tf_op jit(solution)/shard_map/ppermute | solution.py:34
  78.2 0.8 shard_map.83
  (19 shorter events, 0.2 us)
Async XLA Ops:
  2.3 10.9 %collective-permute-start = (bf16[128,256]{1,0:T(8,128)(2,1)}, bf16[128,256]{1,0:T(8,128)(2,1)S(1)}, u32[]{:S(2)}, u32[]{:S(2)}) collective-permute-start(bf16[128,256]{1,0:T(8,128)(2,1)} %get-tuple-element.39), channel_id=1, source_target_pairs={{0,2},{1,3},{2,0},{3,1},{4,6},{5,7},{6,4},{7,5},{8,10},{9,11},{10,... | collective-permute-start | bytes 196616 | tf_op jit(solution)/shard_map/ppermute | solution.py:34
  4.9 9.3 %collective-permute-start.1 = (bf16[128,256]{1,0:T(8,128)(2,1)}, bf16[128,256]{1,0:T(8,128)(2,1)S(1)}, u32[]{:S(2)}, u32[]{:S(2)}) collective-permute-start(bf16[128,256]{1,0:T(8,128)(2,1)} %get-tuple-element.40), channel_id=1, source_target_pairs={{0,48},{16,0},{32,16},{48,32},{64,112},{80,64},{96,80},{112,96},{1... | collective-permute-start | bytes 196616 | tf_op jit(solution)/shard_map/ppermute | solution.py:30
  10.0 7.5 %collective-permute-start.2 = (bf16[128,256]{1,0:T(8,128)(2,1)}, bf16[128,256]{1,0:T(8,128)(2,1)S(1)}, u32[]{:S(2)}, u32[]{:S(2)}) collective-permute-start(bf16[128,256]{1,0:T(8,128)(2,1)} %get-tuple-element.40), channel_id=1, source_target_pairs={{0,32},{16,48},{32,0},{48,16},{64,96},{80,112},{96,64},{112,80},{1... | collective-permute-start | bytes 196616 | tf_op jit(solution)/shard_map/ppermute | solution.py:30
  11.2 6.8 %collective-permute-start.3 = (bf16[128,256]{1,0:T(8,128)(2,1)}, bf16[128,256]{1,0:T(8,128)(2,1)S(1)}, u32[]{:S(2)}, u32[]{:S(2)}) collective-permute-start(bf16[128,256]{1,0:T(8,128)(2,1)} %get-tuple-element.40), channel_id=1, source_target_pairs={{0,16},{16,32},{32,48},{48,0},{64,80},{80,96},{96,112},{112,64},{1... | collective-permute-start | bytes 196616 | tf_op jit(solution)/shard_map/ppermute | solution.py:30
  13.3 4.7 %copy-start = (bf16[128,256]{1,0:T(8,128)(2,1)S(1)}, bf16[128,256]{1,0:T(8,128)(2,1)}, u32[]{:S(2)}) copy-start(bf16[128,256]{1,0:T(8,128)(2,1)} %get-tuple-element.40) | copy-start | bytes 196612
  18.0 9.0 %collective-permute-start.5 = (bf16[2,128,256]{2,1,0:T(8,128)(2,1)S(1)}, bf16[2,128,256]{2,1,0:T(8,128)(2,1)S(1)}, u32[]{:S(2)}, u32[]{:S(2)}) collective-permute-start(bf16[2,128,256]{2,1,0:T(8,128)(2,1)S(1)} %pad_maximum_fusion.2), channel_id=1, source_target_pairs={{0,8},{1,9},{2,10},{3,11},{4,12},{5,13},{6,14},{7,15},{8,0},{9,1},... | collective-permute-start | bytes 393224 | tf_op jit(solution)/shard_map/ppermute | solution.py:25
  20.8 8.4 %collective-permute-start.6 = (bf16[2,128,256]{2,1,0:T(8,128)(2,1)S(1)}, bf16[2,128,256]{2,1,0:T(8,128)(2,1)S(1)}, u32[]{:S(2)}, u32[]{:S(2)}) collective-permute-start(bf16[2,128,256]{2,1,0:T(8,128)(2,1)S(1)} %pad_maximum_fusion.2), channel_id=1, source_target_pairs={{0,4},{1,5},{2,6},{3,7},{4,8},{5,9},{6,10},{7,11},{8,12},{9,13},{1... | collective-permute-start | bytes 393224 | tf_op jit(solution)/shard_map/ppermute | solution.py:25
  21.1 8.1 %collective-permute-start.4 = (bf16[2,128,256]{2,1,0:T(8,128)(2,1)S(1)}, bf16[2,128,256]{2,1,0:T(8,128)(2,1)S(1)}, u32[]{:S(2)}, u32[]{:S(2)}) collective-permute-start(bf16[2,128,256]{2,1,0:T(8,128)(2,1)S(1)} %pad_maximum_fusion.2), channel_id=1, source_target_pairs={{0,12},{1,13},{2,14},{3,15},{4,0},{5,1},{6,2},{7,3},{8,4},{9,5},{1... | collective-permute-start | bytes 393224 | tf_op jit(solution)/shard_map/ppermute | solution.py:25
  23.5 5.8 %collective-permute-start.7 = (bf16[4,128,128]{2,1,0:T(8,128)(2,1)S(1)}, bf16[4,128,128]{2,1,0:T(8,128)(2,1)S(1)}, u32[]{:S(2)}, u32[]{:S(2)}) collective-permute-start(bf16[4,128,128]{2,1,0:T(8,128)(2,1)S(1)} %get-tuple-element.52.refs_2_.refs_4_), channel_id=1, source_target_pairs={{0,128},{16,144},{32,160},{48,176},{64,192},{80,208},{96,224},{112... | collective-permute-start | bytes 393224 | tf_op jit(solution)/shard_map/ppermute | solution.py:25
  26.5 6.6 %collective-permute-start.8 = (bf16[4,128,128]{2,1,0:T(8,128)(2,1)S(1)}, bf16[4,128,128]{2,1,0:T(8,128)(2,1)S(1)}, u32[]{:S(2)}, u32[]{:S(2)}) collective-permute-start(bf16[4,128,128]{2,1,0:T(8,128)(2,1)S(1)} %get-tuple-element.52.refs_2_.refs_4_), channel_id=1, source_target_pairs={{0,64},{16,80},{32,96},{48,112},{64,128},{80,144},{96,160},{112,17... | collective-permute-start | bytes 393224 | tf_op jit(solution)/shard_map/ppermute | solution.py:25
  26.9 6.2 %collective-permute-start.9 = (bf16[4,128,128]{2,1,0:T(8,128)(2,1)S(1)}, bf16[4,128,128]{2,1,0:T(8,128)(2,1)S(1)}, u32[]{:S(2)}, u32[]{:S(2)}) collective-permute-start(bf16[4,128,128]{2,1,0:T(8,128)(2,1)S(1)} %get-tuple-element.52.refs_2_.refs_4_), channel_id=1, source_target_pairs={{0,192},{16,208},{32,224},{48,240},{64,0},{80,16},{96,32},{112,48}... | collective-permute-start | bytes 393224 | tf_op jit(solution)/shard_map/ppermute | solution.py:25
  33.1 6.8 %collective-permute-start.10 = (bf16[2,4,128,256]{3,2,1,0:T(8,128)(2,1)S(1)}, bf16[2,4,128,256]{3,2,1,0:T(8,128)(2,1)S(1)}, u32[]{:S(2)}, u32[]{:S(2)}) collective-permute-start(bf16[2,4,128,256]{3,2,1,0:T(8,128)(2,1)S(1)} %pad_maximum_fusion), channel_id=1, source_target_pairs={{0,1},{1,0},{2,3},{3,2},{4,5},{5,4},{6,7},{7,6},{8,9},{9,8},{10,11... | collective-permute-start | bytes 1572872 | tf_op jit(solution)/shard_map/ppermute | solution.py:34
  36.4 11.0 %collective-permute-start.11 = (bf16[4,128,128]{2,1,0:T(8,128)(2,1)S(1)}, bf16[4,128,128]{2,1,0:T(8,128)(2,1)S(1)}, u32[]{:S(2)}, u32[]{:S(2)}) collective-permute-start(bf16[4,128,128]{2,1,0:T(8,128)(2,1)S(1)} %get-tuple-element.53.refs_6_), channel_id=1, source_target_pairs={{0,192},{16,208},{32,224},{48,240},{64,0},{80,16},{96,32},{112,48}... | collective-permute-start | bytes 393224 | tf_op jit(solution)/shard_map/ppermute | solution.py:25
  39.3 9.3 %collective-permute-start.12 = (bf16[4,128,128]{2,1,0:T(8,128)(2,1)S(1)}, bf16[4,128,128]{2,1,0:T(8,128)(2,1)S(1)}, u32[]{:S(2)}, u32[]{:S(2)}) collective-permute-start(bf16[4,128,128]{2,1,0:T(8,128)(2,1)S(1)} %get-tuple-element.53.refs_6_), channel_id=1, source_target_pairs={{0,128},{16,144},{32,160},{48,176},{64,192},{80,208},{96,224},{112... | collective-permute-start | bytes 393224 | tf_op jit(solution)/shard_map/ppermute | solution.py:25
  39.3 9.3 %collective-permute-start.13 = (bf16[4,128,128]{2,1,0:T(8,128)(2,1)S(1)}, bf16[4,128,128]{2,1,0:T(8,128)(2,1)S(1)}, u32[]{:S(2)}, u32[]{:S(2)}) collective-permute-start(bf16[4,128,128]{2,1,0:T(8,128)(2,1)S(1)} %get-tuple-element.53.refs_6_), channel_id=1, source_target_pairs={{0,64},{16,80},{32,96},{48,112},{64,128},{80,144},{96,160},{112,17... | collective-permute-start | bytes 393224 | tf_op jit(solution)/shard_map/ppermute | solution.py:25
  44.0 13.5 %collective-permute-start.15 = (f32[136,512]{1,0:T(8,128)S(1)}, f32[136,512]{1,0:T(8,128)S(1)}, u32[]{:S(2)}, u32[]{:S(2)}) collective-permute-start(f32[136,512]{1,0:T(8,128)S(1)} %get-tuple-element.56), channel_id=1, source_target_pairs={{0,64},{16,80},{32,96},{48,112},{64,128},{80,144},{96,160},{112,17... | collective-permute-start | bytes 835592 | tf_op jit(solution)/shard_map/ppermute | solution.py:25
  46.1 14.5 %collective-permute-start.16 = (f32[136,512]{1,0:T(8,128)S(1)}, f32[136,512]{1,0:T(8,128)S(1)}, u32[]{:S(2)}, u32[]{:S(2)}) collective-permute-start(f32[136,512]{1,0:T(8,128)S(1)} %get-tuple-element.57), channel_id=1, source_target_pairs={{0,128},{16,144},{32,160},{48,176},{64,192},{80,208},{96,224},{112... | collective-permute-start | bytes 835592 | tf_op jit(solution)/shard_map/ppermute | solution.py:25
  47.3 13.2 %collective-permute-start.17 = (f32[136,512]{1,0:T(8,128)S(1)}, f32[136,512]{1,0:T(8,128)S(1)}, u32[]{:S(2)}, u32[]{:S(2)}) collective-permute-start(f32[136,512]{1,0:T(8,128)S(1)} %get-tuple-element.58), channel_id=1, source_target_pairs={{0,192},{16,208},{32,224},{48,240},{64,0},{80,16},{96,32},{112,48}... | collective-permute-start | bytes 835592 | tf_op jit(solution)/shard_map/ppermute | solution.py:25
  51.4 9.3 %collective-permute-start.14 = (f32[2,136,512]{2,1,0:T(8,128)S(1)}, f32[2,136,512]{2,1,0:T(8,128)S(1)}, u32[]{:S(2)}, u32[]{:S(2)}) collective-permute-start(f32[2,136,512]{2,1,0:T(8,128)S(1)} %shard_map.77), channel_id=1, source_target_pairs={{0,1},{1,0},{2,3},{3,2},{4,5},{5,4},{6,7},{7,6},{8,9},{9,8},{10,11... | collective-permute-start | bytes 1671176 | tf_op jit(solution)/shard_map/ppermute | solution.py:34
  60.8 9.0 %collective-permute-start.18 = (f32[136,256]{1,0:T(8,128)S(1)}, f32[136,256]{1,0:T(8,128)S(1)}, u32[]{:S(2)}, u32[]{:S(2)}) collective-permute-start(f32[136,256]{1,0:T(8,128)S(1)} %get-tuple-element.65), channel_id=1, source_target_pairs={{0,4},{1,5},{2,6},{3,7},{4,8},{5,9},{6,10},{7,11},{8,12},{9,13},{1... | collective-permute-start | bytes 417800 | tf_op jit(solution)/shard_map/ppermute | solution.py:25
  60.9 11.2 %collective-permute-start.19 = (f32[136,256]{1,0:T(8,128)S(1)}, f32[136,256]{1,0:T(8,128)S(1)}, u32[]{:S(2)}, u32[]{:S(2)}) collective-permute-start(f32[136,256]{1,0:T(8,128)S(1)} %get-tuple-element.66), channel_id=1, source_target_pairs={{0,8},{1,9},{2,10},{3,11},{4,12},{5,13},{6,14},{7,15},{8,0},{9,1},... | collective-permute-start | bytes 417800 | tf_op jit(solution)/shard_map/ppermute | solution.py:25
  61.8 10.3 %collective-permute-start.20 = (f32[136,256]{1,0:T(8,128)S(1)}, f32[136,256]{1,0:T(8,128)S(1)}, u32[]{:S(2)}, u32[]{:S(2)}) collective-permute-start(f32[136,256]{1,0:T(8,128)S(1)} %get-tuple-element.67), channel_id=1, source_target_pairs={{0,12},{1,13},{2,14},{3,15},{4,0},{5,1},{6,2},{7,3},{8,4},{9,5},{1... | collective-permute-start | bytes 417800 | tf_op jit(solution)/shard_map/ppermute | solution.py:25
  63.6 9.9 %collective-permute-start.22 = (f32[136,128]{1,0:T(8,128)S(1)}, f32[136,128]{1,0:T(8,128)S(1)}, u32[]{:S(2)}, u32[]{:S(2)}) collective-permute-start(f32[136,128]{1,0:T(8,128)S(1)} %get-tuple-element.71), channel_id=1, source_target_pairs={{0,16},{16,32},{32,48},{48,0},{64,80},{80,96},{96,112},{112,64},{1... | collective-permute-start | bytes 208904 | tf_op jit(solution)/shard_map/ppermute | solution.py:30
  63.6 9.9 %collective-permute-start.23 = (f32[136,128]{1,0:T(8,128)S(1)}, f32[136,128]{1,0:T(8,128)S(1)}, u32[]{:S(2)}, u32[]{:S(2)}) collective-permute-start(f32[136,128]{1,0:T(8,128)S(1)} %get-tuple-element.72), channel_id=1, source_target_pairs={{0,32},{16,48},{32,0},{48,16},{64,96},{80,112},{96,64},{112,80},{1... | collective-permute-start | bytes 208904 | tf_op jit(solution)/shard_map/ppermute | solution.py:30
  69.8 4.9 %collective-permute-start.24 = (f32[136,128]{1,0:T(8,128)S(1)}, f32[136,128]{1,0:T(8,128)S(1)}, u32[]{:S(2)}, u32[]{:S(2)}) collective-permute-start(f32[136,128]{1,0:T(8,128)S(1)} %get-tuple-element.73), channel_id=1, source_target_pairs={{0,48},{16,0},{32,16},{48,32},{64,112},{80,64},{96,80},{112,96},{1... | collective-permute-start | bytes 208904 | tf_op jit(solution)/shard_map/ppermute | solution.py:30
  72.2 6.0 %collective-permute-start.21 = (f32[136,128]{1,0:T(8,128)S(1)}, f32[136,128]{1,0:T(8,128)S(1)}, u32[]{:S(2)}, u32[]{:S(2)}) collective-permute-start(f32[136,128]{1,0:T(8,128)S(1)} %get-tuple-element.69), channel_id=1, source_target_pairs={{0,2},{1,3},{2,0},{3,1},{4,6},{5,7},{6,4},{7,5},{8,10},{9,11},{10,... | collective-permute-start | bytes 208904 | tf_op jit(solution)/shard_map/ppermute | solution.py:34

commit v11 on v9

--- a/solution.py
+++ b/solution.py
@@ -268,8 +268,10 @@
     one = [own_one, fast_swap("col", own_one, 2)]
     one, two = together((jnp.stack(one), jnp.stack(two)))
     one = [one] + [slow_shift("col", one, -step) for step in range(1, SUB)]
-    twos = [two] + [slow_shift("row", two, -step) for step in range(1, SUB)]
+    order = (3, 2, 1)
+    twos = [two] + [slow_shift("row", two, -step) for step in order]
     one, twos = together((jnp.stack(one, axis=1), twos))
+    twos = [twos[0]] + [twos[1 + order.index(step)] for step in range(1, SUB)]
     other = fast_swap("col", one, 1)
     ones = [one[0], one[1], other[0], other[1]]
 
@@ -302,9 +304,8 @@
     cols = spread("row", [cols[0], *far])
     (send_one,) = row_scores(ones[2:], twos, ((0, 0), (0, 1)), 2, 2)
     theirs_one = fast_swap("col", send_one, 1)
-    (keep_one,) = row_scores(ones[:2], twos, ((0, 0), (0, 1)), 2, 2)
-    cols = call(block_kernel, [f32(ROWS, SHARD)] * SUB, cols, work=40 * work)
-    theirs_one, cols = together((theirs_one, cols))
+    (keep_one,) = row_scores(ones[:2], twos, ((0, 0), (0, 1)), 40, 2)
+    cols = call(block_kernel, [f32(ROWS, SHARD)] * SUB, cols, work=1 * work)
     cols = [cols[0]] + [fast_shift("row", cols[step], step) for step in range(1, SUB)]
     rows = spread("col", core_merge(keep_one, theirs_one, 0, 1))
     keep, send = call(chip_kernel, [f32(ROWS, SHARD)] * 2, rows)

time: 79.5 us -> 74.8 us (0.941)
  waiting for transfers between devices: 24.5 us -> 14 us
  starting transfers between devices: 37.7 us -> 43.7 us
    ppermute x12, waiting for transfers between devices: 15.1 us -> 5 us  [slow_shift(): return lax.ppermute(value, axis, pairs)]
    ppermute x12, starting transfers between devices: 15.1 us -> 18 us  [slow_shift(): return lax.ppermute(value, axis, pairs)]
    ppermute x4, starting transfers between devices: 5.11 us -> 8.03 us  [fast_swap(): return lax.ppermute(value, axis, [(i, i ^ step) for i in range(SUB * SUB)])]
  transfers between devices with their start and end apart: 22 -> 22, of which waited for: 11 -> 7; matrix products, arithmetic and copies ran while one was open for 1% -> 1% of each run, Pallas kernels for 9% -> 10%
where the time goes in v11:
time: 74.8 us; the launch traced here: 73.4 us
  starting transfers between devices  43.7 us (58%)
  waiting for transfers between devices  14 us (19%)
  Pallas kernels  13.9 us (19%)
  other arithmetic  0.99 us (1%)
  between operations  0.77 us (1%)
    ppermute x12, starting transfers between devices, slow_shift(): return lax.ppermute(value, axis, pairs)  18 us
    ppermute x6, starting transfers between devices, fast_shift(): return lax.ppermute(value, axis, pairs)  17.6 us
    pallas_call x9, Pallas kernels, call(): pl.pallas_call(kernel, out_shape=shapes, in_specs=specs or [VMEM] * len(a...  13.9 us
    ppermute x4, starting transfers between devices, fast_swap(): return lax.ppermute(value, axis, [(i, i ^ step) for i in range(SUB * SUB)])  8.03 us
    ppermute x6, waiting for transfers between devices, fast_shift(): return lax.ppermute(value, axis, pairs)  6.27 us
    ppermute x12, waiting for transfers between devices, slow_shift(): return lax.ppermute(value, axis, pairs)  5 us
    ppermute x4, waiting for transfers between devices, fast_swap(): return lax.ppermute(value, axis, [(i, i ^ step) for i in range(SUB * SUB)])  2.72 us
  transfers between devices with their start and end apart: 22, of which 7 were waited for; matrix products, arithmetic and copies ran while one was open for 1% of the time, Pallas kernels for 10%

profile of v11, /device:TPU:1, one launch (start us, length us, event | category | flops | bytes accessed | tf_op | source)
XLA Modules:
  0.0 73.4 jit_solution(14069580978788850604)
XLA Ops:
  0.6 1.7 %shard_map.75 = (bf16[128,256]{1,0:T(8,128)(2,1)}, bf16[128,256]{1,0:T(8,128)(2,1)}) custom-call(bf16[128,128]{1,0:T(8,128)(2,1)} %feat_one.1, bf16[128,128]{1,0:T(8,128)(2,1)} %value_one.1, bf16[128,128]{1,0:T(8,128)(2,1)} %feat_two.1, bf16[128,128]{1,0:T(8,128)(2,1)} %value_two.1), custom_call_target="tpu_custom_call" | custom-call | bytes 262144 | tf_op jit(solution)/shard_map/pallas_call | solution.py:226
  2.3 2.6 %collective-permute-start = (bf16[128,256]{1,0:T(8,128)(2,1)}, bf16[128,256]{1,0:T(8,128)(2,1)S(1)}, u32[]{:S(2)}, u32[]{:S(2)}) collective-permute-start(bf16[128,256]{1,0:T(8,128)(2,1)} %get-tuple-element.33), channel_id=1, source_target_pairs={{0,2},{1,3},{2,0},{3,1},{4,6},{5,7},{6,4},{7,5},{8,10},{9,11},{10,... | collective-permute-start | bytes 196616 | tf_op jit(solution)/shard_map/ppermute | solution.py:34
  4.9 5.1 %collective-permute-start.1 = (bf16[128,256]{1,0:T(8,128)(2,1)}, bf16[128,256]{1,0:T(8,128)(2,1)S(1)}, u32[]{:S(2)}, u32[]{:S(2)}) collective-permute-start(bf16[128,256]{1,0:T(8,128)(2,1)} %get-tuple-element.34), channel_id=1, source_target_pairs={{0,48},{16,0},{32,16},{48,32},{64,112},{80,64},{96,80},{112,96},{1... | collective-permute-start | bytes 196616 | tf_op jit(solution)/shard_map/ppermute | solution.py:30
  10.0 1.2 %collective-permute-start.2 = (bf16[128,256]{1,0:T(8,128)(2,1)}, bf16[128,256]{1,0:T(8,128)(2,1)S(1)}, u32[]{:S(2)}, u32[]{:S(2)}) collective-permute-start(bf16[128,256]{1,0:T(8,128)(2,1)} %get-tuple-element.34), channel_id=1, source_target_pairs={{0,32},{16,48},{32,0},{48,16},{64,96},{80,112},{96,64},{112,80},{1... | collective-permute-start | bytes 196616 | tf_op jit(solution)/shard_map/ppermute | solution.py:30
  11.2 2.1 %collective-permute-start.3 = (bf16[128,256]{1,0:T(8,128)(2,1)}, bf16[128,256]{1,0:T(8,128)(2,1)S(1)}, u32[]{:S(2)}, u32[]{:S(2)}) collective-permute-start(bf16[128,256]{1,0:T(8,128)(2,1)} %get-tuple-element.34), channel_id=1, source_target_pairs={{0,16},{16,32},{32,48},{48,0},{64,80},{80,96},{96,112},{112,64},{1... | collective-permute-start | bytes 196616 | tf_op jit(solution)/shard_map/ppermute | solution.py:30
  13.3 0.0 collective-permute-done
  13.3 0.9 %pad_maximum_fusion.2 = bf16[2,128,256]{2,1,0:T(8,128)(2,1)S(1)} fusion(bf16[1,128,256]{2,1,0:T(8,128)(2,1)S(1)} %bitcast.29, bf16[1,128,256]{2,1,0:T(8,128)(2,1)} %bitcast.28), kind=kLoop, calls=%fused_computation.6 | loop fusion | flops 65536 | bytes 262144 | tf_op jit(solution)/shard_map/stack | solution.py:269
  14.1 0.0 collective-permute-done.1
  14.2 3.3 %collective-permute-done.2 = bf16[128,256]{1,0:T(8,128)(2,1)S(1)} collective-permute-done((bf16[128,256]{1,0:T(8,128)(2,1)}, bf16[128,256]{1,0:T(8,128)(2,1)S(1)}, u32[]{:S(2)}, u32[]{:S(2)}) %collective-permute-start.2) | collective-permute-done | bytes 65568 | tf_op jit(solution)/shard_map/ppermute | solution.py:30
  17.5 0.4 collective-permute-done.3
  18.0 2.8 %collective-permute-start.5 = (bf16[2,128,256]{2,1,0:T(8,128)(2,1)S(1)}, bf16[2,128,256]{2,1,0:T(8,128)(2,1)S(1)}, u32[]{:S(2)}, u32[]{:S(2)}) collective-permute-start(bf16[2,128,256]{2,1,0:T(8,128)(2,1)S(1)} %pad_maximum_fusion.2), channel_id=1, source_target_pairs={{0,8},{1,9},{2,10},{3,11},{4,12},{5,13},{6,14},{7,15},{8,0},{9,1},... | collective-permute-start | bytes 393224 | tf_op jit(solution)/shard_map/ppermute | solution.py:25
  20.8 1.3 %collective-permute-start.7 = (bf16[4,128,256]{2,1,0:T(8,128)(2,1)S(1)}, bf16[4,128,256]{2,1,0:T(8,128)(2,1)S(1)}, u32[]{:S(2)}, u32[]{:S(2)}) collective-permute-start(bf16[4,128,256]{2,1,0:T(8,128)(2,1)S(1)} %pad_maximum_fusion.1.refs_2_.refs_4_), channel_id=1, source_target_pairs={{0,64},{16,80},{32,96},{48,112},{64,128},{80,144},{96,160},{112,17... | collective-permute-start | bytes 786440 | tf_op jit(solution)/shard_map/ppermute | solution.py:25
  22.1 2.6 %collective-permute-start.8 = (bf16[4,128,256]{2,1,0:T(8,128)(2,1)S(1)}, bf16[4,128,256]{2,1,0:T(8,128)(2,1)S(1)}, u32[]{:S(2)}, u32[]{:S(2)}) collective-permute-start(bf16[4,128,256]{2,1,0:T(8,128)(2,1)S(1)} %pad_maximum_fusion.1.refs_2_.refs_4_), channel_id=1, source_target_pairs={{0,128},{16,144},{32,160},{48,176},{64,192},{80,208},{96,224},{112... | collective-permute-start | bytes 786440 | tf_op jit(solution)/shard_map/ppermute | solution.py:25
  24.7 1.1 %collective-permute-start.9 = (bf16[4,128,256]{2,1,0:T(8,128)(2,1)S(1)}, bf16[4,128,256]{2,1,0:T(8,128)(2,1)S(1)}, u32[]{:S(2)}, u32[]{:S(2)}) collective-permute-start(bf16[4,128,256]{2,1,0:T(8,128)(2,1)S(1)} %pad_maximum_fusion.1.refs_2_.refs_4_), channel_id=1, source_target_pairs={{0,192},{16,208},{32,224},{48,240},{64,0},{80,16},{96,32},{112,48}... | collective-permute-start | bytes 786440 | tf_op jit(solution)/shard_map/ppermute | solution.py:25
  25.8 0.3 collective-permute-start.6
  26.1 0.0 collective-permute-done.5
  26.1 2.4 %collective-permute-start.4 = (bf16[2,128,256]{2,1,0:T(8,128)(2,1)S(1)}, bf16[2,128,256]{2,1,0:T(8,128)(2,1)S(1)}, u32[]{:S(2)}, u32[]{:S(2)}) collective-permute-start(bf16[2,128,256]{2,1,0:T(8,128)(2,1)S(1)} %pad_maximum_fusion.2), channel_id=1, source_target_pairs={{0,12},{1,13},{2,14},{3,15},{4,0},{5,1},{6,2},{7,3},{8,4},{9,5},{1... | collective-permute-start | bytes 393224 | tf_op jit(solution)/shard_map/ppermute | solution.py:25
  28.5 2.6 %collective-permute-done.6 = bf16[2,128,256]{2,1,0:T(8,128)(2,1)S(1)} collective-permute-done((bf16[2,128,256]{2,1,0:T(8,128)(2,1)S(1)}, bf16[2,128,256]{2,1,0:T(8,128)(2,1)S(1)}, u32[]{:S(2)}, u32[]{:S(2)}) %collective-permute-start.6) | collective-permute-done | bytes 131104 | tf_op jit(solution)/shard_map/ppermute | solution.py:25
  31.1 0.0 collective-permute-done.4
  31.1 0.1 pad_maximum_fusion
  31.2 0.0 collective-permute-done.7.refs_5_
  31.2 2.3 %collective-permute-done.8.refs_4_ = bf16[4,128,256]{2,1,0:T(8,128)(2,1)S(1)} collective-permute-done((bf16[4,128,256]{2,1,0:T(8,128)(2,1)S(1)}, bf16[4,128,256]{2,1,0:T(8,128)(2,1)S(1)}, u32[]{:S(2)}, u32[]{:S(2)}) %collective-permute-start.8) | collective-permute-done | bytes 262176 | tf_op jit(solution)/shard_map/ppermute | solution.py:25
  33.5 0.0 collective-permute-done.9.refs_6_.refs_3_
  33.5 4.1 %collective-permute-start.10 = (bf16[2,4,128,256]{3,2,1,0:T(8,128)(2,1)S(1)}, bf16[2,4,128,256]{3,2,1,0:T(8,128)(2,1)S(1)}, u32[]{:S(2)}, u32[]{:S(2)}) collective-permute-start(bf16[2,4,128,256]{3,2,1,0:T(8,128)(2,1)S(1)} %pad_maximum_fusion), channel_id=1, source_target_pairs={{0,1},{1,0},{2,3},{3,2},{4,5},{5,4},{6,7},{7,6},{8,9},{9,8},{10,11... | collective-permute-start | bytes 1572872 | tf_op jit(solution)/shard_map/ppermute | solution.py:34
  37.6 1.5 %collective-permute-done.10 = bf16[2,4,128,256]{3,2,1,0:T(8,128)(2,1)S(1)} collective-permute-done((bf16[2,4,128,256]{3,2,1,0:T(8,128)(2,1)S(1)}, bf16[2,4,128,256]{3,2,1,0:T(8,128)(2,1)S(1)}, u32[]{:S(2)}, u32[]{:S(2)}) %collective-permute-start.10) | collective-permute-done | bytes 524320 | tf_op jit(solution)/shard_map/ppermute | solution.py:34
  39.2 3.9 %shard_map.76 = (f32[136,512]{1,0:T(8,128)S(1)}, f32[136,512]{1,0:T(8,128)S(1)}, f32[136,512]{1,0:T(8,128)S(1)}) custom-call(bf16[4,128,256]{2,1,0:T(8,128)(2,1)S(1)} %get-tuple-element.47.refs_0_, bf16[4,128,256]{2,1,0:T(8,128)(2,1)S(1)} %get-tuple-element.48.refs_1_, bf16[4,128,256]{2,1,0:T(8,128)(2,1)S(1)} %get-tuple-element.44.refs_2_.refs_0_, ...), custom_call_target="tpu_custom_call" | custom-call | flops 1610612736 | bytes 2670592 | tf_op jit(solution)/shard_map/pallas_call | solution.py:226
  43.1 1.1 %collective-permute-start.16 = (f32[136,512]{1,0:T(8,128)S(1)}, f32[136,512]{1,0:T(8,128)S(1)}, u32[]{:S(2)}, u32[]{:S(2)}) collective-permute-start(f32[136,512]{1,0:T(8,128)S(1)} %get-tuple-element.55), channel_id=1, source_target_pairs={{0,64},{16,80},{32,96},{48,112},{64,128},{80,144},{96,160},{112,17... | collective-permute-start | bytes 835592 | tf_op jit(solution)/shard_map/ppermute | solution.py:25
  44.2 2.1 %collective-permute-start.17 = (f32[136,512]{1,0:T(8,128)S(1)}, f32[136,512]{1,0:T(8,128)S(1)}, u32[]{:S(2)}, u32[]{:S(2)}) collective-permute-start(f32[136,512]{1,0:T(8,128)S(1)} %get-tuple-element.56), channel_id=1, source_target_pairs={{0,128},{16,144},{32,160},{48,176},{64,192},{80,208},{96,224},{112... | collective-permute-start | bytes 835592 | tf_op jit(solution)/shard_map/ppermute | solution.py:25
  46.3 1.4 %collective-permute-start.18 = (f32[136,512]{1,0:T(8,128)S(1)}, f32[136,512]{1,0:T(8,128)S(1)}, u32[]{:S(2)}, u32[]{:S(2)}) collective-permute-start(f32[136,512]{1,0:T(8,128)S(1)} %get-tuple-element.57), channel_id=1, source_target_pairs={{0,192},{16,208},{32,224},{48,240},{64,0},{80,16},{96,32},{112,48}... | collective-permute-start | bytes 835592 | tf_op jit(solution)/shard_map/ppermute | solution.py:25
  47.7 2.8 %shard_map.77 = f32[2,136,512]{2,1,0:T(8,128)S(1)} custom-call(bf16[4,128,256]{2,1,0:T(8,128)(2,1)S(1)} %get-tuple-element.44.refs_2_.refs_0_, bf16[4,128,256]{2,1,0:T(8,128)(2,1)S(1)} %get-tuple-element.45.refs_3_.refs_1_, bf16[4,128,256]{2,1,0:T(8,128)(2,1)S(1)} %pad_maximum_fusion.1.refs_2_.refs_4_, ...), custom_call_target="tpu_custom_call" | custom-call | flops 1073741824 | bytes 2129920 | tf_op jit(solution)/shard_map/pallas_call | solution.py:226
  50.5 1.3 %collective-permute-start.11 = (f32[2,136,512]{2,1,0:T(8,128)S(1)}, f32[2,136,512]{2,1,0:T(8,128)S(1)}, u32[]{:S(2)}, u32[]{:S(2)}) collective-permute-start(f32[2,136,512]{2,1,0:T(8,128)S(1)} %shard_map.77), channel_id=1, source_target_pairs={{0,1},{1,0},{2,3},{3,2},{4,5},{5,4},{6,7},{7,6},{8,9},{9,8},{10,11... | collective-permute-start | bytes 1671176 | tf_op jit(solution)/shard_map/ppermute | solution.py:34
  51.8 2.8 %shard_map.78.refs_1_ = f32[2,136,512]{2,1,0:T(8,128)S(1)} custom-call(bf16[4,128,256]{2,1,0:T(8,128)(2,1)S(1)} %get-tuple-element.47.refs_0_, bf16[4,128,256]{2,1,0:T(8,128)(2,1)S(1)} %get-tuple-element.48.refs_1_, bf16[4,128,256]{2,1,0:T(8,128)(2,1)S(1)} %pad_maximum_fusion.1.refs_2_.refs_4_, ...), custom_call_target="tpu_custom_call" | custom-call | flops 21474836480 | bytes 2129920 | tf_op jit(solution)/shard_map/pallas_call | solution.py:226
  54.6 0.1 shard_map.79
  54.7 0.4 collective-permute-start.12
  55.1 1.7 %collective-permute-start.13 = (f32[136,256]{1,0:T(8,128)S(1)}, f32[136,256]{1,0:T(8,128)S(1)}, u32[]{:S(2)}, u32[]{:S(2)}) collective-permute-start(f32[136,256]{1,0:T(8,128)S(1)} %get-tuple-element.51), channel_id=1, source_target_pairs={{0,8},{1,9},{2,10},{3,11},{4,12},{5,13},{6,14},{7,15},{8,0},{9,1},... | collective-permute-start | bytes 417800 | tf_op jit(solution)/shard_map/ppermute | solution.py:25
  56.8 0.0 collective-permute-done.16.refs_1_
  56.8 0.8 %collective-permute-start.14 = (f32[136,256]{1,0:T(8,128)S(1)}, f32[136,256]{1,0:T(8,128)S(1)}, u32[]{:S(2)}, u32[]{:S(2)}) collective-permute-start(f32[136,256]{1,0:T(8,128)S(1)} %get-tuple-element.52), channel_id=1, source_target_pairs={{0,12},{1,13},{2,14},{3,15},{4,0},{5,1},{6,2},{7,3},{8,4},{9,5},{1... | collective-permute-start | bytes 417800 | tf_op jit(solution)/shard_map/ppermute | solution.py:25
  57.6 1.6 %shard_map.81.refs_0_ = f32[136,512]{1,0:T(8,128)S(1)} custom-call(bf16[4,128,256]{2,1,0:T(8,128)(2,1)S(1)} %get-tuple-element.47.refs_0_, bf16[4,128,256]{2,1,0:T(8,128)(2,1)S(1)} %get-tuple-element.48.refs_1_, bf16[4,128,256]{2,1,0:T(8,128)(2,1)S(1)} %get-tuple-element.44.refs_2_.refs_0_, bf16[4,128,256]{2,1,0:T(8,128)(2,1)S(1)} %get-tuple-element.45.refs_3_.refs_1_, ...), custom_call_target="tpu_custom_call" | custom-call | flops 536870912 | bytes 1589248 | tf_op jit(solution)/shard_map/pallas_call | solution.py:226
  59.2 0.0 collective-permute-done.18.refs_3_
  59.3 0.1 shard_map.82
  59.4 1.0 %collective-permute-start.19 = (f32[136,128]{1,0:T(8,128)S(1)}, f32[136,128]{1,0:T(8,128)S(1)}, u32[]{:S(2)}, u32[]{:S(2)}) collective-permute-start(f32[136,128]{1,0:T(8,128)S(1)} %get-tuple-element.59), channel_id=1, source_target_pairs={{0,16},{16,32},{32,48},{48,0},{64,80},{80,96},{96,112},{112,64},{1... | collective-permute-start | bytes 208904 | tf_op jit(solution)/shard_map/ppermute | solution.py:30
  60.4 4.8 %collective-permute-start.20 = (f32[136,128]{1,0:T(8,128)S(1)}, f32[136,128]{1,0:T(8,128)S(1)}, u32[]{:S(2)}, u32[]{:S(2)}) collective-permute-start(f32[136,128]{1,0:T(8,128)S(1)} %get-tuple-element.60), channel_id=1, source_target_pairs={{0,32},{16,48},{32,0},{48,16},{64,96},{80,112},{96,64},{112,80},{1... | collective-permute-start | bytes 208904 | tf_op jit(solution)/shard_map/ppermute | solution.py:30
  65.2 3.5 %collective-permute-start.21 = (f32[136,128]{1,0:T(8,128)S(1)}, f32[136,128]{1,0:T(8,128)S(1)}, u32[]{:S(2)}, u32[]{:S(2)}) collective-permute-start(f32[136,128]{1,0:T(8,128)S(1)} %get-tuple-element.61), channel_id=1, source_target_pairs={{0,48},{16,0},{32,16},{48,32},{64,112},{80,64},{96,80},{112,96},{1... | collective-permute-start | bytes 208904 | tf_op jit(solution)/shard_map/ppermute | solution.py:30
  68.6 0.1 shard_map.80
  68.7 0.1 collective-permute-start.15
  68.8 2.5 %collective-permute-done.21.refs_5_ = f32[136,128]{1,0:T(8,128)S(1)} collective-permute-done((f32[136,128]{1,0:T(8,128)S(1)}, f32[136,128]{1,0:T(8,128)S(1)}, u32[]{:S(2)}, u32[]{:S(2)}) %collective-permute-start.21) | collective-permute-done | bytes 69664 | tf_op jit(solution)/shard_map/ppermute | solution.py:30
  71.3 1.2 %collective-permute-done.15.refs_1_ = f32[136,128]{1,0:T(8,128)S(1)} collective-permute-done((f32[136,128]{1,0:T(8,128)S(1)}, f32[136,128]{1,0:T(8,128)S(1)}, u32[]{:S(2)}, u32[]{:S(2)}) %collective-permute-start.15) | collective-permute-done | bytes 69664 | tf_op jit(solution)/shard_map/ppermute | solution.py:34
  72.6 0.8 %shard_map.83 = (f32[128,128]{1,0:T(8,128)}, f32[2,128]{1,0:T(2,128)}, f32[128,128]{1,0:T(8,128)}, f32[2,128]{1,0:T(2,128)}) custom-call(f32[136,128]{1,0:T(8,128)S(1)} %get-tuple-element.53.refs_0_, f32[136,128]{1,0:T(8,128)S(1)} %collective-permute-done.15.refs_1_, f32[136,128]{1,0:T(8,128)S(1)} %get-tuple-element.58.refs_2_, ...), custom_call_target="tpu_custom_call" | custom-call | bytes 550912 | tf_op jit(solution)/shard_map/pallas_call | solution.py:226
  (12 shorter events, 0.1 us)
Async XLA Ops:
  2.3 10.9 %collective-permute-start = (bf16[128,256]{1,0:T(8,128)(2,1)}, bf16[128,256]{1,0:T(8,128)(2,1)S(1)}, u32[]{:S(2)}, u32[]{:S(2)}) collective-permute-start(bf16[128,256]{1,0:T(8,128)(2,1)} %get-tuple-element.33), channel_id=1, source_target_pairs={{0,2},{1,3},{2,0},{3,1},{4,6},{5,7},{6,4},{7,5},{8,10},{9,11},{10,... | collective-permute-start | bytes 196616 | tf_op jit(solution)/shard_map/ppermute | solution.py:34
  4.9 9.3 %collective-permute-start.1 = (bf16[128,256]{1,0:T(8,128)(2,1)}, bf16[128,256]{1,0:T(8,128)(2,1)S(1)}, u32[]{:S(2)}, u32[]{:S(2)}) collective-permute-start(bf16[128,256]{1,0:T(8,128)(2,1)} %get-tuple-element.34), channel_id=1, source_target_pairs={{0,48},{16,0},{32,16},{48,32},{64,112},{80,64},{96,80},{112,96},{1... | collective-permute-start | bytes 196616 | tf_op jit(solution)/shard_map/ppermute | solution.py:30
  10.0 7.5 %collective-permute-start.2 = (bf16[128,256]{1,0:T(8,128)(2,1)}, bf16[128,256]{1,0:T(8,128)(2,1)S(1)}, u32[]{:S(2)}, u32[]{:S(2)}) collective-permute-start(bf16[128,256]{1,0:T(8,128)(2,1)} %get-tuple-element.34), channel_id=1, source_target_pairs={{0,32},{16,48},{32,0},{48,16},{64,96},{80,112},{96,64},{112,80},{1... | collective-permute-start | bytes 196616 | tf_op jit(solution)/shard_map/ppermute | solution.py:30
  11.2 6.8 %collective-permute-start.3 = (bf16[128,256]{1,0:T(8,128)(2,1)}, bf16[128,256]{1,0:T(8,128)(2,1)S(1)}, u32[]{:S(2)}, u32[]{:S(2)}) collective-permute-start(bf16[128,256]{1,0:T(8,128)(2,1)} %get-tuple-element.34), channel_id=1, source_target_pairs={{0,16},{16,32},{32,48},{48,0},{64,80},{80,96},{96,112},{112,64},{1... | collective-permute-start | bytes 196616 | tf_op jit(solution)/shard_map/ppermute | solution.py:30
  13.3 4.7 %copy-start = (bf16[128,256]{1,0:T(8,128)(2,1)S(1)}, bf16[128,256]{1,0:T(8,128)(2,1)}, u32[]{:S(2)}) copy-start(bf16[128,256]{1,0:T(8,128)(2,1)} %get-tuple-element.34) | copy-start | bytes 196612
  18.0 8.1 %collective-permute-start.5 = (bf16[2,128,256]{2,1,0:T(8,128)(2,1)S(1)}, bf16[2,128,256]{2,1,0:T(8,128)(2,1)S(1)}, u32[]{:S(2)}, u32[]{:S(2)}) collective-permute-start(bf16[2,128,256]{2,1,0:T(8,128)(2,1)S(1)} %pad_maximum_fusion.2), channel_id=1, source_target_pairs={{0,8},{1,9},{2,10},{3,11},{4,12},{5,13},{6,14},{7,15},{8,0},{9,1},... | collective-permute-start | bytes 393224 | tf_op jit(solution)/shard_map/ppermute | solution.py:25
  20.8 10.4 %collective-permute-start.7 = (bf16[4,128,256]{2,1,0:T(8,128)(2,1)S(1)}, bf16[4,128,256]{2,1,0:T(8,128)(2,1)S(1)}, u32[]{:S(2)}, u32[]{:S(2)}) collective-permute-start(bf16[4,128,256]{2,1,0:T(8,128)(2,1)S(1)} %pad_maximum_fusion.1.refs_2_.refs_4_), channel_id=1, source_target_pairs={{0,64},{16,80},{32,96},{48,112},{64,128},{80,144},{96,160},{112,17... | collective-permute-start | bytes 786440 | tf_op jit(solution)/shard_map/ppermute | solution.py:25
  22.1 11.4 %collective-permute-start.8 = (bf16[4,128,256]{2,1,0:T(8,128)(2,1)S(1)}, bf16[4,128,256]{2,1,0:T(8,128)(2,1)S(1)}, u32[]{:S(2)}, u32[]{:S(2)}) collective-permute-start(bf16[4,128,256]{2,1,0:T(8,128)(2,1)S(1)} %pad_maximum_fusion.1.refs_2_.refs_4_), channel_id=1, source_target_pairs={{0,128},{16,144},{32,160},{48,176},{64,192},{80,208},{96,224},{112... | collective-permute-start | bytes 786440 | tf_op jit(solution)/shard_map/ppermute | solution.py:25
  24.7 8.8 %collective-permute-start.9 = (bf16[4,128,256]{2,1,0:T(8,128)(2,1)S(1)}, bf16[4,128,256]{2,1,0:T(8,128)(2,1)S(1)}, u32[]{:S(2)}, u32[]{:S(2)}) collective-permute-start(bf16[4,128,256]{2,1,0:T(8,128)(2,1)S(1)} %pad_maximum_fusion.1.refs_2_.refs_4_), channel_id=1, source_target_pairs={{0,192},{16,208},{32,224},{48,240},{64,0},{80,16},{96,32},{112,48}... | collective-permute-start | bytes 786440 | tf_op jit(solution)/shard_map/ppermute | solution.py:25
  25.8 5.3 %collective-permute-start.6 = (bf16[2,128,256]{2,1,0:T(8,128)(2,1)S(1)}, bf16[2,128,256]{2,1,0:T(8,128)(2,1)S(1)}, u32[]{:S(2)}, u32[]{:S(2)}) collective-permute-start(bf16[2,128,256]{2,1,0:T(8,128)(2,1)S(1)} %pad_maximum_fusion.2), channel_id=1, source_target_pairs={{0,4},{1,5},{2,6},{3,7},{4,8},{5,9},{6,10},{7,11},{8,12},{9,13},{1... | collective-permute-start | bytes 393224 | tf_op jit(solution)/shard_map/ppermute | solution.py:25
  26.1 5.0 %collective-permute-start.4 = (bf16[2,128,256]{2,1,0:T(8,128)(2,1)S(1)}, bf16[2,128,256]{2,1,0:T(8,128)(2,1)S(1)}, u32[]{:S(2)}, u32[]{:S(2)}) collective-permute-start(bf16[2,128,256]{2,1,0:T(8,128)(2,1)S(1)} %pad_maximum_fusion.2), channel_id=1, source_target_pairs={{0,12},{1,13},{2,14},{3,15},{4,0},{5,1},{6,2},{7,3},{8,4},{9,5},{1... | collective-permute-start | bytes 393224 | tf_op jit(solution)/shard_map/ppermute | solution.py:25
  33.5 5.6 %collective-permute-start.10 = (bf16[2,4,128,256]{3,2,1,0:T(8,128)(2,1)S(1)}, bf16[2,4,128,256]{3,2,1,0:T(8,128)(2,1)S(1)}, u32[]{:S(2)}, u32[]{:S(2)}) collective-permute-start(bf16[2,4,128,256]{3,2,1,0:T(8,128)(2,1)S(1)} %pad_maximum_fusion), channel_id=1, source_target_pairs={{0,1},{1,0},{2,3},{3,2},{4,5},{5,4},{6,7},{7,6},{8,9},{9,8},{10,11... | collective-permute-start | bytes 1572872 | tf_op jit(solution)/shard_map/ppermute | solution.py:34
  43.1 13.7 %collective-permute-start.16 = (f32[136,512]{1,0:T(8,128)S(1)}, f32[136,512]{1,0:T(8,128)S(1)}, u32[]{:S(2)}, u32[]{:S(2)}) collective-permute-start(f32[136,512]{1,0:T(8,128)S(1)} %get-tuple-element.55), channel_id=1, source_target_pairs={{0,64},{16,80},{32,96},{48,112},{64,128},{80,144},{96,160},{112,17... | collective-permute-start | bytes 835592 | tf_op jit(solution)/shard_map/ppermute | solution.py:25
  44.2 15.0 %collective-permute-start.17 = (f32[136,512]{1,0:T(8,128)S(1)}, f32[136,512]{1,0:T(8,128)S(1)}, u32[]{:S(2)}, u32[]{:S(2)}) collective-permute-start(f32[136,512]{1,0:T(8,128)S(1)} %get-tuple-element.56), channel_id=1, source_target_pairs={{0,128},{16,144},{32,160},{48,176},{64,192},{80,208},{96,224},{112... | collective-permute-start | bytes 835592 | tf_op jit(solution)/shard_map/ppermute | solution.py:25
  46.3 12.9 %collective-permute-start.18 = (f32[136,512]{1,0:T(8,128)S(1)}, f32[136,512]{1,0:T(8,128)S(1)}, u32[]{:S(2)}, u32[]{:S(2)}) collective-permute-start(f32[136,512]{1,0:T(8,128)S(1)} %get-tuple-element.57), channel_id=1, source_target_pairs={{0,192},{16,208},{32,224},{48,240},{64,0},{80,16},{96,32},{112,48}... | collective-permute-start | bytes 835592 | tf_op jit(solution)/shard_map/ppermute | solution.py:25
  50.5 4.1 %collective-permute-start.11 = (f32[2,136,512]{2,1,0:T(8,128)S(1)}, f32[2,136,512]{2,1,0:T(8,128)S(1)}, u32[]{:S(2)}, u32[]{:S(2)}) collective-permute-start(f32[2,136,512]{2,1,0:T(8,128)S(1)} %shard_map.77), channel_id=1, source_target_pairs={{0,1},{1,0},{2,3},{3,2},{4,5},{5,4},{6,7},{7,6},{8,9},{9,8},{10,11... | collective-permute-start | bytes 1671176 | tf_op jit(solution)/shard_map/ppermute | solution.py:34
  54.7 10.4 %collective-permute-start.12 = (f32[136,256]{1,0:T(8,128)S(1)}, f32[136,256]{1,0:T(8,128)S(1)}, u32[]{:S(2)}, u32[]{:S(2)}) collective-permute-start(f32[136,256]{1,0:T(8,128)S(1)} %get-tuple-element.50), channel_id=1, source_target_pairs={{0,4},{1,5},{2,6},{3,7},{4,8},{5,9},{6,10},{7,11},{8,12},{9,13},{1... | collective-permute-start | bytes 417800 | tf_op jit(solution)/shard_map/ppermute | solution.py:25
  55.1 13.5 %collective-permute-start.13 = (f32[136,256]{1,0:T(8,128)S(1)}, f32[136,256]{1,0:T(8,128)S(1)}, u32[]{:S(2)}, u32[]{:S(2)}) collective-permute-start(f32[136,256]{1,0:T(8,128)S(1)} %get-tuple-element.51), channel_id=1, source_target_pairs={{0,8},{1,9},{2,10},{3,11},{4,12},{5,13},{6,14},{7,15},{8,0},{9,1},... | collective-permute-start | bytes 417800 | tf_op jit(solution)/shard_map/ppermute | solution.py:25
  56.8 11.8 %collective-permute-start.14 = (f32[136,256]{1,0:T(8,128)S(1)}, f32[136,256]{1,0:T(8,128)S(1)}, u32[]{:S(2)}, u32[]{:S(2)}) collective-permute-start(f32[136,256]{1,0:T(8,128)S(1)} %get-tuple-element.52), channel_id=1, source_target_pairs={{0,12},{1,13},{2,14},{3,15},{4,0},{5,1},{6,2},{7,3},{8,4},{9,5},{1... | collective-permute-start | bytes 417800 | tf_op jit(solution)/shard_map/ppermute | solution.py:25
  59.4 9.5 %collective-permute-start.19 = (f32[136,128]{1,0:T(8,128)S(1)}, f32[136,128]{1,0:T(8,128)S(1)}, u32[]{:S(2)}, u32[]{:S(2)}) collective-permute-start(f32[136,128]{1,0:T(8,128)S(1)} %get-tuple-element.59), channel_id=1, source_target_pairs={{0,16},{16,32},{32,48},{48,0},{64,80},{80,96},{96,112},{112,64},{1... | collective-permute-start | bytes 208904 | tf_op jit(solution)/shard_map/ppermute | solution.py:30
  60.4 8.5 %collective-permute-start.20 = (f32[136,128]{1,0:T(8,128)S(1)}, f32[136,128]{1,0:T(8,128)S(1)}, u32[]{:S(2)}, u32[]{:S(2)}) collective-permute-start(f32[136,128]{1,0:T(8,128)S(1)} %get-tuple-element.60), channel_id=1, source_target_pairs={{0,32},{16,48},{32,0},{48,16},{64,96},{80,112},{96,64},{112,80},{1... | collective-permute-start | bytes 208904 | tf_op jit(solution)/shard_map/ppermute | solution.py:30
  65.2 6.2 %collective-permute-start.21 = (f32[136,128]{1,0:T(8,128)S(1)}, f32[136,128]{1,0:T(8,128)S(1)}, u32[]{:S(2)}, u32[]{:S(2)}) collective-permute-start(f32[136,128]{1,0:T(8,128)S(1)} %get-tuple-element.61), channel_id=1, source_target_pairs={{0,48},{16,0},{32,16},{48,32},{64,112},{80,64},{96,80},{112,96},{1... | collective-permute-start | bytes 208904 | tf_op jit(solution)/shard_map/ppermute | solution.py:30
  68.7 3.8 %collective-permute-start.15 = (f32[136,128]{1,0:T(8,128)S(1)}, f32[136,128]{1,0:T(8,128)S(1)}, u32[]{:S(2)}, u32[]{:S(2)}) collective-permute-start(f32[136,128]{1,0:T(8,128)S(1)} %get-tuple-element.54), channel_id=1, source_target_pairs={{0,2},{1,3},{2,0},{3,1},{4,6},{5,7},{6,4},{7,5},{8,10},{9,11},{10,... | collective-permute-start | bytes 208904 | tf_op jit(solution)/shard_map/ppermute | solution.py:34

commit v12 on v11

--- a/solution.py
+++ b/solution.py
@@ -305,11 +305,12 @@
     (send_one,) = row_scores(ones[2:], twos, ((0, 0), (0, 1)), 2, 2)
     theirs_one = fast_swap("col", send_one, 1)
     (keep_one,) = row_scores(ones[:2], twos, ((0, 0), (0, 1)), 40, 2)
-    cols = call(block_kernel, [f32(ROWS, SHARD)] * SUB, cols, work=1 * work)
-    cols = [cols[0]] + [fast_shift("row", cols[step], step) for step in range(1, SUB)]
+    cols = list(call(block_kernel, [f32(ROWS, SHARD)] * SUB, cols, work=1 * work))
     rows = spread("col", core_merge(keep_one, theirs_one, 0, 1))
     keep, send = call(chip_kernel, [f32(ROWS, SHARD)] * 2, rows)
     theirs = fast_swap("col", send, 2)
+    cols[1], keep = together((cols[1], keep))
+    cols = [cols[0]] + [fast_shift("row", cols[step], step) for step in range(1, SUB)]
     outs = [f32(SHARD, WIDTH), f32(2, SHARD)] * 2
     return tuple(call(functools.partial(finish_kernel, total), outs, (keep, theirs, *cols)))
 

time: 74.8 us -> 73.9 us (0.988); the launches traced: 73.4 us -> 73.6 us
  waiting for transfers between devices: 14 us -> 14.9 us
    ppermute x6, starting transfers between devices: 17.6 us -> 14.2 us  [fast_shift(): return lax.ppermute(value, axis, pairs)]
    ppermute x4, starting transfers between devices: 8.03 us -> 9.62 us  [fast_swap(): return lax.ppermute(value, axis, [(i, i ^ step) for i in range(SUB * SUB)])]
    ppermute x12, starting transfers between devices: 18 us -> 19.1 us  [slow_shift(): return lax.ppermute(value, axis, pairs)]
  transfers between devices with their start and end apart: 22 -> 22, of which waited for: 7 -> 8; matrix products, arithmetic and copies ran while one was open for 1% -> 1% of each run, Pallas kernels for 10% -> 10%
where the time goes in v12:
time: 73.9 us; the launch traced here: 73.6 us
  starting transfers between devices  43 us (58%)
  waiting for transfers between devices  14.9 us (20%)
  Pallas kernels  13.9 us (19%)
  other arithmetic  0.99 us (1%)
  between operations  0.78 us (1%)
    ppermute x12, starting transfers between devices, slow_shift(): return lax.ppermute(value, axis, pairs)  19.1 us
    ppermute x6, starting transfers between devices, fast_shift(): return lax.ppermute(value, axis, pairs)  14.2 us
    pallas_call x9, Pallas kernels, call(): pl.pallas_call(kernel, out_shape=shapes, in_specs=specs or [VMEM] * len(a...  13.9 us
    ppermute x4, starting transfers between devices, fast_swap(): return lax.ppermute(value, axis, [(i, i ^ step) for i in range(SUB * SUB)])  9.62 us
    ppermute x6, waiting for transfers between devices, fast_shift(): return lax.ppermute(value, axis, pairs)  6.78 us
    ppermute x12, waiting for transfers between devices, slow_shift(): return lax.ppermute(value, axis, pairs)  5.12 us
    ppermute x4, waiting for transfers between devices, fast_swap(): return lax.ppermute(value, axis, [(i, i ^ step) for i in range(SUB * SUB)])  2.99 us
  transfers between devices with their start and end apart: 22, of which 8 were waited for; matrix products, arithmetic and copies ran while one was open for 1% of the time, Pallas kernels for 10%

profile of v12, /device:TPU:1, one launch (start us, length us, event | category | flops | bytes accessed | tf_op | source)
XLA Modules:
  0.0 73.6 jit_solution(1060697536129574068)
XLA Ops:
  0.6 1.7 %shard_map.75 = (bf16[128,256]{1,0:T(8,128)(2,1)}, bf16[128,256]{1,0:T(8,128)(2,1)}) custom-call(bf16[128,128]{1,0:T(8,128)(2,1)} %feat_one.1, bf16[128,128]{1,0:T(8,128)(2,1)} %value_one.1, bf16[128,128]{1,0:T(8,128)(2,1)} %feat_two.1, bf16[128,128]{1,0:T(8,128)(2,1)} %value_two.1), custom_call_target="tpu_custom_call" | custom-call | bytes 262144 | tf_op jit(solution)/shard_map/pallas_call | solution.py:226
  2.3 2.6 %collective-permute-start = (bf16[128,256]{1,0:T(8,128)(2,1)}, bf16[128,256]{1,0:T(8,128)(2,1)S(1)}, u32[]{:S(2)}, u32[]{:S(2)}) collective-permute-start(bf16[128,256]{1,0:T(8,128)(2,1)} %get-tuple-element.35), channel_id=1, source_target_pairs={{0,2},{1,3},{2,0},{3,1},{4,6},{5,7},{6,4},{7,5},{8,10},{9,11},{10,... | collective-permute-start | bytes 196616 | tf_op jit(solution)/shard_map/ppermute | solution.py:34
  4.9 3.0 %collective-permute-start.3 = (bf16[128,256]{1,0:T(8,128)(2,1)}, bf16[128,256]{1,0:T(8,128)(2,1)S(1)}, u32[]{:S(2)}, u32[]{:S(2)}) collective-permute-start(bf16[128,256]{1,0:T(8,128)(2,1)} %get-tuple-element.36), channel_id=1, source_target_pairs={{0,16},{16,32},{32,48},{48,0},{64,80},{80,96},{96,112},{112,64},{1... | collective-permute-start | bytes 196616 | tf_op jit(solution)/shard_map/ppermute | solution.py:30
  7.9 4.2 %collective-permute-start.2 = (bf16[128,256]{1,0:T(8,128)(2,1)}, bf16[128,256]{1,0:T(8,128)(2,1)S(1)}, u32[]{:S(2)}, u32[]{:S(2)}) collective-permute-start(bf16[128,256]{1,0:T(8,128)(2,1)} %get-tuple-element.36), channel_id=1, source_target_pairs={{0,32},{16,48},{32,0},{48,16},{64,96},{80,112},{96,64},{112,80},{1... | collective-permute-start | bytes 196616 | tf_op jit(solution)/shard_map/ppermute | solution.py:30
  12.1 2.4 %collective-permute-start.1 = (bf16[128,256]{1,0:T(8,128)(2,1)}, bf16[128,256]{1,0:T(8,128)(2,1)S(1)}, u32[]{:S(2)}, u32[]{:S(2)}) collective-permute-start(bf16[128,256]{1,0:T(8,128)(2,1)} %get-tuple-element.36), channel_id=1, source_target_pairs={{0,48},{16,0},{32,16},{48,32},{64,112},{80,64},{96,80},{112,96},{1... | collective-permute-start | bytes 196616 | tf_op jit(solution)/shard_map/ppermute | solution.py:30
  14.5 0.9 %pad_maximum_fusion.2 = bf16[2,128,256]{2,1,0:T(8,128)(2,1)S(1)} fusion(bf16[1,128,256]{2,1,0:T(8,128)(2,1)S(1)} %bitcast.29, bf16[1,128,256]{2,1,0:T(8,128)(2,1)} %bitcast.28), kind=kLoop, calls=%fused_computation.6 | loop fusion | flops 65536 | bytes 262144 | tf_op jit(solution)/shard_map/stack | solution.py:269
  15.4 0.0 collective-permute-done.3
  15.4 1.9 %collective-permute-done.2 = bf16[128,256]{1,0:T(8,128)(2,1)S(1)} collective-permute-done((bf16[128,256]{1,0:T(8,128)(2,1)}, bf16[128,256]{1,0:T(8,128)(2,1)S(1)}, u32[]{:S(2)}, u32[]{:S(2)}) %collective-permute-start.2) | collective-permute-done | bytes 65568 | tf_op jit(solution)/shard_map/ppermute | solution.py:30
  17.3 1.0 %collective-permute-done.1 = bf16[128,256]{1,0:T(8,128)(2,1)S(1)} collective-permute-done((bf16[128,256]{1,0:T(8,128)(2,1)}, bf16[128,256]{1,0:T(8,128)(2,1)S(1)}, u32[]{:S(2)}, u32[]{:S(2)}) %collective-permute-start.1) | collective-permute-done | bytes 65568 | tf_op jit(solution)/shard_map/ppermute | solution.py:30
  18.3 1.3 %collective-permute-start.6 = (bf16[2,128,256]{2,1,0:T(8,128)(2,1)S(1)}, bf16[2,128,256]{2,1,0:T(8,128)(2,1)S(1)}, u32[]{:S(2)}, u32[]{:S(2)}) collective-permute-start(bf16[2,128,256]{2,1,0:T(8,128)(2,1)S(1)} %pad_maximum_fusion.2), channel_id=1, source_target_pairs={{0,4},{1,5},{2,6},{3,7},{4,8},{5,9},{6,10},{7,11},{8,12},{9,13},{1... | collective-permute-start | bytes 393224 | tf_op jit(solution)/shard_map/ppermute | solution.py:25
  19.6 1.3 %collective-permute-start.7 = (bf16[4,128,256]{2,1,0:T(8,128)(2,1)S(1)}, bf16[4,128,256]{2,1,0:T(8,128)(2,1)S(1)}, u32[]{:S(2)}, u32[]{:S(2)}) collective-permute-start(bf16[4,128,256]{2,1,0:T(8,128)(2,1)S(1)} %pad_maximum_fusion.1.refs_4_.refs_2_), channel_id=1, source_target_pairs={{0,64},{16,80},{32,96},{48,112},{64,128},{80,144},{96,160},{112,17... | collective-permute-start | bytes 786440 | tf_op jit(solution)/shard_map/ppermute | solution.py:25
  20.9 2.6 %collective-permute-start.8 = (bf16[4,128,256]{2,1,0:T(8,128)(2,1)S(1)}, bf16[4,128,256]{2,1,0:T(8,128)(2,1)S(1)}, u32[]{:S(2)}, u32[]{:S(2)}) collective-permute-start(bf16[4,128,256]{2,1,0:T(8,128)(2,1)S(1)} %pad_maximum_fusion.1.refs_4_.refs_2_), channel_id=1, source_target_pairs={{0,128},{16,144},{32,160},{48,176},{64,192},{80,208},{96,224},{112... | collective-permute-start | bytes 786440 | tf_op jit(solution)/shard_map/ppermute | solution.py:25
  23.5 1.1 %collective-permute-start.9 = (bf16[4,128,256]{2,1,0:T(8,128)(2,1)S(1)}, bf16[4,128,256]{2,1,0:T(8,128)(2,1)S(1)}, u32[]{:S(2)}, u32[]{:S(2)}) collective-permute-start(bf16[4,128,256]{2,1,0:T(8,128)(2,1)S(1)} %pad_maximum_fusion.1.refs_4_.refs_2_), channel_id=1, source_target_pairs={{0,192},{16,208},{32,224},{48,240},{64,0},{80,16},{96,32},{112,48}... | collective-permute-start | bytes 786440 | tf_op jit(solution)/shard_map/ppermute | solution.py:25
  24.6 2.5 %collective-permute-start.5 = (bf16[2,128,256]{2,1,0:T(8,128)(2,1)S(1)}, bf16[2,128,256]{2,1,0:T(8,128)(2,1)S(1)}, u32[]{:S(2)}, u32[]{:S(2)}) collective-permute-start(bf16[2,128,256]{2,1,0:T(8,128)(2,1)S(1)} %pad_maximum_fusion.2), channel_id=1, source_target_pairs={{0,8},{1,9},{2,10},{3,11},{4,12},{5,13},{6,14},{7,15},{8,0},{9,1},... | collective-permute-start | bytes 393224 | tf_op jit(solution)/shard_map/ppermute | solution.py:25
  27.1 1.2 %collective-permute-start.4 = (bf16[2,128,256]{2,1,0:T(8,128)(2,1)S(1)}, bf16[2,128,256]{2,1,0:T(8,128)(2,1)S(1)}, u32[]{:S(2)}, u32[]{:S(2)}) collective-permute-start(bf16[2,128,256]{2,1,0:T(8,128)(2,1)S(1)} %pad_maximum_fusion.2), channel_id=1, source_target_pairs={{0,12},{1,13},{2,14},{3,15},{4,0},{5,1},{6,2},{7,3},{8,4},{9,5},{1... | collective-permute-start | bytes 393224 | tf_op jit(solution)/shard_map/ppermute | solution.py:25
  28.2 1.7 %collective-permute-done.5 = bf16[2,128,256]{2,1,0:T(8,128)(2,1)S(1)} collective-permute-done((bf16[2,128,256]{2,1,0:T(8,128)(2,1)S(1)}, bf16[2,128,256]{2,1,0:T(8,128)(2,1)S(1)}, u32[]{:S(2)}, u32[]{:S(2)}) %collective-permute-start.5) | collective-permute-done | bytes 131104 | tf_op jit(solution)/shard_map/ppermute | solution.py:25
  29.9 0.9 %collective-permute-done.4 = bf16[2,128,256]{2,1,0:T(8,128)(2,1)S(1)} collective-permute-done((bf16[2,128,256]{2,1,0:T(8,128)(2,1)S(1)}, bf16[2,128,256]{2,1,0:T(8,128)(2,1)S(1)}, u32[]{:S(2)}, u32[]{:S(2)}) %collective-permute-start.4) | collective-permute-done | bytes 131104 | tf_op jit(solution)/shard_map/ppermute | solution.py:25
  30.9 0.1 pad_maximum_fusion
  31.0 0.0 collective-permute-done.7.refs_5_
  31.0 2.4 %collective-permute-done.8.refs_4_ = bf16[4,128,256]{2,1,0:T(8,128)(2,1)S(1)} collective-permute-done((bf16[4,128,256]{2,1,0:T(8,128)(2,1)S(1)}, bf16[4,128,256]{2,1,0:T(8,128)(2,1)S(1)}, u32[]{:S(2)}, u32[]{:S(2)}) %collective-permute-start.8) | collective-permute-done | bytes 262176 | tf_op jit(solution)/shard_map/ppermute | solution.py:25
  33.4 3.0 %collective-permute-start.10 = (bf16[2,4,128,256]{3,2,1,0:T(8,128)(2,1)S(1)}, bf16[2,4,128,256]{3,2,1,0:T(8,128)(2,1)S(1)}, u32[]{:S(2)}, u32[]{:S(2)}) collective-permute-start(bf16[2,4,128,256]{3,2,1,0:T(8,128)(2,1)S(1)} %pad_maximum_fusion), channel_id=1, source_target_pairs={{0,1},{1,0},{2,3},{3,2},{4,5},{5,4},{6,7},{7,6},{8,9},{9,8},{10,11... | collective-permute-start | bytes 1572872 | tf_op jit(solution)/shard_map/ppermute | solution.py:34
  36.5 1.5 %collective-permute-done.10 = bf16[2,4,128,256]{3,2,1,0:T(8,128)(2,1)S(1)} collective-permute-done((bf16[2,4,128,256]{3,2,1,0:T(8,128)(2,1)S(1)}, bf16[2,4,128,256]{3,2,1,0:T(8,128)(2,1)S(1)}, u32[]{:S(2)}, u32[]{:S(2)}) %collective-permute-start.10) | collective-permute-done | bytes 524320 | tf_op jit(solution)/shard_map/ppermute | solution.py:34
  38.0 3.9 %shard_map.76 = (f32[136,512]{1,0:T(8,128)S(1)}, f32[136,512]{1,0:T(8,128)S(1)}, f32[136,512]{1,0:T(8,128)S(1)}) custom-call(bf16[4,128,256]{2,1,0:T(8,128)(2,1)S(1)} %get-tuple-element.46.refs_0_, bf16[4,128,256]{2,1,0:T(8,128)(2,1)S(1)} %get-tuple-element.47.refs_1_, bf16[4,128,256]{2,1,0:T(8,128)(2,1)S(1)} %get-tuple-element.48.refs_2_.refs_0_, ...), custom_call_target="tpu_custom_call" | custom-call | flops 1610612736 | bytes 2670592 | tf_op jit(solution)/shard_map/pallas_call | solution.py:226
  42.0 1.1 %collective-permute-start.11 = (f32[136,512]{1,0:T(8,128)S(1)}, f32[136,512]{1,0:T(8,128)S(1)}, u32[]{:S(2)}, u32[]{:S(2)}) collective-permute-start(f32[136,512]{1,0:T(8,128)S(1)} %get-tuple-element.51), channel_id=1, source_target_pairs={{0,64},{16,80},{32,96},{48,112},{64,128},{80,144},{96,160},{112,17... | collective-permute-start | bytes 835592 | tf_op jit(solution)/shard_map/ppermute | solution.py:25
  43.1 2.1 %collective-permute-start.12 = (f32[136,512]{1,0:T(8,128)S(1)}, f32[136,512]{1,0:T(8,128)S(1)}, u32[]{:S(2)}, u32[]{:S(2)}) collective-permute-start(f32[136,512]{1,0:T(8,128)S(1)} %get-tuple-element.52), channel_id=1, source_target_pairs={{0,128},{16,144},{32,160},{48,176},{64,192},{80,208},{96,224},{112... | collective-permute-start | bytes 835592 | tf_op jit(solution)/shard_map/ppermute | solution.py:25
  45.2 1.4 %collective-permute-start.13 = (f32[136,512]{1,0:T(8,128)S(1)}, f32[136,512]{1,0:T(8,128)S(1)}, u32[]{:S(2)}, u32[]{:S(2)}) collective-permute-start(f32[136,512]{1,0:T(8,128)S(1)} %get-tuple-element.53), channel_id=1, source_target_pairs={{0,192},{16,208},{32,224},{48,240},{64,0},{80,16},{96,32},{112,48}... | collective-permute-start | bytes 835592 | tf_op jit(solution)/shard_map/ppermute | solution.py:25
  46.6 2.8 %shard_map.79 = f32[2,136,512]{2,1,0:T(8,128)S(1)} custom-call(bf16[4,128,256]{2,1,0:T(8,128)(2,1)S(1)} %get-tuple-element.48.refs_2_.refs_0_, bf16[4,128,256]{2,1,0:T(8,128)(2,1)S(1)} %get-tuple-element.49.refs_3_.refs_1_, bf16[4,128,256]{2,1,0:T(8,128)(2,1)S(1)} %pad_maximum_fusion.1.refs_4_.refs_2_, ...), custom_call_target="tpu_custom_call" | custom-call | flops 1073741824 | bytes 2129920 | tf_op jit(solution)/shard_map/pallas_call | solution.py:226
  49.4 1.3 %collective-permute-start.14 = (f32[2,136,512]{2,1,0:T(8,128)S(1)}, f32[2,136,512]{2,1,0:T(8,128)S(1)}, u32[]{:S(2)}, u32[]{:S(2)}) collective-permute-start(f32[2,136,512]{2,1,0:T(8,128)S(1)} %shard_map.79), channel_id=1, source_target_pairs={{0,1},{1,0},{2,3},{3,2},{4,5},{5,4},{6,7},{7,6},{8,9},{9,8},{10,11... | collective-permute-start | bytes 1671176 | tf_op jit(solution)/shard_map/ppermute | solution.py:34
  50.7 2.8 %shard_map.80.refs_1_ = f32[2,136,512]{2,1,0:T(8,128)S(1)} custom-call(bf16[4,128,256]{2,1,0:T(8,128)(2,1)S(1)} %get-tuple-element.46.refs_0_, bf16[4,128,256]{2,1,0:T(8,128)(2,1)S(1)} %get-tuple-element.47.refs_1_, bf16[4,128,256]{2,1,0:T(8,128)(2,1)S(1)} %pad_maximum_fusion.1.refs_4_.refs_2_, ...), custom_call_target="tpu_custom_call" | custom-call | flops 21474836480 | bytes 2129920 | tf_op jit(solution)/shard_map/pallas_call | solution.py:226
  53.5 0.0 collective-permute-done.14.refs_0_
  53.5 0.1 shard_map.81
  53.6 1.3 %collective-permute-start.15 = (f32[136,256]{1,0:T(8,128)S(1)}, f32[136,256]{1,0:T(8,128)S(1)}, u32[]{:S(2)}, u32[]{:S(2)}) collective-permute-start(f32[136,256]{1,0:T(8,128)S(1)} %get-tuple-element.56), channel_id=1, source_target_pairs={{0,4},{1,5},{2,6},{3,7},{4,8},{5,9},{6,10},{7,11},{8,12},{9,13},{1... | collective-permute-start | bytes 417800 | tf_op jit(solution)/shard_map/ppermute | solution.py:25
  54.9 1.5 %collective-permute-start.16 = (f32[136,256]{1,0:T(8,128)S(1)}, f32[136,256]{1,0:T(8,128)S(1)}, u32[]{:S(2)}, u32[]{:S(2)}) collective-permute-start(f32[136,256]{1,0:T(8,128)S(1)} %get-tuple-element.57), channel_id=1, source_target_pairs={{0,8},{1,9},{2,10},{3,11},{4,12},{5,13},{6,14},{7,15},{8,0},{9,1},... | collective-permute-start | bytes 417800 | tf_op jit(solution)/shard_map/ppermute | solution.py:25
  56.3 0.0 collective-permute-done.11.refs_1_
  56.3 1.9 %collective-permute-start.17 = (f32[136,256]{1,0:T(8,128)S(1)}, f32[136,256]{1,0:T(8,128)S(1)}, u32[]{:S(2)}, u32[]{:S(2)}) collective-permute-start(f32[136,256]{1,0:T(8,128)S(1)} %get-tuple-element.58), channel_id=1, source_target_pairs={{0,12},{1,13},{2,14},{3,15},{4,0},{5,1},{6,2},{7,3},{8,4},{9,5},{1... | collective-permute-start | bytes 417800 | tf_op jit(solution)/shard_map/ppermute | solution.py:25
  58.2 1.6 %shard_map.77.refs_0_ = f32[136,512]{1,0:T(8,128)S(1)} custom-call(bf16[4,128,256]{2,1,0:T(8,128)(2,1)S(1)} %get-tuple-element.46.refs_0_, bf16[4,128,256]{2,1,0:T(8,128)(2,1)S(1)} %get-tuple-element.47.refs_1_, bf16[4,128,256]{2,1,0:T(8,128)(2,1)S(1)} %get-tuple-element.48.refs_2_.refs_0_, bf16[4,128,256]{2,1,0:T(8,128)(2,1)S(1)} %get-tuple-element.49.refs_3_.refs_1_, ...), custom_call_target="tpu_custom_call" | custom-call | flops 536870912 | bytes 1589248 | tf_op jit(solution)/shard_map/pallas_call | solution.py:226
  59.8 0.0 collective-permute-done.12.refs_2_
  59.8 0.1 shard_map.78
  59.9 4.1 %collective-permute-start.20 = (f32[136,128]{1,0:T(8,128)S(1)}, f32[136,128]{1,0:T(8,128)S(1)}, u32[]{:S(2)}, u32[]{:S(2)}) collective-permute-start(f32[136,128]{1,0:T(8,128)S(1)} %get-tuple-element.64), channel_id=1, source_target_pairs={{0,32},{16,48},{32,0},{48,16},{64,96},{80,112},{96,64},{112,80},{1... | collective-permute-start | bytes 208904 | tf_op jit(solution)/shard_map/ppermute | solution.py:30
  64.0 0.0 collective-permute-start.21
  64.0 0.0 collective-permute-done.15.refs_1_
  64.1 0.1 shard_map.82
  64.1 2.8 %collective-permute-start.18 = (f32[136,128]{1,0:T(8,128)S(1)}, f32[136,128]{1,0:T(8,128)S(1)}, u32[]{:S(2)}, u32[]{:S(2)}) collective-permute-start(f32[136,128]{1,0:T(8,128)S(1)} %get-tuple-element.61), channel_id=1, source_target_pairs={{0,2},{1,3},{2,0},{3,1},{4,6},{5,7},{6,4},{7,5},{8,10},{9,11},{10,... | collective-permute-start | bytes 208904 | tf_op jit(solution)/shard_map/ppermute | solution.py:34
  66.9 0.5 collective-permute-start.19
  67.4 3.8 %collective-permute-done.21.refs_5_ = f32[136,128]{1,0:T(8,128)S(1)} collective-permute-done((f32[136,128]{1,0:T(8,128)S(1)}, f32[136,128]{1,0:T(8,128)S(1)}, u32[]{:S(2)}, u32[]{:S(2)}) %collective-permute-start.21) | collective-permute-done | bytes 69664 | tf_op jit(solution)/shard_map/ppermute | solution.py:30
  71.3 1.5 %collective-permute-done.18.refs_1_ = f32[136,128]{1,0:T(8,128)S(1)} collective-permute-done((f32[136,128]{1,0:T(8,128)S(1)}, f32[136,128]{1,0:T(8,128)S(1)}, u32[]{:S(2)}, u32[]{:S(2)}) %collective-permute-start.18) | collective-permute-done | bytes 69664 | tf_op jit(solution)/shard_map/ppermute | solution.py:34
  72.8 0.0 collective-permute-done.19.refs_3_
  72.8 0.8 %shard_map.83 = (f32[128,128]{1,0:T(8,128)}, f32[2,128]{1,0:T(2,128)}, f32[128,128]{1,0:T(8,128)}, f32[2,128]{1,0:T(2,128)}) custom-call(f32[136,128]{1,0:T(8,128)S(1)} %get-tuple-element.60.refs_0_, f32[136,128]{1,0:T(8,128)S(1)} %collective-permute-done.18.refs_1_, f32[136,128]{1,0:T(8,128)S(1)} %get-tuple-element.62.refs_2_, ...), custom_call_target="tpu_custom_call" | custom-call | bytes 550912 | tf_op jit(solution)/shard_map/pallas_call | solution.py:226
  (12 shorter events, 0.1 us)
Async XLA Ops:
  2.3 12.1 %collective-permute-start = (bf16[128,256]{1,0:T(8,128)(2,1)}, bf16[128,256]{1,0:T(8,128)(2,1)S(1)}, u32[]{:S(2)}, u32[]{:S(2)}) collective-permute-start(bf16[128,256]{1,0:T(8,128)(2,1)} %get-tuple-element.35), channel_id=1, source_target_pairs={{0,2},{1,3},{2,0},{3,1},{4,6},{5,7},{6,4},{7,5},{8,10},{9,11},{10,... | collective-permute-start | bytes 196616 | tf_op jit(solution)/shard_map/ppermute | solution.py:34
  4.9 10.5 %collective-permute-start.3 = (bf16[128,256]{1,0:T(8,128)(2,1)}, bf16[128,256]{1,0:T(8,128)(2,1)S(1)}, u32[]{:S(2)}, u32[]{:S(2)}) collective-permute-start(bf16[128,256]{1,0:T(8,128)(2,1)} %get-tuple-element.36), channel_id=1, source_target_pairs={{0,16},{16,32},{32,48},{48,0},{64,80},{80,96},{96,112},{112,64},{1... | collective-permute-start | bytes 196616 | tf_op jit(solution)/shard_map/ppermute | solution.py:30
  7.9 9.4 %collective-permute-start.2 = (bf16[128,256]{1,0:T(8,128)(2,1)}, bf16[128,256]{1,0:T(8,128)(2,1)S(1)}, u32[]{:S(2)}, u32[]{:S(2)}) collective-permute-start(bf16[128,256]{1,0:T(8,128)(2,1)} %get-tuple-element.36), channel_id=1, source_target_pairs={{0,32},{16,48},{32,0},{48,16},{64,96},{80,112},{96,64},{112,80},{1... | collective-permute-start | bytes 196616 | tf_op jit(solution)/shard_map/ppermute | solution.py:30
  12.1 6.2 %collective-permute-start.1 = (bf16[128,256]{1,0:T(8,128)(2,1)}, bf16[128,256]{1,0:T(8,128)(2,1)S(1)}, u32[]{:S(2)}, u32[]{:S(2)}) collective-permute-start(bf16[128,256]{1,0:T(8,128)(2,1)} %get-tuple-element.36), channel_id=1, source_target_pairs={{0,48},{16,0},{32,16},{48,32},{64,112},{80,64},{96,80},{112,96},{1... | collective-permute-start | bytes 196616 | tf_op jit(solution)/shard_map/ppermute | solution.py:30
  14.5 3.8 %copy-start = (bf16[128,256]{1,0:T(8,128)(2,1)S(1)}, bf16[128,256]{1,0:T(8,128)(2,1)}, u32[]{:S(2)}) copy-start(bf16[128,256]{1,0:T(8,128)(2,1)} %get-tuple-element.36) | copy-start | bytes 196612
  18.3 8.7 %collective-permute-start.6 = (bf16[2,128,256]{2,1,0:T(8,128)(2,1)S(1)}, bf16[2,128,256]{2,1,0:T(8,128)(2,1)S(1)}, u32[]{:S(2)}, u32[]{:S(2)}) collective-permute-start(bf16[2,128,256]{2,1,0:T(8,128)(2,1)S(1)} %pad_maximum_fusion.2), channel_id=1, source_target_pairs={{0,4},{1,5},{2,6},{3,7},{4,8},{5,9},{6,10},{7,11},{8,12},{9,13},{1... | collective-permute-start | bytes 393224 | tf_op jit(solution)/shard_map/ppermute | solution.py:25
  19.6 11.3 %collective-permute-start.7 = (bf16[4,128,256]{2,1,0:T(8,128)(2,1)S(1)}, bf16[4,128,256]{2,1,0:T(8,128)(2,1)S(1)}, u32[]{:S(2)}, u32[]{:S(2)}) collective-permute-start(bf16[4,128,256]{2,1,0:T(8,128)(2,1)S(1)} %pad_maximum_fusion.1.refs_4_.refs_2_), channel_id=1, source_target_pairs={{0,64},{16,80},{32,96},{48,112},{64,128},{80,144},{96,160},{112,17... | collective-permute-start | bytes 786440 | tf_op jit(solution)/shard_map/ppermute | solution.py:25
  20.9 12.5 %collective-permute-start.8 = (bf16[4,128,256]{2,1,0:T(8,128)(2,1)S(1)}, bf16[4,128,256]{2,1,0:T(8,128)(2,1)S(1)}, u32[]{:S(2)}, u32[]{:S(2)}) collective-permute-start(bf16[4,128,256]{2,1,0:T(8,128)(2,1)S(1)} %pad_maximum_fusion.1.refs_4_.refs_2_), channel_id=1, source_target_pairs={{0,128},{16,144},{32,160},{48,176},{64,192},{80,208},{96,224},{112... | collective-permute-start | bytes 786440 | tf_op jit(solution)/shard_map/ppermute | solution.py:25
  23.5 9.9 %collective-permute-start.9 = (bf16[4,128,256]{2,1,0:T(8,128)(2,1)S(1)}, bf16[4,128,256]{2,1,0:T(8,128)(2,1)S(1)}, u32[]{:S(2)}, u32[]{:S(2)}) collective-permute-start(bf16[4,128,256]{2,1,0:T(8,128)(2,1)S(1)} %pad_maximum_fusion.1.refs_4_.refs_2_), channel_id=1, source_target_pairs={{0,192},{16,208},{32,224},{48,240},{64,0},{80,16},{96,32},{112,48}... | collective-permute-start | bytes 786440 | tf_op jit(solution)/shard_map/ppermute | solution.py:25
  24.6 5.3 %collective-permute-start.5 = (bf16[2,128,256]{2,1,0:T(8,128)(2,1)S(1)}, bf16[2,128,256]{2,1,0:T(8,128)(2,1)S(1)}, u32[]{:S(2)}, u32[]{:S(2)}) collective-permute-start(bf16[2,128,256]{2,1,0:T(8,128)(2,1)S(1)} %pad_maximum_fusion.2), channel_id=1, source_target_pairs={{0,8},{1,9},{2,10},{3,11},{4,12},{5,13},{6,14},{7,15},{8,0},{9,1},... | collective-permute-start | bytes 393224 | tf_op jit(solution)/shard_map/ppermute | solution.py:25
  27.1 3.8 %collective-permute-start.4 = (bf16[2,128,256]{2,1,0:T(8,128)(2,1)S(1)}, bf16[2,128,256]{2,1,0:T(8,128)(2,1)S(1)}, u32[]{:S(2)}, u32[]{:S(2)}) collective-permute-start(bf16[2,128,256]{2,1,0:T(8,128)(2,1)S(1)} %pad_maximum_fusion.2), channel_id=1, source_target_pairs={{0,12},{1,13},{2,14},{3,15},{4,0},{5,1},{6,2},{7,3},{8,4},{9,5},{1... | collective-permute-start | bytes 393224 | tf_op jit(solution)/shard_map/ppermute | solution.py:25
  33.4 4.5 %collective-permute-start.10 = (bf16[2,4,128,256]{3,2,1,0:T(8,128)(2,1)S(1)}, bf16[2,4,128,256]{3,2,1,0:T(8,128)(2,1)S(1)}, u32[]{:S(2)}, u32[]{:S(2)}) collective-permute-start(bf16[2,4,128,256]{3,2,1,0:T(8,128)(2,1)S(1)} %pad_maximum_fusion), channel_id=1, source_target_pairs={{0,1},{1,0},{2,3},{3,2},{4,5},{5,4},{6,7},{7,6},{8,9},{9,8},{10,11... | collective-permute-start | bytes 1572872 | tf_op jit(solution)/shard_map/ppermute | solution.py:34
  42.0 14.3 %collective-permute-start.11 = (f32[136,512]{1,0:T(8,128)S(1)}, f32[136,512]{1,0:T(8,128)S(1)}, u32[]{:S(2)}, u32[]{:S(2)}) collective-permute-start(f32[136,512]{1,0:T(8,128)S(1)} %get-tuple-element.51), channel_id=1, source_target_pairs={{0,64},{16,80},{32,96},{48,112},{64,128},{80,144},{96,160},{112,17... | collective-permute-start | bytes 835592 | tf_op jit(solution)/shard_map/ppermute | solution.py:25
  43.1 16.7 %collective-permute-start.12 = (f32[136,512]{1,0:T(8,128)S(1)}, f32[136,512]{1,0:T(8,128)S(1)}, u32[]{:S(2)}, u32[]{:S(2)}) collective-permute-start(f32[136,512]{1,0:T(8,128)S(1)} %get-tuple-element.52), channel_id=1, source_target_pairs={{0,128},{16,144},{32,160},{48,176},{64,192},{80,208},{96,224},{112... | collective-permute-start | bytes 835592 | tf_op jit(solution)/shard_map/ppermute | solution.py:25
  45.2 14.6 %collective-permute-start.13 = (f32[136,512]{1,0:T(8,128)S(1)}, f32[136,512]{1,0:T(8,128)S(1)}, u32[]{:S(2)}, u32[]{:S(2)}) collective-permute-start(f32[136,512]{1,0:T(8,128)S(1)} %get-tuple-element.53), channel_id=1, source_target_pairs={{0,192},{16,208},{32,224},{48,240},{64,0},{80,16},{96,32},{112,48}... | collective-permute-start | bytes 835592 | tf_op jit(solution)/shard_map/ppermute | solution.py:25
  49.4 4.1 %collective-permute-start.14 = (f32[2,136,512]{2,1,0:T(8,128)S(1)}, f32[2,136,512]{2,1,0:T(8,128)S(1)}, u32[]{:S(2)}, u32[]{:S(2)}) collective-permute-start(f32[2,136,512]{2,1,0:T(8,128)S(1)} %shard_map.79), channel_id=1, source_target_pairs={{0,1},{1,0},{2,3},{3,2},{4,5},{5,4},{6,7},{7,6},{8,9},{9,8},{10,11... | collective-permute-start | bytes 1671176 | tf_op jit(solution)/shard_map/ppermute | solution.py:34
  53.6 10.5 %collective-permute-start.15 = (f32[136,256]{1,0:T(8,128)S(1)}, f32[136,256]{1,0:T(8,128)S(1)}, u32[]{:S(2)}, u32[]{:S(2)}) collective-permute-start(f32[136,256]{1,0:T(8,128)S(1)} %get-tuple-element.56), channel_id=1, source_target_pairs={{0,4},{1,5},{2,6},{3,7},{4,8},{5,9},{6,10},{7,11},{8,12},{9,13},{1... | collective-permute-start | bytes 417800 | tf_op jit(solution)/shard_map/ppermute | solution.py:25
  54.9 9.2 %collective-permute-start.16 = (f32[136,256]{1,0:T(8,128)S(1)}, f32[136,256]{1,0:T(8,128)S(1)}, u32[]{:S(2)}, u32[]{:S(2)}) collective-permute-start(f32[136,256]{1,0:T(8,128)S(1)} %get-tuple-element.57), channel_id=1, source_target_pairs={{0,8},{1,9},{2,10},{3,11},{4,12},{5,13},{6,14},{7,15},{8,0},{9,1},... | collective-permute-start | bytes 417800 | tf_op jit(solution)/shard_map/ppermute | solution.py:25
  56.3 7.8 %collective-permute-start.17 = (f32[136,256]{1,0:T(8,128)S(1)}, f32[136,256]{1,0:T(8,128)S(1)}, u32[]{:S(2)}, u32[]{:S(2)}) collective-permute-start(f32[136,256]{1,0:T(8,128)S(1)} %get-tuple-element.58), channel_id=1, source_target_pairs={{0,12},{1,13},{2,14},{3,15},{4,0},{5,1},{6,2},{7,3},{8,4},{9,5},{1... | collective-permute-start | bytes 417800 | tf_op jit(solution)/shard_map/ppermute | solution.py:25
  59.9 7.5 %collective-permute-start.20 = (f32[136,128]{1,0:T(8,128)S(1)}, f32[136,128]{1,0:T(8,128)S(1)}, u32[]{:S(2)}, u32[]{:S(2)}) collective-permute-start(f32[136,128]{1,0:T(8,128)S(1)} %get-tuple-element.64), channel_id=1, source_target_pairs={{0,32},{16,48},{32,0},{48,16},{64,96},{80,112},{96,64},{112,80},{1... | collective-permute-start | bytes 208904 | tf_op jit(solution)/shard_map/ppermute | solution.py:30
  64.0 7.2 %collective-permute-start.21 = (f32[136,128]{1,0:T(8,128)S(1)}, f32[136,128]{1,0:T(8,128)S(1)}, u32[]{:S(2)}, u32[]{:S(2)}) collective-permute-start(f32[136,128]{1,0:T(8,128)S(1)} %get-tuple-element.65), channel_id=1, source_target_pairs={{0,48},{16,0},{32,16},{48,32},{64,112},{80,64},{96,80},{112,96},{1... | collective-permute-start | bytes 208904 | tf_op jit(solution)/shard_map/ppermute | solution.py:30
  64.1 8.6 %collective-permute-start.18 = (f32[136,128]{1,0:T(8,128)S(1)}, f32[136,128]{1,0:T(8,128)S(1)}, u32[]{:S(2)}, u32[]{:S(2)}) collective-permute-start(f32[136,128]{1,0:T(8,128)S(1)} %get-tuple-element.61), channel_id=1, source_target_pairs={{0,2},{1,3},{2,0},{3,1},{4,6},{5,7},{6,4},{7,5},{8,10},{9,11},{10,... | collective-permute-start | bytes 208904 | tf_op jit(solution)/shard_map/ppermute | solution.py:34
  66.9 5.9 %collective-permute-start.19 = (f32[136,128]{1,0:T(8,128)S(1)}, f32[136,128]{1,0:T(8,128)S(1)}, u32[]{:S(2)}, u32[]{:S(2)}) collective-permute-start(f32[136,128]{1,0:T(8,128)S(1)} %get-tuple-element.63), channel_id=1, source_target_pairs={{0,16},{16,32},{32,48},{48,0},{64,80},{80,96},{96,112},{112,64},{1... | collective-permute-start | bytes 208904 | tf_op jit(solution)/shard_map/ppermute | solution.py:30

commit v13 on v12

--- a/solution.py
+++ b/solution.py
@@ -10,6 +10,7 @@
 
 GRID_W = 256
 SUB = 4
+WAY = (0, 1, 3, 2)
 SHARD = 128
 WIDTH = 128
 BLOCK = SUB * SHARD
@@ -140,14 +141,14 @@
 
 def one_block(ones, slow, total):
     pieces = [ones[low * 2 + high][slow] for low in range(2) for high in range(2)]
-    starts = [start_one(slow, high, low) for low in range(2) for high in range(2)]
+    starts = [start_one(WAY[slow], high, low) for low in range(2) for high in range(2)]
     return block_of(pieces, starts, total)
 
 
 def two_block(two, slow, total):
     return block_of(
         [two[piece] for piece in range(SUB)],
-        [start_two(slow, piece) for piece in range(SUB)],
+        [start_two(slow, WAY[piece]) for piece in range(SUB)],
         total,
     )
 
@@ -264,11 +265,11 @@
         vmem=62 << 20,
     )
 
-    two = [own_two] + [fast_shift("row", own_two, -step) for step in range(1, SUB)]
+    two = [own_two] + [fast_shift("row", own_two, -step) for step in WAY[1:]]
     one = [own_one, fast_swap("col", own_one, 2)]
     one, two = together((jnp.stack(one), jnp.stack(two)))
-    one = [one] + [slow_shift("col", one, -step) for step in range(1, SUB)]
-    order = (3, 2, 1)
+    one = [one] + [slow_shift("col", one, -step) for step in WAY[1:]]
+    order = (2, 3, 1)
     twos = [two] + [slow_shift("row", two, -step) for step in order]
     one, twos = together((jnp.stack(one, axis=1), twos))
     twos = [twos[0]] + [twos[1 + order.index(step)] for step in range(1, SUB)]
@@ -289,10 +290,9 @@
         shapes = [f32(ROWS, 2 * SHARD)] * (2 * len(halves))
         return call(functools.partial(core_kernel, halves), shapes, (theirs, mine))
 
-    def spread(axis, parts, first=0):
+    def spread(axis, parts, steps):
         return [
-            slow_shift(axis, part, first + step) if first + step else part
-            for step, part in enumerate(parts)
+            slow_shift(axis, part, step) if step else part for step, part in zip(steps, parts)
         ]
 
     work = BLOCK * BLOCK * SUB
@@ -301,16 +301,16 @@
     cols[2], cols[3], cols[1] = col_scores(2, 3, 1)
     ones, far = together((ones, cols[1:]))
     (cols[0],) = col_scores(0)
-    cols = spread("row", [cols[0], *far])
+    cols = spread("row", [cols[0], *far], range(SUB))
     (send_one,) = row_scores(ones[2:], twos, ((0, 0), (0, 1)), 2, 2)
     theirs_one = fast_swap("col", send_one, 1)
     (keep_one,) = row_scores(ones[:2], twos, ((0, 0), (0, 1)), 40, 2)
     cols = list(call(block_kernel, [f32(ROWS, SHARD)] * SUB, cols, work=1 * work))
-    rows = spread("col", core_merge(keep_one, theirs_one, 0, 1))
+    rows = spread("col", core_merge(keep_one, theirs_one, 0, 1), WAY)
     keep, send = call(chip_kernel, [f32(ROWS, SHARD)] * 2, rows)
     theirs = fast_swap("col", send, 2)
     cols[1], keep = together((cols[1], keep))
-    cols = [cols[0]] + [fast_shift("row", cols[step], step) for step in range(1, SUB)]
+    cols = [cols[0]] + [fast_shift("row", cols[at], WAY[at]) for at in range(1, SUB)]
     outs = [f32(SHARD, WIDTH), f32(2, SHARD)] * 2
     return tuple(call(functools.partial(finish_kernel, total), outs, (keep, theirs, *cols)))
 

time: 73.9 us -> 74.3 us (level)
  waiting for transfers between devices: 14.9 us -> 18.8 us
  starting transfers between devices: 43 us -> 39.5 us
    ppermute x6, waiting for transfers between devices: 6.78 us -> 10.4 us  [fast_shift(): return lax.ppermute(value, axis, pairs)]
    ppermute x4, starting transfers between devices: 9.62 us -> 7.81 us  [fast_swap(): return lax.ppermute(value, axis, [(i, i ^ step) for i in range(SUB * SUB)])]
    ppermute x12, waiting for transfers between devices: 5.12 us -> 6.87 us  [slow_shift(): return lax.ppermute(value, axis, pairs)]
    ppermute x4, waiting for transfers between devices: 2.99 us -> 1.51 us  [fast_swap(): return lax.ppermute(value, axis, [(i, i ^ step) for i in range(SUB * SUB)])]
    ppermute x12, starting transfers between devices: 19.1 us -> 18 us  [slow_shift(): return lax.ppermute(value, axis, pairs)]
where the time goes in v13:
time: 74.3 us; the launch traced here: 74 us
  starting transfers between devices  39.5 us (53%)
  waiting for transfers between devices  18.8 us (25%)
  Pallas kernels  13.9 us (19%)
  other arithmetic  0.99 us (1%)
  between operations  0.76 us (1%)
    ppermute x12, starting transfers between devices, slow_shift(): return lax.ppermute(value, axis, pairs)  18 us
    pallas_call x9, Pallas kernels, call(): pl.pallas_call(kernel, out_shape=shapes, in_specs=specs or [VMEM] * len(a...  13.9 us
    ppermute x6, starting transfers between devices, fast_shift(): return lax.ppermute(value, axis, pairs)  13.7 us
    ppermute x6, waiting for transfers between devices, fast_shift(): return lax.ppermute(value, axis, pairs)  10.4 us
    ppermute x4, starting transfers between devices, fast_swap(): return lax.ppermute(value, axis, [(i, i ^ step) for i in range(SUB * SUB)])  7.81 us
    ppermute x12, waiting for transfers between devices, slow_shift(): return lax.ppermute(value, axis, pairs)  6.87 us
    ppermute x4, waiting for transfers between devices, fast_swap(): return lax.ppermute(value, axis, [(i, i ^ step) for i in range(SUB * SUB)])  1.51 us
  transfers between devices with their start and end apart: 22, of which 8 were waited for; matrix products, arithmetic and copies ran while one was open for 1% of the time, Pallas kernels for 10%

profile of v13, /device:TPU:1, one launch (start us, length us, event | category | flops | bytes accessed | tf_op | source)
XLA Modules:
  0.0 74.0 jit_solution(9472691539704074401)
XLA Ops:
  0.6 1.7 %shard_map.75 = (bf16[128,256]{1,0:T(8,128)(2,1)}, bf16[128,256]{1,0:T(8,128)(2,1)}) custom-call(bf16[128,128]{1,0:T(8,128)(2,1)} %feat_one.1, bf16[128,128]{1,0:T(8,128)(2,1)} %value_one.1, bf16[128,128]{1,0:T(8,128)(2,1)} %feat_two.1, bf16[128,128]{1,0:T(8,128)(2,1)} %value_two.1), custom_call_target="tpu_custom_call" | custom-call | bytes 262144 | tf_op jit(solution)/shard_map/pallas_call | solution.py:227
  2.3 2.6 %collective-permute-start = (bf16[128,256]{1,0:T(8,128)(2,1)}, bf16[128,256]{1,0:T(8,128)(2,1)S(1)}, u32[]{:S(2)}, u32[]{:S(2)}) collective-permute-start(bf16[128,256]{1,0:T(8,128)(2,1)} %get-tuple-element.35), channel_id=1, source_target_pairs={{0,2},{1,3},{2,0},{3,1},{4,6},{5,7},{6,4},{7,5},{8,10},{9,11},{10,... | collective-permute-start | bytes 196616 | tf_op jit(solution)/shard_map/ppermute | solution.py:35
  4.9 6.0 %collective-permute-start.3 = (bf16[128,256]{1,0:T(8,128)(2,1)}, bf16[128,256]{1,0:T(8,128)(2,1)S(1)}, u32[]{:S(2)}, u32[]{:S(2)}) collective-permute-start(bf16[128,256]{1,0:T(8,128)(2,1)} %get-tuple-element.36), channel_id=1, source_target_pairs={{0,32},{16,48},{32,0},{48,16},{64,96},{80,112},{96,64},{112,80},{1... | collective-permute-start | bytes 196616 | tf_op jit(solution)/shard_map/ppermute | solution.py:31
  10.9 1.2 %collective-permute-start.2 = (bf16[128,256]{1,0:T(8,128)(2,1)}, bf16[128,256]{1,0:T(8,128)(2,1)S(1)}, u32[]{:S(2)}, u32[]{:S(2)}) collective-permute-start(bf16[128,256]{1,0:T(8,128)(2,1)} %get-tuple-element.36), channel_id=1, source_target_pairs={{0,16},{16,32},{32,48},{48,0},{64,80},{80,96},{96,112},{112,64},{1... | collective-permute-start | bytes 196616 | tf_op jit(solution)/shard_map/ppermute | solution.py:31
  12.1 2.4 %collective-permute-start.1 = (bf16[128,256]{1,0:T(8,128)(2,1)}, bf16[128,256]{1,0:T(8,128)(2,1)S(1)}, u32[]{:S(2)}, u32[]{:S(2)}) collective-permute-start(bf16[128,256]{1,0:T(8,128)(2,1)} %get-tuple-element.36), channel_id=1, source_target_pairs={{0,48},{16,0},{32,16},{48,32},{64,112},{80,64},{96,80},{112,96},{1... | collective-permute-start | bytes 196616 | tf_op jit(solution)/shard_map/ppermute | solution.py:31
  14.5 0.0 collective-permute-done
  14.5 0.9 %pad_maximum_fusion.2 = bf16[2,128,256]{2,1,0:T(8,128)(2,1)S(1)} fusion(bf16[1,128,256]{2,1,0:T(8,128)(2,1)S(1)} %bitcast.29, bf16[1,128,256]{2,1,0:T(8,128)(2,1)} %bitcast.28), kind=kLoop, calls=%fused_computation.6 | loop fusion | flops 65536 | bytes 262144 | tf_op jit(solution)/shard_map/stack | solution.py:270
  15.4 2.9 %collective-permute-done.2 = bf16[128,256]{1,0:T(8,128)(2,1)S(1)} collective-permute-done((bf16[128,256]{1,0:T(8,128)(2,1)}, bf16[128,256]{1,0:T(8,128)(2,1)S(1)}, u32[]{:S(2)}, u32[]{:S(2)}) %collective-permute-start.2) | collective-permute-done | bytes 65568 | tf_op jit(solution)/shard_map/ppermute | solution.py:31
  18.2 0.2 collective-permute-done.1
  18.5 2.8 %collective-permute-start.6 = (bf16[2,128,256]{2,1,0:T(8,128)(2,1)S(1)}, bf16[2,128,256]{2,1,0:T(8,128)(2,1)S(1)}, u32[]{:S(2)}, u32[]{:S(2)}) collective-permute-start(bf16[2,128,256]{2,1,0:T(8,128)(2,1)S(1)} %pad_maximum_fusion.2), channel_id=1, source_target_pairs={{0,8},{1,9},{2,10},{3,11},{4,12},{5,13},{6,14},{7,15},{8,0},{9,1},... | collective-permute-start | bytes 393224 | tf_op jit(solution)/shard_map/ppermute | solution.py:26
  21.3 2.9 %collective-permute-start.7 = (bf16[4,128,256]{2,1,0:T(8,128)(2,1)S(1)}, bf16[4,128,256]{2,1,0:T(8,128)(2,1)S(1)}, u32[]{:S(2)}, u32[]{:S(2)}) collective-permute-start(bf16[4,128,256]{2,1,0:T(8,128)(2,1)S(1)} %pad_maximum_fusion.1.refs_4_.refs_2_), channel_id=1, source_target_pairs={{0,128},{16,144},{32,160},{48,176},{64,192},{80,208},{96,224},{112... | collective-permute-start | bytes 786440 | tf_op jit(solution)/shard_map/ppermute | solution.py:26
  24.3 0.4 collective-permute-start.8
  24.7 2.3 %collective-permute-start.9 = (bf16[4,128,256]{2,1,0:T(8,128)(2,1)S(1)}, bf16[4,128,256]{2,1,0:T(8,128)(2,1)S(1)}, u32[]{:S(2)}, u32[]{:S(2)}) collective-permute-start(bf16[4,128,256]{2,1,0:T(8,128)(2,1)S(1)} %pad_maximum_fusion.1.refs_4_.refs_2_), channel_id=1, source_target_pairs={{0,192},{16,208},{32,224},{48,240},{64,0},{80,16},{96,32},{112,48}... | collective-permute-start | bytes 786440 | tf_op jit(solution)/shard_map/ppermute | solution.py:26
  26.9 0.3 collective-permute-start.5
  27.2 0.0 collective-permute-done.6
  27.3 2.4 %collective-permute-start.4 = (bf16[2,128,256]{2,1,0:T(8,128)(2,1)S(1)}, bf16[2,128,256]{2,1,0:T(8,128)(2,1)S(1)}, u32[]{:S(2)}, u32[]{:S(2)}) collective-permute-start(bf16[2,128,256]{2,1,0:T(8,128)(2,1)S(1)} %pad_maximum_fusion.2), channel_id=1, source_target_pairs={{0,12},{1,13},{2,14},{3,15},{4,0},{5,1},{6,2},{7,3},{8,4},{9,5},{1... | collective-permute-start | bytes 393224 | tf_op jit(solution)/shard_map/ppermute | solution.py:26
  29.6 2.6 %collective-permute-done.5 = bf16[2,128,256]{2,1,0:T(8,128)(2,1)S(1)} collective-permute-done((bf16[2,128,256]{2,1,0:T(8,128)(2,1)S(1)}, bf16[2,128,256]{2,1,0:T(8,128)(2,1)S(1)}, u32[]{:S(2)}, u32[]{:S(2)}) %collective-permute-start.5) | collective-permute-done | bytes 131104 | tf_op jit(solution)/shard_map/ppermute | solution.py:26
  32.3 0.0 collective-permute-done.4
  32.3 0.1 pad_maximum_fusion
  32.3 0.0 collective-permute-done.7.refs_4_
  32.3 3.5 %collective-permute-done.8.refs_5_ = bf16[4,128,256]{2,1,0:T(8,128)(2,1)S(1)} collective-permute-done((bf16[4,128,256]{2,1,0:T(8,128)(2,1)S(1)}, bf16[4,128,256]{2,1,0:T(8,128)(2,1)S(1)}, u32[]{:S(2)}, u32[]{:S(2)}) %collective-permute-start.8) | collective-permute-done | bytes 262176 | tf_op jit(solution)/shard_map/ppermute | solution.py:26
  35.8 1.7 %collective-permute-start.10 = (bf16[2,4,128,256]{3,2,1,0:T(8,128)(2,1)S(1)}, bf16[2,4,128,256]{3,2,1,0:T(8,128)(2,1)S(1)}, u32[]{:S(2)}, u32[]{:S(2)}) collective-permute-start(bf16[2,4,128,256]{3,2,1,0:T(8,128)(2,1)S(1)} %pad_maximum_fusion), channel_id=1, source_target_pairs={{0,1},{1,0},{2,3},{3,2},{4,5},{5,4},{6,7},{7,6},{8,9},{9,8},{10,11... | collective-permute-start | bytes 1572872 | tf_op jit(solution)/shard_map/ppermute | solution.py:35
  37.6 1.5 %collective-permute-done.10 = bf16[2,4,128,256]{3,2,1,0:T(8,128)(2,1)S(1)} collective-permute-done((bf16[2,4,128,256]{3,2,1,0:T(8,128)(2,1)S(1)}, bf16[2,4,128,256]{3,2,1,0:T(8,128)(2,1)S(1)}, u32[]{:S(2)}, u32[]{:S(2)}) %collective-permute-start.10) | collective-permute-done | bytes 524320 | tf_op jit(solution)/shard_map/ppermute | solution.py:35
  39.1 4.0 %shard_map.76 = (f32[136,512]{1,0:T(8,128)S(1)}, f32[136,512]{1,0:T(8,128)S(1)}, f32[136,512]{1,0:T(8,128)S(1)}) custom-call(bf16[4,128,256]{2,1,0:T(8,128)(2,1)S(1)} %get-tuple-element.46.refs_0_, bf16[4,128,256]{2,1,0:T(8,128)(2,1)S(1)} %get-tuple-element.47.refs_1_, bf16[4,128,256]{2,1,0:T(8,128)(2,1)S(1)} %get-tuple-element.48.refs_2_.refs_0_, ...), custom_call_target="tpu_custom_call" | custom-call | flops 1610612736 | bytes 2670592 | tf_op jit(solution)/shard_map/pallas_call | solution.py:227
  43.1 1.4 %collective-permute-start.11 = (f32[136,512]{1,0:T(8,128)S(1)}, f32[136,512]{1,0:T(8,128)S(1)}, u32[]{:S(2)}, u32[]{:S(2)}) collective-permute-start(f32[136,512]{1,0:T(8,128)S(1)} %get-tuple-element.51), channel_id=1, source_target_pairs={{0,64},{16,80},{32,96},{48,112},{64,128},{80,144},{96,160},{112,17... | collective-permute-start | bytes 835592 | tf_op jit(solution)/shard_map/ppermute | solution.py:26
  44.4 2.5 %collective-permute-start.12 = (f32[136,512]{1,0:T(8,128)S(1)}, f32[136,512]{1,0:T(8,128)S(1)}, u32[]{:S(2)}, u32[]{:S(2)}) collective-permute-start(f32[136,512]{1,0:T(8,128)S(1)} %get-tuple-element.52), channel_id=1, source_target_pairs={{0,128},{16,144},{32,160},{48,176},{64,192},{80,208},{96,224},{112... | collective-permute-start | bytes 835592 | tf_op jit(solution)/shard_map/ppermute | solution.py:26
  46.9 0.3 collective-permute-start.13
  47.2 2.8 %shard_map.79 = f32[2,136,512]{2,1,0:T(8,128)S(1)} custom-call(bf16[4,128,256]{2,1,0:T(8,128)(2,1)S(1)} %get-tuple-element.48.refs_2_.refs_0_, bf16[4,128,256]{2,1,0:T(8,128)(2,1)S(1)} %get-tuple-element.49.refs_3_.refs_1_, bf16[4,128,256]{2,1,0:T(8,128)(2,1)S(1)} %pad_maximum_fusion.1.refs_4_.refs_2_, ...), custom_call_target="tpu_custom_call" | custom-call | flops 1073741824 | bytes 2129920 | tf_op jit(solution)/shard_map/pallas_call | solution.py:227
  50.0 1.3 %collective-permute-start.14 = (f32[2,136,512]{2,1,0:T(8,128)S(1)}, f32[2,136,512]{2,1,0:T(8,128)S(1)}, u32[]{:S(2)}, u32[]{:S(2)}) collective-permute-start(f32[2,136,512]{2,1,0:T(8,128)S(1)} %shard_map.79), channel_id=1, source_target_pairs={{0,1},{1,0},{2,3},{3,2},{4,5},{5,4},{6,7},{7,6},{8,9},{9,8},{10,11... | collective-permute-start | bytes 1671176 | tf_op jit(solution)/shard_map/ppermute | solution.py:35
  51.3 2.8 %shard_map.80.refs_1_ = f32[2,136,512]{2,1,0:T(8,128)S(1)} custom-call(bf16[4,128,256]{2,1,0:T(8,128)(2,1)S(1)} %get-tuple-element.46.refs_0_, bf16[4,128,256]{2,1,0:T(8,128)(2,1)S(1)} %get-tuple-element.47.refs_1_, bf16[4,128,256]{2,1,0:T(8,128)(2,1)S(1)} %pad_maximum_fusion.1.refs_4_.refs_2_, ...), custom_call_target="tpu_custom_call" | custom-call | flops 21474836480 | bytes 2129920 | tf_op jit(solution)/shard_map/pallas_call | solution.py:227
  54.1 0.0 collective-permute-done.14.refs_0_
  54.1 0.1 shard_map.81
  54.2 0.4 collective-permute-start.15
  54.6 2.4 %collective-permute-start.16 = (f32[136,256]{1,0:T(8,128)S(1)}, f32[136,256]{1,0:T(8,128)S(1)}, u32[]{:S(2)}, u32[]{:S(2)}) collective-permute-start(f32[136,256]{1,0:T(8,128)S(1)} %get-tuple-element.57), channel_id=1, source_target_pairs={{0,12},{1,13},{2,14},{3,15},{4,0},{5,1},{6,2},{7,3},{8,4},{9,5},{1... | collective-permute-start | bytes 417800 | tf_op jit(solution)/shard_map/ppermute | solution.py:26
  56.9 0.0 collective-permute-done.11.refs_1_
  56.9 0.0 collective-permute-start.17
  56.9 1.6 %shard_map.77.refs_0_ = f32[136,512]{1,0:T(8,128)S(1)} custom-call(bf16[4,128,256]{2,1,0:T(8,128)(2,1)S(1)} %get-tuple-element.46.refs_0_, bf16[4,128,256]{2,1,0:T(8,128)(2,1)S(1)} %get-tuple-element.47.refs_1_, bf16[4,128,256]{2,1,0:T(8,128)(2,1)S(1)} %get-tuple-element.48.refs_2_.refs_0_, bf16[4,128,256]{2,1,0:T(8,128)(2,1)S(1)} %get-tuple-element.49.refs_3_.refs_1_, ...), custom_call_target="tpu_custom_call" | custom-call | flops 536870912 | bytes 1589248 | tf_op jit(solution)/shard_map/pallas_call | solution.py:227
  58.6 0.7 collective-permute-done.12.refs_2_
  59.3 0.0 collective-permute-done.13.refs_3_
  59.3 0.1 shard_map.78
  59.4 2.4 %collective-permute-start.20 = (f32[136,128]{1,0:T(8,128)S(1)}, f32[136,128]{1,0:T(8,128)S(1)}, u32[]{:S(2)}, u32[]{:S(2)}) collective-permute-start(f32[136,128]{1,0:T(8,128)S(1)} %get-tuple-element.64), channel_id=1, source_target_pairs={{0,48},{16,0},{32,16},{48,32},{64,112},{80,64},{96,80},{112,96},{1... | collective-permute-start | bytes 208904 | tf_op jit(solution)/shard_map/ppermute | solution.py:31
  61.8 1.4 %collective-permute-start.21 = (f32[136,128]{1,0:T(8,128)S(1)}, f32[136,128]{1,0:T(8,128)S(1)}, u32[]{:S(2)}, u32[]{:S(2)}) collective-permute-start(f32[136,128]{1,0:T(8,128)S(1)} %get-tuple-element.65), channel_id=1, source_target_pairs={{0,32},{16,48},{32,0},{48,16},{64,96},{80,112},{96,64},{112,80},{1... | collective-permute-start | bytes 208904 | tf_op jit(solution)/shard_map/ppermute | solution.py:31
  63.2 0.1 shard_map.82
  63.3 2.3 %collective-permute-start.18 = (f32[136,128]{1,0:T(8,128)S(1)}, f32[136,128]{1,0:T(8,128)S(1)}, u32[]{:S(2)}, u32[]{:S(2)}) collective-permute-start(f32[136,128]{1,0:T(8,128)S(1)} %get-tuple-element.61), channel_id=1, source_target_pairs={{0,2},{1,3},{2,0},{3,1},{4,6},{5,7},{6,4},{7,5},{8,10},{9,11},{10,... | collective-permute-start | bytes 208904 | tf_op jit(solution)/shard_map/ppermute | solution.py:35
  65.6 0.3 collective-permute-start.19
  65.9 3.1 %collective-permute-done.21.refs_5_ = f32[136,128]{1,0:T(8,128)S(1)} collective-permute-done((f32[136,128]{1,0:T(8,128)S(1)}, f32[136,128]{1,0:T(8,128)S(1)}, u32[]{:S(2)}, u32[]{:S(2)}) %collective-permute-start.21) | collective-permute-done | bytes 69664 | tf_op jit(solution)/shard_map/ppermute | solution.py:31
  69.0 4.2 %collective-permute-done.19.refs_3_ = f32[136,128]{1,0:T(8,128)S(1)} collective-permute-done((f32[136,128]{1,0:T(8,128)S(1)}, f32[136,128]{1,0:T(8,128)S(1)}, u32[]{:S(2)}, u32[]{:S(2)}) %collective-permute-start.19) | collective-permute-done | bytes 69664 | tf_op jit(solution)/shard_map/ppermute | solution.py:31
  73.2 0.8 %shard_map.83 = (f32[128,128]{1,0:T(8,128)}, f32[2,128]{1,0:T(2,128)}, f32[128,128]{1,0:T(8,128)}, f32[2,128]{1,0:T(2,128)}) custom-call(f32[136,128]{1,0:T(8,128)S(1)} %get-tuple-element.60.refs_0_, f32[136,128]{1,0:T(8,128)S(1)} %collective-permute-done.18.refs_1_, f32[136,128]{1,0:T(8,128)S(1)} %get-tuple-element.62.refs_2_, ...), custom_call_target="tpu_custom_call" | custom-call | bytes 550912 | tf_op jit(solution)/shard_map/pallas_call | solution.py:227
  (12 shorter events, 0.1 us)
Async XLA Ops:
  2.3 12.1 %collective-permute-start = (bf16[128,256]{1,0:T(8,128)(2,1)}, bf16[128,256]{1,0:T(8,128)(2,1)S(1)}, u32[]{:S(2)}, u32[]{:S(2)}) collective-permute-start(bf16[128,256]{1,0:T(8,128)(2,1)} %get-tuple-element.35), channel_id=1, source_target_pairs={{0,2},{1,3},{2,0},{3,1},{4,6},{5,7},{6,4},{7,5},{8,10},{9,11},{10,... | collective-permute-start | bytes 196616 | tf_op jit(solution)/shard_map/ppermute | solution.py:35
  4.9 10.5 %collective-permute-start.3 = (bf16[128,256]{1,0:T(8,128)(2,1)}, bf16[128,256]{1,0:T(8,128)(2,1)S(1)}, u32[]{:S(2)}, u32[]{:S(2)}) collective-permute-start(bf16[128,256]{1,0:T(8,128)(2,1)} %get-tuple-element.36), channel_id=1, source_target_pairs={{0,32},{16,48},{32,0},{48,16},{64,96},{80,112},{96,64},{112,80},{1... | collective-permute-start | bytes 196616 | tf_op jit(solution)/shard_map/ppermute | solution.py:31
  10.9 7.3 %collective-permute-start.2 = (bf16[128,256]{1,0:T(8,128)(2,1)}, bf16[128,256]{1,0:T(8,128)(2,1)S(1)}, u32[]{:S(2)}, u32[]{:S(2)}) collective-permute-start(bf16[128,256]{1,0:T(8,128)(2,1)} %get-tuple-element.36), channel_id=1, source_target_pairs={{0,16},{16,32},{32,48},{48,0},{64,80},{80,96},{96,112},{112,64},{1... | collective-permute-start | bytes 196616 | tf_op jit(solution)/shard_map/ppermute | solution.py:31
  12.1 6.4 %collective-permute-start.1 = (bf16[128,256]{1,0:T(8,128)(2,1)}, bf16[128,256]{1,0:T(8,128)(2,1)S(1)}, u32[]{:S(2)}, u32[]{:S(2)}) collective-permute-start(bf16[128,256]{1,0:T(8,128)(2,1)} %get-tuple-element.36), channel_id=1, source_target_pairs={{0,48},{16,0},{32,16},{48,32},{64,112},{80,64},{96,80},{112,96},{1... | collective-permute-start | bytes 196616 | tf_op jit(solution)/shard_map/ppermute | solution.py:31
  14.5 4.0 %copy-start = (bf16[128,256]{1,0:T(8,128)(2,1)S(1)}, bf16[128,256]{1,0:T(8,128)(2,1)}, u32[]{:S(2)}) copy-start(bf16[128,256]{1,0:T(8,128)(2,1)} %get-tuple-element.36) | copy-start | bytes 196612
  18.5 8.7 %collective-permute-start.6 = (bf16[2,128,256]{2,1,0:T(8,128)(2,1)S(1)}, bf16[2,128,256]{2,1,0:T(8,128)(2,1)S(1)}, u32[]{:S(2)}, u32[]{:S(2)}) collective-permute-start(bf16[2,128,256]{2,1,0:T(8,128)(2,1)S(1)} %pad_maximum_fusion.2), channel_id=1, source_target_pairs={{0,8},{1,9},{2,10},{3,11},{4,12},{5,13},{6,14},{7,15},{8,0},{9,1},... | collective-permute-start | bytes 393224 | tf_op jit(solution)/shard_map/ppermute | solution.py:26
  21.3 11.0 %collective-permute-start.7 = (bf16[4,128,256]{2,1,0:T(8,128)(2,1)S(1)}, bf16[4,128,256]{2,1,0:T(8,128)(2,1)S(1)}, u32[]{:S(2)}, u32[]{:S(2)}) collective-permute-start(bf16[4,128,256]{2,1,0:T(8,128)(2,1)S(1)} %pad_maximum_fusion.1.refs_4_.refs_2_), channel_id=1, source_target_pairs={{0,128},{16,144},{32,160},{48,176},{64,192},{80,208},{96,224},{112... | collective-permute-start | bytes 786440 | tf_op jit(solution)/shard_map/ppermute | solution.py:26
  24.3 11.6 %collective-permute-start.8 = (bf16[4,128,256]{2,1,0:T(8,128)(2,1)S(1)}, bf16[4,128,256]{2,1,0:T(8,128)(2,1)S(1)}, u32[]{:S(2)}, u32[]{:S(2)}) collective-permute-start(bf16[4,128,256]{2,1,0:T(8,128)(2,1)S(1)} %pad_maximum_fusion.1.refs_4_.refs_2_), channel_id=1, source_target_pairs={{0,64},{16,80},{32,96},{48,112},{64,128},{80,144},{96,160},{112,17... | collective-permute-start | bytes 786440 | tf_op jit(solution)/shard_map/ppermute | solution.py:26
  24.7 11.2 %collective-permute-start.9 = (bf16[4,128,256]{2,1,0:T(8,128)(2,1)S(1)}, bf16[4,128,256]{2,1,0:T(8,128)(2,1)S(1)}, u32[]{:S(2)}, u32[]{:S(2)}) collective-permute-start(bf16[4,128,256]{2,1,0:T(8,128)(2,1)S(1)} %pad_maximum_fusion.1.refs_4_.refs_2_), channel_id=1, source_target_pairs={{0,192},{16,208},{32,224},{48,240},{64,0},{80,16},{96,32},{112,48}... | collective-permute-start | bytes 786440 | tf_op jit(solution)/shard_map/ppermute | solution.py:26
  26.9 5.3 %collective-permute-start.5 = (bf16[2,128,256]{2,1,0:T(8,128)(2,1)S(1)}, bf16[2,128,256]{2,1,0:T(8,128)(2,1)S(1)}, u32[]{:S(2)}, u32[]{:S(2)}) collective-permute-start(bf16[2,128,256]{2,1,0:T(8,128)(2,1)S(1)} %pad_maximum_fusion.2), channel_id=1, source_target_pairs={{0,4},{1,5},{2,6},{3,7},{4,8},{5,9},{6,10},{7,11},{8,12},{9,13},{1... | collective-permute-start | bytes 393224 | tf_op jit(solution)/shard_map/ppermute | solution.py:26
  27.3 5.0 %collective-permute-start.4 = (bf16[2,128,256]{2,1,0:T(8,128)(2,1)S(1)}, bf16[2,128,256]{2,1,0:T(8,128)(2,1)S(1)}, u32[]{:S(2)}, u32[]{:S(2)}) collective-permute-start(bf16[2,128,256]{2,1,0:T(8,128)(2,1)S(1)} %pad_maximum_fusion.2), channel_id=1, source_target_pairs={{0,12},{1,13},{2,14},{3,15},{4,0},{5,1},{6,2},{7,3},{8,4},{9,5},{1... | collective-permute-start | bytes 393224 | tf_op jit(solution)/shard_map/ppermute | solution.py:26
  35.8 3.2 %collective-permute-start.10 = (bf16[2,4,128,256]{3,2,1,0:T(8,128)(2,1)S(1)}, bf16[2,4,128,256]{3,2,1,0:T(8,128)(2,1)S(1)}, u32[]{:S(2)}, u32[]{:S(2)}) collective-permute-start(bf16[2,4,128,256]{3,2,1,0:T(8,128)(2,1)S(1)} %pad_maximum_fusion), channel_id=1, source_target_pairs={{0,1},{1,0},{2,3},{3,2},{4,5},{5,4},{6,7},{7,6},{8,9},{9,8},{10,11... | collective-permute-start | bytes 1572872 | tf_op jit(solution)/shard_map/ppermute | solution.py:35
  43.1 13.9 %collective-permute-start.11 = (f32[136,512]{1,0:T(8,128)S(1)}, f32[136,512]{1,0:T(8,128)S(1)}, u32[]{:S(2)}, u32[]{:S(2)}) collective-permute-start(f32[136,512]{1,0:T(8,128)S(1)} %get-tuple-element.51), channel_id=1, source_target_pairs={{0,64},{16,80},{32,96},{48,112},{64,128},{80,144},{96,160},{112,17... | collective-permute-start | bytes 835592 | tf_op jit(solution)/shard_map/ppermute | solution.py:26
  44.4 14.8 %collective-permute-start.12 = (f32[136,512]{1,0:T(8,128)S(1)}, f32[136,512]{1,0:T(8,128)S(1)}, u32[]{:S(2)}, u32[]{:S(2)}) collective-permute-start(f32[136,512]{1,0:T(8,128)S(1)} %get-tuple-element.52), channel_id=1, source_target_pairs={{0,128},{16,144},{32,160},{48,176},{64,192},{80,208},{96,224},{112... | collective-permute-start | bytes 835592 | tf_op jit(solution)/shard_map/ppermute | solution.py:26
  46.9 12.4 %collective-permute-start.13 = (f32[136,512]{1,0:T(8,128)S(1)}, f32[136,512]{1,0:T(8,128)S(1)}, u32[]{:S(2)}, u32[]{:S(2)}) collective-permute-start(f32[136,512]{1,0:T(8,128)S(1)} %get-tuple-element.53), channel_id=1, source_target_pairs={{0,192},{16,208},{32,224},{48,240},{64,0},{80,16},{96,32},{112,48}... | collective-permute-start | bytes 835592 | tf_op jit(solution)/shard_map/ppermute | solution.py:26
  50.0 4.1 %collective-permute-start.14 = (f32[2,136,512]{2,1,0:T(8,128)S(1)}, f32[2,136,512]{2,1,0:T(8,128)S(1)}, u32[]{:S(2)}, u32[]{:S(2)}) collective-permute-start(f32[2,136,512]{2,1,0:T(8,128)S(1)} %shard_map.79), channel_id=1, source_target_pairs={{0,1},{1,0},{2,3},{3,2},{4,5},{5,4},{6,7},{7,6},{8,9},{9,8},{10,11... | collective-permute-start | bytes 1671176 | tf_op jit(solution)/shard_map/ppermute | solution.py:35
  54.2 9.0 %collective-permute-start.15 = (f32[136,256]{1,0:T(8,128)S(1)}, f32[136,256]{1,0:T(8,128)S(1)}, u32[]{:S(2)}, u32[]{:S(2)}) collective-permute-start(f32[136,256]{1,0:T(8,128)S(1)} %get-tuple-element.56), channel_id=1, source_target_pairs={{0,4},{1,5},{2,6},{3,7},{4,8},{5,9},{6,10},{7,11},{8,12},{9,13},{1... | collective-permute-start | bytes 417800 | tf_op jit(solution)/shard_map/ppermute | solution.py:26
  54.6 8.6 %collective-permute-start.16 = (f32[136,256]{1,0:T(8,128)S(1)}, f32[136,256]{1,0:T(8,128)S(1)}, u32[]{:S(2)}, u32[]{:S(2)}) collective-permute-start(f32[136,256]{1,0:T(8,128)S(1)} %get-tuple-element.57), channel_id=1, source_target_pairs={{0,12},{1,13},{2,14},{3,15},{4,0},{5,1},{6,2},{7,3},{8,4},{9,5},{1... | collective-permute-start | bytes 417800 | tf_op jit(solution)/shard_map/ppermute | solution.py:26
  56.9 6.3 %collective-permute-start.17 = (f32[136,256]{1,0:T(8,128)S(1)}, f32[136,256]{1,0:T(8,128)S(1)}, u32[]{:S(2)}, u32[]{:S(2)}) collective-permute-start(f32[136,256]{1,0:T(8,128)S(1)} %get-tuple-element.58), channel_id=1, source_target_pairs={{0,8},{1,9},{2,10},{3,11},{4,12},{5,13},{6,14},{7,15},{8,0},{9,1},... | collective-permute-start | bytes 417800 | tf_op jit(solution)/shard_map/ppermute | solution.py:26
  59.4 6.5 %collective-permute-start.20 = (f32[136,128]{1,0:T(8,128)S(1)}, f32[136,128]{1,0:T(8,128)S(1)}, u32[]{:S(2)}, u32[]{:S(2)}) collective-permute-start(f32[136,128]{1,0:T(8,128)S(1)} %get-tuple-element.64), channel_id=1, source_target_pairs={{0,48},{16,0},{32,16},{48,32},{64,112},{80,64},{96,80},{112,96},{1... | collective-permute-start | bytes 208904 | tf_op jit(solution)/shard_map/ppermute | solution.py:31
  61.8 7.2 %collective-permute-start.21 = (f32[136,128]{1,0:T(8,128)S(1)}, f32[136,128]{1,0:T(8,128)S(1)}, u32[]{:S(2)}, u32[]{:S(2)}) collective-permute-start(f32[136,128]{1,0:T(8,128)S(1)} %get-tuple-element.65), channel_id=1, source_target_pairs={{0,32},{16,48},{32,0},{48,16},{64,96},{80,112},{96,64},{112,80},{1... | collective-permute-start | bytes 208904 | tf_op jit(solution)/shard_map/ppermute | solution.py:31
  63.3 5.7 %collective-permute-start.18 = (f32[136,128]{1,0:T(8,128)S(1)}, f32[136,128]{1,0:T(8,128)S(1)}, u32[]{:S(2)}, u32[]{:S(2)}) collective-permute-start(f32[136,128]{1,0:T(8,128)S(1)} %get-tuple-element.61), channel_id=1, source_target_pairs={{0,2},{1,3},{2,0},{3,1},{4,6},{5,7},{6,4},{7,5},{8,10},{9,11},{10,... | collective-permute-start | bytes 208904 | tf_op jit(solution)/shard_map/ppermute | solution.py:35
  65.6 7.6 %collective-permute-start.19 = (f32[136,128]{1,0:T(8,128)S(1)}, f32[136,128]{1,0:T(8,128)S(1)}, u32[]{:S(2)}, u32[]{:S(2)}) collective-permute-start(f32[136,128]{1,0:T(8,128)S(1)} %get-tuple-element.63), channel_id=1, source_target_pairs={{0,16},{16,32},{32,48},{48,0},{64,80},{80,96},{96,112},{112,64},{1... | collective-permute-start | bytes 208904 | tf_op jit(solution)/shard_map/ppermute | solution.py:31

commit v14 on v13

--- a/solution.py
+++ b/solution.py
@@ -141,7 +141,7 @@
 
 def one_block(ones, slow, total):
     pieces = [ones[low * 2 + high][slow] for low in range(2) for high in range(2)]
-    starts = [start_one(WAY[slow], high, low) for low in range(2) for high in range(2)]
+    starts = [start_one(slow, high, low) for low in range(2) for high in range(2)]
     return block_of(pieces, starts, total)
 
 
@@ -268,8 +268,8 @@
     two = [own_two] + [fast_shift("row", own_two, -step) for step in WAY[1:]]
     one = [own_one, fast_swap("col", own_one, 2)]
     one, two = together((jnp.stack(one), jnp.stack(two)))
-    one = [one] + [slow_shift("col", one, -step) for step in WAY[1:]]
-    order = (2, 3, 1)
+    one = [one] + [slow_shift("col", one, -step) for step in range(1, SUB)]
+    order = (3, 2, 1)
     twos = [two] + [slow_shift("row", two, -step) for step in order]
     one, twos = together((jnp.stack(one, axis=1), twos))
     twos = [twos[0]] + [twos[1 + order.index(step)] for step in range(1, SUB)]
@@ -306,7 +306,7 @@
     theirs_one = fast_swap("col", send_one, 1)
     (keep_one,) = row_scores(ones[:2], twos, ((0, 0), (0, 1)), 40, 2)
     cols = list(call(block_kernel, [f32(ROWS, SHARD)] * SUB, cols, work=1 * work))
-    rows = spread("col", core_merge(keep_one, theirs_one, 0, 1), WAY)
+    rows = spread("col", core_merge(keep_one, theirs_one, 0, 1), range(SUB))
     keep, send = call(chip_kernel, [f32(ROWS, SHARD)] * 2, rows)
     theirs = fast_swap("col", send, 2)
     cols[1], keep = together((cols[1], keep))

time: 74.3 us -> 75.3 us (1.013)
  starting transfers between devices: 39.5 us -> 41.4 us
  waiting for transfers between devices: 18.8 us -> 18 us
    ppermute x4, waiting for transfers between devices: 1.51 us -> 3.5 us  [fast_swap(): return lax.ppermute(value, axis, [(i, i ^ step) for i in range(SUB * SUB)])]
    ppermute x12, waiting for transfers between devices: 6.87 us -> 5.45 us  [slow_shift(): return lax.ppermute(value, axis, pairs)]
    ppermute x6, waiting for transfers between devices: 10.4 us -> 9.03 us  [fast_shift(): return lax.ppermute(value, axis, pairs)]
    ppermute x12, starting transfers between devices: 18 us -> 19.1 us  [slow_shift(): return lax.ppermute(value, axis, pairs)]
    ppermute x4, starting transfers between devices: 7.81 us -> 8.81 us  [fast_swap(): return lax.ppermute(value, axis, [(i, i ^ step) for i in range(SUB * SUB)])]
  transfers between devices with their start and end apart: 22 -> 22, of which waited for: 8 -> 9; matrix products, arithmetic and copies ran while one was open for 1% -> 1% of each run, Pallas kernels for 10% -> 10%
where the time goes in v14:
time: 75.3 us; the launch traced here: 75.1 us
  starting transfers between devices  41.4 us (55%)
  waiting for transfers between devices  18 us (24%)
  Pallas kernels  13.9 us (18%)
  other arithmetic  0.99 us (1%)
  between operations  0.77 us (1%)
    ppermute x12, starting transfers between devices, slow_shift(): return lax.ppermute(value, axis, pairs)  19.1 us
    pallas_call x9, Pallas kernels, call(): pl.pallas_call(kernel, out_shape=shapes, in_specs=specs or [VMEM] * len(a...  13.9 us
    ppermute x6, starting transfers between devices, fast_shift(): return lax.ppermute(value, axis, pairs)  13.5 us
    ppermute x6, waiting for transfers between devices, fast_shift(): return lax.ppermute(value, axis, pairs)  9.03 us
    ppermute x4, starting transfers between devices, fast_swap(): return lax.ppermute(value, axis, [(i, i ^ step) for i in range(SUB * SUB)])  8.81 us
    ppermute x12, waiting for transfers between devices, slow_shift(): return lax.ppermute(value, axis, pairs)  5.45 us
    ppermute x4, waiting for transfers between devices, fast_swap(): return lax.ppermute(value, axis, [(i, i ^ step) for i in range(SUB * SUB)])  3.5 us
  transfers between devices with their start and end apart: 22, of which 9 were waited for; matrix products, arithmetic and copies ran while one was open for 1% of the time, Pallas kernels for 10%

profile of v14, /device:TPU:1, one launch (start us, length us, event | category | flops | bytes accessed | tf_op | source)
XLA Modules:
  0.0 75.1 jit_solution(16865624585509114694)
XLA Ops:
  0.6 1.7 %shard_map.75 = (bf16[128,256]{1,0:T(8,128)(2,1)}, bf16[128,256]{1,0:T(8,128)(2,1)}) custom-call(bf16[128,128]{1,0:T(8,128)(2,1)} %feat_one.1, bf16[128,128]{1,0:T(8,128)(2,1)} %value_one.1, bf16[128,128]{1,0:T(8,128)(2,1)} %feat_two.1, bf16[128,128]{1,0:T(8,128)(2,1)} %value_two.1), custom_call_target="tpu_custom_call" | custom-call | bytes 262144 | tf_op jit(solution)/shard_map/pallas_call | solution.py:227
  2.3 2.6 %collective-permute-start = (bf16[128,256]{1,0:T(8,128)(2,1)}, bf16[128,256]{1,0:T(8,128)(2,1)S(1)}, u32[]{:S(2)}, u32[]{:S(2)}) collective-permute-start(bf16[128,256]{1,0:T(8,128)(2,1)} %get-tuple-element.35), channel_id=1, source_target_pairs={{0,2},{1,3},{2,0},{3,1},{4,6},{5,7},{6,4},{7,5},{8,10},{9,11},{10,... | collective-permute-start | bytes 196616 | tf_op jit(solution)/shard_map/ppermute | solution.py:35
  4.9 6.0 %collective-permute-start.3 = (bf16[128,256]{1,0:T(8,128)(2,1)}, bf16[128,256]{1,0:T(8,128)(2,1)S(1)}, u32[]{:S(2)}, u32[]{:S(2)}) collective-permute-start(bf16[128,256]{1,0:T(8,128)(2,1)} %get-tuple-element.36), channel_id=1, source_target_pairs={{0,32},{16,48},{32,0},{48,16},{64,96},{80,112},{96,64},{112,80},{1... | collective-permute-start | bytes 196616 | tf_op jit(solution)/shard_map/ppermute | solution.py:31
  10.9 1.2 %collective-permute-start.2 = (bf16[128,256]{1,0:T(8,128)(2,1)}, bf16[128,256]{1,0:T(8,128)(2,1)S(1)}, u32[]{:S(2)}, u32[]{:S(2)}) collective-permute-start(bf16[128,256]{1,0:T(8,128)(2,1)} %get-tuple-element.36), channel_id=1, source_target_pairs={{0,16},{16,32},{32,48},{48,0},{64,80},{80,96},{96,112},{112,64},{1... | collective-permute-start | bytes 196616 | tf_op jit(solution)/shard_map/ppermute | solution.py:31
  12.1 2.4 %collective-permute-start.1 = (bf16[128,256]{1,0:T(8,128)(2,1)}, bf16[128,256]{1,0:T(8,128)(2,1)S(1)}, u32[]{:S(2)}, u32[]{:S(2)}) collective-permute-start(bf16[128,256]{1,0:T(8,128)(2,1)} %get-tuple-element.36), channel_id=1, source_target_pairs={{0,48},{16,0},{32,16},{48,32},{64,112},{80,64},{96,80},{112,96},{1... | collective-permute-start | bytes 196616 | tf_op jit(solution)/shard_map/ppermute | solution.py:31
  14.5 0.9 %pad_maximum_fusion.2 = bf16[2,128,256]{2,1,0:T(8,128)(2,1)S(1)} fusion(bf16[1,128,256]{2,1,0:T(8,128)(2,1)S(1)} %bitcast.29, bf16[1,128,256]{2,1,0:T(8,128)(2,1)} %bitcast.28), kind=kLoop, calls=%fused_computation.6 | loop fusion | flops 65536 | bytes 262144 | tf_op jit(solution)/shard_map/stack | solution.py:270
  15.4 0.0 collective-permute-done.3
  15.4 2.9 %collective-permute-done.2 = bf16[128,256]{1,0:T(8,128)(2,1)S(1)} collective-permute-done((bf16[128,256]{1,0:T(8,128)(2,1)}, bf16[128,256]{1,0:T(8,128)(2,1)S(1)}, u32[]{:S(2)}, u32[]{:S(2)}) %collective-permute-start.2) | collective-permute-done | bytes 65568 | tf_op jit(solution)/shard_map/ppermute | solution.py:31
  18.2 0.2 collective-permute-done.1
  18.5 1.3 %collective-permute-start.6 = (bf16[2,128,256]{2,1,0:T(8,128)(2,1)S(1)}, bf16[2,128,256]{2,1,0:T(8,128)(2,1)S(1)}, u32[]{:S(2)}, u32[]{:S(2)}) collective-permute-start(bf16[2,128,256]{2,1,0:T(8,128)(2,1)S(1)} %pad_maximum_fusion.2), channel_id=1, source_target_pairs={{0,4},{1,5},{2,6},{3,7},{4,8},{5,9},{6,10},{7,11},{8,12},{9,13},{1... | collective-permute-start | bytes 393224 | tf_op jit(solution)/shard_map/ppermute | solution.py:26
  19.8 1.3 %collective-permute-start.7 = (bf16[4,128,256]{2,1,0:T(8,128)(2,1)S(1)}, bf16[4,128,256]{2,1,0:T(8,128)(2,1)S(1)}, u32[]{:S(2)}, u32[]{:S(2)}) collective-permute-start(bf16[4,128,256]{2,1,0:T(8,128)(2,1)S(1)} %pad_maximum_fusion.1.refs_4_.refs_2_), channel_id=1, source_target_pairs={{0,64},{16,80},{32,96},{48,112},{64,128},{80,144},{96,160},{112,17... | collective-permute-start | bytes 786440 | tf_op jit(solution)/shard_map/ppermute | solution.py:26
  21.1 2.6 %collective-permute-start.8 = (bf16[4,128,256]{2,1,0:T(8,128)(2,1)S(1)}, bf16[4,128,256]{2,1,0:T(8,128)(2,1)S(1)}, u32[]{:S(2)}, u32[]{:S(2)}) collective-permute-start(bf16[4,128,256]{2,1,0:T(8,128)(2,1)S(1)} %pad_maximum_fusion.1.refs_4_.refs_2_), channel_id=1, source_target_pairs={{0,128},{16,144},{32,160},{48,176},{64,192},{80,208},{96,224},{112... | collective-permute-start | bytes 786440 | tf_op jit(solution)/shard_map/ppermute | solution.py:26
  23.7 1.1 %collective-permute-start.9 = (bf16[4,128,256]{2,1,0:T(8,128)(2,1)S(1)}, bf16[4,128,256]{2,1,0:T(8,128)(2,1)S(1)}, u32[]{:S(2)}, u32[]{:S(2)}) collective-permute-start(bf16[4,128,256]{2,1,0:T(8,128)(2,1)S(1)} %pad_maximum_fusion.1.refs_4_.refs_2_), channel_id=1, source_target_pairs={{0,192},{16,208},{32,224},{48,240},{64,0},{80,16},{96,32},{112,48}... | collective-permute-start | bytes 786440 | tf_op jit(solution)/shard_map/ppermute | solution.py:26
  24.8 2.5 %collective-permute-start.5 = (bf16[2,128,256]{2,1,0:T(8,128)(2,1)S(1)}, bf16[2,128,256]{2,1,0:T(8,128)(2,1)S(1)}, u32[]{:S(2)}, u32[]{:S(2)}) collective-permute-start(bf16[2,128,256]{2,1,0:T(8,128)(2,1)S(1)} %pad_maximum_fusion.2), channel_id=1, source_target_pairs={{0,8},{1,9},{2,10},{3,11},{4,12},{5,13},{6,14},{7,15},{8,0},{9,1},... | collective-permute-start | bytes 393224 | tf_op jit(solution)/shard_map/ppermute | solution.py:26
  27.2 0.0 collective-permute-done.6
  27.2 1.2 %collective-permute-start.4 = (bf16[2,128,256]{2,1,0:T(8,128)(2,1)S(1)}, bf16[2,128,256]{2,1,0:T(8,128)(2,1)S(1)}, u32[]{:S(2)}, u32[]{:S(2)}) collective-permute-start(bf16[2,128,256]{2,1,0:T(8,128)(2,1)S(1)} %pad_maximum_fusion.2), channel_id=1, source_target_pairs={{0,12},{1,13},{2,14},{3,15},{4,0},{5,1},{6,2},{7,3},{8,4},{9,5},{1... | collective-permute-start | bytes 393224 | tf_op jit(solution)/shard_map/ppermute | solution.py:26
  28.4 1.7 %collective-permute-done.5 = bf16[2,128,256]{2,1,0:T(8,128)(2,1)S(1)} collective-permute-done((bf16[2,128,256]{2,1,0:T(8,128)(2,1)S(1)}, bf16[2,128,256]{2,1,0:T(8,128)(2,1)S(1)}, u32[]{:S(2)}, u32[]{:S(2)}) %collective-permute-start.5) | collective-permute-done | bytes 131104 | tf_op jit(solution)/shard_map/ppermute | solution.py:26
  30.1 1.2 %collective-permute-done.4 = bf16[2,128,256]{2,1,0:T(8,128)(2,1)S(1)} collective-permute-done((bf16[2,128,256]{2,1,0:T(8,128)(2,1)S(1)}, bf16[2,128,256]{2,1,0:T(8,128)(2,1)S(1)}, u32[]{:S(2)}, u32[]{:S(2)}) %collective-permute-start.4) | collective-permute-done | bytes 131104 | tf_op jit(solution)/shard_map/ppermute | solution.py:26
  31.3 0.1 pad_maximum_fusion
  31.3 0.0 collective-permute-done.7.refs_5_
  31.3 2.6 %collective-permute-done.8.refs_4_ = bf16[4,128,256]{2,1,0:T(8,128)(2,1)S(1)} collective-permute-done((bf16[4,128,256]{2,1,0:T(8,128)(2,1)S(1)}, bf16[4,128,256]{2,1,0:T(8,128)(2,1)S(1)}, u32[]{:S(2)}, u32[]{:S(2)}) %collective-permute-start.8) | collective-permute-done | bytes 262176 | tf_op jit(solution)/shard_map/ppermute | solution.py:26
  33.9 0.0 collective-permute-done.9.refs_6_.refs_3_
  33.9 2.7 %collective-permute-start.10 = (bf16[2,4,128,256]{3,2,1,0:T(8,128)(2,1)S(1)}, bf16[2,4,128,256]{3,2,1,0:T(8,128)(2,1)S(1)}, u32[]{:S(2)}, u32[]{:S(2)}) collective-permute-start(bf16[2,4,128,256]{3,2,1,0:T(8,128)(2,1)S(1)} %pad_maximum_fusion), channel_id=1, source_target_pairs={{0,1},{1,0},{2,3},{3,2},{4,5},{5,4},{6,7},{7,6},{8,9},{9,8},{10,11... | collective-permute-start | bytes 1572872 | tf_op jit(solution)/shard_map/ppermute | solution.py:35
  36.6 1.5 %collective-permute-done.10 = bf16[2,4,128,256]{3,2,1,0:T(8,128)(2,1)S(1)} collective-permute-done((bf16[2,4,128,256]{3,2,1,0:T(8,128)(2,1)S(1)}, bf16[2,4,128,256]{3,2,1,0:T(8,128)(2,1)S(1)}, u32[]{:S(2)}, u32[]{:S(2)}) %collective-permute-start.10) | collective-permute-done | bytes 524320 | tf_op jit(solution)/shard_map/ppermute | solution.py:35
  38.2 4.0 %shard_map.76 = (f32[136,512]{1,0:T(8,128)S(1)}, f32[136,512]{1,0:T(8,128)S(1)}, f32[136,512]{1,0:T(8,128)S(1)}) custom-call(bf16[4,128,256]{2,1,0:T(8,128)(2,1)S(1)} %get-tuple-element.46.refs_0_, bf16[4,128,256]{2,1,0:T(8,128)(2,1)S(1)} %get-tuple-element.47.refs_1_, bf16[4,128,256]{2,1,0:T(8,128)(2,1)S(1)} %get-tuple-element.48.refs_2_.refs_0_, ...), custom_call_target="tpu_custom_call" | custom-call | flops 1610612736 | bytes 2670592 | tf_op jit(solution)/shard_map/pallas_call | solution.py:227
  42.1 1.1 %collective-permute-start.11 = (f32[136,512]{1,0:T(8,128)S(1)}, f32[136,512]{1,0:T(8,128)S(1)}, u32[]{:S(2)}, u32[]{:S(2)}) collective-permute-start(f32[136,512]{1,0:T(8,128)S(1)} %get-tuple-element.51), channel_id=1, source_target_pairs={{0,64},{16,80},{32,96},{48,112},{64,128},{80,144},{96,160},{112,17... | collective-permute-start | bytes 835592 | tf_op jit(solution)/shard_map/ppermute | solution.py:26
  43.3 2.1 %collective-permute-start.12 = (f32[136,512]{1,0:T(8,128)S(1)}, f32[136,512]{1,0:T(8,128)S(1)}, u32[]{:S(2)}, u32[]{:S(2)}) collective-permute-start(f32[136,512]{1,0:T(8,128)S(1)} %get-tuple-element.52), channel_id=1, source_target_pairs={{0,128},{16,144},{32,160},{48,176},{64,192},{80,208},{96,224},{112... | collective-permute-start | bytes 835592 | tf_op jit(solution)/shard_map/ppermute | solution.py:26
  45.4 1.4 %collective-permute-start.13 = (f32[136,512]{1,0:T(8,128)S(1)}, f32[136,512]{1,0:T(8,128)S(1)}, u32[]{:S(2)}, u32[]{:S(2)}) collective-permute-start(f32[136,512]{1,0:T(8,128)S(1)} %get-tuple-element.53), channel_id=1, source_target_pairs={{0,192},{16,208},{32,224},{48,240},{64,0},{80,16},{96,32},{112,48}... | collective-permute-start | bytes 835592 | tf_op jit(solution)/shard_map/ppermute | solution.py:26
  46.8 2.8 %shard_map.79 = f32[2,136,512]{2,1,0:T(8,128)S(1)} custom-call(bf16[4,128,256]{2,1,0:T(8,128)(2,1)S(1)} %get-tuple-element.48.refs_2_.refs_0_, bf16[4,128,256]{2,1,0:T(8,128)(2,1)S(1)} %get-tuple-element.49.refs_3_.refs_1_, bf16[4,128,256]{2,1,0:T(8,128)(2,1)S(1)} %pad_maximum_fusion.1.refs_4_.refs_2_, ...), custom_call_target="tpu_custom_call" | custom-call | flops 1073741824 | bytes 2129920 | tf_op jit(solution)/shard_map/pallas_call | solution.py:227
  49.5 1.3 %collective-permute-start.14 = (f32[2,136,512]{2,1,0:T(8,128)S(1)}, f32[2,136,512]{2,1,0:T(8,128)S(1)}, u32[]{:S(2)}, u32[]{:S(2)}) collective-permute-start(f32[2,136,512]{2,1,0:T(8,128)S(1)} %shard_map.79), channel_id=1, source_target_pairs={{0,1},{1,0},{2,3},{3,2},{4,5},{5,4},{6,7},{7,6},{8,9},{9,8},{10,11... | collective-permute-start | bytes 1671176 | tf_op jit(solution)/shard_map/ppermute | solution.py:35
  50.8 2.8 %shard_map.80.refs_1_ = f32[2,136,512]{2,1,0:T(8,128)S(1)} custom-call(bf16[4,128,256]{2,1,0:T(8,128)(2,1)S(1)} %get-tuple-element.46.refs_0_, bf16[4,128,256]{2,1,0:T(8,128)(2,1)S(1)} %get-tuple-element.47.refs_1_, bf16[4,128,256]{2,1,0:T(8,128)(2,1)S(1)} %pad_maximum_fusion.1.refs_4_.refs_2_, ...), custom_call_target="tpu_custom_call" | custom-call | flops 21474836480 | bytes 2129920 | tf_op jit(solution)/shard_map/pallas_call | solution.py:227
  53.7 0.1 shard_map.81
  53.7 1.3 %collective-permute-start.15 = (f32[136,256]{1,0:T(8,128)S(1)}, f32[136,256]{1,0:T(8,128)S(1)}, u32[]{:S(2)}, u32[]{:S(2)}) collective-permute-start(f32[136,256]{1,0:T(8,128)S(1)} %get-tuple-element.56), channel_id=1, source_target_pairs={{0,4},{1,5},{2,6},{3,7},{4,8},{5,9},{6,10},{7,11},{8,12},{9,13},{1... | collective-permute-start | bytes 417800 | tf_op jit(solution)/shard_map/ppermute | solution.py:26
  55.0 1.4 %collective-permute-start.16 = (f32[136,256]{1,0:T(8,128)S(1)}, f32[136,256]{1,0:T(8,128)S(1)}, u32[]{:S(2)}, u32[]{:S(2)}) collective-permute-start(f32[136,256]{1,0:T(8,128)S(1)} %get-tuple-element.57), channel_id=1, source_target_pairs={{0,8},{1,9},{2,10},{3,11},{4,12},{5,13},{6,14},{7,15},{8,0},{9,1},... | collective-permute-start | bytes 417800 | tf_op jit(solution)/shard_map/ppermute | solution.py:26
  56.5 0.0 collective-permute-done.11.refs_1_
  56.5 1.9 %collective-permute-start.17 = (f32[136,256]{1,0:T(8,128)S(1)}, f32[136,256]{1,0:T(8,128)S(1)}, u32[]{:S(2)}, u32[]{:S(2)}) collective-permute-start(f32[136,256]{1,0:T(8,128)S(1)} %get-tuple-element.58), channel_id=1, source_target_pairs={{0,12},{1,13},{2,14},{3,15},{4,0},{5,1},{6,2},{7,3},{8,4},{9,5},{1... | collective-permute-start | bytes 417800 | tf_op jit(solution)/shard_map/ppermute | solution.py:26
  58.4 1.6 %shard_map.77.refs_0_ = f32[136,512]{1,0:T(8,128)S(1)} custom-call(bf16[4,128,256]{2,1,0:T(8,128)(2,1)S(1)} %get-tuple-element.46.refs_0_, bf16[4,128,256]{2,1,0:T(8,128)(2,1)S(1)} %get-tuple-element.47.refs_1_, bf16[4,128,256]{2,1,0:T(8,128)(2,1)S(1)} %get-tuple-element.48.refs_2_.refs_0_, bf16[4,128,256]{2,1,0:T(8,128)(2,1)S(1)} %get-tuple-element.49.refs_3_.refs_1_, ...), custom_call_target="tpu_custom_call" | custom-call | flops 536870912 | bytes 1589248 | tf_op jit(solution)/shard_map/pallas_call | solution.py:227
  60.0 0.0 collective-permute-done.13.refs_3_
  60.0 0.1 shard_map.78
  60.1 2.4 %collective-permute-start.20 = (f32[136,128]{1,0:T(8,128)S(1)}, f32[136,128]{1,0:T(8,128)S(1)}, u32[]{:S(2)}, u32[]{:S(2)}) collective-permute-start(f32[136,128]{1,0:T(8,128)S(1)} %get-tuple-element.64), channel_id=1, source_target_pairs={{0,48},{16,0},{32,16},{48,32},{64,112},{80,64},{96,80},{112,96},{1... | collective-permute-start | bytes 208904 | tf_op jit(solution)/shard_map/ppermute | solution.py:31
  62.5 1.4 %collective-permute-start.21 = (f32[136,128]{1,0:T(8,128)S(1)}, f32[136,128]{1,0:T(8,128)S(1)}, u32[]{:S(2)}, u32[]{:S(2)}) collective-permute-start(f32[136,128]{1,0:T(8,128)S(1)} %get-tuple-element.65), channel_id=1, source_target_pairs={{0,32},{16,48},{32,0},{48,16},{64,96},{80,112},{96,64},{112,80},{1... | collective-permute-start | bytes 208904 | tf_op jit(solution)/shard_map/ppermute | solution.py:31
  63.9 0.1 shard_map.82
  64.0 2.3 %collective-permute-start.18 = (f32[136,128]{1,0:T(8,128)S(1)}, f32[136,128]{1,0:T(8,128)S(1)}, u32[]{:S(2)}, u32[]{:S(2)}) collective-permute-start(f32[136,128]{1,0:T(8,128)S(1)} %get-tuple-element.61), channel_id=1, source_target_pairs={{0,2},{1,3},{2,0},{3,1},{4,6},{5,7},{6,4},{7,5},{8,10},{9,11},{10,... | collective-permute-start | bytes 208904 | tf_op jit(solution)/shard_map/ppermute | solution.py:35
  66.3 0.1 collective-permute-start.19
  66.4 3.4 %collective-permute-done.21.refs_5_ = f32[136,128]{1,0:T(8,128)S(1)} collective-permute-done((f32[136,128]{1,0:T(8,128)S(1)}, f32[136,128]{1,0:T(8,128)S(1)}, u32[]{:S(2)}, u32[]{:S(2)}) %collective-permute-start.21) | collective-permute-done | bytes 69664 | tf_op jit(solution)/shard_map/ppermute | solution.py:31
  69.7 2.0 %collective-permute-done.18.refs_1_ = f32[136,128]{1,0:T(8,128)S(1)} collective-permute-done((f32[136,128]{1,0:T(8,128)S(1)}, f32[136,128]{1,0:T(8,128)S(1)}, u32[]{:S(2)}, u32[]{:S(2)}) %collective-permute-start.18) | collective-permute-done | bytes 69664 | tf_op jit(solution)/shard_map/ppermute | solution.py:35
  71.7 2.5 %collective-permute-done.19.refs_3_ = f32[136,128]{1,0:T(8,128)S(1)} collective-permute-done((f32[136,128]{1,0:T(8,128)S(1)}, f32[136,128]{1,0:T(8,128)S(1)}, u32[]{:S(2)}, u32[]{:S(2)}) %collective-permute-start.19) | collective-permute-done | bytes 69664 | tf_op jit(solution)/shard_map/ppermute | solution.py:31
  74.3 0.8 %shard_map.83 = (f32[128,128]{1,0:T(8,128)}, f32[2,128]{1,0:T(2,128)}, f32[128,128]{1,0:T(8,128)}, f32[2,128]{1,0:T(2,128)}) custom-call(f32[136,128]{1,0:T(8,128)S(1)} %get-tuple-element.60.refs_0_, f32[136,128]{1,0:T(8,128)S(1)} %collective-permute-done.18.refs_1_, f32[136,128]{1,0:T(8,128)S(1)} %get-tuple-element.62.refs_2_, ...), custom_call_target="tpu_custom_call" | custom-call | bytes 550912 | tf_op jit(solution)/shard_map/pallas_call | solution.py:227
  (12 shorter events, 0.1 us)
Async XLA Ops:
  2.3 12.1 %collective-permute-start = (bf16[128,256]{1,0:T(8,128)(2,1)}, bf16[128,256]{1,0:T(8,128)(2,1)S(1)}, u32[]{:S(2)}, u32[]{:S(2)}) collective-permute-start(bf16[128,256]{1,0:T(8,128)(2,1)} %get-tuple-element.35), channel_id=1, source_target_pairs={{0,2},{1,3},{2,0},{3,1},{4,6},{5,7},{6,4},{7,5},{8,10},{9,11},{10,... | collective-permute-start | bytes 196616 | tf_op jit(solution)/shard_map/ppermute | solution.py:35
  4.9 10.5 %collective-permute-start.3 = (bf16[128,256]{1,0:T(8,128)(2,1)}, bf16[128,256]{1,0:T(8,128)(2,1)S(1)}, u32[]{:S(2)}, u32[]{:S(2)}) collective-permute-start(bf16[128,256]{1,0:T(8,128)(2,1)} %get-tuple-element.36), channel_id=1, source_target_pairs={{0,32},{16,48},{32,0},{48,16},{64,96},{80,112},{96,64},{112,80},{1... | collective-permute-start | bytes 196616 | tf_op jit(solution)/shard_map/ppermute | solution.py:31
  10.9 7.3 %collective-permute-start.2 = (bf16[128,256]{1,0:T(8,128)(2,1)}, bf16[128,256]{1,0:T(8,128)(2,1)S(1)}, u32[]{:S(2)}, u32[]{:S(2)}) collective-permute-start(bf16[128,256]{1,0:T(8,128)(2,1)} %get-tuple-element.36), channel_id=1, source_target_pairs={{0,16},{16,32},{32,48},{48,0},{64,80},{80,96},{96,112},{112,64},{1... | collective-permute-start | bytes 196616 | tf_op jit(solution)/shard_map/ppermute | solution.py:31
  12.1 6.4 %collective-permute-start.1 = (bf16[128,256]{1,0:T(8,128)(2,1)}, bf16[128,256]{1,0:T(8,128)(2,1)S(1)}, u32[]{:S(2)}, u32[]{:S(2)}) collective-permute-start(bf16[128,256]{1,0:T(8,128)(2,1)} %get-tuple-element.36), channel_id=1, source_target_pairs={{0,48},{16,0},{32,16},{48,32},{64,112},{80,64},{96,80},{112,96},{1... | collective-permute-start | bytes 196616 | tf_op jit(solution)/shard_map/ppermute | solution.py:31
  14.5 4.0 %copy-start = (bf16[128,256]{1,0:T(8,128)(2,1)S(1)}, bf16[128,256]{1,0:T(8,128)(2,1)}, u32[]{:S(2)}) copy-start(bf16[128,256]{1,0:T(8,128)(2,1)} %get-tuple-element.36) | copy-start | bytes 196612
  18.5 8.7 %collective-permute-start.6 = (bf16[2,128,256]{2,1,0:T(8,128)(2,1)S(1)}, bf16[2,128,256]{2,1,0:T(8,128)(2,1)S(1)}, u32[]{:S(2)}, u32[]{:S(2)}) collective-permute-start(bf16[2,128,256]{2,1,0:T(8,128)(2,1)S(1)} %pad_maximum_fusion.2), channel_id=1, source_target_pairs={{0,4},{1,5},{2,6},{3,7},{4,8},{5,9},{6,10},{7,11},{8,12},{9,13},{1... | collective-permute-start | bytes 393224 | tf_op jit(solution)/shard_map/ppermute | solution.py:26
  19.8 11.5 %collective-permute-start.7 = (bf16[4,128,256]{2,1,0:T(8,128)(2,1)S(1)}, bf16[4,128,256]{2,1,0:T(8,128)(2,1)S(1)}, u32[]{:S(2)}, u32[]{:S(2)}) collective-permute-start(bf16[4,128,256]{2,1,0:T(8,128)(2,1)S(1)} %pad_maximum_fusion.1.refs_4_.refs_2_), channel_id=1, source_target_pairs={{0,64},{16,80},{32,96},{48,112},{64,128},{80,144},{96,160},{112,17... | collective-permute-start | bytes 786440 | tf_op jit(solution)/shard_map/ppermute | solution.py:26
  21.1 12.8 %collective-permute-start.8 = (bf16[4,128,256]{2,1,0:T(8,128)(2,1)S(1)}, bf16[4,128,256]{2,1,0:T(8,128)(2,1)S(1)}, u32[]{:S(2)}, u32[]{:S(2)}) collective-permute-start(bf16[4,128,256]{2,1,0:T(8,128)(2,1)S(1)} %pad_maximum_fusion.1.refs_4_.refs_2_), channel_id=1, source_target_pairs={{0,128},{16,144},{32,160},{48,176},{64,192},{80,208},{96,224},{112... | collective-permute-start | bytes 786440 | tf_op jit(solution)/shard_map/ppermute | solution.py:26
  23.7 10.2 %collective-permute-start.9 = (bf16[4,128,256]{2,1,0:T(8,128)(2,1)S(1)}, bf16[4,128,256]{2,1,0:T(8,128)(2,1)S(1)}, u32[]{:S(2)}, u32[]{:S(2)}) collective-permute-start(bf16[4,128,256]{2,1,0:T(8,128)(2,1)S(1)} %pad_maximum_fusion.1.refs_4_.refs_2_), channel_id=1, source_target_pairs={{0,192},{16,208},{32,224},{48,240},{64,0},{80,16},{96,32},{112,48}... | collective-permute-start | bytes 786440 | tf_op jit(solution)/shard_map/ppermute | solution.py:26
  24.8 5.3 %collective-permute-start.5 = (bf16[2,128,256]{2,1,0:T(8,128)(2,1)S(1)}, bf16[2,128,256]{2,1,0:T(8,128)(2,1)S(1)}, u32[]{:S(2)}, u32[]{:S(2)}) collective-permute-start(bf16[2,128,256]{2,1,0:T(8,128)(2,1)S(1)} %pad_maximum_fusion.2), channel_id=1, source_target_pairs={{0,8},{1,9},{2,10},{3,11},{4,12},{5,13},{6,14},{7,15},{8,0},{9,1},... | collective-permute-start | bytes 393224 | tf_op jit(solution)/shard_map/ppermute | solution.py:26
  27.2 4.0 %collective-permute-start.4 = (bf16[2,128,256]{2,1,0:T(8,128)(2,1)S(1)}, bf16[2,128,256]{2,1,0:T(8,128)(2,1)S(1)}, u32[]{:S(2)}, u32[]{:S(2)}) collective-permute-start(bf16[2,128,256]{2,1,0:T(8,128)(2,1)S(1)} %pad_maximum_fusion.2), channel_id=1, source_target_pairs={{0,12},{1,13},{2,14},{3,15},{4,0},{5,1},{6,2},{7,3},{8,4},{9,5},{1... | collective-permute-start | bytes 393224 | tf_op jit(solution)/shard_map/ppermute | solution.py:26
  33.9 4.2 %collective-permute-start.10 = (bf16[2,4,128,256]{3,2,1,0:T(8,128)(2,1)S(1)}, bf16[2,4,128,256]{3,2,1,0:T(8,128)(2,1)S(1)}, u32[]{:S(2)}, u32[]{:S(2)}) collective-permute-start(bf16[2,4,128,256]{3,2,1,0:T(8,128)(2,1)S(1)} %pad_maximum_fusion), channel_id=1, source_target_pairs={{0,1},{1,0},{2,3},{3,2},{4,5},{5,4},{6,7},{7,6},{8,9},{9,8},{10,11... | collective-permute-start | bytes 1572872 | tf_op jit(solution)/shard_map/ppermute | solution.py:35
  42.1 14.3 %collective-permute-start.11 = (f32[136,512]{1,0:T(8,128)S(1)}, f32[136,512]{1,0:T(8,128)S(1)}, u32[]{:S(2)}, u32[]{:S(2)}) collective-permute-start(f32[136,512]{1,0:T(8,128)S(1)} %get-tuple-element.51), channel_id=1, source_target_pairs={{0,64},{16,80},{32,96},{48,112},{64,128},{80,144},{96,160},{112,17... | collective-permute-start | bytes 835592 | tf_op jit(solution)/shard_map/ppermute | solution.py:26
  43.3 16.7 %collective-permute-start.12 = (f32[136,512]{1,0:T(8,128)S(1)}, f32[136,512]{1,0:T(8,128)S(1)}, u32[]{:S(2)}, u32[]{:S(2)}) collective-permute-start(f32[136,512]{1,0:T(8,128)S(1)} %get-tuple-element.52), channel_id=1, source_target_pairs={{0,128},{16,144},{32,160},{48,176},{64,192},{80,208},{96,224},{112... | collective-permute-start | bytes 835592 | tf_op jit(solution)/shard_map/ppermute | solution.py:26
  45.4 14.6 %collective-permute-start.13 = (f32[136,512]{1,0:T(8,128)S(1)}, f32[136,512]{1,0:T(8,128)S(1)}, u32[]{:S(2)}, u32[]{:S(2)}) collective-permute-start(f32[136,512]{1,0:T(8,128)S(1)} %get-tuple-element.53), channel_id=1, source_target_pairs={{0,192},{16,208},{32,224},{48,240},{64,0},{80,16},{96,32},{112,48}... | collective-permute-start | bytes 835592 | tf_op jit(solution)/shard_map/ppermute | solution.py:26
  49.5 4.1 %collective-permute-start.14 = (f32[2,136,512]{2,1,0:T(8,128)S(1)}, f32[2,136,512]{2,1,0:T(8,128)S(1)}, u32[]{:S(2)}, u32[]{:S(2)}) collective-permute-start(f32[2,136,512]{2,1,0:T(8,128)S(1)} %shard_map.79), channel_id=1, source_target_pairs={{0,1},{1,0},{2,3},{3,2},{4,5},{5,4},{6,7},{7,6},{8,9},{9,8},{10,11... | collective-permute-start | bytes 1671176 | tf_op jit(solution)/shard_map/ppermute | solution.py:35
  53.7 10.2 %collective-permute-start.15 = (f32[136,256]{1,0:T(8,128)S(1)}, f32[136,256]{1,0:T(8,128)S(1)}, u32[]{:S(2)}, u32[]{:S(2)}) collective-permute-start(f32[136,256]{1,0:T(8,128)S(1)} %get-tuple-element.56), channel_id=1, source_target_pairs={{0,4},{1,5},{2,6},{3,7},{4,8},{5,9},{6,10},{7,11},{8,12},{9,13},{1... | collective-permute-start | bytes 417800 | tf_op jit(solution)/shard_map/ppermute | solution.py:26
  55.0 8.9 %collective-permute-start.16 = (f32[136,256]{1,0:T(8,128)S(1)}, f32[136,256]{1,0:T(8,128)S(1)}, u32[]{:S(2)}, u32[]{:S(2)}) collective-permute-start(f32[136,256]{1,0:T(8,128)S(1)} %get-tuple-element.57), channel_id=1, source_target_pairs={{0,8},{1,9},{2,10},{3,11},{4,12},{5,13},{6,14},{7,15},{8,0},{9,1},... | collective-permute-start | bytes 417800 | tf_op jit(solution)/shard_map/ppermute | solution.py:26
  56.5 7.4 %collective-permute-start.17 = (f32[136,256]{1,0:T(8,128)S(1)}, f32[136,256]{1,0:T(8,128)S(1)}, u32[]{:S(2)}, u32[]{:S(2)}) collective-permute-start(f32[136,256]{1,0:T(8,128)S(1)} %get-tuple-element.58), channel_id=1, source_target_pairs={{0,12},{1,13},{2,14},{3,15},{4,0},{5,1},{6,2},{7,3},{8,4},{9,5},{1... | collective-permute-start | bytes 417800 | tf_op jit(solution)/shard_map/ppermute | solution.py:26
  60.1 6.2 %collective-permute-start.20 = (f32[136,128]{1,0:T(8,128)S(1)}, f32[136,128]{1,0:T(8,128)S(1)}, u32[]{:S(2)}, u32[]{:S(2)}) collective-permute-start(f32[136,128]{1,0:T(8,128)S(1)} %get-tuple-element.64), channel_id=1, source_target_pairs={{0,48},{16,0},{32,16},{48,32},{64,112},{80,64},{96,80},{112,96},{1... | collective-permute-start | bytes 208904 | tf_op jit(solution)/shard_map/ppermute | solution.py:31
  62.5 7.2 %collective-permute-start.21 = (f32[136,128]{1,0:T(8,128)S(1)}, f32[136,128]{1,0:T(8,128)S(1)}, u32[]{:S(2)}, u32[]{:S(2)}) collective-permute-start(f32[136,128]{1,0:T(8,128)S(1)} %get-tuple-element.65), channel_id=1, source_target_pairs={{0,32},{16,48},{32,0},{48,16},{64,96},{80,112},{96,64},{112,80},{1... | collective-permute-start | bytes 208904 | tf_op jit(solution)/shard_map/ppermute | solution.py:31
  64.0 7.7 %collective-permute-start.18 = (f32[136,128]{1,0:T(8,128)S(1)}, f32[136,128]{1,0:T(8,128)S(1)}, u32[]{:S(2)}, u32[]{:S(2)}) collective-permute-start(f32[136,128]{1,0:T(8,128)S(1)} %get-tuple-element.61), channel_id=1, source_target_pairs={{0,2},{1,3},{2,0},{3,1},{4,6},{5,7},{6,4},{7,5},{8,10},{9,11},{10,... | collective-permute-start | bytes 208904 | tf_op jit(solution)/shard_map/ppermute | solution.py:35
  66.3 8.0 %collective-permute-start.19 = (f32[136,128]{1,0:T(8,128)S(1)}, f32[136,128]{1,0:T(8,128)S(1)}, u32[]{:S(2)}, u32[]{:S(2)}) collective-permute-start(f32[136,128]{1,0:T(8,128)S(1)} %get-tuple-element.63), channel_id=1, source_target_pairs={{0,16},{16,32},{32,48},{48,0},{64,80},{80,96},{96,112},{112,64},{1... | collective-permute-start | bytes 208904 | tf_op jit(solution)/shard_map/ppermute | solution.py:31

commit v15 on v12

--- a/solution.py
+++ b/solution.py
@@ -309,7 +309,7 @@
     rows = spread("col", core_merge(keep_one, theirs_one, 0, 1))
     keep, send = call(chip_kernel, [f32(ROWS, SHARD)] * 2, rows)
     theirs = fast_swap("col", send, 2)
-    cols[1], keep = together((cols[1], keep))
+    cols[1], cols[3], keep = together((cols[1], cols[3], keep))
     cols = [cols[0]] + [fast_shift("row", cols[step], step) for step in range(1, SUB)]
     outs = [f32(SHARD, WIDTH), f32(2, SHARD)] * 2
     return tuple(call(functools.partial(finish_kernel, total), outs, (keep, theirs, *cols)))

time: 73.9 us -> 73.8 us (level)
  starting transfers between devices: 43 us -> 44.2 us
  waiting for transfers between devices: 14.9 us -> 13.7 us
    ppermute x6, starting transfers between devices: 14.2 us -> 17.3 us  [fast_shift(): return lax.ppermute(value, axis, pairs)]
    ppermute x4, starting transfers between devices: 9.62 us -> 7.8 us  [fast_swap(): return lax.ppermute(value, axis, [(i, i ^ step) for i in range(SUB * SUB)])]
    ppermute x4, waiting for transfers between devices: 2.99 us -> 1.51 us  [fast_swap(): return lax.ppermute(value, axis, [(i, i ^ step) for i in range(SUB * SUB)])]
  transfers between devices with their start and end apart: 22 -> 22, of which waited for: 8 -> 7; matrix products, arithmetic and copies ran while one was open for 1% -> 1% of each run, Pallas kernels for 10% -> 10%
where the time goes in v15:
time: 73.8 us; the launch traced here: 73.6 us
  starting transfers between devices  44.2 us (60%)
  Pallas kernels  13.9 us (19%)
  waiting for transfers between devices  13.7 us (19%)
  other arithmetic  0.99 us (1%)
  between operations  0.77 us (1%)
    ppermute x12, starting transfers between devices, slow_shift(): return lax.ppermute(value, axis, pairs)  19.1 us
    ppermute x6, starting transfers between devices, fast_shift(): return lax.ppermute(value, axis, pairs)  17.3 us
    pallas_call x9, Pallas kernels, call(): pl.pallas_call(kernel, out_shape=shapes, in_specs=specs or [VMEM] * len(a...  13.9 us
    ppermute x4, starting transfers between devices, fast_swap(): return lax.ppermute(value, axis, [(i, i ^ step) for i in range(SUB * SUB)])  7.8 us
    ppermute x6, waiting for transfers between devices, fast_shift(): return lax.ppermute(value, axis, pairs)  7.05 us
    ppermute x12, waiting for transfers between devices, slow_shift(): return lax.ppermute(value, axis, pairs)  5.12 us
    ppermute x4, waiting for transfers between devices, fast_swap(): return lax.ppermute(value, axis, [(i, i ^ step) for i in range(SUB * SUB)])  1.51 us
  transfers between devices with their start and end apart: 22, of which 7 were waited for; matrix products, arithmetic and copies ran while one was open for 1% of the time, Pallas kernels for 10%

profile of v15, /device:TPU:1, one launch (start us, length us, event | category | flops | bytes accessed | tf_op | source)
XLA Modules:
  0.0 73.6 jit_solution(248138665199354446)
XLA Ops:
  0.6 1.7 %shard_map.75 = (bf16[128,256]{1,0:T(8,128)(2,1)}, bf16[128,256]{1,0:T(8,128)(2,1)}) custom-call(bf16[128,128]{1,0:T(8,128)(2,1)} %feat_one.1, bf16[128,128]{1,0:T(8,128)(2,1)} %value_one.1, bf16[128,128]{1,0:T(8,128)(2,1)} %feat_two.1, bf16[128,128]{1,0:T(8,128)(2,1)} %value_two.1), custom_call_target="tpu_custom_call" | custom-call | bytes 262144 | tf_op jit(solution)/shard_map/pallas_call | solution.py:226
  2.3 2.6 %collective-permute-start = (bf16[128,256]{1,0:T(8,128)(2,1)}, bf16[128,256]{1,0:T(8,128)(2,1)S(1)}, u32[]{:S(2)}, u32[]{:S(2)}) collective-permute-start(bf16[128,256]{1,0:T(8,128)(2,1)} %get-tuple-element.36), channel_id=1, source_target_pairs={{0,2},{1,3},{2,0},{3,1},{4,6},{5,7},{6,4},{7,5},{8,10},{9,11},{10,... | collective-permute-start | bytes 196616 | tf_op jit(solution)/shard_map/ppermute | solution.py:34
  4.9 3.0 %collective-permute-start.3 = (bf16[128,256]{1,0:T(8,128)(2,1)}, bf16[128,256]{1,0:T(8,128)(2,1)S(1)}, u32[]{:S(2)}, u32[]{:S(2)}) collective-permute-start(bf16[128,256]{1,0:T(8,128)(2,1)} %get-tuple-element.37), channel_id=1, source_target_pairs={{0,16},{16,32},{32,48},{48,0},{64,80},{80,96},{96,112},{112,64},{1... | collective-permute-start | bytes 196616 | tf_op jit(solution)/shard_map/ppermute | solution.py:30
  7.9 4.2 %collective-permute-start.2 = (bf16[128,256]{1,0:T(8,128)(2,1)}, bf16[128,256]{1,0:T(8,128)(2,1)S(1)}, u32[]{:S(2)}, u32[]{:S(2)}) collective-permute-start(bf16[128,256]{1,0:T(8,128)(2,1)} %get-tuple-element.37), channel_id=1, source_target_pairs={{0,32},{16,48},{32,0},{48,16},{64,96},{80,112},{96,64},{112,80},{1... | collective-permute-start | bytes 196616 | tf_op jit(solution)/shard_map/ppermute | solution.py:30
  12.1 2.4 %collective-permute-start.1 = (bf16[128,256]{1,0:T(8,128)(2,1)}, bf16[128,256]{1,0:T(8,128)(2,1)S(1)}, u32[]{:S(2)}, u32[]{:S(2)}) collective-permute-start(bf16[128,256]{1,0:T(8,128)(2,1)} %get-tuple-element.37), channel_id=1, source_target_pairs={{0,48},{16,0},{32,16},{48,32},{64,112},{80,64},{96,80},{112,96},{1... | collective-permute-start | bytes 196616 | tf_op jit(solution)/shard_map/ppermute | solution.py:30
  14.5 0.0 collective-permute-done
  14.5 0.9 %pad_maximum_fusion.2 = bf16[2,128,256]{2,1,0:T(8,128)(2,1)S(1)} fusion(bf16[1,128,256]{2,1,0:T(8,128)(2,1)S(1)} %bitcast.29, bf16[1,128,256]{2,1,0:T(8,128)(2,1)} %bitcast.28), kind=kLoop, calls=%fused_computation.6 | loop fusion | flops 65536 | bytes 262144 | tf_op jit(solution)/shard_map/stack | solution.py:269
  15.4 0.0 collective-permute-done.3
  15.4 1.9 %collective-permute-done.2 = bf16[128,256]{1,0:T(8,128)(2,1)S(1)} collective-permute-done((bf16[128,256]{1,0:T(8,128)(2,1)}, bf16[128,256]{1,0:T(8,128)(2,1)S(1)}, u32[]{:S(2)}, u32[]{:S(2)}) %collective-permute-start.2) | collective-permute-done | bytes 65568 | tf_op jit(solution)/shard_map/ppermute | solution.py:30
  17.3 1.0 %collective-permute-done.1 = bf16[128,256]{1,0:T(8,128)(2,1)S(1)} collective-permute-done((bf16[128,256]{1,0:T(8,128)(2,1)}, bf16[128,256]{1,0:T(8,128)(2,1)S(1)}, u32[]{:S(2)}, u32[]{:S(2)}) %collective-permute-start.1) | collective-permute-done | bytes 65568 | tf_op jit(solution)/shard_map/ppermute | solution.py:30
  18.3 1.3 %collective-permute-start.6 = (bf16[2,128,256]{2,1,0:T(8,128)(2,1)S(1)}, bf16[2,128,256]{2,1,0:T(8,128)(2,1)S(1)}, u32[]{:S(2)}, u32[]{:S(2)}) collective-permute-start(bf16[2,128,256]{2,1,0:T(8,128)(2,1)S(1)} %pad_maximum_fusion.2), channel_id=1, source_target_pairs={{0,4},{1,5},{2,6},{3,7},{4,8},{5,9},{6,10},{7,11},{8,12},{9,13},{1... | collective-permute-start | bytes 393224 | tf_op jit(solution)/shard_map/ppermute | solution.py:25
  19.6 1.3 %collective-permute-start.7 = (bf16[4,128,256]{2,1,0:T(8,128)(2,1)S(1)}, bf16[4,128,256]{2,1,0:T(8,128)(2,1)S(1)}, u32[]{:S(2)}, u32[]{:S(2)}) collective-permute-start(bf16[4,128,256]{2,1,0:T(8,128)(2,1)S(1)} %pad_maximum_fusion.1.refs_4_.refs_2_), channel_id=1, source_target_pairs={{0,64},{16,80},{32,96},{48,112},{64,128},{80,144},{96,160},{112,17... | collective-permute-start | bytes 786440 | tf_op jit(solution)/shard_map/ppermute | solution.py:25
  20.9 2.6 %collective-permute-start.8 = (bf16[4,128,256]{2,1,0:T(8,128)(2,1)S(1)}, bf16[4,128,256]{2,1,0:T(8,128)(2,1)S(1)}, u32[]{:S(2)}, u32[]{:S(2)}) collective-permute-start(bf16[4,128,256]{2,1,0:T(8,128)(2,1)S(1)} %pad_maximum_fusion.1.refs_4_.refs_2_), channel_id=1, source_target_pairs={{0,128},{16,144},{32,160},{48,176},{64,192},{80,208},{96,224},{112... | collective-permute-start | bytes 786440 | tf_op jit(solution)/shard_map/ppermute | solution.py:25
  23.5 1.1 %collective-permute-start.9 = (bf16[4,128,256]{2,1,0:T(8,128)(2,1)S(1)}, bf16[4,128,256]{2,1,0:T(8,128)(2,1)S(1)}, u32[]{:S(2)}, u32[]{:S(2)}) collective-permute-start(bf16[4,128,256]{2,1,0:T(8,128)(2,1)S(1)} %pad_maximum_fusion.1.refs_4_.refs_2_), channel_id=1, source_target_pairs={{0,192},{16,208},{32,224},{48,240},{64,0},{80,16},{96,32},{112,48}... | collective-permute-start | bytes 786440 | tf_op jit(solution)/shard_map/ppermute | solution.py:25
  24.6 2.5 %collective-permute-start.5 = (bf16[2,128,256]{2,1,0:T(8,128)(2,1)S(1)}, bf16[2,128,256]{2,1,0:T(8,128)(2,1)S(1)}, u32[]{:S(2)}, u32[]{:S(2)}) collective-permute-start(bf16[2,128,256]{2,1,0:T(8,128)(2,1)S(1)} %pad_maximum_fusion.2), channel_id=1, source_target_pairs={{0,8},{1,9},{2,10},{3,11},{4,12},{5,13},{6,14},{7,15},{8,0},{9,1},... | collective-permute-start | bytes 393224 | tf_op jit(solution)/shard_map/ppermute | solution.py:25
  27.1 0.0 collective-permute-done.6
  27.1 1.2 %collective-permute-start.4 = (bf16[2,128,256]{2,1,0:T(8,128)(2,1)S(1)}, bf16[2,128,256]{2,1,0:T(8,128)(2,1)S(1)}, u32[]{:S(2)}, u32[]{:S(2)}) collective-permute-start(bf16[2,128,256]{2,1,0:T(8,128)(2,1)S(1)} %pad_maximum_fusion.2), channel_id=1, source_target_pairs={{0,12},{1,13},{2,14},{3,15},{4,0},{5,1},{6,2},{7,3},{8,4},{9,5},{1... | collective-permute-start | bytes 393224 | tf_op jit(solution)/shard_map/ppermute | solution.py:25
  28.2 1.7 %collective-permute-done.5 = bf16[2,128,256]{2,1,0:T(8,128)(2,1)S(1)} collective-permute-done((bf16[2,128,256]{2,1,0:T(8,128)(2,1)S(1)}, bf16[2,128,256]{2,1,0:T(8,128)(2,1)S(1)}, u32[]{:S(2)}, u32[]{:S(2)}) %collective-permute-start.5) | collective-permute-done | bytes 131104 | tf_op jit(solution)/shard_map/ppermute | solution.py:25
  29.9 0.9 %collective-permute-done.4 = bf16[2,128,256]{2,1,0:T(8,128)(2,1)S(1)} collective-permute-done((bf16[2,128,256]{2,1,0:T(8,128)(2,1)S(1)}, bf16[2,128,256]{2,1,0:T(8,128)(2,1)S(1)}, u32[]{:S(2)}, u32[]{:S(2)}) %collective-permute-start.4) | collective-permute-done | bytes 131104 | tf_op jit(solution)/shard_map/ppermute | solution.py:25
  30.9 0.1 pad_maximum_fusion
  31.0 0.0 collective-permute-done.7.refs_5_
  31.0 2.4 %collective-permute-done.8.refs_4_ = bf16[4,128,256]{2,1,0:T(8,128)(2,1)S(1)} collective-permute-done((bf16[4,128,256]{2,1,0:T(8,128)(2,1)S(1)}, bf16[4,128,256]{2,1,0:T(8,128)(2,1)S(1)}, u32[]{:S(2)}, u32[]{:S(2)}) %collective-permute-start.8) | collective-permute-done | bytes 262176 | tf_op jit(solution)/shard_map/ppermute | solution.py:25
  33.4 3.0 %collective-permute-start.10 = (bf16[2,4,128,256]{3,2,1,0:T(8,128)(2,1)S(1)}, bf16[2,4,128,256]{3,2,1,0:T(8,128)(2,1)S(1)}, u32[]{:S(2)}, u32[]{:S(2)}) collective-permute-start(bf16[2,4,128,256]{3,2,1,0:T(8,128)(2,1)S(1)} %pad_maximum_fusion), channel_id=1, source_target_pairs={{0,1},{1,0},{2,3},{3,2},{4,5},{5,4},{6,7},{7,6},{8,9},{9,8},{10,11... | collective-permute-start | bytes 1572872 | tf_op jit(solution)/shard_map/ppermute | solution.py:34
  36.5 1.5 %collective-permute-done.10 = bf16[2,4,128,256]{3,2,1,0:T(8,128)(2,1)S(1)} collective-permute-done((bf16[2,4,128,256]{3,2,1,0:T(8,128)(2,1)S(1)}, bf16[2,4,128,256]{3,2,1,0:T(8,128)(2,1)S(1)}, u32[]{:S(2)}, u32[]{:S(2)}) %collective-permute-start.10) | collective-permute-done | bytes 524320 | tf_op jit(solution)/shard_map/ppermute | solution.py:34
  38.0 3.9 %shard_map.76 = (f32[136,512]{1,0:T(8,128)S(1)}, f32[136,512]{1,0:T(8,128)S(1)}, f32[136,512]{1,0:T(8,128)S(1)}) custom-call(bf16[4,128,256]{2,1,0:T(8,128)(2,1)S(1)} %get-tuple-element.47.refs_0_, bf16[4,128,256]{2,1,0:T(8,128)(2,1)S(1)} %get-tuple-element.48.refs_1_, bf16[4,128,256]{2,1,0:T(8,128)(2,1)S(1)} %get-tuple-element.49.refs_2_.refs_0_, ...), custom_call_target="tpu_custom_call" | custom-call | flops 1610612736 | bytes 2670592 | tf_op jit(solution)/shard_map/pallas_call | solution.py:226
  42.0 1.1 %collective-permute-start.11 = (f32[136,512]{1,0:T(8,128)S(1)}, f32[136,512]{1,0:T(8,128)S(1)}, u32[]{:S(2)}, u32[]{:S(2)}) collective-permute-start(f32[136,512]{1,0:T(8,128)S(1)} %get-tuple-element.52), channel_id=1, source_target_pairs={{0,64},{16,80},{32,96},{48,112},{64,128},{80,144},{96,160},{112,17... | collective-permute-start | bytes 835592 | tf_op jit(solution)/shard_map/ppermute | solution.py:25
  43.1 2.1 %collective-permute-start.12 = (f32[136,512]{1,0:T(8,128)S(1)}, f32[136,512]{1,0:T(8,128)S(1)}, u32[]{:S(2)}, u32[]{:S(2)}) collective-permute-start(f32[136,512]{1,0:T(8,128)S(1)} %get-tuple-element.53), channel_id=1, source_target_pairs={{0,128},{16,144},{32,160},{48,176},{64,192},{80,208},{96,224},{112... | collective-permute-start | bytes 835592 | tf_op jit(solution)/shard_map/ppermute | solution.py:25
  45.2 1.4 %collective-permute-start.13 = (f32[136,512]{1,0:T(8,128)S(1)}, f32[136,512]{1,0:T(8,128)S(1)}, u32[]{:S(2)}, u32[]{:S(2)}) collective-permute-start(f32[136,512]{1,0:T(8,128)S(1)} %get-tuple-element.54), channel_id=1, source_target_pairs={{0,192},{16,208},{32,224},{48,240},{64,0},{80,16},{96,32},{112,48}... | collective-permute-start | bytes 835592 | tf_op jit(solution)/shard_map/ppermute | solution.py:25
  46.6 2.8 %shard_map.79 = f32[2,136,512]{2,1,0:T(8,128)S(1)} custom-call(bf16[4,128,256]{2,1,0:T(8,128)(2,1)S(1)} %get-tuple-element.49.refs_2_.refs_0_, bf16[4,128,256]{2,1,0:T(8,128)(2,1)S(1)} %get-tuple-element.50.refs_3_.refs_1_, bf16[4,128,256]{2,1,0:T(8,128)(2,1)S(1)} %pad_maximum_fusion.1.refs_4_.refs_2_, ...), custom_call_target="tpu_custom_call" | custom-call | flops 1073741824 | bytes 2129920 | tf_op jit(solution)/shard_map/pallas_call | solution.py:226
  49.4 1.3 %collective-permute-start.14 = (f32[2,136,512]{2,1,0:T(8,128)S(1)}, f32[2,136,512]{2,1,0:T(8,128)S(1)}, u32[]{:S(2)}, u32[]{:S(2)}) collective-permute-start(f32[2,136,512]{2,1,0:T(8,128)S(1)} %shard_map.79), channel_id=1, source_target_pairs={{0,1},{1,0},{2,3},{3,2},{4,5},{5,4},{6,7},{7,6},{8,9},{9,8},{10,11... | collective-permute-start | bytes 1671176 | tf_op jit(solution)/shard_map/ppermute | solution.py:34
  50.7 2.8 %shard_map.80.refs_1_ = f32[2,136,512]{2,1,0:T(8,128)S(1)} custom-call(bf16[4,128,256]{2,1,0:T(8,128)(2,1)S(1)} %get-tuple-element.47.refs_0_, bf16[4,128,256]{2,1,0:T(8,128)(2,1)S(1)} %get-tuple-element.48.refs_1_, bf16[4,128,256]{2,1,0:T(8,128)(2,1)S(1)} %pad_maximum_fusion.1.refs_4_.refs_2_, ...), custom_call_target="tpu_custom_call" | custom-call | flops 21474836480 | bytes 2129920 | tf_op jit(solution)/shard_map/pallas_call | solution.py:226
  53.5 0.0 collective-permute-done.14.refs_0_
  53.5 0.1 shard_map.81
  53.6 1.3 %collective-permute-start.15 = (f32[136,256]{1,0:T(8,128)S(1)}, f32[136,256]{1,0:T(8,128)S(1)}, u32[]{:S(2)}, u32[]{:S(2)}) collective-permute-start(f32[136,256]{1,0:T(8,128)S(1)} %get-tuple-element.58), channel_id=1, source_target_pairs={{0,4},{1,5},{2,6},{3,7},{4,8},{5,9},{6,10},{7,11},{8,12},{9,13},{1... | collective-permute-start | bytes 417800 | tf_op jit(solution)/shard_map/ppermute | solution.py:25
  54.9 1.5 %collective-permute-start.16 = (f32[136,256]{1,0:T(8,128)S(1)}, f32[136,256]{1,0:T(8,128)S(1)}, u32[]{:S(2)}, u32[]{:S(2)}) collective-permute-start(f32[136,256]{1,0:T(8,128)S(1)} %get-tuple-element.59), channel_id=1, source_target_pairs={{0,8},{1,9},{2,10},{3,11},{4,12},{5,13},{6,14},{7,15},{8,0},{9,1},... | collective-permute-start | bytes 417800 | tf_op jit(solution)/shard_map/ppermute | solution.py:25
  56.3 0.0 collective-permute-done.11.refs_1_
  56.3 1.9 %collective-permute-start.17 = (f32[136,256]{1,0:T(8,128)S(1)}, f32[136,256]{1,0:T(8,128)S(1)}, u32[]{:S(2)}, u32[]{:S(2)}) collective-permute-start(f32[136,256]{1,0:T(8,128)S(1)} %get-tuple-element.60), channel_id=1, source_target_pairs={{0,12},{1,13},{2,14},{3,15},{4,0},{5,1},{6,2},{7,3},{8,4},{9,5},{1... | collective-permute-start | bytes 417800 | tf_op jit(solution)/shard_map/ppermute | solution.py:25
  58.2 1.6 %shard_map.77.refs_0_ = f32[136,512]{1,0:T(8,128)S(1)} custom-call(bf16[4,128,256]{2,1,0:T(8,128)(2,1)S(1)} %get-tuple-element.47.refs_0_, bf16[4,128,256]{2,1,0:T(8,128)(2,1)S(1)} %get-tuple-element.48.refs_1_, bf16[4,128,256]{2,1,0:T(8,128)(2,1)S(1)} %get-tuple-element.49.refs_2_.refs_0_, bf16[4,128,256]{2,1,0:T(8,128)(2,1)S(1)} %get-tuple-element.50.refs_3_.refs_1_, ...), custom_call_target="tpu_custom_call" | custom-call | flops 536870912 | bytes 1589248 | tf_op jit(solution)/shard_map/pallas_call | solution.py:226
  59.8 0.0 collective-permute-done.12.refs_2_
  59.8 0.1 shard_map.78
  59.9 4.1 %collective-permute-start.20 = (f32[136,128]{1,0:T(8,128)S(1)}, f32[136,128]{1,0:T(8,128)S(1)}, u32[]{:S(2)}, u32[]{:S(2)}) collective-permute-start(f32[136,128]{1,0:T(8,128)S(1)} %get-tuple-element.66), channel_id=1, source_target_pairs={{0,32},{16,48},{32,0},{48,16},{64,96},{80,112},{96,64},{112,80},{1... | collective-permute-start | bytes 208904 | tf_op jit(solution)/shard_map/ppermute | solution.py:30
  64.0 0.0 collective-permute-done.15.refs_1_
  64.1 0.1 shard_map.82
  64.1 0.9 %collective-permute-start.18 = (f32[136,128]{1,0:T(8,128)S(1)}, f32[136,128]{1,0:T(8,128)S(1)}, u32[]{:S(2)}, u32[]{:S(2)}) collective-permute-start(f32[136,128]{1,0:T(8,128)S(1)} %get-tuple-element.63), channel_id=1, source_target_pairs={{0,2},{1,3},{2,0},{3,1},{4,6},{5,7},{6,4},{7,5},{8,10},{9,11},{10,... | collective-permute-start | bytes 208904 | tf_op jit(solution)/shard_map/ppermute | solution.py:34
  65.1 0.3 collective-permute-start.19
  65.3 3.3 %collective-permute-start.21 = (f32[136,128]{1,0:T(8,128)S(1)}, f32[136,128]{1,0:T(8,128)S(1)}, u32[]{:S(2)}, u32[]{:S(2)}) collective-permute-start(f32[136,128]{1,0:T(8,128)S(1)} %get-tuple-element.67), channel_id=1, source_target_pairs={{0,48},{16,0},{32,16},{48,32},{64,112},{80,64},{96,80},{112,96},{1... | collective-permute-start | bytes 208904 | tf_op jit(solution)/shard_map/ppermute | solution.py:30
  68.7 4.1 %collective-permute-done.19.refs_3_ = f32[136,128]{1,0:T(8,128)S(1)} collective-permute-done((f32[136,128]{1,0:T(8,128)S(1)}, f32[136,128]{1,0:T(8,128)S(1)}, u32[]{:S(2)}, u32[]{:S(2)}) %collective-permute-start.19) | collective-permute-done | bytes 69664 | tf_op jit(solution)/shard_map/ppermute | solution.py:30
  72.8 0.8 %shard_map.83 = (f32[128,128]{1,0:T(8,128)}, f32[2,128]{1,0:T(2,128)}, f32[128,128]{1,0:T(8,128)}, f32[2,128]{1,0:T(2,128)}) custom-call(f32[136,128]{1,0:T(8,128)S(1)} %get-tuple-element.62.refs_0_, f32[136,128]{1,0:T(8,128)S(1)} %collective-permute-done.18.refs_1_, f32[136,128]{1,0:T(8,128)S(1)} %get-tuple-element.64.refs_2_, ...), custom_call_target="tpu_custom_call" | custom-call | bytes 550912 | tf_op jit(solution)/shard_map/pallas_call | solution.py:226
  (12 shorter events, 0.1 us)
Async XLA Ops:
  2.3 12.1 %collective-permute-start = (bf16[128,256]{1,0:T(8,128)(2,1)}, bf16[128,256]{1,0:T(8,128)(2,1)S(1)}, u32[]{:S(2)}, u32[]{:S(2)}) collective-permute-start(bf16[128,256]{1,0:T(8,128)(2,1)} %get-tuple-element.36), channel_id=1, source_target_pairs={{0,2},{1,3},{2,0},{3,1},{4,6},{5,7},{6,4},{7,5},{8,10},{9,11},{10,... | collective-permute-start | bytes 196616 | tf_op jit(solution)/shard_map/ppermute | solution.py:34
  4.9 10.5 %collective-permute-start.3 = (bf16[128,256]{1,0:T(8,128)(2,1)}, bf16[128,256]{1,0:T(8,128)(2,1)S(1)}, u32[]{:S(2)}, u32[]{:S(2)}) collective-permute-start(bf16[128,256]{1,0:T(8,128)(2,1)} %get-tuple-element.37), channel_id=1, source_target_pairs={{0,16},{16,32},{32,48},{48,0},{64,80},{80,96},{96,112},{112,64},{1... | collective-permute-start | bytes 196616 | tf_op jit(solution)/shard_map/ppermute | solution.py:30
  7.9 9.4 %collective-permute-start.2 = (bf16[128,256]{1,0:T(8,128)(2,1)}, bf16[128,256]{1,0:T(8,128)(2,1)S(1)}, u32[]{:S(2)}, u32[]{:S(2)}) collective-permute-start(bf16[128,256]{1,0:T(8,128)(2,1)} %get-tuple-element.37), channel_id=1, source_target_pairs={{0,32},{16,48},{32,0},{48,16},{64,96},{80,112},{96,64},{112,80},{1... | collective-permute-start | bytes 196616 | tf_op jit(solution)/shard_map/ppermute | solution.py:30
  12.1 6.2 %collective-permute-start.1 = (bf16[128,256]{1,0:T(8,128)(2,1)}, bf16[128,256]{1,0:T(8,128)(2,1)S(1)}, u32[]{:S(2)}, u32[]{:S(2)}) collective-permute-start(bf16[128,256]{1,0:T(8,128)(2,1)} %get-tuple-element.37), channel_id=1, source_target_pairs={{0,48},{16,0},{32,16},{48,32},{64,112},{80,64},{96,80},{112,96},{1... | collective-permute-start | bytes 196616 | tf_op jit(solution)/shard_map/ppermute | solution.py:30
  14.5 3.8 %copy-start = (bf16[128,256]{1,0:T(8,128)(2,1)S(1)}, bf16[128,256]{1,0:T(8,128)(2,1)}, u32[]{:S(2)}) copy-start(bf16[128,256]{1,0:T(8,128)(2,1)} %get-tuple-element.37) | copy-start | bytes 196612
  18.3 8.7 %collective-permute-start.6 = (bf16[2,128,256]{2,1,0:T(8,128)(2,1)S(1)}, bf16[2,128,256]{2,1,0:T(8,128)(2,1)S(1)}, u32[]{:S(2)}, u32[]{:S(2)}) collective-permute-start(bf16[2,128,256]{2,1,0:T(8,128)(2,1)S(1)} %pad_maximum_fusion.2), channel_id=1, source_target_pairs={{0,4},{1,5},{2,6},{3,7},{4,8},{5,9},{6,10},{7,11},{8,12},{9,13},{1... | collective-permute-start | bytes 393224 | tf_op jit(solution)/shard_map/ppermute | solution.py:25
  19.6 11.3 %collective-permute-start.7 = (bf16[4,128,256]{2,1,0:T(8,128)(2,1)S(1)}, bf16[4,128,256]{2,1,0:T(8,128)(2,1)S(1)}, u32[]{:S(2)}, u32[]{:S(2)}) collective-permute-start(bf16[4,128,256]{2,1,0:T(8,128)(2,1)S(1)} %pad_maximum_fusion.1.refs_4_.refs_2_), channel_id=1, source_target_pairs={{0,64},{16,80},{32,96},{48,112},{64,128},{80,144},{96,160},{112,17... | collective-permute-start | bytes 786440 | tf_op jit(solution)/shard_map/ppermute | solution.py:25
  20.9 12.5 %collective-permute-start.8 = (bf16[4,128,256]{2,1,0:T(8,128)(2,1)S(1)}, bf16[4,128,256]{2,1,0:T(8,128)(2,1)S(1)}, u32[]{:S(2)}, u32[]{:S(2)}) collective-permute-start(bf16[4,128,256]{2,1,0:T(8,128)(2,1)S(1)} %pad_maximum_fusion.1.refs_4_.refs_2_), channel_id=1, source_target_pairs={{0,128},{16,144},{32,160},{48,176},{64,192},{80,208},{96,224},{112... | collective-permute-start | bytes 786440 | tf_op jit(solution)/shard_map/ppermute | solution.py:25
  23.5 9.9 %collective-permute-start.9 = (bf16[4,128,256]{2,1,0:T(8,128)(2,1)S(1)}, bf16[4,128,256]{2,1,0:T(8,128)(2,1)S(1)}, u32[]{:S(2)}, u32[]{:S(2)}) collective-permute-start(bf16[4,128,256]{2,1,0:T(8,128)(2,1)S(1)} %pad_maximum_fusion.1.refs_4_.refs_2_), channel_id=1, source_target_pairs={{0,192},{16,208},{32,224},{48,240},{64,0},{80,16},{96,32},{112,48}... | collective-permute-start | bytes 786440 | tf_op jit(solution)/shard_map/ppermute | solution.py:25
  24.6 5.3 %collective-permute-start.5 = (bf16[2,128,256]{2,1,0:T(8,128)(2,1)S(1)}, bf16[2,128,256]{2,1,0:T(8,128)(2,1)S(1)}, u32[]{:S(2)}, u32[]{:S(2)}) collective-permute-start(bf16[2,128,256]{2,1,0:T(8,128)(2,1)S(1)} %pad_maximum_fusion.2), channel_id=1, source_target_pairs={{0,8},{1,9},{2,10},{3,11},{4,12},{5,13},{6,14},{7,15},{8,0},{9,1},... | collective-permute-start | bytes 393224 | tf_op jit(solution)/shard_map/ppermute | solution.py:25
  27.1 3.8 %collective-permute-start.4 = (bf16[2,128,256]{2,1,0:T(8,128)(2,1)S(1)}, bf16[2,128,256]{2,1,0:T(8,128)(2,1)S(1)}, u32[]{:S(2)}, u32[]{:S(2)}) collective-permute-start(bf16[2,128,256]{2,1,0:T(8,128)(2,1)S(1)} %pad_maximum_fusion.2), channel_id=1, source_target_pairs={{0,12},{1,13},{2,14},{3,15},{4,0},{5,1},{6,2},{7,3},{8,4},{9,5},{1... | collective-permute-start | bytes 393224 | tf_op jit(solution)/shard_map/ppermute | solution.py:25
  33.4 4.5 %collective-permute-start.10 = (bf16[2,4,128,256]{3,2,1,0:T(8,128)(2,1)S(1)}, bf16[2,4,128,256]{3,2,1,0:T(8,128)(2,1)S(1)}, u32[]{:S(2)}, u32[]{:S(2)}) collective-permute-start(bf16[2,4,128,256]{3,2,1,0:T(8,128)(2,1)S(1)} %pad_maximum_fusion), channel_id=1, source_target_pairs={{0,1},{1,0},{2,3},{3,2},{4,5},{5,4},{6,7},{7,6},{8,9},{9,8},{10,11... | collective-permute-start | bytes 1572872 | tf_op jit(solution)/shard_map/ppermute | solution.py:34
  42.0 14.3 %collective-permute-start.11 = (f32[136,512]{1,0:T(8,128)S(1)}, f32[136,512]{1,0:T(8,128)S(1)}, u32[]{:S(2)}, u32[]{:S(2)}) collective-permute-start(f32[136,512]{1,0:T(8,128)S(1)} %get-tuple-element.52), channel_id=1, source_target_pairs={{0,64},{16,80},{32,96},{48,112},{64,128},{80,144},{96,160},{112,17... | collective-permute-start | bytes 835592 | tf_op jit(solution)/shard_map/ppermute | solution.py:25
  43.1 16.7 %collective-permute-start.12 = (f32[136,512]{1,0:T(8,128)S(1)}, f32[136,512]{1,0:T(8,128)S(1)}, u32[]{:S(2)}, u32[]{:S(2)}) collective-permute-start(f32[136,512]{1,0:T(8,128)S(1)} %get-tuple-element.53), channel_id=1, source_target_pairs={{0,128},{16,144},{32,160},{48,176},{64,192},{80,208},{96,224},{112... | collective-permute-start | bytes 835592 | tf_op jit(solution)/shard_map/ppermute | solution.py:25
  45.2 14.6 %collective-permute-start.13 = (f32[136,512]{1,0:T(8,128)S(1)}, f32[136,512]{1,0:T(8,128)S(1)}, u32[]{:S(2)}, u32[]{:S(2)}) collective-permute-start(f32[136,512]{1,0:T(8,128)S(1)} %get-tuple-element.54), channel_id=1, source_target_pairs={{0,192},{16,208},{32,224},{48,240},{64,0},{80,16},{96,32},{112,48}... | collective-permute-start | bytes 835592 | tf_op jit(solution)/shard_map/ppermute | solution.py:25
  49.4 4.1 %collective-permute-start.14 = (f32[2,136,512]{2,1,0:T(8,128)S(1)}, f32[2,136,512]{2,1,0:T(8,128)S(1)}, u32[]{:S(2)}, u32[]{:S(2)}) collective-permute-start(f32[2,136,512]{2,1,0:T(8,128)S(1)} %shard_map.79), channel_id=1, source_target_pairs={{0,1},{1,0},{2,3},{3,2},{4,5},{5,4},{6,7},{7,6},{8,9},{9,8},{10,11... | collective-permute-start | bytes 1671176 | tf_op jit(solution)/shard_map/ppermute | solution.py:34
  53.6 10.5 %collective-permute-start.15 = (f32[136,256]{1,0:T(8,128)S(1)}, f32[136,256]{1,0:T(8,128)S(1)}, u32[]{:S(2)}, u32[]{:S(2)}) collective-permute-start(f32[136,256]{1,0:T(8,128)S(1)} %get-tuple-element.58), channel_id=1, source_target_pairs={{0,4},{1,5},{2,6},{3,7},{4,8},{5,9},{6,10},{7,11},{8,12},{9,13},{1... | collective-permute-start | bytes 417800 | tf_op jit(solution)/shard_map/ppermute | solution.py:25
  54.9 9.2 %collective-permute-start.16 = (f32[136,256]{1,0:T(8,128)S(1)}, f32[136,256]{1,0:T(8,128)S(1)}, u32[]{:S(2)}, u32[]{:S(2)}) collective-permute-start(f32[136,256]{1,0:T(8,128)S(1)} %get-tuple-element.59), channel_id=1, source_target_pairs={{0,8},{1,9},{2,10},{3,11},{4,12},{5,13},{6,14},{7,15},{8,0},{9,1},... | collective-permute-start | bytes 417800 | tf_op jit(solution)/shard_map/ppermute | solution.py:25
  56.3 7.8 %collective-permute-start.17 = (f32[136,256]{1,0:T(8,128)S(1)}, f32[136,256]{1,0:T(8,128)S(1)}, u32[]{:S(2)}, u32[]{:S(2)}) collective-permute-start(f32[136,256]{1,0:T(8,128)S(1)} %get-tuple-element.60), channel_id=1, source_target_pairs={{0,12},{1,13},{2,14},{3,15},{4,0},{5,1},{6,2},{7,3},{8,4},{9,5},{1... | collective-permute-start | bytes 417800 | tf_op jit(solution)/shard_map/ppermute | solution.py:25
  59.9 8.7 %collective-permute-start.20 = (f32[136,128]{1,0:T(8,128)S(1)}, f32[136,128]{1,0:T(8,128)S(1)}, u32[]{:S(2)}, u32[]{:S(2)}) collective-permute-start(f32[136,128]{1,0:T(8,128)S(1)} %get-tuple-element.66), channel_id=1, source_target_pairs={{0,32},{16,48},{32,0},{48,16},{64,96},{80,112},{96,64},{112,80},{1... | collective-permute-start | bytes 208904 | tf_op jit(solution)/shard_map/ppermute | solution.py:30
  64.1 4.5 %collective-permute-start.18 = (f32[136,128]{1,0:T(8,128)S(1)}, f32[136,128]{1,0:T(8,128)S(1)}, u32[]{:S(2)}, u32[]{:S(2)}) collective-permute-start(f32[136,128]{1,0:T(8,128)S(1)} %get-tuple-element.63), channel_id=1, source_target_pairs={{0,2},{1,3},{2,0},{3,1},{4,6},{5,7},{6,4},{7,5},{8,10},{9,11},{10,... | collective-permute-start | bytes 208904 | tf_op jit(solution)/shard_map/ppermute | solution.py:34
  65.1 7.7 %collective-permute-start.19 = (f32[136,128]{1,0:T(8,128)S(1)}, f32[136,128]{1,0:T(8,128)S(1)}, u32[]{:S(2)}, u32[]{:S(2)}) collective-permute-start(f32[136,128]{1,0:T(8,128)S(1)} %get-tuple-element.65), channel_id=1, source_target_pairs={{0,16},{16,32},{32,48},{48,0},{64,80},{80,96},{96,112},{112,64},{1... | collective-permute-start | bytes 208904 | tf_op jit(solution)/shard_map/ppermute | solution.py:30
  65.3 7.4 %collective-permute-start.21 = (f32[136,128]{1,0:T(8,128)S(1)}, f32[136,128]{1,0:T(8,128)S(1)}, u32[]{:S(2)}, u32[]{:S(2)}) collective-permute-start(f32[136,128]{1,0:T(8,128)S(1)} %get-tuple-element.67), channel_id=1, source_target_pairs={{0,48},{16,0},{32,16},{48,32},{64,112},{80,64},{96,80},{112,96},{1... | collective-permute-start | bytes 208904 | tf_op jit(solution)/shard_map/ppermute | solution.py:30
